TPU v7x, 128 devices: a whole 4x4x4 slice. The times are simulated.
128 devices in a mesh: tile: 32 (over z, y, core), date: 4 (over x).
Axes of the slice: x: 4, y: 4, z: 4, core: 2. Of those that a mesh axis runs over, the one named last changes fastest.
Arguments:
- complex_images: bfloat16 [8, 32, 32, 2, 10, 1920], P('date', 'tile')
- segment_position_map: int32 [32, 32], P('tile'), may hold values from 0 to 31, each once within a row
- usable_position_total: int32 [32], P('tile'), may hold values from 16 to 32
- interferogram_epochs: int32 [16, 2], replicated, may hold values from 0 to 7, as said below
Outputs:
- coherence: float32 [16, 2, 64, 4096], P('date', None, None, 'tile')
Inputs may be any that keep to these rules, and one draw needn't show every extreme that they name: Each row of segment_position_map names every block position once. `interferogram_epochs`: the two dates of a pair differ.
All inputs are finite; a program needn't handle non-finite values.
Results may differ from a plain program's by a relative error of at most 0.0003.
Values may be sent and summed in bfloat16 or wider, within the bound.
No kernel may reach another device: no remote copies, remote signals or barrier semaphores. Data moves between devices by JAX's collectives and lax.ppermute only.
A program may use at most 128 MiB of HBM per device.

v0:
```python
import jax
import jax.numpy as jnp
from jax import lax
from jax.sharding import PartitionSpec as P

LOOK_RG = 15
LOOK_AZ = 5


EPS = 1e-05


def tile_looks(stack, first_idx, second_idx, valid, box):
    scale = 1.0 / (LOOK_AZ * LOOK_RG)

    def looks(values):
        ranged = jnp.dot(
            values, box, precision=lax.Precision.HIGHEST, preferred_element_type=jnp.float32
        )
        extent = ranged.shape
        return (
            ranged.reshape(extent[:-2] + (extent[-2] // LOOK_AZ, LOOK_AZ, extent[-1])).sum(axis=-2)
            * scale
        )

    def date_power(image):
        image = image.astype(jnp.float32)
        return looks(image[:, 0] * image[:, 0] + image[:, 1] * image[:, 1])

    power = lax.map(date_power, stack)

    def one_pair(indices):
        first = lax.dynamic_index_in_dim(stack, indices[0], 0, keepdims=False).astype(jnp.float32)
        second = lax.dynamic_index_in_dim(stack, indices[1], 0, keepdims=False).astype(jnp.float32)
        cross_re = looks(first[:, 0] * second[:, 0] + first[:, 1] * second[:, 1])
        cross_im = looks(first[:, 1] * second[:, 0] - first[:, 0] * second[:, 1])
        power_first = lax.dynamic_index_in_dim(power, indices[0], 0, keepdims=False)
        power_second = lax.dynamic_index_in_dim(power, indices[1], 0, keepdims=False)
        weight = valid[:, None, None] / jnp.sqrt((power_first + EPS) * (power_second + EPS))
        return jnp.stack([cross_re * weight, cross_im * weight], axis=0)

    return lax.map(one_pair, jnp.stack([first_idx, second_idx], axis=1))


def place_rows(gamma, positions):
    ranking = jnp.argsort(positions)
    placed = jnp.take(gamma, ranking, axis=2)
    extent = placed.shape
    return placed.reshape(extent[0], extent[1], extent[2] * extent[3], extent[4])


def on_device(complex_images, segment_position_map, usable_position_total, interferogram_epochs):
    groups = lax.axis_size("date")
    tile_cols = complex_images.shape[-1]
    box = (
        jnp.arange(tile_cols)[:, None] // LOOK_RG == jnp.arange(tile_cols // LOOK_RG)[None, :]
    ).astype(jnp.float32)
    positions = segment_position_map[0]
    moved = lax.all_to_all(complex_images, "tile", split_axis=2, concat_axis=1, tiled=True)
    stack = moved[:, :, 0]
    valid = (positions < usable_position_total[0]).astype(jnp.float32)
    gathered = lax.all_gather(stack, "date", axis=0, tiled=True)
    mine = interferogram_epochs.shape[0] // groups
    local_pairs = lax.dynamic_slice_in_dim(
        interferogram_epochs, lax.axis_index("date") * mine, mine, 0
    )
    gamma = tile_looks(gathered, local_pairs[:, 0], local_pairs[:, 1], valid, box)
    return place_rows(gamma, positions)


def solution(mesh):
    in_specs = (P("date", "tile", None, None, None, None), P("tile", None), P("tile"), P())
    out_specs = P("date", None, None, "tile")
    return jax.shard_map(
        on_device, mesh=mesh, in_specs=in_specs, out_specs=out_specs, check_vma=False
    )
```

profile of v0, /device:TPU:1, one launch (start us, length us, event | category | flops | bytes accessed | tf_op | source)
XLA Modules:
  0.0 369.3 jit_solution(17248082565630182619)
XLA Ops:
  6.5 8.0 %copy.19 = bf16[2,1,32,2,10,1920]{5,3,4,1,0,2:T(2,128)(2,1)} copy(bf16[2,1,32,2,10,1920]{5,3,4,2,1,0:T(2,128)(2,1)} %param.8) | data formatting | bytes 9830400 | tf_op args[0]
  14.5 68.1 %all_to_all.4 = bf16[2,1,32,2,10,1920]{5,3,4,1,0,2:T(2,128)(2,1)S(1)} all-to-all(bf16[2,1,32,2,10,1920]{5,3,4,1,0,2:T(2,128)(2,1)} %copy.19), channel_id=1, replica_groups=mesh['tile'=32,'date'=4] {'tile'}, dimensions={2} | all-to-all | bytes 9830400 | tf_op jit(solution)/shard_map/all_to_all | solution.py:59
  82.6 2.8 copy.20
  88.1 174.1 %all-gather.3.cloned.1.call-done = bf16[8,1,32,2,10,1920]{5,2,4,3,1,0:T(8,128)(2,1)} async-done(((bf16[2,1,32,2,10,1920]{5,2,4,3,1,0:T(8,128)(2,1)}), bf16[8,1,32,2,10,1920]{5,2,4,3,1,0:T(8,128)(2,1)}) %all-gather.3.cloned.1.call-update) | async-done | bytes 19660816 | tf_op jit(solution)/shard_map/all_gather | solution.py:62
  262.3 39.0 %while.23 = (s32[]{:T(128)}, f32[8,32,2,128]{3,1,2,0:T(8,128)S(1)}, bf16[8,32,2,10,1920]{4,1,3,2,0:T(8,128)(2,1)}, s32[1920]{0:T(1024)S(1)}, s32[]{:T(128)}) while((s32[]{:T(128)}, f32[8,32,2,128]{3,1,2,0:T(8,128)S(1)}, bf16[8,32,2,10,1920]{4,1,3,2,0:T(8,128)(2,1)}, s32[1920]{0:T(1024)S(1)}, s32[]{:T(128)}) %tuple.60), condition=%wide.region_3.4_spmd.clone, body=%wide.region_1.3_spmd.clone.sunk | while | flops 947322880 | bytes 17309252 | solution.py:30
  262.3 2.3 bitcast_convert_fusion.5
  267.1 2.3 bitcast_convert_fusion.5
  272.0 2.3 bitcast_convert_fusion.5
  276.9 2.3 bitcast_convert_fusion.5
  281.7 2.3 bitcast_convert_fusion.5
  286.6 2.3 bitcast_convert_fusion.5
  291.5 2.3 bitcast_convert_fusion.5
  296.3 2.3 bitcast_convert_fusion.5
  301.2 59.6 %while.24 = (s32[]{:T(128)}, f32[4,2,32,2,128]{4,0,3,2,1:T(4,128)S(1)}, s32[4,2]{0,1:T(2,128)S(1)}, bf16[8,32,2,10,1920]{4,1,3,2,0:T(8,128)(2,1)}, f32[32]{0:T(1...) while((s32[]{:T(128)}, ...), condition=%wide.region_7.8_spmd.clone.clone, body=%wide.region_4.7_spmd.clone.clone.sunk | while | flops 1894711296 | bytes 35077472 | solution.py:42
  305.6 3.7 %bitcast_convert_fusion.6 = (f32[32,2,10,1920]{3,0,2,1:T(8,128)S(1)}, f32[32,2,10,1920]{3,0,2,1:T(8,128)S(1)}) fusion(bf16[8,32,2,10,1920]{4,1,3,2,0:T(8,128)(2,1)} %get-tuple-element.269, s32[]{:T(128)S(6)} %select_n.52, s32[]{:T(128)S(6)} %select_n.53), kind=kLoop, calls=%fused_computation.14.clone.1 | loop fusion | flops 2457600 | bytes 14745608 | tf_op jit(solution)/shard_map/while/body/eval_jaxpr/convert_element_type | solution.py:33
  310.1 2.2 convolution_reduce_fusion.7
  312.3 2.2 convolution_reduce_fusion.8
  320.5 3.7 %bitcast_convert_fusion.6 = (f32[32,2,10,1920]{3,0,2,1:T(8,128)S(1)}, f32[32,2,10,1920]{3,0,2,1:T(8,128)S(1)}) fusion(bf16[8,32,2,10,1920]{4,1,3,2,0:T(8,128)(2,1)} %get-tuple-element.269, s32[]{:T(128)S(6)} %select_n.52, s32[]{:T(128)S(6)} %select_n.53), kind=kLoop, calls=%fused_computation.14.clone.1 | loop fusion | flops 2457600 | bytes 14745608 | tf_op jit(solution)/shard_map/while/body/eval_jaxpr/convert_element_type | solution.py:33
  325.0 2.2 convolution_reduce_fusion.7
  327.2 2.2 convolution_reduce_fusion.8
  335.4 3.7 %bitcast_convert_fusion.6 = (f32[32,2,10,1920]{3,0,2,1:T(8,128)S(1)}, f32[32,2,10,1920]{3,0,2,1:T(8,128)S(1)}) fusion(bf16[8,32,2,10,1920]{4,1,3,2,0:T(8,128)(2,1)} %get-tuple-element.269, s32[]{:T(128)S(6)} %select_n.52, s32[]{:T(128)S(6)} %select_n.53), kind=kLoop, calls=%fused_computation.14.clone.1 | loop fusion | flops 2457600 | bytes 14745608 | tf_op jit(solution)/shard_map/while/body/eval_jaxpr/convert_element_type | solution.py:33
  339.9 2.2 convolution_reduce_fusion.7
  342.1 2.2 convolution_reduce_fusion.8
  350.3 3.7 %bitcast_convert_fusion.6 = (f32[32,2,10,1920]{3,0,2,1:T(8,128)S(1)}, f32[32,2,10,1920]{3,0,2,1:T(8,128)S(1)}) fusion(bf16[8,32,2,10,1920]{4,1,3,2,0:T(8,128)(2,1)} %get-tuple-element.269, s32[]{:T(128)S(6)} %select_n.52, s32[]{:T(128)S(6)} %select_n.53), kind=kLoop, calls=%fused_computation.14.clone.1 | loop fusion | flops 2457600 | bytes 14745608 | tf_op jit(solution)/shard_map/while/body/eval_jaxpr/convert_element_type | solution.py:33
  (75 shorter events, 40.1 us)
Async XLA Ops:
  6.5 81.5 %copy-start = (s32[16,2]{0,1:T(2,128)S(1)}, s32[16,2]{0,1:T(2,128)}, u32[]{:S(2)}) copy-start(s32[16,2]{0,1:T(2,128)} %param.11) | copy-start | bytes 388
  6.5 255.7 %all-gather.3.cloned.1.call-start = ((), (), s32[]{:S(2)}) async-start(), calls=%async_computation.1 | async-start | bytes 24576000 | tf_op jit(solution)/shard_map/all_gather | solution.py:62
  85.4 0.7 copy-start.1
Sparse Core Ops, SparseCore 0:
  85.6 176.6 all-gather.2
where the time goes:
time: 370 us; the launch traced here: 369 us
  waiting for transfers between devices  174 us (47%)
  blocking collectives  68.1 us (18%)
  other arithmetic  41.7 us (11%)
  matrix products  35.6 us (10%)
  local copies, waits for them, and re-layouts  20.2 us (5%)
  loops' own time  15.4 us (4%)
  between operations  14.1 us (4%)
    all_gather x1, waiting for transfers between devices, on_device(): gathered = lax.all_gather(stack, 'date', axis=0, tiled=True)  174 us
    all_to_all x1, blocking collectives, on_device(): lax.all_to_all(complex_images, 'tile', split_axis=2, concat_axis=1, tiled...  68.1 us
    dot_general x16, matrix products, looks(): jnp.dot(values, box, precision=lax.Precision.HIGHEST, preferred_element_t...  35.6 us
    convert_element_type x8, other arithmetic, date_power(): image = image.astype(jnp.float32)  18.4 us
    another operation x1, loops' own time, tile_looks(): return lax.map(one_pair, jnp.stack([first_idx, second_idx], axis=1))  15 us
    convert_element_type x4, other arithmetic, one_pair(): lax.dynamic_index_in_dim(stack, indices[0], 0, keepdims=False)  14.9 us
    unnamed x5, local copies, waits for them, and re-layouts  7.98 us
  transfers between devices with their start and end apart: 1, of which 1 were waited for; matrix products, arithmetic and copies ran while one was open for 1% of the time, Pallas kernels for 0%

commit v1 on v0

v1 whole, which is shorter than its diff:
```python
import functools

import jax
import jax.numpy as jnp
from jax import lax
from jax.experimental import pallas as pl
from jax.experimental.pallas import tpu as pltpu
from jax.sharding import PartitionSpec as P

LOOK_RG = 15
LOOK_AZ = 5
EPS = 1e-05
SCALE = 1.0 / (LOOK_AZ * LOOK_RG)
DATES = 8
PAIRS = 16
ITEMS = 8
RG = 1920
LCOL = 128


def look_kernel(info, own, one, two, three, box, out, img, hi, lo, sums):
    group = info[2 * PAIRS]
    for step, block in enumerate((own, one, two, three)):
        base = lax.rem(group + step, 4) * 2
        for date in range(2):
            for line in range(LOOK_AZ):
                img[base + date, line] = block[date, line].astype(jnp.float32)

    def split(values, row):
        upper = values.astype(jnp.bfloat16)
        hi[pl.ds(row, 16), :] = upper
        lo[pl.ds(row, 16), :] = (values - upper.astype(jnp.float32)).astype(jnp.bfloat16)

    def power(half, carry):
        total = []
        for date in range(2):
            acc = jnp.zeros((ITEMS, RG), jnp.float32)
            for line in range(LOOK_AZ):
                re = img[2 * half + date, line, 0:8, :]
                im = img[2 * half + date, line, 8:16, :]
                acc = acc + (re * re + im * im)
            total.append(acc)
        split(jnp.concatenate(total, axis=0), pl.multiple_of(half * 16, 16))
        return carry

    lax.fori_loop(0, DATES // 2, power, 0)

    def cross(k, carry):
        a, b = info[2 * k], info[2 * k + 1]
        acc_re = jnp.zeros((ITEMS, RG), jnp.float32)
        acc_im = jnp.zeros((ITEMS, RG), jnp.float32)
        for line in range(LOOK_AZ):
            re_a, im_a = img[a, line, 0:8, :], img[a, line, 8:16, :]
            re_b, im_b = img[b, line, 0:8, :], img[b, line, 8:16, :]
            acc_re = acc_re + (re_a * re_b + im_a * im_b)
            acc_im = acc_im + (im_a * re_b - re_a * im_b)
        split(jnp.concatenate([acc_re, acc_im], axis=0), pl.multiple_of(64 + k * 16, 16))
        return carry

    lax.fori_loop(0, PAIRS, cross, 0)
    sums[...] = (
        jnp.dot(hi[...], box[...], preferred_element_type=jnp.float32)
        + jnp.dot(lo[...], box[...], preferred_element_type=jnp.float32)
    ) * SCALE

    for owner in range(4):
        rows = []
        for kk in range(4):
            k = owner * 4 + kk
            power_a = sums[pl.ds(pl.multiple_of(info[2 * k] * 8, 8), 8), :]
            power_b = sums[pl.ds(pl.multiple_of(info[2 * k + 1] * 8, 8), 8), :]
            weight = 1.0 / jnp.sqrt((power_a + EPS) * (power_b + EPS))
            rows.append(sums[64 + k * 16 : 72 + k * 16, :] * weight)
            rows.append(sums[72 + k * 16 : 80 + k * 16, :] * weight)
        out[owner] = jnp.swapaxes(jnp.stack(rows, axis=0), 0, 1)


def place_kernel(positions, usable, got, out, rows):
    for block in range(32):
        position = positions[block]
        valid = jnp.where(position < usable[0], 1.0, 0.0).astype(jnp.float32)
        rows[pl.ds(pl.multiple_of(position * 16, 16), 16), :] = got[block] * valid
    for plane in range(8):
        for part in range(8):
            out[plane // 2, plane % 2, part * 8 : part * 8 + 8, :] = rows[
                pl.ds(part * 64 + plane, 8, stride=8), :
            ]


def on_device(complex_images, segment_position_map, usable_position_total, interferogram_epochs):
    group = lax.axis_index("date")
    images = complex_images[:, 0]

    def block_for(step):
        part = lax.dynamic_slice_in_dim(images, lax.rem(group + step, 4) * ITEMS, ITEMS, 1)
        return part.transpose(0, 3, 2, 1, 4).reshape(2, 10, 16, RG)

    def ring(step):
        return [(i, (i + step) % 4) for i in range(4)]

    own = block_for(0)
    two = lax.ppermute(block_for(2), "date", ring(2))
    three = lax.ppermute(block_for(1), "date", ring(1))
    one = lax.ppermute(block_for(3), "date", ring(3))

    box = (
        jnp.arange(RG)[:, None] // LOOK_RG == jnp.arange(LCOL)[None, :]
    ).astype(jnp.bfloat16)
    info = jnp.concatenate(
        [interferogram_epochs.reshape(-1), group.reshape(1)]
    ).astype(jnp.int32)

    block = pl.BlockSpec((2, LOOK_AZ, 16, RG), lambda r, info: (0, r, 0, 0))
    gamma = pl.pallas_call(
        look_kernel,
        out_shape=jax.ShapeDtypeStruct((4, ITEMS, 16, LCOL), jnp.float32),
        grid_spec=pltpu.PrefetchScalarGridSpec(
            num_scalar_prefetch=1,
            grid=(2,),
            in_specs=[block] * 4 + [pl.BlockSpec((RG, LCOL), lambda r, info: (0, 0))],
            out_specs=pl.BlockSpec((4, ITEMS, 8, LCOL), lambda r, info: (0, 0, r, 0)),
            scratch_shapes=[
                pltpu.VMEM((DATES, LOOK_AZ, 16, RG), jnp.float32),
                pltpu.VMEM((320, RG), jnp.bfloat16),
                pltpu.VMEM((320, RG), jnp.bfloat16),
                pltpu.VMEM((320, LCOL), jnp.float32),
            ],
        ),
        compiler_params=pltpu.CompilerParams(vmem_limit_bytes=40 << 20),
    )(info, own, one, two, three, box)

    moved = lax.all_to_all(gamma, "date", split_axis=0, concat_axis=0, tiled=True)
    moved = moved.reshape(32, 16, LCOL)
    got = lax.all_to_all(moved, "tile", split_axis=0, concat_axis=0, tiled=True)

    return pl.pallas_call(
        place_kernel,
        out_shape=jax.ShapeDtypeStruct((4, 2, 64, LCOL), jnp.float32),
        grid_spec=pltpu.PrefetchScalarGridSpec(
            num_scalar_prefetch=2,
            grid=(),
            in_specs=[pl.BlockSpec(memory_space=pltpu.VMEM)],
            out_specs=pl.BlockSpec(memory_space=pltpu.VMEM),
            scratch_shapes=[pltpu.VMEM((512, LCOL), jnp.float32)],
        ),
    )(segment_position_map[0], usable_position_total, got)


def solution(mesh):
    in_specs = (P("date", "tile", None, None, None, None), P("tile", None), P("tile"), P())
    out_specs = P("date", None, None, "tile")
    return jax.shard_map(
        on_device, mesh=mesh, in_specs=in_specs, out_specs=out_specs, check_vma=False
    )
```

time: 370 us -> 108 us (0.29)
  waiting for transfers between devices: 174 us -> 61.8 us
  blocking collectives: 68.1 us -> 9.34 us
  other arithmetic: 41.7 us -> 0.41 us
  matrix products: 35.6 us -> 0 us
  loops' own time: 15.4 us -> 0 us
  starting transfers between devices: 0.01 us -> 13.9 us
  between operations: 14.1 us -> 0.69 us
  Pallas kernels: 0 us -> 11.9 us
  local copies, waits for them, and re-layouts: 20.2 us -> 10.1 us
    all_gather x1 -> x0, waiting for transfers between devices: 174 us -> none  [on_device(): gathered = lax.all_gather(stack, 'date', axis=0, tiled=True)]
    all_to_all x1, blocking collectives: 68.1 us -> 9.34 us  [on_device(): lax.all_to_all(gamma, 'date', split_axis=0, concat_axis=0, tiled=True)]
    ppermute x0 -> x3, waiting for transfers between devices: none -> 53.5 us  [the longest x1 27.7 us: on_device(): three = lax.ppermute(block_for(1), 'date', ring(1))]
    dot_general x16 -> x0, matrix products: 35.6 us -> none  [looks(): jnp.dot(values, box, precision=lax.Precision.HIGHEST, preferred_element_t...]
    convert_element_type x13 -> x1, other arithmetic: 33.3 us -> 0.33 us  [on_device(): box = (jnp.arange(RG)[:, None] // LOOK_RG == jnp.arange(LCOL)[None, :]).a...]
    another operation x2 -> x0, loops' own time: 15.4 us -> none  [the longest x1 15 us: tile_looks(): return lax.map(one_pair, jnp.stack([first_idx, second_idx], axis=1))]
    pallas_call x0 -> x2, Pallas kernels: none -> 11.9 us  [the longest x1 9.52 us: on_device(): pl.pallas_call(look_kernel, out_shape=jax.ShapeDtypeStruct((4, ITEMS, 16,...]
    all_to_all x0 -> x1, starting transfers between devices: none -> 9.43 us  [on_device(): got = lax.all_to_all(moved, 'tile', split_axis=0, concat_axis=0, tiled=True)]
  transfers between devices with their start and end apart: 1 -> 4, of which waited for: 1 -> 4; matrix products, arithmetic and copies ran while one was open for 1% -> 3% of each run, Pallas kernels for 0% -> 0%
where the time goes in v1:
time: 108 us
  waiting for transfers between devices  61.8 us (57%)
  starting transfers between devices  13.9 us (13%)
  Pallas kernels  11.9 us (11%)
  local copies, waits for them, and re-layouts  10.1 us (9%)
  blocking collectives  9.34 us (9%)
    ppermute x1, waiting for transfers between devices, on_device(): three = lax.ppermute(block_for(1), 'date', ring(1))  27.7 us
    ppermute x1, waiting for transfers between devices, on_device(): one = lax.ppermute(block_for(3), 'date', ring(3))  22.5 us
    pallas_call x1, Pallas kernels, on_device(): pl.pallas_call(look_kernel, out_shape=jax.ShapeDtypeStruct((4, ITEMS, 16,...  9.52 us
    all_to_all x1, starting transfers between devices, on_device(): got = lax.all_to_all(moved, 'tile', split_axis=0, concat_axis=0, tiled=True)  9.43 us
    all_to_all x1, blocking collectives, on_device(): lax.all_to_all(gamma, 'date', split_axis=0, concat_axis=0, tiled=True)  9.34 us
    all_to_all x1, waiting for transfers between devices, on_device(): got = lax.all_to_all(moved, 'tile', split_axis=0, concat_axis=0, tiled=True)  8.25 us
    dynamic_slice x1, local copies, waits for them, and re-layouts, block_for(): lax.dynamic_slice_in_dim(images, lax.rem(group + step, 4) * ITEMS, ITEMS, 1)  5.05 us
    transpose x4, local copies, waits for them, and re-layouts, block_for(): return part.transpose(0, 3, 2, 1, 4).reshape(2, 10, 16, RG)  3.65 us
  transfers between devices with their start and end apart: 4, of which 4 were waited for; matrix products, arithmetic and copies ran while one was open for 3% of the time, Pallas kernels for 0%

profile of v1, /device:TPU:1, one launch (start us, length us, event | category | flops | bytes accessed | tf_op | source)
XLA Modules:
  0.0 108.1 jit_solution(11160588013703637236)
XLA Ops:
  0.0 5.1 %constant_dynamic-slice_fusion = (bf16[2,1,8,2,10,1920]{5,3,4,2,1,0:T(2,128)(2,1)S(1)}, bf16[2,1,8,2,10,1920]{5,3,4,2,1,0:T(2,128)(2,1)S(1)}, bf16[2,1,8,2,10,19...) fusion(bf16[2,1,32,2,10,1920]{5,3,4,2,1,0:T(2,128)(2,1)} %param.4, s32[]{:T(128)S(6)} %select_n.25, ...), kind=kLoop, calls=%fused_computation.13 | loop fusion | bytes 9830416 | tf_op jit(solution)/shard_map/dynamic_slice | solution.py:95
  5.1 1.2 %copy.29 = bf16[2,1,8,2,10,1920]{5,2,3,4,0,1:T(8,128)(2,1)} copy(bf16[2,1,8,2,10,1920]{5,3,4,2,1,0:T(2,128)(2,1)S(1)} %get-tuple-element.7) | data formatting | bytes 2457600 | tf_op jit(solution)/shard_map/transpose | solution.py:96
  6.2 3.3 %collective-permute-start = (bf16[2,10,16,1920]{3,2,1,0:T(8,128)(2,1)}, bf16[2,10,16,1920]{3,2,1,0:T(8,128)(2,1)S(1)}, u32[]{:S(2)}, u32[]{:S(2)}) collective-permute-start(bf16[2,10,16,1920]{3,2,1,0:T(8,128)(2,1)} %bitcast.33), channel_id=1, source_target_pairs={{0,3},{1,0},{2,1},{3,2},{4,7},{5,4},{6,5},{7,6},{8,11},{9,8},{10,9... | collective-permute-start | bytes 3686408 | tf_op jit(solution)/shard_map/ppermute | solution.py:104
  9.5 1.2 %copy.28 = bf16[2,1,8,2,10,1920]{5,2,3,4,0,1:T(8,128)(2,1)} copy(bf16[2,1,8,2,10,1920]{5,3,4,2,1,0:T(2,128)(2,1)S(1)} %get-tuple-element.6) | data formatting | bytes 2457600 | tf_op jit(solution)/shard_map/transpose | solution.py:96
  10.7 0.5 collective-permute-start.1
  11.2 1.2 %copy.27 = bf16[2,1,8,2,10,1920]{5,2,3,4,0,1:T(8,128)(2,1)} copy(bf16[2,1,8,2,10,1920]{5,3,4,2,1,0:T(2,128)(2,1)S(1)} %get-tuple-element.5) | data formatting | bytes 2457600 | tf_op jit(solution)/shard_map/transpose | solution.py:96
  12.4 0.6 collective-permute-start.2
  13.0 0.0 copy-start.1
  13.0 0.1 copy.30
  13.1 0.5 copy-done.1
  13.7 0.1 copy.6
  13.8 0.1 reshape.48
  13.9 0.1 pad_add_fusion.info
  14.0 0.3 fusion.box
  14.3 22.5 %collective-permute-done.one = bf16[2,10,16,1920]{3,2,1,0:T(8,128)(2,1)S(1)} collective-permute-done((bf16[2,10,16,1920]{3,2,1,0:T(8,128)(2,1)}, bf16[2,10,16,1920]{3,2,1,0:T(8,128)(2,1)S(1)}, u32[]{:S(2)}, u32[]{:S(2)}) %collective-permute-start) | collective-permute-done | bytes 1228832 | tf_op jit(solution)/shard_map/ppermute | solution.py:104
  36.8 3.4 %collective-permute-done.1.two = bf16[2,10,16,1920]{3,2,1,0:T(8,128)(2,1)} collective-permute-done((bf16[2,10,16,1920]{3,2,1,0:T(8,128)(2,1)}, bf16[2,10,16,1920]{3,2,1,0:T(8,128)(2,1)}, u32[]{:S(2)}, u32[]{:S(2)}) %collective-permute-start.1) | collective-permute-done | bytes 1228832 | tf_op jit(solution)/shard_map/ppermute | solution.py:102
  40.1 27.7 %collective-permute-done.2.three = bf16[2,10,16,1920]{3,2,1,0:T(8,128)(2,1)} collective-permute-done((bf16[2,10,16,1920]{3,2,1,0:T(8,128)(2,1)}, bf16[2,10,16,1920]{3,2,1,0:T(8,128)(2,1)}, u32[]{:S(2)}, u32[]{:S(2)}) %collective-permute-start.2) | collective-permute-done | bytes 1228832 | tf_op jit(solution)/shard_map/ppermute | solution.py:103
  67.8 9.5 %shard_map.46 = f32[4,8,16,128]{3,2,1,0:T(8,128)S(1)} custom-call(s32[33]{0:T(128)S(1)} %pad_add_fusion.info, bf16[2,10,16,1920]{3,2,1,0:T(8,128)(2,1)S(1)} %bitcast.35, bf16[2,10,16,1920]{3,2,1,0:T(8,128)(2,1)S(1)} %collective-permute-done.one, bf16[2,10,16,1920]{3,2,1,0:T(8,128)(2,1)} %collective-permute-done.1.two, ...), custom_call_target="tpu_custom_call" | custom-call | tf_op jit(solution)/shard_map/pallas_call | solution.py:114
  77.3 9.3 %all_to_all.10 = f32[4,8,16,128]{3,2,1,0:T(8,128)} all-to-all(f32[4,8,16,128]{3,2,1,0:T(8,128)S(1)} %shard_map.46), channel_id=1, replica_groups=mesh['tile'=32,'date'=4] {'date'}, dimensions={0} | all-to-all | bytes 524288 | tf_op jit(solution)/shard_map/all_to_all | solution.py:132
  86.7 9.4 %all-to-all-start.1 = ((f32[32,16,128]{2,1,0:T(8,128)}), f32[32,16,128]{2,1,0:T(8,128)S(1)}, u32[]{:S(2)}, u32[]{:S(2)}) async-start(f32[32,16,128]{2,1,0:T(8,128)} %bitcast.14), calls=%async_computation.1 | async-start | bytes 524288 | tf_op jit(solution)/shard_map/all_to_all | solution.py:134
  96.8 8.3 %all-to-all-done.1.got = f32[32,16,128]{2,1,0:T(8,128)S(1)} async-done(((f32[32,16,128]{2,1,0:T(8,128)}), f32[32,16,128]{2,1,0:T(8,128)S(1)}, u32[]{:S(2)}, u32[]{:S(2)}) %all-to-all-start.1) | async-done | bytes 262176 | tf_op jit(solution)/shard_map/all_to_all | solution.py:134
  105.0 0.0 copy-start
  105.0 0.7 copy-done
  105.7 2.4 %shard_map.47 = f32[4,2,64,128]{3,2,1,0:T(8,128)} custom-call(s32[32]{0:T(128)} %bitcast.36, s32[1]{0:T(128)S(6)} %copy.31.usable, f32[32,16,128]{2,1,0:T(8,128)} %copy-done), custom_call_target="tpu_custom_call" | custom-call | tf_op jit(solution)/shard_map/pallas_call | solution.py:136
  (1 shorter events, 0.0 us)
Async XLA Ops:
  6.2 30.5 %collective-permute-start = (bf16[2,10,16,1920]{3,2,1,0:T(8,128)(2,1)}, bf16[2,10,16,1920]{3,2,1,0:T(8,128)(2,1)S(1)}, u32[]{:S(2)}, u32[]{:S(2)}) collective-permute-start(bf16[2,10,16,1920]{3,2,1,0:T(8,128)(2,1)} %bitcast.33), channel_id=1, source_target_pairs={{0,3},{1,0},{2,1},{3,2},{4,7},{5,4},{6,5},{7,6},{8,11},{9,8},{10,9... | collective-permute-start | bytes 3686408 | tf_op jit(solution)/shard_map/ppermute | solution.py:104
  10.7 29.4 %collective-permute-start.1 = (bf16[2,10,16,1920]{3,2,1,0:T(8,128)(2,1)}, bf16[2,10,16,1920]{3,2,1,0:T(8,128)(2,1)}, u32[]{:S(2)}, u32[]{:S(2)}) collective-permute-start(bf16[2,10,16,1920]{3,2,1,0:T(8,128)(2,1)} %bitcast.32), channel_id=1, source_target_pairs={{0,2},{1,3},{2,0},{3,1},{4,6},{5,7},{6,4},{7,5},{8,10},{9,11},{10,... | collective-permute-start | bytes 3686408 | tf_op jit(solution)/shard_map/ppermute | solution.py:102
  12.4 55.4 %collective-permute-start.2 = (bf16[2,10,16,1920]{3,2,1,0:T(8,128)(2,1)}, bf16[2,10,16,1920]{3,2,1,0:T(8,128)(2,1)}, u32[]{:S(2)}, u32[]{:S(2)}) collective-permute-start(bf16[2,10,16,1920]{3,2,1,0:T(8,128)(2,1)} %bitcast.31), channel_id=1, source_target_pairs={{0,1},{1,2},{2,3},{3,0},{4,5},{5,6},{6,7},{7,4},{8,9},{9,10},{10,1... | collective-permute-start | bytes 3686408 | tf_op jit(solution)/shard_map/ppermute | solution.py:103
  13.0 0.7 copy-start.1
  86.7 18.3 %all-to-all-start.1 = ((f32[32,16,128]{2,1,0:T(8,128)}), f32[32,16,128]{2,1,0:T(8,128)S(1)}, u32[]{:S(2)}, u32[]{:S(2)}) async-start(f32[32,16,128]{2,1,0:T(8,128)} %bitcast.14), calls=%async_computation.1 | async-start | bytes 524288 | tf_op jit(solution)/shard_map/all_to_all | solution.py:134
  105.0 0.7 copy-start

commit v2 on v1

v2 whole, which is shorter than its diff:
```python
import functools

import jax
import jax.numpy as jnp
from jax import lax
from jax.experimental import pallas as pl
from jax.experimental.pallas import tpu as pltpu
from jax.sharding import PartitionSpec as P

LOOK_RG = 15
LOOK_AZ = 5
EPS = 1e-05
SCALE = 1.0 / (LOOK_AZ * LOOK_RG)
DATES = 8
PAIRS = 16
ITEMS = 8
RG = 1920
LCOL = 128
ROWS = 320
SPLIT = 7


def look_kernel(lines, first, last, info, own, one, two, three, box, *rest):
    if first:
        out, img, hi, lo, sums = rest
    else:
        before, out, img, hi, lo, sums = rest
    group = info[2 * PAIRS]
    for step, block in enumerate((own, one, two, three)):
        base = lax.rem(group + step, 4) * 2
        for date in range(2):
            for line in range(lines):
                pixels = jnp.swapaxes(block[:, date, line], 0, 1).reshape(16, RG)
                img[base + date, line] = pixels.astype(jnp.float32)

    def split(values, row):
        upper = values.astype(jnp.bfloat16)
        hi[pl.ds(row, 16), :] = upper
        lo[pl.ds(row, 16), :] = (values - upper.astype(jnp.float32)).astype(jnp.bfloat16)

    def power(half, carry):
        total = []
        for date in range(2):
            acc = jnp.zeros((ITEMS, RG), jnp.float32)
            for line in range(lines):
                re = img[2 * half + date, line, 0:8, :]
                im = img[2 * half + date, line, 8:16, :]
                acc = acc + (re * re + im * im)
            total.append(acc)
        split(jnp.concatenate(total, axis=0), pl.multiple_of(half * 16, 16))
        return carry

    lax.fori_loop(0, DATES // 2, power, 0)

    def cross(k, carry):
        a, b = info[2 * k], info[2 * k + 1]
        acc_re = jnp.zeros((ITEMS, RG), jnp.float32)
        acc_im = jnp.zeros((ITEMS, RG), jnp.float32)
        for line in range(lines):
            re_a, im_a = img[a, line, 0:8, :], img[a, line, 8:16, :]
            re_b, im_b = img[b, line, 0:8, :], img[b, line, 8:16, :]
            acc_re = acc_re + (re_a * re_b + im_a * im_b)
            acc_im = acc_im + (im_a * re_b - re_a * im_b)
        split(jnp.concatenate([acc_re, acc_im], axis=0), pl.multiple_of(64 + k * 16, 16))
        return carry

    lax.fori_loop(0, PAIRS, cross, 0)
    total = jnp.dot(hi[...], box[...], preferred_element_type=jnp.float32) + jnp.dot(
        lo[...], box[...], preferred_element_type=jnp.float32
    )
    if not first:
        total = total + before[...]
    if not last:
        out[...] = total
        return
    sums[...] = total * SCALE

    for owner in range(4):
        rows = []
        for kk in range(4):
            k = owner * 4 + kk
            power_a = sums[pl.ds(pl.multiple_of(info[2 * k] * 8, 8), 8), :]
            power_b = sums[pl.ds(pl.multiple_of(info[2 * k + 1] * 8, 8), 8), :]
            weight = 1.0 / jnp.sqrt((power_a + EPS) * (power_b + EPS))
            rows.append(sums[64 + k * 16 : 72 + k * 16, :] * weight)
            rows.append(sums[72 + k * 16 : 80 + k * 16, :] * weight)
        out[owner] = jnp.swapaxes(jnp.stack(rows, axis=0), 0, 1)


def looks(info, blocks, box, before, last):
    lines = blocks[0].shape[2]
    first = before is None
    vmem = pl.BlockSpec(memory_space=pltpu.VMEM)
    operands = (info, *blocks, box) + (() if first else (before,))
    shape = (4, ITEMS, 8, LCOL) if last else (ROWS, LCOL)
    work = lines * ITEMS * RG * (PAIRS * 8 + DATES * 4) + 4 * ROWS * RG * LCOL
    return pl.pallas_call(
        functools.partial(look_kernel, lines, first, last),
        out_shape=jax.ShapeDtypeStruct(shape, jnp.float32),
        grid_spec=pltpu.PrefetchScalarGridSpec(
            num_scalar_prefetch=1,
            grid=(),
            in_specs=[vmem] * (len(operands) - 1),
            out_specs=vmem,
            scratch_shapes=[
                pltpu.VMEM((DATES, lines, 16, RG), jnp.float32),
                pltpu.VMEM((ROWS, RG), jnp.bfloat16),
                pltpu.VMEM((ROWS, RG), jnp.bfloat16),
                pltpu.VMEM((ROWS, LCOL), jnp.float32),
            ],
        ),
        cost_estimate=pl.CostEstimate(
            flops=work, bytes_accessed=DATES * lines * 16 * RG * 2, transcendentals=0
        ),
        compiler_params=pltpu.CompilerParams(vmem_limit_bytes=24 << 20),
    )(*operands)


def place_kernel(positions, usable, got0, got1, out, rows):
    for block in range(32):
        position = positions[block]
        valid = jnp.where(position < usable[0], 1.0, 0.0).astype(jnp.float32)
        base = pl.multiple_of(position * 16, 16)
        rows[pl.ds(base, 8), :] = got0[block] * valid
        rows[pl.ds(base + 8, 8), :] = got1[block] * valid
    for plane in range(8):
        for part in range(8):
            out[plane // 2, plane % 2, part * 8 : part * 8 + 8, :] = rows[
                pl.ds(part * 64 + plane, 8, stride=8), :
            ]


def cut_direct_kernel(info, images, own, to1, to2, to3, sem):
    group = info[2 * PAIRS]
    copies = []
    for step, out in ((1, to1), (3, to3), (2, to2), (0, own)):
        tiles = pl.ds(lax.rem(group + step, 4) * ITEMS, ITEMS)
        for date in range(2):
            copies.append(
                pltpu.make_async_copy(
                    images.at[date, tiles, 0:LOOK_AZ], out.at[:, date], sem.at[len(copies)]
                )
            )
            copies[-1].start()
    for copy in copies:
        copy.wait()


def cut_tile_kernel(images, after, part_a, part_b, sem):
    del after
    copies = []
    for low, high, out in ((5, SPLIT, part_a), (SPLIT, 10, part_b)):
        for date in range(2):
            copies.append(
                pltpu.make_async_copy(
                    images.at[date, :, low:high], out.at[:, date], sem.at[len(copies)]
                )
            )
            copies[-1].start()
    for copy in copies:
        copy.wait()


def cut_direct(info, images):
    block = jax.ShapeDtypeStruct((ITEMS, 2, LOOK_AZ, 2, RG), jnp.bfloat16)
    anywhere = pl.BlockSpec(memory_space=pl.ANY)
    return pl.pallas_call(
        cut_direct_kernel,
        out_shape=[block] * 4,
        grid_spec=pltpu.PrefetchScalarGridSpec(
            num_scalar_prefetch=1,
            grid=(),
            in_specs=[anywhere],
            out_specs=[anywhere] * 4,
            scratch_shapes=[pltpu.SemaphoreType.DMA((8,))],
        ),
    )(info, images)


def cut_tile(images, after):
    anywhere = pl.BlockSpec(memory_space=pl.ANY)
    return pl.pallas_call(
        cut_tile_kernel,
        out_shape=[
            jax.ShapeDtypeStruct((32, 2, lines, 2, RG), jnp.bfloat16)
            for lines in (SPLIT - 5, 10 - SPLIT)
        ],
        in_specs=[anywhere] * 2,
        out_specs=[anywhere] * 2,
        scratch_shapes=[pltpu.SemaphoreType.DMA((4,))],
    )(images, after)


def meet(own, to1, to2, to3):
    def ring(step):
        return [(i, (i + step) % 4) for i in range(4)]

    three = lax.ppermute(to1, "date", ring(1))
    one = lax.ppermute(to3, "date", ring(3))
    two = lax.ppermute(to2, "date", ring(2))
    return own, one, two, three


def on_device(complex_images, segment_position_map, usable_position_total, interferogram_epochs):
    group = lax.axis_index("date")
    images = complex_images[:, 0].transpose(0, 1, 3, 2, 4)
    info = jnp.concatenate(
        [interferogram_epochs.reshape(-1), group.reshape(1)]
    ).astype(jnp.int32)
    box = (
        jnp.arange(RG)[:, None] // LOOK_RG == jnp.arange(LCOL)[None, :]
    ).astype(jnp.bfloat16)

    def through_tile(part):
        came = lax.all_to_all(part, "tile", split_axis=0, concat_axis=0, tiled=True)
        return [
            lax.dynamic_slice_in_dim(came, lax.rem(group + step, 4) * ITEMS, ITEMS, 0)
            for step in range(4)
        ]

    direct = cut_direct(info, images)
    row0 = meet(*direct)
    part_a, part_b = cut_tile(images, direct[2])
    row1a = meet(*through_tile(part_a))
    row1b = meet(*through_tile(part_b))

    gamma0 = looks(info, row0, box, None, True)
    moved = lax.all_to_all(gamma0, "date", split_axis=0, concat_axis=0, tiled=True)
    got0 = lax.all_to_all(
        moved.reshape(32, 8, LCOL), "tile", split_axis=0, concat_axis=0, tiled=True
    )

    sums1 = looks(info, row1a, box, None, False)
    gamma1 = looks(info, row1b, box, sums1, True)
    got1 = lax.all_to_all(gamma1, "date", split_axis=0, concat_axis=0, tiled=True)

    vmem = pl.BlockSpec(memory_space=pltpu.VMEM)
    return pl.pallas_call(
        place_kernel,
        out_shape=jax.ShapeDtypeStruct((4, 2, 64, LCOL), jnp.float32),
        grid_spec=pltpu.PrefetchScalarGridSpec(
            num_scalar_prefetch=2,
            grid=(),
            in_specs=[vmem, vmem],
            out_specs=vmem,
            scratch_shapes=[pltpu.VMEM((512, LCOL), jnp.float32)],
        ),
    )(segment_position_map[0], usable_position_total, got0, got1.reshape(32, 8, LCOL))


def solution(mesh):
    in_specs = (P("date", "tile", None, None, None, None), P("tile", None), P("tile"), P())
    out_specs = P("date", None, None, "tile")
    return jax.shard_map(
        on_device, mesh=mesh, in_specs=in_specs, out_specs=out_specs, check_vma=False
    )
```

time: 108 us -> 273 us (2.53)
  Pallas kernels: 11.9 us -> 169 us
  waiting for transfers between devices: 61.8 us -> 24.3 us
  blocking collectives: 9.34 us -> 39.3 us
  starting transfers between devices: 13.9 us -> 30.1 us
    pallas_call x1 -> x5, Pallas kernels: 9.52 us -> 167 us  [the longest x1 76.3 us: cut_direct(): pl.pallas_call(cut_direct_kernel, out_shape=[block] * 4, grid_spec=pltpu....]
    ppermute x3 -> x9, waiting for transfers between devices: 53.5 us -> 6.92 us  [the longest x3 6.9 us: meet(): one = lax.ppermute(to3, 'date', ring(3))]
    all_to_all x1 -> x2, blocking collectives: 9.34 us -> 39.3 us  [the longest x1 26.1 us: through_tile(): came = lax.all_to_all(part, 'tile', split_axis=0, concat_axis=0, tiled=True)]
    all_to_all x1 -> x3, waiting for transfers between devices: 8.25 us -> 17.4 us  [the longest x1 13.2 us: through_tile(): came = lax.all_to_all(part, 'tile', split_axis=0, concat_axis=0, tiled=True)]
    ppermute x3 -> x9, starting transfers between devices: 4.43 us -> 13.1 us  [the longest x3 4.89 us: meet(): three = lax.ppermute(to1, 'date', ring(1))]
    all_to_all x1 -> x3, starting transfers between devices: 9.43 us -> 17 us  [the longest x1 8.27 us: on_device(): lax.all_to_all(moved.reshape(32, 8, LCOL), 'tile', split_axis=0, concat_a...]
    transpose x4 -> x0, local copies, waits for them, and re-layouts: 3.65 us -> none  [block_for(): return part.transpose(0, 3, 2, 1, 4).reshape(2, 10, 16, RG)]
  transfers between devices with their start and end apart: 4 -> 12, of which waited for: 4 -> 4; matrix products, arithmetic and copies ran while one was open for 3% -> 2% of each run, Pallas kernels for 0% -> 5%
where the time goes in v2:
time: 273 us; the launch traced here: 272 us
  Pallas kernels  169 us (62%)
  blocking collectives  39.3 us (14%)
  starting transfers between devices  30.1 us (11%)
  waiting for transfers between devices  24.3 us (9%)
  local copies, waits for them, and re-layouts  7.8 us (3%)
    pallas_call x1, Pallas kernels, cut_direct(): pl.pallas_call(cut_direct_kernel, out_shape=[block] * 4, grid_spec=pltpu....  76.3 us
    pallas_call x1, Pallas kernels, cut_tile(): pl.pallas_call(cut_tile_kernel, out_shape=[jax.ShapeDtypeStruct((32, 2, l...  75.6 us
    all_to_all x1, blocking collectives, through_tile(): came = lax.all_to_all(part, 'tile', split_axis=0, concat_axis=0, tiled=True)  26.1 us
    pallas_call x3, Pallas kernels, looks(): pl.pallas_call(functools.partial(look_kernel, lines, first, last), out_sh...  14.9 us
    all_to_all x1, waiting for transfers between devices, through_tile(): came = lax.all_to_all(part, 'tile', split_axis=0, concat_axis=0, tiled=True)  13.2 us
    all_to_all x1, blocking collectives, on_device(): lax.all_to_all(gamma0, 'date', split_axis=0, concat_axis=0, tiled=True)  13.2 us
    all_to_all x1, starting transfers between devices, on_device(): lax.all_to_all(moved.reshape(32, 8, LCOL), 'tile', split_axis=0, concat_a...  8.27 us
    ppermute x3, waiting for transfers between devices, meet(): one = lax.ppermute(to3, 'date', ring(3))  6.9 us
  transfers between devices with their start and end apart: 12, of which 4 were waited for; matrix products, arithmetic and copies ran while one was open for 2% of the time, Pallas kernels for 5%

profile of v2, /device:TPU:1, one launch (start us, length us, event | category | flops | bytes accessed | tf_op | source)
XLA Modules:
  0.0 272.4 jit_solution(14459236472158450315)
XLA Ops:
  1.5 76.3 %shard_map.46 = (bf16[8,2,5,2,1920]{4,3,2,1,0:T(2,128)(2,1)}, bf16[8,2,5,2,1920]{4,3,2,1,0:T(2,128)(2,1)}, bf16[8,2,5,2,1920]{4,3,2,1,0:T(2,128)(2,1)}, bf16[8,2,5,2,1920]{4,3,2,1,0:T(2,128)(2,1)}) custom-call(s32[33]{0:T(128)} %pad_add_fusion.info, bf16[2,32,10,2,1920]{4,3,2,1,0:T(2,128)(2,1)} %bitcast.7), custom_call_target="tpu_custom_call" | custom-call | tf_op jit(solution)/shard_map/pallas_call | solution.py:167
  77.8 75.6 %shard_map.48 = (bf16[32,2,2,2,1920]{4,3,2,1,0:T(2,128)(2,1)}, bf16[32,2,3,2,1920]{4,3,2,1,0:T(2,128)(2,1)}) custom-call(bf16[2,32,10,2,1920]{4,3,2,1,0:T(2,128)(2,1)} %bitcast.8, bf16[8,2,5,2,1920]{4,3,2,1,0:T(2,128)(2,1)} %get-tuple-element.13.after), custom_call_target="tpu_custom_call" | custom-call | tf_op jit(solution)/shard_map/pallas_call | solution.py:182
  153.4 26.1 %all_to_all.25 = bf16[32,2,2,2,1920]{4,3,2,1,0:T(2,128)(2,1)S(1)} all-to-all(bf16[32,2,2,2,1920]{4,3,2,1,0:T(2,128)(2,1)} %get-tuple-element.16), channel_id=1, replica_groups=mesh['tile'=32,'date'=4] {'tile'}, dimensions={0} | all-to-all | bytes 1966080 | tf_op jit(solution)/shard_map/all_to_all | solution.py:215
  179.4 4.7 %all-to-all-start.2 = ((bf16[32,2,3,2,1920]{4,3,2,1,0:T(2,128)(2,1)}), bf16[32,2,3,2,1920]{4,3,2,1,0:T(2,128)(2,1)}, u32[]{:S(2)}, u32[]{:S(2)}) async-start(bf16[32,2,3,2,1920]{4,3,2,1,0:T(2,128)(2,1)} %get-tuple-element.15), calls=%async_computation.2 | async-start | bytes 2949120 | tf_op jit(solution)/shard_map/all_to_all | solution.py:215
  184.1 2.8 %collective-permute-start.1 = (bf16[8,2,5,2,1920]{4,3,2,1,0:T(2,128)(2,1)}, bf16[8,2,5,2,1920]{4,3,2,1,0:T(2,128)(2,1)S(1)}, u32[]{:S(2)}, u32[]{:S(2)}) collective-permute-start(bf16[8,2,5,2,1920]{4,3,2,1,0:T(2,128)(2,1)} %get-tuple-element.13.after), channel_id=1, source_target_pairs={{0,2},{1,3},{2,0},{3,1},{4,6},{5,7},{6,4},{7,5},{8,10},{9,11},{10,... | collective-permute-start | bytes 1843208 | tf_op jit(solution)/shard_map/ppermute | solution.py:200
  188.4 1.5 constant_dynamic-slice_fusion
  189.9 2.1 collective-permute-start.6
  192.0 13.2 %all-to-all-done.2 = bf16[32,2,3,2,1920]{4,3,2,1,0:T(2,128)(2,1)} async-done(((bf16[32,2,3,2,1920]{4,3,2,1,0:T(2,128)(2,1)}), bf16[32,2,3,2,1920]{4,3,2,1,0:T(2,128)(2,1)}, u32[]{:S(2)}, u32[]{:S(2)}) %all-to-all-start.2) | async-done | bytes 1474592 | tf_op jit(solution)/shard_map/all_to_all | solution.py:215
  205.2 3.2 %constant_dynamic-slice_fusion.4 = (bf16[8,2,3,2,1920]{4,3,2,1,0:T(2,128)(2,1)}, bf16[8,2,3,2,1920]{4,3,2,1,0:T(2,128)(2,1)}, bf16[8,2,3,2,1920]{4,3,2,1,0:T(2,128)(2,1)}, bf16[8,2,3,2,1920]{4,3,2,1,0:T(2,128)(2,1)S(1)}) fusion(bf16[32,2,3,2,1920]{4,3,2,1,0:T(2,128)(2,1)} %all-to-all-done.2, s32[]{:T(128)S(6)} %select_n.34, s32[]{:T(128)S(6)} %select_n.33, ...), kind=kLoop, calls=%fused_computation.13 | loop fusion | bytes 2949136 | tf_op jit(solution)/shard_map/dynamic_slice | solution.py:217
  208.4 5.9 %collective-permute-done.one = bf16[8,2,5,2,1920]{4,3,2,1,0:T(2,128)(2,1)S(1)} collective-permute-done((bf16[8,2,5,2,1920]{4,3,2,1,0:T(2,128)(2,1)}, bf16[8,2,5,2,1920]{4,3,2,1,0:T(2,128)(2,1)S(1)}, u32[]{:S(2)}, u32[]{:S(2)}) %collective-permute-start) | collective-permute-done | bytes 614432 | tf_op jit(solution)/shard_map/ppermute | solution.py:199
  214.3 1.8 collective-permute-start.8
  216.2 1.2 collective-permute-start.3
  217.4 1.3 collective-permute-start.4
  218.6 1.0 collective-permute-done.6.one
  220.3 2.4 collective-permute-start.5
  223.1 5.9 %shard_map.47 = f32[4,8,8,128]{3,2,1,0:T(8,128)S(1)} custom-call(s32[33]{0:T(128)S(1)} %copy-done.3, bf16[8,2,5,2,1920]{4,3,2,1,0:T(2,128)(2,1)S(1)} %copy-done, bf16[8,2,5,2,1920]{4,3,2,1,0:T(2,128)(2,1)S(1)} %collective-permute-done.one, bf16[8,2,5,2,1920]{4,3,2,1,0:T(2,128)(2,1)S(1)} %collective-permute-done.1.two, ...), custom_call_target="tpu_custom_call" | custom-call | flops 326860800 | bytes 2457600 | tf_op jit(solution)/shard_map/pallas_call | solution.py:97
  229.0 13.2 %all_to_all.26 = f32[4,8,8,128]{3,2,1,0:T(8,128)} all-to-all(f32[4,8,8,128]{3,2,1,0:T(8,128)S(1)} %shard_map.47), channel_id=1, replica_groups=mesh['tile'=32,'date'=4] {'date'}, dimensions={0} | all-to-all | bytes 262144 | tf_op jit(solution)/shard_map/all_to_all | solution.py:228
  242.2 8.3 %all-to-all-start.1 = ((f32[32,8,128]{2,1,0:T(8,128)}), f32[32,8,128]{2,1,0:T(8,128)S(1)}, u32[]{:S(2)}, u32[]{:S(2)}) async-start(f32[32,8,128]{2,1,0:T(8,128)} %bitcast.4), calls=%async_computation.1 | async-start | bytes 262144 | tf_op jit(solution)/shard_map/all_to_all | solution.py:229
  250.5 0.9 copy-done.2
  251.4 3.7 %shard_map.49.rest_0_ = f32[320,128]{1,0:T(8,128)S(1)} custom-call(s32[33]{0:T(128)S(1)} %copy-done.3, bf16[8,2,2,2,1920]{4,3,2,1,0:T(2,128)(2,1)S(1)} %get-tuple-element.24.own, bf16[8,2,2,2,1920]{4,3,2,1,0:T(2,128)(2,1)S(1)} %copy-done.2, bf16[8,2,2,2,1920]{4,3,2,1,0:T(2,128)(2,1)} %collective-permute-done.7.two, ...), custom_call_target="tpu_custom_call" | custom-call | flops 319488000 | bytes 983040 | tf_op jit(solution)/shard_map/pallas_call | solution.py:97
  255.2 5.3 %shard_map.50 = f32[4,8,8,128]{3,2,1,0:T(8,128)} custom-call(s32[33]{0:T(128)S(1)} %copy-done.3, bf16[8,2,3,2,1920]{4,3,2,1,0:T(2,128)(2,1)S(1)} %get-tuple-element.20.own, bf16[8,2,3,2,1920]{4,3,2,1,0:T(2,128)(2,1)S(1)} %collective-permute-done.3.one, bf16[8,2,3,2,1920]{4,3,2,1,0:T(2,128)(2,1)} %collective-permute-done.4.two, ...), custom_call_target="tpu_custom_call" | custom-call | flops 321945600 | bytes 1474560 | tf_op jit(solution)/shard_map/pallas_call | solution.py:97
  260.4 4.1 %all-to-all-start.4 = ((f32[4,8,8,128]{3,2,1,0:T(8,128)}), f32[4,8,8,128]{3,2,1,0:T(8,128)S(1)}, u32[]{:S(2)}, u32[]{:S(2)}) async-start(f32[4,8,8,128]{3,2,1,0:T(8,128)} %shard_map.50), calls=%async_computation.4 | async-start | bytes 262144 | tf_op jit(solution)/shard_map/all_to_all | solution.py:235
  265.1 4.2 %all-to-all-done.4 = f32[4,8,8,128]{3,2,1,0:T(8,128)S(1)} async-done(((f32[4,8,8,128]{3,2,1,0:T(8,128)}), f32[4,8,8,128]{3,2,1,0:T(8,128)S(1)}, u32[]{:S(2)}, u32[]{:S(2)}) %all-to-all-start.4) | async-done | bytes 131104 | tf_op jit(solution)/shard_map/all_to_all | solution.py:235
  270.0 2.4 shard_map.51
  (27 shorter events, 4.7 us)
Async XLA Ops:
  179.4 25.8 %all-to-all-start.2 = ((bf16[32,2,3,2,1920]{4,3,2,1,0:T(2,128)(2,1)}), bf16[32,2,3,2,1920]{4,3,2,1,0:T(2,128)(2,1)}, u32[]{:S(2)}, u32[]{:S(2)}) async-start(bf16[32,2,3,2,1920]{4,3,2,1,0:T(2,128)(2,1)} %get-tuple-element.15), calls=%async_computation.2 | async-start | bytes 2949120 | tf_op jit(solution)/shard_map/all_to_all | solution.py:215
  184.1 32.1 %collective-permute-start.1 = (bf16[8,2,5,2,1920]{4,3,2,1,0:T(2,128)(2,1)}, bf16[8,2,5,2,1920]{4,3,2,1,0:T(2,128)(2,1)S(1)}, u32[]{:S(2)}, u32[]{:S(2)}) collective-permute-start(bf16[8,2,5,2,1920]{4,3,2,1,0:T(2,128)(2,1)} %get-tuple-element.13.after), channel_id=1, source_target_pairs={{0,2},{1,3},{2,0},{3,1},{4,6},{5,7},{6,4},{7,5},{8,10},{9,11},{10,... | collective-permute-start | bytes 1843208 | tf_op jit(solution)/shard_map/ppermute | solution.py:200
  187.0 27.4 %collective-permute-start = (bf16[8,2,5,2,1920]{4,3,2,1,0:T(2,128)(2,1)}, bf16[8,2,5,2,1920]{4,3,2,1,0:T(2,128)(2,1)S(1)}, u32[]{:S(2)}, u32[]{:S(2)}) collective-permute-start(bf16[8,2,5,2,1920]{4,3,2,1,0:T(2,128)(2,1)} %get-tuple-element.12), channel_id=1, source_target_pairs={{0,3},{1,0},{2,1},{3,2},{4,7},{5,4},{6,5},{7,6},{8,11},{9,8},{10,9... | collective-permute-start | bytes 1843208 | tf_op jit(solution)/shard_map/ppermute | solution.py:199
  187.8 29.5 %collective-permute-start.2 = (bf16[8,2,5,2,1920]{4,3,2,1,0:T(2,128)(2,1)}, bf16[8,2,5,2,1920]{4,3,2,1,0:T(2,128)(2,1)}, u32[]{:S(2)}, u32[]{:S(2)}) collective-permute-start(bf16[8,2,5,2,1920]{4,3,2,1,0:T(2,128)(2,1)} %get-tuple-element.14), channel_id=1, source_target_pairs={{0,1},{1,2},{2,3},{3,0},{4,5},{5,6},{6,7},{7,4},{8,9},{9,10},{10,1... | collective-permute-start | bytes 1843208 | tf_op jit(solution)/shard_map/ppermute | solution.py:198
  189.9 29.7 %collective-permute-start.6 = (bf16[8,2,2,2,1920]{4,3,2,1,0:T(2,128)(2,1)S(1)}, bf16[8,2,2,2,1920]{4,3,2,1,0:T(2,128)(2,1)S(1)}, u32[]{:S(2)}, u32[]{:S(2)}) collective-permute-start(bf16[8,2,2,2,1920]{4,3,2,1,0:T(2,128)(2,1)S(1)} %get-tuple-element.23), channel_id=1, source_target_pairs={{0,3},{1,0},{2,1},{3,2},{4,7},{5,4},{6,5},{7,6},{8,11},{9,8},{10,9... | collective-permute-start | bytes 737288 | tf_op jit(solution)/shard_map/ppermute | solution.py:199
  192.0 31.1 %copy-start = (bf16[8,2,5,2,1920]{4,3,2,1,0:T(2,128)(2,1)S(1)}, bf16[8,2,5,2,1920]{4,3,2,1,0:T(2,128)(2,1)}, u32[]{:S(2)}) copy-start(bf16[8,2,5,2,1920]{4,3,2,1,0:T(2,128)(2,1)} %get-tuple-element.11.own) | copy-start | bytes 1843204
  192.0 31.1 %copy-start.3 = (s32[33]{0:T(128)S(1)}, s32[33]{0:T(128)}, u32[]{:S(2)}) copy-start(s32[33]{0:T(128)} %pad_add_fusion.info) | copy-start | bytes 400
  192.0 58.5 %collective-permute-start.7 = (bf16[8,2,2,2,1920]{4,3,2,1,0:T(2,128)(2,1)}, bf16[8,2,2,2,1920]{4,3,2,1,0:T(2,128)(2,1)}, u32[]{:S(2)}, u32[]{:S(2)}) collective-permute-start(bf16[8,2,2,2,1920]{4,3,2,1,0:T(2,128)(2,1)} %get-tuple-element.22), channel_id=1, source_target_pairs={{0,2},{1,3},{2,0},{3,1},{4,6},{5,7},{6,4},{7,5},{8,10},{9,11},{10,... | collective-permute-start | bytes 737288 | tf_op jit(solution)/shard_map/ppermute | solution.py:200
  214.3 36.1 %collective-permute-start.8 = (bf16[8,2,2,2,1920]{4,3,2,1,0:T(2,128)(2,1)}, bf16[8,2,2,2,1920]{4,3,2,1,0:T(2,128)(2,1)}, u32[]{:S(2)}, u32[]{:S(2)}) collective-permute-start(bf16[8,2,2,2,1920]{4,3,2,1,0:T(2,128)(2,1)} %get-tuple-element.21), channel_id=1, source_target_pairs={{0,1},{1,2},{2,3},{3,0},{4,5},{5,6},{6,7},{7,4},{8,9},{9,10},{10,1... | collective-permute-start | bytes 737288 | tf_op jit(solution)/shard_map/ppermute | solution.py:198
  216.2 39.0 %collective-permute-start.3 = (bf16[8,2,3,2,1920]{4,3,2,1,0:T(2,128)(2,1)}, bf16[8,2,3,2,1920]{4,3,2,1,0:T(2,128)(2,1)S(1)}, u32[]{:S(2)}, u32[]{:S(2)}) collective-permute-start(bf16[8,2,3,2,1920]{4,3,2,1,0:T(2,128)(2,1)} %get-tuple-element.19), channel_id=1, source_target_pairs={{0,3},{1,0},{2,1},{3,2},{4,7},{5,4},{6,5},{7,6},{8,11},{9,8},{10,9... | collective-permute-start | bytes 1105928 | tf_op jit(solution)/shard_map/ppermute | solution.py:199
  217.4 37.8 %collective-permute-start.4 = (bf16[8,2,3,2,1920]{4,3,2,1,0:T(2,128)(2,1)}, bf16[8,2,3,2,1920]{4,3,2,1,0:T(2,128)(2,1)}, u32[]{:S(2)}, u32[]{:S(2)}) collective-permute-start(bf16[8,2,3,2,1920]{4,3,2,1,0:T(2,128)(2,1)} %get-tuple-element.18), channel_id=1, source_target_pairs={{0,2},{1,3},{2,0},{3,1},{4,6},{5,7},{6,4},{7,5},{8,10},{9,11},{10,... | collective-permute-start | bytes 1105928 | tf_op jit(solution)/shard_map/ppermute | solution.py:200
  219.6 0.7 copy-start.1
  220.3 34.8 %collective-permute-start.5 = (bf16[8,2,3,2,1920]{4,3,2,1,0:T(2,128)(2,1)}, bf16[8,2,3,2,1920]{4,3,2,1,0:T(2,128)(2,1)}, u32[]{:S(2)}, u32[]{:S(2)}) collective-permute-start(bf16[8,2,3,2,1920]{4,3,2,1,0:T(2,128)(2,1)} %get-tuple-element.17), channel_id=1, source_target_pairs={{0,1},{1,2},{2,3},{3,0},{4,5},{5,6},{6,7},{7,4},{8,9},{9,10},{10,1... | collective-permute-start | bytes 1105928 | tf_op jit(solution)/shard_map/ppermute | solution.py:198
  242.2 18.3 %all-to-all-start.1 = ((f32[32,8,128]{2,1,0:T(8,128)}), f32[32,8,128]{2,1,0:T(8,128)S(1)}, u32[]{:S(2)}, u32[]{:S(2)}) async-start(f32[32,8,128]{2,1,0:T(8,128)} %bitcast.4), calls=%async_computation.1 | async-start | bytes 262144 | tf_op jit(solution)/shard_map/all_to_all | solution.py:229
  250.5 0.9 copy-start.2
  260.4 8.9 %copy-start.4 = (f32[32,8,128]{2,1,0:T(8,128)}, f32[32,8,128]{2,1,0:T(8,128)S(1)}, u32[]{:S(2)}) copy-start(f32[32,8,128]{2,1,0:T(8,128)S(1)} %all-to-all-done.1.got0) | copy-start | bytes 393220
  260.4 8.9 %all-to-all-start.4 = ((f32[4,8,8,128]{3,2,1,0:T(8,128)}), f32[4,8,8,128]{3,2,1,0:T(8,128)S(1)}, u32[]{:S(2)}, u32[]{:S(2)}) async-start(f32[4,8,8,128]{3,2,1,0:T(8,128)} %shard_map.50), calls=%async_computation.4 | async-start | bytes 262144 | tf_op jit(solution)/shard_map/all_to_all | solution.py:235
  269.3 0.7 copy-start.5

commit v3 on v1

v3 whole, which is shorter than its diff:
```python
import functools

import jax
import jax.numpy as jnp
from jax import lax
from jax.experimental import pallas as pl
from jax.experimental.pallas import tpu as pltpu
from jax.sharding import PartitionSpec as P

LOOK_RG = 15
LOOK_AZ = 5
EPS = 1e-05
SCALE = 1.0 / (LOOK_AZ * LOOK_RG)
DATES = 8
PAIRS = 16
ITEMS = 8
LINES = 10
RG = 1920
LCOL = 128
ROWS = 320
SPLIT = 8

VMEM = pl.BlockSpec(memory_space=pltpu.VMEM)
HBM = pl.BlockSpec(memory_space=pltpu.HBM)
ANYWHERE = pl.BlockSpec(memory_space=pl.ANY)


def cut_kernel(low, high, info, images, *rest):
    to1, to2, to3, own, sem = rest[-5:]
    group = info[2 * PAIRS]
    copies = []
    for step, out in ((1, to1), (3, to3), (2, to2), (0, own)):
        tiles = pl.ds(lax.rem(group + step, 4) * ITEMS, ITEMS)
        for date in range(2):
            copies.append(
                pltpu.make_async_copy(
                    images.at[date, tiles, low:high], out.at[:, date], sem.at[len(copies)]
                )
            )
            copies[-1].start()
    for copy in copies:
        copy.wait()


def cut(info, images, low, high, after=None):
    block = jax.ShapeDtypeStruct((ITEMS, 2, high - low, 2, RG), jnp.bfloat16)
    operands = (info, images) + (() if after is None else (after,))
    return pl.pallas_call(
        functools.partial(cut_kernel, low, high),
        out_shape=[block] * 4,
        grid_spec=pltpu.PrefetchScalarGridSpec(
            num_scalar_prefetch=1,
            grid=(),
            in_specs=[HBM, ANYWHERE][: len(operands) - 1],
            out_specs=[VMEM] * 4,
            scratch_shapes=[pltpu.SemaphoreType.DMA((8,))],
        ),
        compiler_params=pltpu.CompilerParams(vmem_limit_bytes=8 << 20),
    )(*operands)


def meet(to1, to2, to3, own):
    def ring(step):
        return [(i, (i + step) % 4) for i in range(4)]

    three = lax.ppermute(to1, "date", ring(1))
    one = lax.ppermute(to3, "date", ring(3))
    two = lax.ppermute(to2, "date", ring(2))
    return own, one, two, three


def add_lines(info, blocks, low, high, box, img, hi, lo):
    group = info[2 * PAIRS]
    lines = high - low
    for step, block in enumerate(blocks):
        base = lax.rem(group + step, 4) * 2
        for date in range(2):
            for line in range(lines):
                pixels = jnp.swapaxes(block[:, date, low + line], 0, 1).reshape(16, RG)
                img[base + date, line] = pixels.astype(jnp.float32)

    def split(values, row):
        upper = values.astype(jnp.bfloat16)
        hi[pl.ds(row, 16), :] = upper
        lo[pl.ds(row, 16), :] = (values - upper.astype(jnp.float32)).astype(jnp.bfloat16)

    def power(half, carry):
        total = []
        for date in range(2):
            acc = jnp.zeros((ITEMS, RG), jnp.float32)
            for line in range(lines):
                re = img[2 * half + date, line, 0:8, :]
                im = img[2 * half + date, line, 8:16, :]
                acc = acc + (re * re + im * im)
            total.append(acc)
        split(jnp.concatenate(total, axis=0), pl.multiple_of(half * 16, 16))
        return carry

    lax.fori_loop(0, DATES // 2, power, 0)

    def cross(k, carry):
        a, b = info[2 * k], info[2 * k + 1]
        acc_re = jnp.zeros((ITEMS, RG), jnp.float32)
        acc_im = jnp.zeros((ITEMS, RG), jnp.float32)
        for line in range(lines):
            re_a, im_a = img[a, line, 0:8, :], img[a, line, 8:16, :]
            re_b, im_b = img[b, line, 0:8, :], img[b, line, 8:16, :]
            acc_re = acc_re + (re_a * re_b + im_a * im_b)
            acc_im = acc_im + (im_a * re_b - re_a * im_b)
        split(jnp.concatenate([acc_re, acc_im], axis=0), pl.multiple_of(64 + k * 16, 16))
        return carry

    lax.fori_loop(0, PAIRS, cross, 0)
    return jnp.dot(hi[...], box[...], preferred_element_type=jnp.float32) + jnp.dot(
        lo[...], box[...], preferred_element_type=jnp.float32
    )


def early_kernel(info, own, one, two, three, box, sums0, sums1, img, hi, lo):
    blocks = (own, one, two, three)
    sums0[...] = add_lines(info, blocks, 0, LOOK_AZ, box, img, hi, lo)
    sums1[...] = add_lines(info, blocks, LOOK_AZ, SPLIT, box, img, hi, lo)


def late_kernel(info, own, one, two, three, box, early0, early1, out, img, hi, lo, sums):
    blocks = (own, one, two, three)
    sums[0] = early0[...] * SCALE
    total = add_lines(info, blocks, 0, LINES - SPLIT, box, img, hi, lo)
    sums[1] = (total + early1[...]) * SCALE
    for owner in range(4):
        for look in range(2):
            rows = []
            for kk in range(4):
                k = owner * 4 + kk
                power_a = sums[look, pl.ds(pl.multiple_of(info[2 * k] * 8, 8), 8), :]
                power_b = sums[look, pl.ds(pl.multiple_of(info[2 * k + 1] * 8, 8), 8), :]
                weight = 1.0 / jnp.sqrt((power_a + EPS) * (power_b + EPS))
                rows.append(sums[look, 64 + k * 16 : 72 + k * 16, :] * weight)
                rows.append(sums[look, 72 + k * 16 : 80 + k * 16, :] * weight)
            out[owner, :, look * 8 : look * 8 + 8, :] = jnp.swapaxes(
                jnp.stack(rows, axis=0), 0, 1
            )


def looks(kernel, info, operands, out_shape, lines, scratch=()):
    work = lines * ITEMS * RG * (PAIRS * 8 + DATES * 4) + 4 * ROWS * RG * LCOL
    return pl.pallas_call(
        kernel,
        out_shape=out_shape,
        grid_spec=pltpu.PrefetchScalarGridSpec(
            num_scalar_prefetch=1,
            grid=(),
            in_specs=[VMEM] * len(operands),
            out_specs=jax.tree.map(lambda _: VMEM, out_shape),
            scratch_shapes=[
                pltpu.VMEM((DATES, min(lines, LOOK_AZ), 16, RG), jnp.float32),
                pltpu.VMEM((ROWS, RG), jnp.bfloat16),
                pltpu.VMEM((ROWS, RG), jnp.bfloat16),
                *scratch,
            ],
        ),
        cost_estimate=pl.CostEstimate(
            flops=work, bytes_accessed=DATES * lines * 16 * RG * 2, transcendentals=0
        ),
        compiler_params=pltpu.CompilerParams(vmem_limit_bytes=24 << 20),
    )(info, *operands)


def place_kernel(positions, usable, got, out, rows):
    for block in range(32):
        position = positions[block]
        valid = jnp.where(position < usable[0], 1.0, 0.0).astype(jnp.float32)
        rows[pl.ds(pl.multiple_of(position * 16, 16), 16), :] = got[block] * valid
    for plane in range(8):
        for part in range(8):
            out[plane // 2, plane % 2, part * 8 : part * 8 + 8, :] = rows[
                pl.ds(part * 64 + plane, 8, stride=8), :
            ]


def on_device(complex_images, segment_position_map, usable_position_total, interferogram_epochs):
    group = lax.axis_index("date")
    images = complex_images[:, 0].transpose(0, 1, 3, 2, 4)
    info = jnp.concatenate(
        [interferogram_epochs.reshape(-1), group.reshape(1)]
    ).astype(jnp.int32)
    box = (
        jnp.arange(RG)[:, None] // LOOK_RG == jnp.arange(LCOL)[None, :]
    ).astype(jnp.bfloat16)

    early = meet(*cut(info, images, 0, SPLIT))
    late = meet(*cut(info, images, SPLIT, LINES, early[3]))

    partial = jax.ShapeDtypeStruct((ROWS, LCOL), jnp.float32)
    sums0, sums1 = looks(early_kernel, info, (*early, box), (partial, partial), SPLIT)
    gamma = looks(
        late_kernel,
        info,
        (*late, box, sums0, sums1),
        jax.ShapeDtypeStruct((4, ITEMS, 16, LCOL), jnp.float32),
        LINES - SPLIT,
        (pltpu.VMEM((2, ROWS, LCOL), jnp.float32),),
    )

    moved = lax.all_to_all(gamma, "date", split_axis=0, concat_axis=0, tiled=True)
    got = lax.all_to_all(
        moved.reshape(32, 16, LCOL), "tile", split_axis=0, concat_axis=0, tiled=True
    )
    return pl.pallas_call(
        place_kernel,
        out_shape=jax.ShapeDtypeStruct((4, 2, 64, LCOL), jnp.float32),
        grid_spec=pltpu.PrefetchScalarGridSpec(
            num_scalar_prefetch=2,
            grid=(),
            in_specs=[VMEM],
            out_specs=VMEM,
            scratch_shapes=[pltpu.VMEM((512, LCOL), jnp.float32)],
        ),
        compiler_params=pltpu.CompilerParams(vmem_limit_bytes=4 << 20),
    )(segment_position_map[0], usable_position_total, got)


def solution(mesh):
    in_specs = (P("date", "tile", None, None, None, None), P("tile", None), P("tile"), P())
    out_specs = P("date", None, None, "tile")
    return jax.shard_map(
        on_device, mesh=mesh, in_specs=in_specs, out_specs=out_specs, check_vma=False
    )
```

time: 108 us -> 94.9 us (0.88)
  waiting for transfers between devices: 61.8 us -> 49.9 us
  local copies, waits for them, and re-layouts: 10.1 us -> 3.25 us
  starting transfers between devices: 13.9 us -> 17.3 us
  Pallas kernels: 11.9 us -> 13.6 us
    ppermute x3 -> x6, waiting for transfers between devices: 53.5 us -> 41.7 us  [the longest x2 23.2 us: meet(): three = lax.ppermute(to1, 'date', ring(1))]
    dynamic_slice x1 -> x0, local copies, waits for them, and re-layouts: 5.05 us -> none  [block_for(): lax.dynamic_slice_in_dim(images, lax.rem(group + step, 4) * ITEMS, ITEMS, 1)]
    transpose x4 -> x0, local copies, waits for them, and re-layouts: 3.65 us -> none  [block_for(): return part.transpose(0, 3, 2, 1, 4).reshape(2, 10, 16, RG)]
    ppermute x3 -> x6, starting transfers between devices: 4.43 us -> 7.91 us  [the longest x2 3 us: meet(): one = lax.ppermute(to3, 'date', ring(3))]
    pallas_call x1 -> x4, Pallas kernels: 9.52 us -> 12.3 us  [the longest x2 10.4 us: looks(): pl.pallas_call(kernel, out_shape=out_shape, grid_spec=pltpu.PrefetchScala...]
    unnamed x5 -> x7, local copies, waits for them, and re-layouts: 1.33 us -> 3.16 us
  transfers between devices with their start and end apart: 4 -> 7, of which waited for: 4 -> 4; matrix products, arithmetic and copies ran while one was open for 3% -> 0% of each run, Pallas kernels for 0% -> 9%
where the time goes in v3:
time: 94.9 us; the launch traced here: 94.6 us
  waiting for transfers between devices  49.9 us (53%)
  starting transfers between devices  17.3 us (18%)
  Pallas kernels  13.6 us (14%)
  blocking collectives  9.35 us (10%)
  local copies, waits for them, and re-layouts  3.25 us (3%)
    ppermute x2, waiting for transfers between devices, meet(): three = lax.ppermute(to1, 'date', ring(1))  23.2 us
    ppermute x2, waiting for transfers between devices, meet(): two = lax.ppermute(to2, 'date', ring(2))  18.5 us
    pallas_call x2, Pallas kernels, looks(): pl.pallas_call(kernel, out_shape=out_shape, grid_spec=pltpu.PrefetchScala...  10.4 us
    all_to_all x1, starting transfers between devices, on_device(): lax.all_to_all(moved.reshape(32, 16, LCOL), 'tile', split_axis=0, concat_...  9.43 us
    all_to_all x1, blocking collectives, on_device(): lax.all_to_all(gamma, 'date', split_axis=0, concat_axis=0, tiled=True)  9.35 us
    all_to_all x1, waiting for transfers between devices, on_device(): lax.all_to_all(moved.reshape(32, 16, LCOL), 'tile', split_axis=0, concat_...  8.25 us
    unnamed x7, local copies, waits for them, and re-layouts  3.16 us
    ppermute x2, starting transfers between devices, meet(): one = lax.ppermute(to3, 'date', ring(3))  3 us
  transfers between devices with their start and end apart: 7, of which 4 were waited for; matrix products, arithmetic and copies ran while one was open for 0% of the time, Pallas kernels for 9%

profile of v3, /device:TPU:1, one launch (start us, length us, event | category | flops | bytes accessed | tf_op | source)
XLA Modules:
  0.0 94.6 jit_solution(1811600350644313823)
XLA Ops:
  0.0 0.8 copy.6
  0.8 0.1 reshape.32
  0.8 0.1 pad_add_fusion.info
  0.9 2.4 %copy-done = bf16[2,1,32,2,10,1920]{5,3,4,2,1,0:T(2,128)(2,1)S(1)} copy-done((bf16[2,1,32,2,10,1920]{5,3,4,2,1,0:T(2,128)(2,1)S(1)}, bf16[2,1,32,2,10,1920]{5,3,4,2,1,0:T(2,128)(2,1)}, u32[]{:S(2)}) %copy-start) | copy-done | bytes 4915224
  3.3 1.1 %shard_map.46 = (bf16[8,2,8,2,1920]{4,3,2,1,0:T(2,128)(2,1)S(1)}, bf16[8,2,8,2,1920]{4,3,2,1,0:T(2,128)(2,1)S(1)}, bf16[8,2,8,2,1920]{4,3,2,1,0:T(2,128)(2,1)S(1)}, bf16[8,2,8,2,1920]{4,3,2,1,0:T(2,128)(2,1)S(1)}) custom-call(s32[33]{0:T(128)S(1)} %pad_add_fusion.info, bf16[2,32,10,2,1920]{4,3,2,1,0:T(2,128)(2,1)S(1)} %bitcast.6), custom_call_target="tpu_custom_call" | custom-call | tf_op jit(solution)/shard_map/pallas_call | solution.py:48
  4.4 2.1 %collective-permute-start = (bf16[8,2,8,2,1920]{4,3,2,1,0:T(2,128)(2,1)S(1)}, bf16[8,2,8,2,1920]{4,3,2,1,0:T(2,128)(2,1)S(1)}, u32[]{:S(2)}, u32[]{:S(2)}) collective-permute-start(bf16[8,2,8,2,1920]{4,3,2,1,0:T(2,128)(2,1)S(1)} %get-tuple-element.15), channel_id=1, source_target_pairs={{0,1},{1,2},{2,3},{3,0},{4,5},{5,6},{6,7},{7,4},{8,9},{9,10},{10,1... | collective-permute-start | bytes 2949128 | tf_op jit(solution)/shard_map/ppermute | solution.py:66
  6.5 1.3 %collective-permute-start.4 = (bf16[8,2,8,2,1920]{4,3,2,1,0:T(2,128)(2,1)S(1)}, bf16[8,2,8,2,1920]{4,3,2,1,0:T(2,128)(2,1)S(1)}, u32[]{:S(2)}, u32[]{:S(2)}) collective-permute-start(bf16[8,2,8,2,1920]{4,3,2,1,0:T(2,128)(2,1)S(1)} %get-tuple-element.21), channel_id=1, source_target_pairs={{0,3},{1,0},{2,1},{3,2},{4,7},{5,4},{6,5},{7,6},{8,11},{9,8},{10,9... | collective-permute-start | bytes 2949128 | tf_op jit(solution)/shard_map/ppermute | solution.py:67
  7.9 1.6 %collective-permute-start.5 = (bf16[8,2,8,2,1920]{4,3,2,1,0:T(2,128)(2,1)S(1)}, bf16[8,2,8,2,1920]{4,3,2,1,0:T(2,128)(2,1)S(1)}, u32[]{:S(2)}, u32[]{:S(2)}) collective-permute-start(bf16[8,2,8,2,1920]{4,3,2,1,0:T(2,128)(2,1)S(1)} %get-tuple-element.22), channel_id=1, source_target_pairs={{0,2},{1,3},{2,0},{3,1},{4,6},{5,7},{6,4},{7,5},{8,10},{9,11},{10,... | collective-permute-start | bytes 2949128 | tf_op jit(solution)/shard_map/ppermute | solution.py:68
  9.5 19.3 %collective-permute-done.rest_0_.three = bf16[8,2,8,2,1920]{4,3,2,1,0:T(2,128)(2,1)S(1)} collective-permute-done((bf16[8,2,8,2,1920]{4,3,2,1,0:T(2,128)(2,1)S(1)}, bf16[8,2,8,2,1920]{4,3,2,1,0:T(2,128)(2,1)S(1)}, u32[]{:S(2)}, u32[]{:S(2)}) %collective-permute-start) | collective-permute-done | bytes 983072 | tf_op jit(solution)/shard_map/ppermute | solution.py:66
  28.8 0.8 shard_map.47
  29.6 0.0 copy-start.2
  29.6 1.7 %collective-permute-start.1 = (bf16[8,2,2,2,1920]{4,3,2,1,0:T(2,128)(2,1)S(1)}, bf16[8,2,2,2,1920]{4,3,2,1,0:T(2,128)(2,1)S(1)}, u32[]{:S(2)}, u32[]{:S(2)}) collective-permute-start(bf16[8,2,2,2,1920]{4,3,2,1,0:T(2,128)(2,1)S(1)} %get-tuple-element.17), channel_id=1, source_target_pairs={{0,3},{1,0},{2,1},{3,2},{4,7},{5,4},{6,5},{7,6},{8,11},{9,8},{10,9... | collective-permute-start | bytes 737288 | tf_op jit(solution)/shard_map/ppermute | solution.py:67
  31.3 0.5 collective-permute-start.2
  31.8 0.6 collective-permute-start.3
  32.4 0.3 fusion.box
  32.8 18.5 %collective-permute-done.5.two = bf16[8,2,8,2,1920]{4,3,2,1,0:T(2,128)(2,1)S(1)} collective-permute-done((bf16[8,2,8,2,1920]{4,3,2,1,0:T(2,128)(2,1)S(1)}, bf16[8,2,8,2,1920]{4,3,2,1,0:T(2,128)(2,1)S(1)}, u32[]{:S(2)}, u32[]{:S(2)}) %collective-permute-start.5) | collective-permute-done | bytes 983072 | tf_op jit(solution)/shard_map/ppermute | solution.py:68
  51.2 7.6 %shard_map.48 = (f32[320,128]{1,0:T(8,128)S(1)}, f32[320,128]{1,0:T(8,128)S(1)}) custom-call(s32[33]{0:T(128)S(1)} %pad_add_fusion.info, bf16[8,2,8,2,1920]{4,3,2,1,0:T(2,128)(2,1)S(1)} %get-tuple-element.20.own, bf16[8,2,8,2,1920]{4,3,2,1,0:T(2,128)(2,1)S(1)} %collective-permute-done.4.one, bf16[8,2,8,2,1920]{4,3,2,1,0:T(2,128)(2,1)S(1)} %collective-permute-done.5.two, ...), custom_call_target="tpu_custom_call" | custom-call | flops 334233600 | bytes 3932160 | tf_op jit(solution)/shard_map/pallas_call | solution.py:147
  58.9 0.0 collective-permute-done.1.one
  58.9 3.9 %collective-permute-done.3.three = bf16[8,2,2,2,1920]{4,3,2,1,0:T(2,128)(2,1)S(1)} collective-permute-done((bf16[8,2,2,2,1920]{4,3,2,1,0:T(2,128)(2,1)S(1)}, bf16[8,2,2,2,1920]{4,3,2,1,0:T(2,128)(2,1)S(1)}, u32[]{:S(2)}, u32[]{:S(2)}) %collective-permute-start.3) | collective-permute-done | bytes 245792 | tf_op jit(solution)/shard_map/ppermute | solution.py:66
  62.8 2.8 %shard_map.49 = f32[4,8,16,128]{3,2,1,0:T(8,128)S(1)} custom-call(s32[33]{0:T(128)S(1)} %pad_add_fusion.info, bf16[8,2,2,2,1920]{4,3,2,1,0:T(2,128)(2,1)S(1)} %get-tuple-element.16.own, bf16[8,2,2,2,1920]{4,3,2,1,0:T(2,128)(2,1)S(1)} %collective-permute-done.1.one, bf16[8,2,2,2,1920]{4,3,2,1,0:T(2,128)(2,1)S(1)} %collective-permute-done.2.two, ...), custom_call_target="tpu_custom_call" | custom-call | flops 319488000 | bytes 983040 | tf_op jit(solution)/shard_map/pallas_call | solution.py:147
  65.6 9.3 %all_to_all.10 = f32[4,8,16,128]{3,2,1,0:T(8,128)} all-to-all(f32[4,8,16,128]{3,2,1,0:T(8,128)S(1)} %shard_map.49), channel_id=1, replica_groups=mesh['tile'=32,'date'=4] {'date'}, dimensions={0} | all-to-all | bytes 524288 | tf_op jit(solution)/shard_map/all_to_all | solution.py:205
  74.9 9.4 %all-to-all-start.1 = ((f32[32,16,128]{2,1,0:T(8,128)}), f32[32,16,128]{2,1,0:T(8,128)S(1)}, u32[]{:S(2)}, u32[]{:S(2)}) async-start(f32[32,16,128]{2,1,0:T(8,128)} %bitcast.5), calls=%async_computation.1 | async-start | bytes 524288 | tf_op jit(solution)/shard_map/all_to_all | solution.py:206
  85.0 8.3 %all-to-all-done.1.got = f32[32,16,128]{2,1,0:T(8,128)S(1)} async-done(((f32[32,16,128]{2,1,0:T(8,128)}), f32[32,16,128]{2,1,0:T(8,128)S(1)}, u32[]{:S(2)}, u32[]{:S(2)}) %all-to-all-start.1) | async-done | bytes 262176 | tf_op jit(solution)/shard_map/all_to_all | solution.py:206
  93.3 1.3 %shard_map.50 = f32[4,2,64,128]{3,2,1,0:T(8,128)} custom-call(s32[32]{0:T(128)S(1)} %bitcast.8, s32[1]{0:T(128)S(6)} %copy.7.usable, f32[32,16,128]{2,1,0:T(8,128)S(1)} %all-to-all-done.1.got), custom_call_target="tpu_custom_call" | custom-call | tf_op jit(solution)/shard_map/pallas_call | solution.py:209
  (7 shorter events, 0.0 us)
Async XLA Ops:
  0.9 2.4 %copy-start = (bf16[2,1,32,2,10,1920]{5,3,4,2,1,0:T(2,128)(2,1)S(1)}, bf16[2,1,32,2,10,1920]{5,3,4,2,1,0:T(2,128)(2,1)}, u32[]{:S(2)}) copy-start(bf16[2,1,32,2,10,1920]{5,3,4,2,1,0:T(2,128)(2,1)} %param.4) | copy-start | bytes 14745604
  3.3 25.5 %copy-start.1 = (bf16[2,1,32,2,10,1920]{5,3,4,2,1,0:T(2,128)(2,1)S(1)}, bf16[2,1,32,2,10,1920]{5,3,4,2,1,0:T(2,128)(2,1)}, u32[]{:S(2)}) copy-start(bf16[2,1,32,2,10,1920]{5,3,4,2,1,0:T(2,128)(2,1)} %param.4) | copy-start | bytes 14745604
  4.4 24.4 %collective-permute-start = (bf16[8,2,8,2,1920]{4,3,2,1,0:T(2,128)(2,1)S(1)}, bf16[8,2,8,2,1920]{4,3,2,1,0:T(2,128)(2,1)S(1)}, u32[]{:S(2)}, u32[]{:S(2)}) collective-permute-start(bf16[8,2,8,2,1920]{4,3,2,1,0:T(2,128)(2,1)S(1)} %get-tuple-element.15), channel_id=1, source_target_pairs={{0,1},{1,2},{2,3},{3,0},{4,5},{5,6},{6,7},{7,4},{8,9},{9,10},{10,1... | collective-permute-start | bytes 2949128 | tf_op jit(solution)/shard_map/ppermute | solution.py:66
  6.5 26.2 %collective-permute-start.4 = (bf16[8,2,8,2,1920]{4,3,2,1,0:T(2,128)(2,1)S(1)}, bf16[8,2,8,2,1920]{4,3,2,1,0:T(2,128)(2,1)S(1)}, u32[]{:S(2)}, u32[]{:S(2)}) collective-permute-start(bf16[8,2,8,2,1920]{4,3,2,1,0:T(2,128)(2,1)S(1)} %get-tuple-element.21), channel_id=1, source_target_pairs={{0,3},{1,0},{2,1},{3,2},{4,7},{5,4},{6,5},{7,6},{8,11},{9,8},{10,9... | collective-permute-start | bytes 2949128 | tf_op jit(solution)/shard_map/ppermute | solution.py:67
  7.9 43.4 %collective-permute-start.5 = (bf16[8,2,8,2,1920]{4,3,2,1,0:T(2,128)(2,1)S(1)}, bf16[8,2,8,2,1920]{4,3,2,1,0:T(2,128)(2,1)S(1)}, u32[]{:S(2)}, u32[]{:S(2)}) collective-permute-start(bf16[8,2,8,2,1920]{4,3,2,1,0:T(2,128)(2,1)S(1)} %get-tuple-element.22), channel_id=1, source_target_pairs={{0,2},{1,3},{2,0},{3,1},{4,6},{5,7},{6,4},{7,5},{8,10},{9,11},{10,... | collective-permute-start | bytes 2949128 | tf_op jit(solution)/shard_map/ppermute | solution.py:68
  29.6 63.7 %copy-start.2 = (s32[1,32]{1,0:T(1,128)S(1)}, s32[1,32]{1,0:T(1,128)}, u32[]{:S(2)}) copy-start(s32[1,32]{1,0:T(1,128)} %param.5) | copy-start | bytes 388
  29.6 29.2 %collective-permute-start.1 = (bf16[8,2,2,2,1920]{4,3,2,1,0:T(2,128)(2,1)S(1)}, bf16[8,2,2,2,1920]{4,3,2,1,0:T(2,128)(2,1)S(1)}, u32[]{:S(2)}, u32[]{:S(2)}) collective-permute-start(bf16[8,2,2,2,1920]{4,3,2,1,0:T(2,128)(2,1)S(1)} %get-tuple-element.17), channel_id=1, source_target_pairs={{0,3},{1,0},{2,1},{3,2},{4,7},{5,4},{6,5},{7,6},{8,11},{9,8},{10,9... | collective-permute-start | bytes 737288 | tf_op jit(solution)/shard_map/ppermute | solution.py:67
  31.3 27.6 %collective-permute-start.2 = (bf16[8,2,2,2,1920]{4,3,2,1,0:T(2,128)(2,1)S(1)}, bf16[8,2,2,2,1920]{4,3,2,1,0:T(2,128)(2,1)S(1)}, u32[]{:S(2)}, u32[]{:S(2)}) collective-permute-start(bf16[8,2,2,2,1920]{4,3,2,1,0:T(2,128)(2,1)S(1)} %get-tuple-element.18), channel_id=1, source_target_pairs={{0,2},{1,3},{2,0},{3,1},{4,6},{5,7},{6,4},{7,5},{8,10},{9,11},{10,... | collective-permute-start | bytes 737288 | tf_op jit(solution)/shard_map/ppermute | solution.py:68
  31.8 31.0 %collective-permute-start.3 = (bf16[8,2,2,2,1920]{4,3,2,1,0:T(2,128)(2,1)S(1)}, bf16[8,2,2,2,1920]{4,3,2,1,0:T(2,128)(2,1)S(1)}, u32[]{:S(2)}, u32[]{:S(2)}) collective-permute-start(bf16[8,2,2,2,1920]{4,3,2,1,0:T(2,128)(2,1)S(1)} %get-tuple-element.19), channel_id=1, source_target_pairs={{0,1},{1,2},{2,3},{3,0},{4,5},{5,6},{6,7},{7,4},{8,9},{9,10},{10,1... | collective-permute-start | bytes 737288 | tf_op jit(solution)/shard_map/ppermute | solution.py:66
  74.9 18.3 %all-to-all-start.1 = ((f32[32,16,128]{2,1,0:T(8,128)}), f32[32,16,128]{2,1,0:T(8,128)S(1)}, u32[]{:S(2)}, u32[]{:S(2)}) async-start(f32[32,16,128]{2,1,0:T(8,128)} %bitcast.5), calls=%async_computation.1 | async-start | bytes 524288 | tf_op jit(solution)/shard_map/all_to_all | solution.py:206

commit v4 on v1

v4 whole, which is shorter than its diff:
```python
import functools

import jax
import jax.numpy as jnp
from jax import lax
from jax.experimental import pallas as pl
from jax.experimental.pallas import tpu as pltpu
from jax.sharding import Mesh, PartitionSpec as P

LOOK_RG = 15
LOOK_AZ = 5
EPS = 1e-05
SCALE = 1.0 / (LOOK_AZ * LOOK_RG)
DATES = 8
PAIRS = 16
LINES = 10
RG = 1920
LCOL = 128
ROWS = (DATES + PAIRS) * 8
UNIT = (2, 2, LINES, 2, RG)

VMEM = pl.BlockSpec(memory_space=pltpu.VMEM)
HBM = pl.BlockSpec(memory_space=pltpu.HBM)
TOKEN = jax.ShapeDtypeStruct((8, LCOL), jnp.float32)


def cut_date_kernel(turns, images, *rest):
    to1, to2, to3, own, token, sem = rest[-6:]
    token[...] = jnp.zeros_like(token)
    group, y = lax.axis_index("date"), lax.axis_index("y")
    copies = []
    for step, out in ((1, to1), (3, to3), (2, to2), (0, own)):
        z = lax.rem(group + step, 4)
        for unit, turn in enumerate(turns):
            tiles = pl.ds(z * 8 + lax.rem(y + turn, 4) * 2, 2)
            for date in range(2):
                copies.append(
                    pltpu.make_async_copy(
                        images.at[date, tiles], out.at[unit, :, date], sem.at[len(copies)]
                    )
                )
                copies[-1].start()
    for copy in copies:
        copy.wait()


def cut_date(images, turns, after=None):
    operands = (images,) + (() if after is None else (after,))
    return pl.pallas_call(
        functools.partial(cut_date_kernel, turns),
        out_shape=[jax.ShapeDtypeStruct((len(turns), *UNIT), jnp.bfloat16)] * 4 + [TOKEN],
        in_specs=[HBM, VMEM][: len(operands)],
        out_specs=[VMEM] * 5,
        scratch_shapes=[pltpu.SemaphoreType.DMA((8 * len(turns),))],
        compiler_params=pltpu.CompilerParams(vmem_limit_bytes=48 << 20),
    )(*operands)


def cut_tile_kernel(images, after, out, sem):
    del after
    y = lax.axis_index("y")
    copies = []
    for z in range(4):
        for date in range(2):
            copies.append(
                pltpu.make_async_copy(
                    images.at[date, pl.ds(z * 8 + y * 2, 2)],
                    out.at[2 * z : 2 * z + 2, date],
                    sem.at[len(copies)],
                )
            )
            copies[-1].start()
    for copy in copies:
        copy.wait()


def cut_tile(images, after):
    return pl.pallas_call(
        cut_tile_kernel,
        out_shape=jax.ShapeDtypeStruct((8, 2, LINES, 2, RG), jnp.bfloat16),
        in_specs=[HBM, VMEM],
        out_specs=VMEM,
        scratch_shapes=[pltpu.SemaphoreType.DMA((8,))],
        compiler_params=pltpu.CompilerParams(vmem_limit_bytes=48 << 20),
    )(images, after)


def cut_crossed_kernel(crossed, to1, to2, to3, own, token, sem):
    token[...] = jnp.zeros_like(token)
    group = lax.axis_index("date")
    copies = []
    for step, out in ((1, to1), (3, to3), (2, to2), (0, own)):
        bursts = pl.ds(lax.rem(group + step, 4) * 2, 2)
        copies.append(pltpu.make_async_copy(crossed.at[bursts], out.at[0], sem.at[step]))
        copies[-1].start()
    for copy in copies:
        copy.wait()


def cut_crossed(crossed):
    return pl.pallas_call(
        cut_crossed_kernel,
        out_shape=[jax.ShapeDtypeStruct((1, *UNIT), jnp.bfloat16)] * 4 + [TOKEN],
        in_specs=[HBM],
        out_specs=[VMEM] * 5,
        scratch_shapes=[pltpu.SemaphoreType.DMA((4,))],
        compiler_params=pltpu.CompilerParams(vmem_limit_bytes=8 << 20),
    )(crossed)


def meet(to1, to2, to3, own):
    def ring(step):
        return [(i, (i + step) % 4) for i in range(4)]

    three = lax.ppermute(to1, "date", ring(1))
    one = lax.ppermute(to3, "date", ring(3))
    two = lax.ppermute(to2, "date", ring(2))
    return own, one, two, three


def unit_looks(epochs, blocks, box, img, swp, hi, lo, sums, gamma):
    group = lax.axis_index("date")
    even = lax.broadcasted_iota(jnp.int32, (8, RG), 0) % 2 == 0

    for step, block in enumerate(blocks):
        base = lax.rem(group + step, 4) * 2
        for date in range(2):
            for line in range(LOOK_AZ):
                pixels = jnp.concatenate(
                    [block[:, date, line], block[:, date, LOOK_AZ + line]], axis=0
                )
                pixels = pixels.reshape(8, RG).astype(jnp.float32)
                img[base + date, line] = pixels
                swp[base + date, line] = jnp.where(
                    even, -pltpu.roll(pixels, 7, 0), pltpu.roll(pixels, 1, 0)
                )

    def split(values, row):
        upper = values.astype(jnp.bfloat16)
        hi[pl.ds(row, 16), :] = upper
        lo[pl.ds(row, 16), :] = (values - upper.astype(jnp.float32)).astype(jnp.bfloat16)

    def joined(first, second):
        return jnp.where(
            even, first + pltpu.roll(first, 7, 0), second + pltpu.roll(second, 1, 0)
        )

    def power(half, carry):
        total = []
        for date in range(2):
            acc = jnp.zeros((8, RG), jnp.float32)
            for line in range(LOOK_AZ):
                pixels = img[2 * half + date, line]
                acc = acc + pixels * pixels
            total.append(joined(acc, acc))
        split(jnp.concatenate(total, axis=0), pl.multiple_of(half * 16, 16))
        return carry

    lax.fori_loop(0, DATES // 2, power, 0)

    def cross(half, carry):
        total = []
        for k in (2 * half, 2 * half + 1):
            a, b = epochs[0, k], epochs[1, k]
            same = jnp.zeros((8, RG), jnp.float32)
            other = jnp.zeros((8, RG), jnp.float32)
            for line in range(LOOK_AZ):
                pixels = img[a, line]
                same = same + pixels * img[b, line]
                other = other + pixels * swp[b, line]
            total.append(joined(same, other))
        split(jnp.concatenate(total, axis=0), pl.multiple_of(64 + half * 16, 16))
        return carry

    lax.fori_loop(0, PAIRS // 2, cross, 0)
    sums[...] = (
        jnp.dot(hi[...], box[...], preferred_element_type=jnp.float32)
        + jnp.dot(lo[...], box[...], preferred_element_type=jnp.float32)
    ) * SCALE
    for k in range(PAIRS):
        power_a = sums[pl.ds(pl.multiple_of(epochs[0, k] * 8, 8), 8), :]
        power_b = sums[pl.ds(pl.multiple_of(epochs[1, k] * 8, 8), 8), :]
        weight = 1.0 / jnp.sqrt((power_a + EPS) * (power_b + EPS))
        gamma[8 * k : 8 * k + 8, :] = sums[64 + 8 * k : 72 + 8 * k, :] * weight


def to_owner(gamma, owner, out):
    for item in range(2):
        for look in range(2):
            for part in range(2):
                row = look * 8 + part * 4
                out[item, row : row + 4, :] = gamma[
                    pl.ds(owner * 32 + look * 4 + item * 2 + part, 4, stride=8), :
                ]


def to_owners(gamma, out):
    for owner in range(4):
        to_owner(gamma, owner, out.at[:, owner])


WORK = [
    pltpu.VMEM((DATES, LOOK_AZ, 8, RG), jnp.float32),
    pltpu.VMEM((DATES, LOOK_AZ, 8, RG), jnp.float32),
    pltpu.VMEM((ROWS, RG), jnp.bfloat16),
    pltpu.VMEM((ROWS, RG), jnp.bfloat16),
    pltpu.VMEM((ROWS, LCOL), jnp.float32),
    pltpu.VMEM((PAIRS * 8, LCOL), jnp.float32),
]


def plain_kernel(units, epochs, own, one, two, three, box, out, *work):
    for unit in range(units):
        blocks = [block.at[unit] for block in (own, one, two, three)]
        unit_looks(epochs, blocks, box, *work)
        to_owners(work[-1], out.at[unit])


def last_kernel(epochs, own, one, two, three, box, after, to1, to2, to3, stay, *work):
    del after
    group = lax.axis_index("date")
    unit_looks(epochs, [block.at[0] for block in (own, one, two, three)], box, *work)
    for step, out in ((1, to1), (2, to2), (3, to3), (0, stay)):
        to_owner(work[-1], lax.rem(group + step, 4), out)


def address_kernel(epochs, own, one, two, three, box, early, after, out, token, *work):
    del after
    token[...] = jnp.zeros_like(token)
    y = lax.axis_index("y")
    for turn in (1, 2):
        for item in range(2):
            out[lax.rem(y + turn, 4) * 2 + item] = early[turn - 1, item]
    unit_looks(epochs, [block.at[0] for block in (own, one, two, three)], box, *work)
    to_owners(work[-1], out.at[pl.ds(lax.rem(y + 3, 4) * 2, 2)])


def looks(kernel, epochs, operands, out_shape, out_spec, after=()):
    return pl.pallas_call(
        kernel,
        out_shape=jax.tree.map(
            lambda shape: jax.ShapeDtypeStruct(shape, jnp.float32),
            out_shape,
            is_leaf=lambda shape: isinstance(shape, tuple),
        ),
        grid_spec=pltpu.PrefetchScalarGridSpec(
            num_scalar_prefetch=1,
            grid=(),
            in_specs=[VMEM] * (len(operands) + len(after)),
            out_specs=out_spec,
            scratch_shapes=WORK,
        ),
        cost_estimate=pl.CostEstimate(
            flops=1, bytes_accessed=1, transcendentals=0
        ),
        compiler_params=pltpu.CompilerParams(vmem_limit_bytes=24 << 20),
    )(epochs, *operands, *after)


def place_kernel(positions, usable, other, own, one, two, three, out, rows):
    y, group = lax.axis_index("y"), lax.axis_index("date")

    def put(burst, block):
        position = positions[burst]
        valid = jnp.where(position < usable[0], 1.0, 0.0).astype(jnp.float32)
        rows[pl.ds(pl.multiple_of(position * 16, 16), 16), :] = block * valid

    for turn in (1, 2, 3):
        y_from = lax.rem(y + turn, 4)
        for core in range(2):
            for z in range(4):
                put(z * 8 + y_from * 2 + core, other[y_from * 8 + core * 4 + z])
    for step, block in enumerate((own, one, two, three)):
        for core in range(2):
            put(lax.rem(group + step, 4) * 8 + y * 2 + core, block[core])
    for pair in range(4):
        for part in range(2):
            for eight in range(8):
                out[pair, part, eight * 8 : eight * 8 + 8, :] = rows[
                    pl.ds(eight * 64 + part * 4 + pair, 8, stride=8), :
                ]


def on_device(complex_images, segment_position_map, usable_position_total, interferogram_epochs):
    images = complex_images[:, 0].transpose(0, 1, 3, 2, 4)
    epochs = interferogram_epochs.T
    box = (
        jnp.arange(RG)[:, None] // LOOK_RG == jnp.arange(LCOL)[None, :]
    ).astype(jnp.bfloat16)

    cut_early = cut_date(images, (1, 2))
    cut_late = cut_date(images, (3,), cut_early[4])
    early = meet(*cut_early[:4])
    late = meet(*cut_late[:4])

    crossed = lax.all_to_all(
        cut_tile(images, cut_late[4]), ("z", "core"), split_axis=0, concat_axis=0, tiled=True
    )
    cut_last = cut_crossed(crossed)
    last = meet(*cut_last[:4])

    gamma_early = looks(
        functools.partial(plain_kernel, 2), epochs, (*early, box), (2, 2, 4, 16, LCOL), VMEM
    )
    addressed, computed = looks(
        address_kernel,
        epochs,
        (*late, box, gamma_early),
        [(8, 4, 16, LCOL), TOKEN.shape],
        [VMEM] * 2,
        (cut_last[4],),
    )
    swapped = lax.ppermute(
        addressed.reshape(32, 16, LCOL),
        ("z", "date"),
        [(z * 4 + date, date * 4 + z) for z in range(4) for date in range(4)],
    )
    other = lax.all_to_all(
        swapped, ("y", "core", "date"), split_axis=0, concat_axis=0, tiled=True
    )

    gamma_last = looks(
        last_kernel, epochs, (*last, box), [(2, 16, LCOL)] * 4, [VMEM] * 4, (computed,)
    )
    same = meet(*gamma_last)

    return pl.pallas_call(
        place_kernel,
        out_shape=jax.ShapeDtypeStruct((4, 2, 64, LCOL), jnp.float32),
        grid_spec=pltpu.PrefetchScalarGridSpec(
            num_scalar_prefetch=2,
            grid=(),
            in_specs=[VMEM] * 5,
            out_specs=VMEM,
            scratch_shapes=[pltpu.VMEM((512, LCOL), jnp.float32)],
        ),
        compiler_params=pltpu.CompilerParams(vmem_limit_bytes=4 << 20),
    )(segment_position_map[0], usable_position_total, other, *same)


def solution(mesh):
    fine = Mesh(mesh.devices.reshape(4, 4, 2, 4), ("z", "y", "core", "date"))
    tile = ("z", "y", "core")
    return jax.shard_map(
        on_device,
        mesh=fine,
        in_specs=(P("date", tile, None, None, None, None), P(tile, None), P(tile), P()),
        out_specs=P("date", None, None, tile),
        check_vma=False,
    )
```

time: 108 us -> 109 us (level); the launches traced: 108 us -> 108 us
  starting transfers between devices: 13.9 us -> 47.3 us
  waiting for transfers between devices: 61.8 us -> 35.6 us
  Pallas kernels: 11.9 us -> 22.7 us
  blocking collectives: 9.34 us -> 0 us
  local copies, waits for them, and re-layouts: 10.1 us -> 0.84 us
    all_to_all x1 -> x2, starting transfers between devices: 9.43 us -> 28.5 us  [the longest x1 22.2 us: on_device(): lax.all_to_all(swapped, ('y', 'core', 'date'), split_axis=0, concat_axis=...]
    ppermute x3 -> x13, waiting for transfers between devices: 53.5 us -> 35.6 us  [the longest x4 21 us: meet(): three = lax.ppermute(to1, 'date', ring(1))]
    ppermute x3 -> x13, starting transfers between devices: 4.43 us -> 18.9 us  [the longest x4 12.4 us: meet(): one = lax.ppermute(to3, 'date', ring(3))]
    pallas_call x1 -> x7, Pallas kernels: 9.52 us -> 21.3 us  [the longest x3 13.5 us: looks(): pl.pallas_call(kernel, out_shape=jax.tree.map(lambda shape: jax.ShapeDtyp...]
    all_to_all x1 -> x0, blocking collectives: 9.34 us -> none  [on_device(): lax.all_to_all(gamma, 'date', split_axis=0, concat_axis=0, tiled=True)]
    all_to_all x1 -> x2, waiting for transfers between devices: 8.25 us -> 0.01 us  [the longest x1 0.01 us: on_device(): lax.all_to_all(swapped, ('y', 'core', 'date'), split_axis=0, concat_axis=...]
    dynamic_slice x1 -> x0, local copies, waits for them, and re-layouts: 5.05 us -> none  [block_for(): lax.dynamic_slice_in_dim(images, lax.rem(group + step, 4) * ITEMS, ITEMS, 1)]
    transpose x4 -> x0, local copies, waits for them, and re-layouts: 3.65 us -> none  [block_for(): return part.transpose(0, 3, 2, 1, 4).reshape(2, 10, 16, RG)]
  transfers between devices with their start and end apart: 4 -> 15, of which waited for: 4 -> 6; matrix products, arithmetic and copies ran while one was open for 3% -> 0% of each run, Pallas kernels for 0% -> 13%
where the time goes in v4:
time: 109 us; the launch traced here: 108 us
  starting transfers between devices  47.3 us (43%)
  waiting for transfers between devices  35.6 us (33%)
  Pallas kernels  22.7 us (21%)
    all_to_all x1, starting transfers between devices, on_device(): lax.all_to_all(swapped, ('y', 'core', 'date'), split_axis=0, concat_axis=...  22.2 us
    ppermute x4, waiting for transfers between devices, meet(): three = lax.ppermute(to1, 'date', ring(1))  21 us
    ppermute x4, waiting for transfers between devices, meet(): two = lax.ppermute(to2, 'date', ring(2))  14.7 us
    pallas_call x3, Pallas kernels, looks(): pl.pallas_call(kernel, out_shape=jax.tree.map(lambda shape: jax.ShapeDtyp...  13.5 us
    ppermute x4, starting transfers between devices, meet(): one = lax.ppermute(to3, 'date', ring(3))  12.4 us
    all_to_all x1, starting transfers between devices, on_device(): lax.all_to_all(cut_tile(images, cut_late[4]), ('z', 'core'), split_axis=0...  6.28 us
    pallas_call x2, Pallas kernels, cut_date(): pl.pallas_call(functools.partial(cut_date_kernel, turns), out_shape=[jax....  4.62 us
    ppermute x4, starting transfers between devices, meet(): two = lax.ppermute(to2, 'date', ring(2))  3.02 us
  transfers between devices with their start and end apart: 15, of which 6 were waited for; matrix products, arithmetic and copies ran while one was open for 0% of the time, Pallas kernels for 13%

profile of v4, /device:TPU:1, one launch (start us, length us, event | category | flops | bytes accessed | tf_op | source)
XLA Modules:
  0.0 107.6 jit_solution(11244777947240544256)
XLA Ops:
  0.0 2.8 %shard_map.46 = (bf16[2,2,2,10,2,1920]{5,4,3,2,1,0:T(2,128)(2,1)S(1)}, bf16[2,2,2,10,2,1920]{5,4,3,2,1,0:T(2,128)(2,1)S(1)}, bf16[2,2,2,10,2,1920]{5,4,3,2,1,0:T...) custom-call(bf16[2,32,10,2,1920]{4,3,2,1,0:T(2,128)(2,1)} %bitcast.6), custom_call_target="tpu_custom_call" | custom-call | tf_op jit(solution)/shard_map/pallas_call | solution.py:49
  2.9 0.8 copy-done.4
  3.7 3.3 %collective-permute-start.3 = (bf16[2,2,2,10,2,1920]{5,4,3,2,1,0:T(2,128)(2,1)}, bf16[2,2,2,10,2,1920]{5,4,3,2,1,0:T(2,128)(2,1)S(1)}, u32[]{:S(2)}, u32[]{:S(2)}) collective-permute-start(bf16[2,2,2,10,2,1920]{5,4,3,2,1,0:T(2,128)(2,1)} %get-tuple-element.32), channel_id=1, source_target_pairs={{0,3},{1,0},{2,1},{3,2},{4,7},{5,4},{6,5},{7,6},{8,11},{9,8},{10,9... | collective-permute-start | bytes 1843208 | tf_op jit(solution)/shard_map/ppermute | solution.py:116
  7.0 1.8 %shard_map.47 = (bf16[1,2,2,10,2,1920]{5,4,3,2,1,0:T(2,128)(2,1)}, bf16[1,2,2,10,2,1920]{5,4,3,2,1,0:T(2,128)(2,1)}, bf16[1,2,2,10,2,1920]{5,4,3,2,1,0:T(2,128)(...) custom-call(bf16[2,32,10,2,1920]{4,3,2,1,0:T(2,128)(2,1)S(1)} %bitcast.7, ...), custom_call_target="tpu_custom_call" | custom-call | tf_op jit(solution)/shard_map/pallas_call | solution.py:49
  8.8 1.9 %shard_map.49 = bf16[8,2,10,2,1920]{4,3,2,1,0:T(2,128)(2,1)} custom-call(bf16[2,32,10,2,1920]{4,3,2,1,0:T(2,128)(2,1)S(1)} %bitcast.8, f32[8,128]{1,0:T(8,128)S(1)} %get-tuple-element.35.after), custom_call_target="tpu_custom_call" | custom-call | tf_op jit(solution)/shard_map/pallas_call | solution.py:78
  10.7 6.3 %all-to-all-start = ((bf16[8,2,10,2,1920]{4,3,2,1,0:T(2,128)(2,1)}), bf16[8,2,10,2,1920]{4,3,2,1,0:T(2,128)(2,1)S(1)}, u32[]{:S(2)}, u32[]{:S(2)}) async-start(bf16[8,2,10,2,1920]{4,3,2,1,0:T(2,128)(2,1)} %shard_map.49), calls=%async_computation | async-start | bytes 2457600 | tf_op jit(solution)/shard_map/all_to_all | solution.py:296
  18.1 2.1 %collective-permute-start = (bf16[1,2,2,10,2,1920]{5,4,3,2,1,0:T(2,128)(2,1)}, bf16[1,2,2,10,2,1920]{5,4,3,2,1,0:T(2,128)(2,1)}, u32[]{:S(2)}, u32[]{:S(2)}) collective-permute-start(bf16[1,2,2,10,2,1920]{5,4,3,2,1,0:T(2,128)(2,1)} %get-tuple-element.28), channel_id=1, source_target_pairs={{0,3},{1,0},{2,1},{3,2},{4,7},{5,4},{6,5},{7,6},{8,11},{9,8},{10,9... | collective-permute-start | bytes 921608 | tf_op jit(solution)/shard_map/ppermute | solution.py:116
  20.2 1.2 %collective-permute-start.1 = (bf16[1,2,2,10,2,1920]{5,4,3,2,1,0:T(2,128)(2,1)}, bf16[1,2,2,10,2,1920]{5,4,3,2,1,0:T(2,128)(2,1)}, u32[]{:S(2)}, u32[]{:S(2)}) collective-permute-start(bf16[1,2,2,10,2,1920]{5,4,3,2,1,0:T(2,128)(2,1)} %get-tuple-element.29), channel_id=1, source_target_pairs={{0,2},{1,3},{2,0},{3,1},{4,6},{5,7},{6,4},{7,5},{8,10},{9,11},{10,... | collective-permute-start | bytes 921608 | tf_op jit(solution)/shard_map/ppermute | solution.py:117
  21.9 12.4 %collective-permute-done.4.two = bf16[2,2,2,10,2,1920]{5,4,3,2,1,0:T(2,128)(2,1)S(1)} collective-permute-done((bf16[2,2,2,10,2,1920]{5,4,3,2,1,0:T(2,128)(2,1)}, bf16[2,2,2,10,2,1920]{5,4,3,2,1,0:T(2,128)(2,1)S(1)}, u32[]{:S(2)}, u32[]{:S(2)}) %collective-permute-start.4) | collective-permute-done | bytes 614432 | tf_op jit(solution)/shard_map/ppermute | solution.py:117
  34.2 13.7 %collective-permute-done.5.three = bf16[2,2,2,10,2,1920]{5,4,3,2,1,0:T(2,128)(2,1)S(1)} collective-permute-done((bf16[2,2,2,10,2,1920]{5,4,3,2,1,0:T(2,128)(2,1)}, bf16[2,2,2,10,2,1920]{5,4,3,2,1,0:T(2,128)(2,1)S(1)}, u32[]{:S(2)}, u32[]{:S(2)}) %collective-permute-start.5) | collective-permute-done | bytes 614432 | tf_op jit(solution)/shard_map/ppermute | solution.py:115
  48.0 5.9 %shard_map.48.early = f32[2,2,4,16,128]{4,3,2,1,0:T(8,128)S(1)} custom-call(s32[2,16]{1,0:T(2,128)S(1)} %bitcast.9, bf16[2,2,2,10,2,1920]{5,4,3,2,1,0:T(2,128)(2,1)S(1)} %get-tuple-element.31.own, bf16[2,2,2,10,2,1920]{5,4,3,2,1,0:T(2,128)(2,1)S(1)} %collective-permute-done.3.one, bf16[2,2,2,10,2,1920]{5,4,3,2,1,0:T(2,128)(2,1)S(1)} %collective-permute-done.4.two, ...), custom_call_target="tpu_custom_call" | custom-call | flops 1 | bytes 1 | tf_op jit(solution)/shard_map/pallas_call | solution.py:239
  53.9 1.3 %shard_map.50 = (bf16[1,2,2,10,2,1920]{5,4,3,2,1,0:T(2,128)(2,1)}, bf16[1,2,2,10,2,1920]{5,4,3,2,1,0:T(2,128)(2,1)}, bf16[1,2,2,10,2,1920]{5,4,3,2,1,0:T(2,128)(...) custom-call(bf16[8,2,10,2,1920]{4,3,2,1,0:T(2,128)(2,1)S(1)} %all-to-all-done.crossed), custom_call_target="tpu_custom_call" | custom-call | tf_op jit(solution)/shard_map/pallas_call | solution.py:101
  55.2 5.8 %collective-permute-done.2.three = bf16[1,2,2,10,2,1920]{5,4,3,2,1,0:T(2,128)(2,1)} collective-permute-done((bf16[1,2,2,10,2,1920]{5,4,3,2,1,0:T(2,128)(2,1)}, bf16[1,2,2,10,2,1920]{5,4,3,2,1,0:T(2,128)(2,1)}, u32[]{:S(2)}, u32[]{:S(2)}) %collective-permute-start.2) | collective-permute-done | bytes 307232 | tf_op jit(solution)/shard_map/ppermute | solution.py:115
  61.0 4.4 %shard_map.51 = (f32[8,4,16,128]{3,2,1,0:T(8,128)S(1)}, f32[8,128]{1,0:T(8,128)S(1)}) custom-call(s32[2,16]{1,0:T(2,128)S(1)} %bitcast.10, bf16[1,2,2,10,2,1920]{5,4,3,2,1,0:T(2,128)(2,1)S(1)} %get-tuple-element.27.own, bf16[1,2,2,10,2,1920]{5,4,3,2,1,0:T(2,128)(2,1)} %collective-permute-done.one, ...), custom_call_target="tpu_custom_call" | custom-call | flops 1 | bytes 1 | tf_op jit(solution)/shard_map/pallas_call | solution.py:239
  65.3 1.4 %collective-permute-start.6 = (f32[32,16,128]{2,1,0:T(8,128)S(1)}, f32[32,16,128]{2,1,0:T(8,128)}, u32[]{:S(2)}, u32[]{:S(2)}) collective-permute-start(f32[32,16,128]{2,1,0:T(8,128)S(1)} %bitcast.13), channel_id=1, source_target_pairs={{0,0},{1,32},{2,64},{3,96},{32,1},{33,33},{34,65},{35,97},{64,2},{... | collective-permute-start | bytes 786440 | tf_op jit(solution)/shard_map/ppermute | solution.py:313
  66.7 5.6 %collective-permute-start.7 = (bf16[1,2,2,10,2,1920]{5,4,3,2,1,0:T(2,128)(2,1)}, bf16[1,2,2,10,2,1920]{5,4,3,2,1,0:T(2,128)(2,1)S(1)}, u32[]{:S(2)}, u32[]{:S(2)}) collective-permute-start(bf16[1,2,2,10,2,1920]{5,4,3,2,1,0:T(2,128)(2,1)} %get-tuple-element.39), channel_id=1, source_target_pairs={{0,3},{1,0},{2,1},{3,2},{4,7},{5,4},{6,5},{7,6},{8,11},{9,8},{10,9... | collective-permute-start | bytes 921608 | tf_op jit(solution)/shard_map/ppermute | solution.py:116
  72.3 0.7 collective-permute-start.8
  73.0 0.8 collective-permute-start.9
  73.7 22.2 %all-to-all-start.1 = ((f32[32,16,128]{2,1,0:T(8,128)}), f32[32,16,128]{2,1,0:T(8,128)S(1)}, u32[]{:S(2)}, u32[]{:S(2)}) async-start(f32[32,16,128]{2,1,0:T(8,128)} %collective-permute-done.6), calls=%async_computation.1 | async-start | bytes 524288 | tf_op jit(solution)/shard_map/all_to_all | solution.py:318
  96.0 1.2 %collective-permute-done.9.three = bf16[1,2,2,10,2,1920]{5,4,3,2,1,0:T(2,128)(2,1)S(1)} collective-permute-done((bf16[1,2,2,10,2,1920]{5,4,3,2,1,0:T(2,128)(2,1)}, bf16[1,2,2,10,2,1920]{5,4,3,2,1,0:T(2,128)(2,1)S(1)}, u32[]{:S(2)}, u32[]{:S(2)}) %collective-permute-start.9) | collective-permute-done | bytes 307232 | tf_op jit(solution)/shard_map/ppermute | solution.py:115
  97.2 3.2 %shard_map.52 = (f32[2,16,128]{2,1,0:T(8,128)S(1)}, f32[2,16,128]{2,1,0:T(8,128)S(1)}, f32[2,16,128]{2,1,0:T(8,128)S(1)}, f32[2,16,128]{2,1,0:T(8,128)S(1)}) custom-call(s32[2,16]{1,0:T(2,128)S(1)} %bitcast.11, bf16[1,2,2,10,2,1920]{5,4,3,2,1,0:T(2,128)(2,1)S(1)} %get-tuple-element.38.own, bf16[1,2,2,10,2,1920]{5,4,3,2,1,0:T(2,128)(2,1)S(1)} %collective-permute-done.7.one, ...), custom_call_target="tpu_custom_call" | custom-call | flops 1 | bytes 1 | tf_op jit(solution)/shard_map/pallas_call | solution.py:239
  100.4 1.5 %collective-permute-start.10 = (f32[2,16,128]{2,1,0:T(8,128)S(1)}, f32[2,16,128]{2,1,0:T(8,128)S(1)}, u32[]{:S(2)}, u32[]{:S(2)}) collective-permute-start(f32[2,16,128]{2,1,0:T(8,128)S(1)} %get-tuple-element.44), channel_id=1, source_target_pairs={{0,3},{1,0},{2,1},{3,2},{4,7},{5,4},{6,5},{7,6},{8,11},{9,8},{10,9... | collective-permute-start | bytes 49160 | tf_op jit(solution)/shard_map/ppermute | solution.py:116
  103.7 2.3 %collective-permute-done.11.two = f32[2,16,128]{2,1,0:T(8,128)S(1)} collective-permute-done((f32[2,16,128]{2,1,0:T(8,128)S(1)}, f32[2,16,128]{2,1,0:T(8,128)S(1)}, u32[]{:S(2)}, u32[]{:S(2)}) %collective-permute-start.11) | collective-permute-done | bytes 16416 | tf_op jit(solution)/shard_map/ppermute | solution.py:117
  106.2 1.4 %shard_map.53 = f32[4,2,64,128]{3,2,1,0:T(8,128)} custom-call(s32[32]{0:T(128)S(1)} %bitcast.12, s32[1]{0:T(128)S(6)} %copy.5.usable, f32[32,16,128]{2,1,0:T(8,128)S(1)} %all-to-all-done.1.other, f32[2,16,128]{2,1,0:T(8,128)S(1)} %get-tuple-element.43.own, f32[2,16,128]{2,1,0:T(8,128)S(1)} %collective-permute-done.10.one, ...), custom_call_target="tpu_custom_call" | custom-call | tf_op jit(solution)/shard_map/pallas_call | solution.py:327
  (26 shorter events, 3.0 us)
Async XLA Ops:
  0.0 7.0 %copy-start = (bf16[2,1,32,2,10,1920]{5,3,4,2,1,0:T(2,128)(2,1)S(1)}, bf16[2,1,32,2,10,1920]{5,3,4,2,1,0:T(2,128)(2,1)}, u32[]{:S(2)}) copy-start(bf16[2,1,32,2,10,1920]{5,3,4,2,1,0:T(2,128)(2,1)} %param.4) | copy-start | bytes 14745604
  2.8 0.8 copy-start.4
  3.7 5.1 %copy-start.3 = (bf16[2,2,2,10,2,1920]{5,4,3,2,1,0:T(2,128)(2,1)}, bf16[2,2,2,10,2,1920]{5,4,3,2,1,0:T(2,128)(2,1)S(1)}, u32[]{:S(2)}) copy-start(bf16[2,2,2,10,2,1920]{5,4,3,2,1,0:T(2,128)(2,1)S(1)} %get-tuple-element.34) | copy-start | bytes 1843204
  3.7 17.8 %collective-permute-start.3 = (bf16[2,2,2,10,2,1920]{5,4,3,2,1,0:T(2,128)(2,1)}, bf16[2,2,2,10,2,1920]{5,4,3,2,1,0:T(2,128)(2,1)S(1)}, u32[]{:S(2)}, u32[]{:S(2)}) collective-permute-start(bf16[2,2,2,10,2,1920]{5,4,3,2,1,0:T(2,128)(2,1)} %get-tuple-element.32), channel_id=1, source_target_pairs={{0,3},{1,0},{2,1},{3,2},{4,7},{5,4},{6,5},{7,6},{8,11},{9,8},{10,9... | collective-permute-start | bytes 1843208 | tf_op jit(solution)/shard_map/ppermute | solution.py:116
  10.7 37.2 %copy-start.1 = (s32[16,2]{0,1:T(2,128)S(1)}, s32[16,2]{0,1:T(2,128)}, u32[]{:S(2)}) copy-start(s32[16,2]{0,1:T(2,128)} %param.7) | copy-start | bytes 388
  10.7 43.1 %all-to-all-start = ((bf16[8,2,10,2,1920]{4,3,2,1,0:T(2,128)(2,1)}), bf16[8,2,10,2,1920]{4,3,2,1,0:T(2,128)(2,1)S(1)}, u32[]{:S(2)}, u32[]{:S(2)}) async-start(bf16[8,2,10,2,1920]{4,3,2,1,0:T(2,128)(2,1)} %shard_map.49), calls=%async_computation | async-start | bytes 2457600 | tf_op jit(solution)/shard_map/all_to_all | solution.py:296
  17.0 17.2 %collective-permute-start.4 = (bf16[2,2,2,10,2,1920]{5,4,3,2,1,0:T(2,128)(2,1)}, bf16[2,2,2,10,2,1920]{5,4,3,2,1,0:T(2,128)(2,1)S(1)}, u32[]{:S(2)}, u32[]{:S(2)}) collective-permute-start(bf16[2,2,2,10,2,1920]{5,4,3,2,1,0:T(2,128)(2,1)} %copy-done.4), channel_id=1, source_target_pairs={{0,2},{1,3},{2,0},{3,1},{4,6},{5,7},{6,4},{7,5},{8,10},{9,11},{10,... | collective-permute-start | bytes 1843208 | tf_op jit(solution)/shard_map/ppermute | solution.py:117
  17.5 30.4 %collective-permute-start.5 = (bf16[2,2,2,10,2,1920]{5,4,3,2,1,0:T(2,128)(2,1)}, bf16[2,2,2,10,2,1920]{5,4,3,2,1,0:T(2,128)(2,1)S(1)}, u32[]{:S(2)}, u32[]{:S(2)}) collective-permute-start(bf16[2,2,2,10,2,1920]{5,4,3,2,1,0:T(2,128)(2,1)} %copy-done.3), channel_id=1, source_target_pairs={{0,1},{1,2},{2,3},{3,0},{4,5},{5,6},{6,7},{7,4},{8,9},{9,10},{10,1... | collective-permute-start | bytes 1843208 | tf_op jit(solution)/shard_map/ppermute | solution.py:115
  18.1 37.1 %collective-permute-start = (bf16[1,2,2,10,2,1920]{5,4,3,2,1,0:T(2,128)(2,1)}, bf16[1,2,2,10,2,1920]{5,4,3,2,1,0:T(2,128)(2,1)}, u32[]{:S(2)}, u32[]{:S(2)}) collective-permute-start(bf16[1,2,2,10,2,1920]{5,4,3,2,1,0:T(2,128)(2,1)} %get-tuple-element.28), channel_id=1, source_target_pairs={{0,3},{1,0},{2,1},{3,2},{4,7},{5,4},{6,5},{7,6},{8,11},{9,8},{10,9... | collective-permute-start | bytes 921608 | tf_op jit(solution)/shard_map/ppermute | solution.py:116
  20.2 35.0 %collective-permute-start.1 = (bf16[1,2,2,10,2,1920]{5,4,3,2,1,0:T(2,128)(2,1)}, bf16[1,2,2,10,2,1920]{5,4,3,2,1,0:T(2,128)(2,1)}, u32[]{:S(2)}, u32[]{:S(2)}) collective-permute-start(bf16[1,2,2,10,2,1920]{5,4,3,2,1,0:T(2,128)(2,1)} %get-tuple-element.29), channel_id=1, source_target_pairs={{0,2},{1,3},{2,0},{3,1},{4,6},{5,7},{6,4},{7,5},{8,10},{9,11},{10,... | collective-permute-start | bytes 921608 | tf_op jit(solution)/shard_map/ppermute | solution.py:117
  21.4 39.5 %collective-permute-start.2 = (bf16[1,2,2,10,2,1920]{5,4,3,2,1,0:T(2,128)(2,1)}, bf16[1,2,2,10,2,1920]{5,4,3,2,1,0:T(2,128)(2,1)}, u32[]{:S(2)}, u32[]{:S(2)}) collective-permute-start(bf16[1,2,2,10,2,1920]{5,4,3,2,1,0:T(2,128)(2,1)} %get-tuple-element.30), channel_id=1, source_target_pairs={{0,1},{1,2},{2,3},{3,0},{4,5},{5,6},{6,7},{7,4},{8,9},{9,10},{10,1... | collective-permute-start | bytes 921608 | tf_op jit(solution)/shard_map/ppermute | solution.py:115
  65.3 40.9 %copy-start.2 = (s32[1,32]{1,0:T(1,128)S(1)}, s32[1,32]{1,0:T(1,128)}, u32[]{:S(2)}) copy-start(s32[1,32]{1,0:T(1,128)} %param.5) | copy-start | bytes 388
  65.3 8.4 %collective-permute-start.6 = (f32[32,16,128]{2,1,0:T(8,128)S(1)}, f32[32,16,128]{2,1,0:T(8,128)}, u32[]{:S(2)}, u32[]{:S(2)}) collective-permute-start(f32[32,16,128]{2,1,0:T(8,128)S(1)} %bitcast.13), channel_id=1, source_target_pairs={{0,0},{1,32},{2,64},{3,96},{32,1},{33,33},{34,65},{35,97},{64,2},{... | collective-permute-start | bytes 786440 | tf_op jit(solution)/shard_map/ppermute | solution.py:313
  66.7 29.2 %collective-permute-start.7 = (bf16[1,2,2,10,2,1920]{5,4,3,2,1,0:T(2,128)(2,1)}, bf16[1,2,2,10,2,1920]{5,4,3,2,1,0:T(2,128)(2,1)S(1)}, u32[]{:S(2)}, u32[]{:S(2)}) collective-permute-start(bf16[1,2,2,10,2,1920]{5,4,3,2,1,0:T(2,128)(2,1)} %get-tuple-element.39), channel_id=1, source_target_pairs={{0,3},{1,0},{2,1},{3,2},{4,7},{5,4},{6,5},{7,6},{8,11},{9,8},{10,9... | collective-permute-start | bytes 921608 | tf_op jit(solution)/shard_map/ppermute | solution.py:116
  72.3 23.7 %collective-permute-start.8 = (bf16[1,2,2,10,2,1920]{5,4,3,2,1,0:T(2,128)(2,1)}, bf16[1,2,2,10,2,1920]{5,4,3,2,1,0:T(2,128)(2,1)S(1)}, u32[]{:S(2)}, u32[]{:S(2)}) collective-permute-start(bf16[1,2,2,10,2,1920]{5,4,3,2,1,0:T(2,128)(2,1)} %get-tuple-element.40), channel_id=1, source_target_pairs={{0,2},{1,3},{2,0},{3,1},{4,6},{5,7},{6,4},{7,5},{8,10},{9,11},{10,... | collective-permute-start | bytes 921608 | tf_op jit(solution)/shard_map/ppermute | solution.py:117
  73.0 24.2 %collective-permute-start.9 = (bf16[1,2,2,10,2,1920]{5,4,3,2,1,0:T(2,128)(2,1)}, bf16[1,2,2,10,2,1920]{5,4,3,2,1,0:T(2,128)(2,1)S(1)}, u32[]{:S(2)}, u32[]{:S(2)}) collective-permute-start(bf16[1,2,2,10,2,1920]{5,4,3,2,1,0:T(2,128)(2,1)} %get-tuple-element.41), channel_id=1, source_target_pairs={{0,1},{1,2},{2,3},{3,0},{4,5},{5,6},{6,7},{7,4},{8,9},{9,10},{10,1... | collective-permute-start | bytes 921608 | tf_op jit(solution)/shard_map/ppermute | solution.py:115
  73.7 32.5 %all-to-all-start.1 = ((f32[32,16,128]{2,1,0:T(8,128)}), f32[32,16,128]{2,1,0:T(8,128)S(1)}, u32[]{:S(2)}, u32[]{:S(2)}) async-start(f32[32,16,128]{2,1,0:T(8,128)} %collective-permute-done.6), calls=%async_computation.1 | async-start | bytes 524288 | tf_op jit(solution)/shard_map/all_to_all | solution.py:318
  100.4 3.3 %collective-permute-start.10 = (f32[2,16,128]{2,1,0:T(8,128)S(1)}, f32[2,16,128]{2,1,0:T(8,128)S(1)}, u32[]{:S(2)}, u32[]{:S(2)}) collective-permute-start(f32[2,16,128]{2,1,0:T(8,128)S(1)} %get-tuple-element.44), channel_id=1, source_target_pairs={{0,3},{1,0},{2,1},{3,2},{4,7},{5,4},{6,5},{7,6},{8,11},{9,8},{10,9... | collective-permute-start | bytes 49160 | tf_op jit(solution)/shard_map/ppermute | solution.py:116
  101.9 4.1 %collective-permute-start.11 = (f32[2,16,128]{2,1,0:T(8,128)S(1)}, f32[2,16,128]{2,1,0:T(8,128)S(1)}, u32[]{:S(2)}, u32[]{:S(2)}) collective-permute-start(f32[2,16,128]{2,1,0:T(8,128)S(1)} %get-tuple-element.45), channel_id=1, source_target_pairs={{0,2},{1,3},{2,0},{3,1},{4,6},{5,7},{6,4},{7,5},{8,10},{9,11},{10,... | collective-permute-start | bytes 49160 | tf_op jit(solution)/shard_map/ppermute | solution.py:117
  102.4 3.8 %collective-permute-start.12 = (f32[2,16,128]{2,1,0:T(8,128)S(1)}, f32[2,16,128]{2,1,0:T(8,128)S(1)}, u32[]{:S(2)}, u32[]{:S(2)}) collective-permute-start(f32[2,16,128]{2,1,0:T(8,128)S(1)} %get-tuple-element.46), channel_id=1, source_target_pairs={{0,1},{1,2},{2,3},{3,0},{4,5},{5,6},{6,7},{7,4},{8,9},{9,10},{10,1... | collective-permute-start | bytes 49160 | tf_op jit(solution)/shard_map/ppermute | solution.py:115

commit v5 on v3

v5 whole, which is shorter than its diff:
```python
import functools

import jax
import jax.numpy as jnp
from jax import lax
from jax.experimental import pallas as pl
from jax.experimental.pallas import tpu as pltpu
from jax.sharding import Mesh, PartitionSpec as P

LOOK_RG = 15
LOOK_AZ = 5
EPS = 1e-05
SCALE = 1.0 / (LOOK_AZ * LOOK_RG)
DATES = 8
PAIRS = 16
ITEMS = 8
RG = 1920
LCOL = 128
ROWS = 320
SPLIT = 8
LINES = 10

VMEM = pl.BlockSpec(memory_space=pltpu.VMEM)
SMEM = pl.BlockSpec(memory_space=pltpu.SMEM)
HBM = pl.BlockSpec(memory_space=pltpu.HBM)
ANYWHERE = pl.BlockSpec(memory_space=pl.ANY)


def cut_kernel(low, high, images, *rest):
    to1, to2, to3, own, sem = rest[-5:]
    group = lax.axis_index("date")
    copies = []
    for step, out in ((1, to1), (3, to3), (2, to2), (0, own)):
        tiles = pl.ds(lax.rem(group + step, 4) * ITEMS, ITEMS)
        for date in range(2):
            copies.append(
                pltpu.make_async_copy(
                    images.at[date, tiles, low:high], out.at[:, date], sem.at[len(copies)]
                )
            )
            copies[-1].start()
    for copy in copies:
        copy.wait()


def cut(images, low, high, after=None):
    block = jax.ShapeDtypeStruct((ITEMS, 2, high - low, 2, RG), jnp.bfloat16)
    operands = (images,) + (() if after is None else (after,))
    return pl.pallas_call(
        functools.partial(cut_kernel, low, high),
        out_shape=[block] * 4,
        in_specs=[HBM, ANYWHERE][: len(operands)],
        out_specs=[VMEM] * 4,
        scratch_shapes=[pltpu.SemaphoreType.DMA((8,))],
        compiler_params=pltpu.CompilerParams(vmem_limit_bytes=8 << 20),
    )(*operands)


def meet(to1, to2, to3, own):
    def ring(step):
        return [(i, (i + step) % 4) for i in range(4)]

    three = lax.ppermute(to1, "date", ring(1))
    one = lax.ppermute(to3, "date", ring(3))
    two = lax.ppermute(to2, "date", ring(2))
    return own, one, two, three


def add_lines(epochs, blocks, low, high, box, img, hi, lo):
    group = lax.axis_index("date")
    lines = high - low
    for step, block in enumerate(blocks):
        base = lax.rem(group + step, 4) * 2
        for date in range(2):
            for line in range(lines):
                pixels = jnp.swapaxes(block[:, date, low + line], 0, 1).reshape(16, RG)
                img[base + date, line] = pixels.astype(jnp.float32)

    def split(values, row):
        upper = values.astype(jnp.bfloat16)
        hi[pl.ds(row, 16), :] = upper
        lo[pl.ds(row, 16), :] = (values - upper.astype(jnp.float32)).astype(jnp.bfloat16)

    def power(half, carry):
        total = []
        for date in range(2):
            acc = jnp.zeros((ITEMS, RG), jnp.float32)
            for line in range(lines):
                re = img[2 * half + date, line, 0:8, :]
                im = img[2 * half + date, line, 8:16, :]
                acc = acc + (re * re + im * im)
            total.append(acc)
        split(jnp.concatenate(total, axis=0), pl.multiple_of(half * 16, 16))
        return carry

    lax.fori_loop(0, DATES // 2, power, 0)

    def cross(k, carry):
        a, b = epochs[0, k], epochs[1, k]
        acc_re = jnp.zeros((ITEMS, RG), jnp.float32)
        acc_im = jnp.zeros((ITEMS, RG), jnp.float32)
        for line in range(lines):
            re_a, im_a = img[a, line, 0:8, :], img[a, line, 8:16, :]
            re_b, im_b = img[b, line, 0:8, :], img[b, line, 8:16, :]
            acc_re = acc_re + (re_a * re_b + im_a * im_b)
            acc_im = acc_im + (im_a * re_b - re_a * im_b)
        split(jnp.concatenate([acc_re, acc_im], axis=0), pl.multiple_of(64 + k * 16, 16))
        return carry

    lax.fori_loop(0, PAIRS, cross, 0)
    return jnp.dot(hi[...], box[...], preferred_element_type=jnp.float32) + jnp.dot(
        lo[...], box[...], preferred_element_type=jnp.float32
    )


def early_kernel(epochs, own, one, two, three, box, sums0, sums1, img, hi, lo):
    blocks = (own, one, two, three)
    sums0[...] = add_lines(epochs, blocks, 0, LOOK_AZ, box, img, hi, lo)
    sums1[...] = add_lines(epochs, blocks, LOOK_AZ, SPLIT, box, img, hi, lo)


def late_kernel(epochs, own, one, two, three, box, early0, early1, table, out, img, hi, lo, sums):
    del table
    sums[0] = early0[...] * SCALE
    total = add_lines(epochs, (own, one, two, three), 0, LINES - SPLIT, box, img, hi, lo)
    sums[1] = (total + early1[...]) * SCALE
    for owner in range(4):
        for look in range(2):
            rows = []
            for kk in range(4):
                k = owner * 4 + kk
                power_a = sums[look, pl.ds(pl.multiple_of(epochs[0, k] * 8, 8), 8), :]
                power_b = sums[look, pl.ds(pl.multiple_of(epochs[1, k] * 8, 8), 8), :]
                weight = 1.0 / jnp.sqrt((power_a + EPS) * (power_b + EPS))
                rows.append(sums[look, 64 + k * 16 : 72 + k * 16, :] * weight)
                rows.append(sums[look, 72 + k * 16 : 80 + k * 16, :] * weight)
            out[:, owner, look * 8 : look * 8 + 8, :] = jnp.swapaxes(
                jnp.stack(rows, axis=0), 0, 1
            )


def looks(kernel, epochs, operands, out_shape, lines, scratch=()):
    work = lines * ITEMS * RG * (PAIRS * 8 + DATES * 4) + 4 * ROWS * RG * LCOL
    return pl.pallas_call(
        kernel,
        out_shape=out_shape,
        grid_spec=pltpu.PrefetchScalarGridSpec(
            num_scalar_prefetch=1,
            grid=(),
            in_specs=[VMEM if x.ndim > 1 else SMEM for x in operands],
            out_specs=jax.tree.map(lambda _: VMEM, out_shape),
            scratch_shapes=[
                pltpu.VMEM((DATES, min(lines, LOOK_AZ), 16, RG), jnp.float32),
                pltpu.VMEM((ROWS, RG), jnp.bfloat16),
                pltpu.VMEM((ROWS, RG), jnp.bfloat16),
                *scratch,
            ],
        ),
        cost_estimate=pl.CostEstimate(
            flops=work, bytes_accessed=DATES * lines * 16 * RG * 2, transcendentals=0
        ),
        compiler_params=pltpu.CompilerParams(vmem_limit_bytes=24 << 20),
    )(epochs, *operands)


def place_kernel(table, got, out, rows):
    for y in range(4):
        for core in range(2):
            for z in range(4):
                position = table[z * 8 + y * 2 + core]
                valid = jnp.where(position < table[32], 1.0, 0.0).astype(jnp.float32)
                rows[pl.ds(pl.multiple_of(position * 16, 16), 16), :] = (
                    got[y * 8 + core * 4 + z] * valid
                )
    for plane in range(8):
        for part in range(8):
            out[plane // 2, plane % 2, part * 8 : part * 8 + 8, :] = rows[
                pl.ds(part * 64 + plane, 8, stride=8), :
            ]


def on_device(complex_images, segment_position_map, usable_position_total, interferogram_epochs):
    images = complex_images[:, 0].transpose(0, 1, 3, 2, 4)
    epochs = interferogram_epochs.T
    table = jnp.concatenate([segment_position_map[0], usable_position_total])
    box = (
        jnp.arange(RG)[:, None] // LOOK_RG == jnp.arange(LCOL)[None, :]
    ).astype(jnp.bfloat16)

    early = meet(*cut(images, 0, SPLIT))
    late = meet(*cut(images, SPLIT, LINES, early[3]))

    partial = jax.ShapeDtypeStruct((ROWS, LCOL), jnp.float32)
    sums0, sums1 = looks(
        early_kernel, epochs, (*early, box), (partial, partial), SPLIT
    )
    gamma = looks(
        late_kernel,
        epochs,
        (*late, box, sums0, sums1, table),
        jax.ShapeDtypeStruct((ITEMS, 4, 16, LCOL), jnp.float32),
        LINES - SPLIT,
        (pltpu.VMEM((2, ROWS, LCOL), jnp.float32),),
    )

    swapped = lax.ppermute(
        gamma.reshape(32, 16, LCOL),
        ("z", "date"),
        [(z * 4 + date, date * 4 + z) for z in range(4) for date in range(4)],
    )
    got = lax.all_to_all(
        swapped, ("y", "core", "date"), split_axis=0, concat_axis=0, tiled=True
    )
    return pl.pallas_call(
        place_kernel,
        out_shape=jax.ShapeDtypeStruct((4, 2, 64, LCOL), jnp.float32),
        grid_spec=pltpu.PrefetchScalarGridSpec(
            num_scalar_prefetch=1,
            grid=(),
            in_specs=[VMEM],
            out_specs=VMEM,
            scratch_shapes=[pltpu.VMEM((512, LCOL), jnp.float32)],
        ),
        compiler_params=pltpu.CompilerParams(vmem_limit_bytes=4 << 20),
    )(table, got)


def solution(mesh):
    fine = Mesh(mesh.devices.reshape(4, 4, 2, 4), ("z", "y", "core", "date"))
    tile = ("z", "y", "core")
    return jax.shard_map(
        on_device,
        mesh=fine,
        in_specs=(P("date", tile, None, None, None, None), P(tile, None), P(tile), P()),
        out_specs=P("date", None, None, tile),
        check_vma=False,
    )
```

time: 94.9 us -> 100 us (1.054)
  blocking collectives: 9.35 us -> 33.6 us
  starting transfers between devices: 17.3 us -> 8.59 us
  waiting for transfers between devices: 49.9 us -> 41.3 us
    all_to_all x1, blocking collectives: 9.35 us -> 33.6 us  [on_device(): lax.all_to_all(swapped, ('y', 'core', 'date'), split_axis=0, concat_axis=...]
    all_to_all x1 -> x0, starting transfers between devices: 9.43 us -> none  [on_device(): lax.all_to_all(moved.reshape(32, 16, LCOL), 'tile', split_axis=0, concat_...]
    all_to_all x1 -> x0, waiting for transfers between devices: 8.25 us -> none  [on_device(): lax.all_to_all(moved.reshape(32, 16, LCOL), 'tile', split_axis=0, concat_...]
    pallas_call x2, Pallas kernels: 1.86 us -> 0.76 us  [cut(): pl.pallas_call(functools.partial(cut_kernel, low, high), out_shape=[block...]
    unnamed x7 -> x8, local copies, waits for them, and re-layouts: 3.16 us -> 2.4 us
  transfers between devices with their start and end apart: 7 -> 7, of which waited for: 4 -> 3; matrix products, arithmetic and copies ran while one was open for 0% -> 0% of each run, Pallas kernels for 9% -> 8%
where the time goes in v5:
time: 100 us
  waiting for transfers between devices  41.3 us (41%)
  blocking collectives  33.6 us (34%)
  Pallas kernels  13.3 us (13%)
  starting transfers between devices  8.59 us (9%)
  local copies, waits for them, and re-layouts  2.4 us (2%)
    all_to_all x1, blocking collectives, on_device(): lax.all_to_all(swapped, ('y', 'core', 'date'), split_axis=0, concat_axis=...  33.6 us
    ppermute x2, waiting for transfers between devices, meet(): three = lax.ppermute(to1, 'date', ring(1))  23 us
    ppermute x2, waiting for transfers between devices, meet(): two = lax.ppermute(to2, 'date', ring(2))  18.3 us
    pallas_call x2, Pallas kernels, looks(): pl.pallas_call(kernel, out_shape=out_shape, grid_spec=pltpu.PrefetchScala...  11.2 us
    ppermute x2, starting transfers between devices, meet(): one = lax.ppermute(to3, 'date', ring(3))  3 us
    ppermute x2, starting transfers between devices, meet(): three = lax.ppermute(to1, 'date', ring(1))  2.74 us
    unnamed x8, local copies, waits for them, and re-layouts  2.4 us
    ppermute x2, starting transfers between devices, meet(): two = lax.ppermute(to2, 'date', ring(2))  2.17 us
  transfers between devices with their start and end apart: 7, of which 3 were waited for; matrix products, arithmetic and copies ran while one was open for 0% of the time, Pallas kernels for 8%

profile of v5, /device:TPU:1, one launch (start us, length us, event | category | flops | bytes accessed | tf_op | source)
XLA Modules:
  0.0 100.3 jit_solution(286433127944823732)
XLA Ops:
  0.0 2.4 %copy-done = bf16[2,1,32,2,10,1920]{5,3,4,2,1,0:T(2,128)(2,1)S(1)} copy-done((bf16[2,1,32,2,10,1920]{5,3,4,2,1,0:T(2,128)(2,1)S(1)}, bf16[2,1,32,2,10,1920]{5,3,4,2,1,0:T(2,128)(2,1)}, u32[]{:S(2)}) %copy-start) | copy-done | bytes 4915224
  2.4 0.5 shard_map.46
  2.9 2.1 %collective-permute-start = (bf16[8,2,8,2,1920]{4,3,2,1,0:T(2,128)(2,1)S(1)}, bf16[8,2,8,2,1920]{4,3,2,1,0:T(2,128)(2,1)S(1)}, u32[]{:S(2)}, u32[]{:S(2)}) collective-permute-start(bf16[8,2,8,2,1920]{4,3,2,1,0:T(2,128)(2,1)S(1)} %get-tuple-element.15), channel_id=1, source_target_pairs={{0,1},{1,2},{2,3},{3,0},{4,5},{5,6},{6,7},{7,4},{8,9},{9,10},{10,1... | collective-permute-start | bytes 2949128 | tf_op jit(solution)/shard_map/ppermute | solution.py:63
  5.0 1.3 %collective-permute-start.4 = (bf16[8,2,8,2,1920]{4,3,2,1,0:T(2,128)(2,1)S(1)}, bf16[8,2,8,2,1920]{4,3,2,1,0:T(2,128)(2,1)S(1)}, u32[]{:S(2)}, u32[]{:S(2)}) collective-permute-start(bf16[8,2,8,2,1920]{4,3,2,1,0:T(2,128)(2,1)S(1)} %get-tuple-element.21), channel_id=1, source_target_pairs={{0,3},{1,0},{2,1},{3,2},{4,7},{5,4},{6,5},{7,6},{8,11},{9,8},{10,9... | collective-permute-start | bytes 2949128 | tf_op jit(solution)/shard_map/ppermute | solution.py:64
  6.4 1.6 %collective-permute-start.5 = (bf16[8,2,8,2,1920]{4,3,2,1,0:T(2,128)(2,1)S(1)}, bf16[8,2,8,2,1920]{4,3,2,1,0:T(2,128)(2,1)S(1)}, u32[]{:S(2)}, u32[]{:S(2)}) collective-permute-start(bf16[8,2,8,2,1920]{4,3,2,1,0:T(2,128)(2,1)S(1)} %get-tuple-element.22), channel_id=1, source_target_pairs={{0,2},{1,3},{2,0},{3,1},{4,6},{5,7},{6,4},{7,5},{8,10},{9,11},{10,... | collective-permute-start | bytes 2949128 | tf_op jit(solution)/shard_map/ppermute | solution.py:65
  8.1 19.3 %collective-permute-done.rest_0_.three = bf16[8,2,8,2,1920]{4,3,2,1,0:T(2,128)(2,1)S(1)} collective-permute-done((bf16[8,2,8,2,1920]{4,3,2,1,0:T(2,128)(2,1)S(1)}, bf16[8,2,8,2,1920]{4,3,2,1,0:T(2,128)(2,1)S(1)}, u32[]{:S(2)}, u32[]{:S(2)}) %collective-permute-start) | collective-permute-done | bytes 983072 | tf_op jit(solution)/shard_map/ppermute | solution.py:63
  27.4 0.0 copy-done.1
  27.4 0.2 shard_map.47
  27.6 1.7 %collective-permute-start.1 = (bf16[8,2,2,2,1920]{4,3,2,1,0:T(2,128)(2,1)S(1)}, bf16[8,2,2,2,1920]{4,3,2,1,0:T(2,128)(2,1)S(1)}, u32[]{:S(2)}, u32[]{:S(2)}) collective-permute-start(bf16[8,2,2,2,1920]{4,3,2,1,0:T(2,128)(2,1)S(1)} %get-tuple-element.17), channel_id=1, source_target_pairs={{0,3},{1,0},{2,1},{3,2},{4,7},{5,4},{6,5},{7,6},{8,11},{9,8},{10,9... | collective-permute-start | bytes 737288 | tf_op jit(solution)/shard_map/ppermute | solution.py:64
  29.2 0.5 collective-permute-start.2
  29.8 0.6 collective-permute-start.3
  30.4 0.3 fusion.box
  31.4 0.1 pad_add_fusion.table
  31.5 0.0 collective-permute-done.4.one
  31.5 18.3 %collective-permute-done.5.two = bf16[8,2,8,2,1920]{4,3,2,1,0:T(2,128)(2,1)S(1)} collective-permute-done((bf16[8,2,8,2,1920]{4,3,2,1,0:T(2,128)(2,1)S(1)}, bf16[8,2,8,2,1920]{4,3,2,1,0:T(2,128)(2,1)S(1)}, u32[]{:S(2)}, u32[]{:S(2)}) %collective-permute-start.5) | collective-permute-done | bytes 983072 | tf_op jit(solution)/shard_map/ppermute | solution.py:65
  49.8 7.8 %shard_map.48 = (f32[320,128]{1,0:T(8,128)S(1)}, f32[320,128]{1,0:T(8,128)S(1)}) custom-call(s32[2,16]{1,0:T(2,128)S(1)} %bitcast.9, bf16[8,2,8,2,1920]{4,3,2,1,0:T(2,128)(2,1)S(1)} %get-tuple-element.20.own, bf16[8,2,8,2,1920]{4,3,2,1,0:T(2,128)(2,1)S(1)} %collective-permute-done.4.one, bf16[8,2,8,2,1920]{4,3,2,1,0:T(2,128)(2,1)S(1)} %collective-permute-done.5.two, ...), custom_call_target="tpu_custom_call" | custom-call | flops 334233600 | bytes 3932160 | tf_op jit(solution)/shard_map/pallas_call | solution.py:144
  57.6 0.0 collective-permute-done.1.one
  57.6 0.0 collective-permute-done.2.two
  57.6 3.7 %collective-permute-done.3.three = bf16[8,2,2,2,1920]{4,3,2,1,0:T(2,128)(2,1)S(1)} collective-permute-done((bf16[8,2,2,2,1920]{4,3,2,1,0:T(2,128)(2,1)S(1)}, bf16[8,2,2,2,1920]{4,3,2,1,0:T(2,128)(2,1)S(1)}, u32[]{:S(2)}, u32[]{:S(2)}) %collective-permute-start.3) | collective-permute-done | bytes 245792 | tf_op jit(solution)/shard_map/ppermute | solution.py:63
  61.3 3.4 %shard_map.49 = f32[8,4,16,128]{3,2,1,0:T(8,128)S(1)} custom-call(s32[2,16]{1,0:T(2,128)S(1)} %bitcast.10, bf16[8,2,2,2,1920]{4,3,2,1,0:T(2,128)(2,1)S(1)} %get-tuple-element.16.own, bf16[8,2,2,2,1920]{4,3,2,1,0:T(2,128)(2,1)S(1)} %collective-permute-done.1.one, bf16[8,2,2,2,1920]{4,3,2,1,0:T(2,128)(2,1)S(1)} %collective-permute-done.2.two, ...), custom_call_target="tpu_custom_call" | custom-call | flops 319488000 | bytes 983040 | tf_op jit(solution)/shard_map/pallas_call | solution.py:144
  64.7 0.7 collective-permute-start.6
  65.4 0.0 collective-permute-done.6
  65.4 33.6 %all_to_all.5.got = f32[32,16,128]{2,1,0:T(8,128)S(1)} all-to-all(f32[32,16,128]{2,1,0:T(8,128)S(1)} %collective-permute-done.6), channel_id=1, replica_groups=mesh['z'=4,'y'=4,'core'=2,'date'=4] {'y','core','date'}, dimensions={0} | all-to-all | bytes 524288 | tf_op jit(solution)/shard_map/all_to_all | solution.py:211
  98.9 1.3 %shard_map.50 = f32[4,2,64,128]{3,2,1,0:T(8,128)} custom-call(s32[33]{0:T(128)S(1)} %pad_add_fusion.table, f32[32,16,128]{2,1,0:T(8,128)S(1)} %all_to_all.5.got), custom_call_target="tpu_custom_call" | custom-call | tf_op jit(solution)/shard_map/pallas_call | solution.py:214
  (7 shorter events, 0.0 us)
Async XLA Ops:
  0.0 2.4 %copy-start = (bf16[2,1,32,2,10,1920]{5,3,4,2,1,0:T(2,128)(2,1)S(1)}, bf16[2,1,32,2,10,1920]{5,3,4,2,1,0:T(2,128)(2,1)}, u32[]{:S(2)}) copy-start(bf16[2,1,32,2,10,1920]{5,3,4,2,1,0:T(2,128)(2,1)} %param.4) | copy-start | bytes 14745604
  2.4 25.0 %copy-start.1 = (bf16[2,1,32,2,10,1920]{5,3,4,2,1,0:T(2,128)(2,1)S(1)}, bf16[2,1,32,2,10,1920]{5,3,4,2,1,0:T(2,128)(2,1)}, u32[]{:S(2)}) copy-start(bf16[2,1,32,2,10,1920]{5,3,4,2,1,0:T(2,128)(2,1)} %param.4) | copy-start | bytes 14745604
  2.4 29.0 %copy-start.3 = (s32[1,32]{1,0:T(1,128)S(1)}, s32[1,32]{1,0:T(1,128)}, u32[]{:S(2)}) copy-start(s32[1,32]{1,0:T(1,128)} %param.5) | copy-start | bytes 388
  2.4 47.4 %copy-start.2 = (s32[16,2]{0,1:T(2,128)S(1)}, s32[16,2]{0,1:T(2,128)}, u32[]{:S(2)}) copy-start(s32[16,2]{0,1:T(2,128)} %param.7) | copy-start | bytes 388
  2.9 24.4 %collective-permute-start = (bf16[8,2,8,2,1920]{4,3,2,1,0:T(2,128)(2,1)S(1)}, bf16[8,2,8,2,1920]{4,3,2,1,0:T(2,128)(2,1)S(1)}, u32[]{:S(2)}, u32[]{:S(2)}) collective-permute-start(bf16[8,2,8,2,1920]{4,3,2,1,0:T(2,128)(2,1)S(1)} %get-tuple-element.15), channel_id=1, source_target_pairs={{0,1},{1,2},{2,3},{3,0},{4,5},{5,6},{6,7},{7,4},{8,9},{9,10},{10,1... | collective-permute-start | bytes 2949128 | tf_op jit(solution)/shard_map/ppermute | solution.py:63
  5.0 26.4 %collective-permute-start.4 = (bf16[8,2,8,2,1920]{4,3,2,1,0:T(2,128)(2,1)S(1)}, bf16[8,2,8,2,1920]{4,3,2,1,0:T(2,128)(2,1)S(1)}, u32[]{:S(2)}, u32[]{:S(2)}) collective-permute-start(bf16[8,2,8,2,1920]{4,3,2,1,0:T(2,128)(2,1)S(1)} %get-tuple-element.21), channel_id=1, source_target_pairs={{0,3},{1,0},{2,1},{3,2},{4,7},{5,4},{6,5},{7,6},{8,11},{9,8},{10,9... | collective-permute-start | bytes 2949128 | tf_op jit(solution)/shard_map/ppermute | solution.py:64
  6.4 43.4 %collective-permute-start.5 = (bf16[8,2,8,2,1920]{4,3,2,1,0:T(2,128)(2,1)S(1)}, bf16[8,2,8,2,1920]{4,3,2,1,0:T(2,128)(2,1)S(1)}, u32[]{:S(2)}, u32[]{:S(2)}) collective-permute-start(bf16[8,2,8,2,1920]{4,3,2,1,0:T(2,128)(2,1)S(1)} %get-tuple-element.22), channel_id=1, source_target_pairs={{0,2},{1,3},{2,0},{3,1},{4,6},{5,7},{6,4},{7,5},{8,10},{9,11},{10,... | collective-permute-start | bytes 2949128 | tf_op jit(solution)/shard_map/ppermute | solution.py:65
  27.6 30.0 %collective-permute-start.1 = (bf16[8,2,2,2,1920]{4,3,2,1,0:T(2,128)(2,1)S(1)}, bf16[8,2,2,2,1920]{4,3,2,1,0:T(2,128)(2,1)S(1)}, u32[]{:S(2)}, u32[]{:S(2)}) collective-permute-start(bf16[8,2,2,2,1920]{4,3,2,1,0:T(2,128)(2,1)S(1)} %get-tuple-element.17), channel_id=1, source_target_pairs={{0,3},{1,0},{2,1},{3,2},{4,7},{5,4},{6,5},{7,6},{8,11},{9,8},{10,9... | collective-permute-start | bytes 737288 | tf_op jit(solution)/shard_map/ppermute | solution.py:64
  29.2 28.3 %collective-permute-start.2 = (bf16[8,2,2,2,1920]{4,3,2,1,0:T(2,128)(2,1)S(1)}, bf16[8,2,2,2,1920]{4,3,2,1,0:T(2,128)(2,1)S(1)}, u32[]{:S(2)}, u32[]{:S(2)}) collective-permute-start(bf16[8,2,2,2,1920]{4,3,2,1,0:T(2,128)(2,1)S(1)} %get-tuple-element.18), channel_id=1, source_target_pairs={{0,2},{1,3},{2,0},{3,1},{4,6},{5,7},{6,4},{7,5},{8,10},{9,11},{10,... | collective-permute-start | bytes 737288 | tf_op jit(solution)/shard_map/ppermute | solution.py:65
  29.8 31.5 %collective-permute-start.3 = (bf16[8,2,2,2,1920]{4,3,2,1,0:T(2,128)(2,1)S(1)}, bf16[8,2,2,2,1920]{4,3,2,1,0:T(2,128)(2,1)S(1)}, u32[]{:S(2)}, u32[]{:S(2)}) collective-permute-start(bf16[8,2,2,2,1920]{4,3,2,1,0:T(2,128)(2,1)S(1)} %get-tuple-element.19), channel_id=1, source_target_pairs={{0,1},{1,2},{2,3},{3,0},{4,5},{5,6},{6,7},{7,4},{8,9},{9,10},{10,1... | collective-permute-start | bytes 737288 | tf_op jit(solution)/shard_map/ppermute | solution.py:63
  64.7 0.7 collective-permute-start.6

commit v6 on v5

v6 whole, which is shorter than its diff:
```python
import functools

import jax
import jax.numpy as jnp
from jax import lax
from jax.experimental import pallas as pl
from jax.experimental.pallas import tpu as pltpu
from jax.sharding import PartitionSpec as P

LOOK_RG = 15
LOOK_AZ = 5
EPS = 1e-05
SCALE = 1.0 / (LOOK_AZ * LOOK_RG)
DATES = 8
PAIRS = 16
ITEMS = 8
RG = 1920
LCOL = 128
ROWS = 320
SPLIT = 4
HALF = 16

VMEM = pl.BlockSpec(memory_space=pltpu.VMEM)
SMEM = pl.BlockSpec(memory_space=pltpu.SMEM)
HBM = pl.BlockSpec(memory_space=pltpu.HBM)
ANYWHERE = pl.BlockSpec(memory_space=pl.ANY)


def cut_kernel(low, high, images, *rest):
    to1, to2, to3, own, sem = rest[-5:]
    group = lax.axis_index("date")
    copies = []
    for step, out in ((1, to1), (3, to3), (2, to2), (0, own)):
        taker = lax.rem(group + step, 4)
        tiles = pl.ds(lax.rem(taker, 2) * HALF, HALF)
        lines = pl.ds(lax.div(taker, 2) * LOOK_AZ + low, high - low)
        for date in range(2):
            copies.append(
                pltpu.make_async_copy(
                    images.at[date, tiles, lines], out.at[:, date], sem.at[len(copies)]
                )
            )
            copies[-1].start()
    for copy in copies:
        copy.wait()


def cut(images, low, high, after=None):
    block = jax.ShapeDtypeStruct((HALF, 2, high - low, 2, RG), jnp.bfloat16)
    operands = (images,) + (() if after is None else (after,))
    return pl.pallas_call(
        functools.partial(cut_kernel, low, high),
        out_shape=[block] * 4,
        in_specs=[HBM, ANYWHERE][: len(operands)],
        out_specs=[VMEM] * 4,
        scratch_shapes=[pltpu.SemaphoreType.DMA((8,))],
        compiler_params=pltpu.CompilerParams(vmem_limit_bytes=8 << 20),
    )(*operands)


def meet(to1, to2, to3, own):
    def ring(step):
        return [(i, (i + step) % 4) for i in range(4)]

    three = lax.ppermute(to1, "date", ring(1))
    one = lax.ppermute(to3, "date", ring(3))
    two = lax.ppermute(to2, "date", ring(2))
    return own, one, two, three


def add_lines(epochs, blocks, first, lines, box, img, hi, lo):
    group = lax.axis_index("date")
    for step, block in enumerate(blocks):
        base = lax.rem(group + step, 4) * 2
        for date in range(2):
            for line in range(lines):
                pixels = block[first : first + ITEMS, date, line]
                pixels = jnp.swapaxes(pixels, 0, 1).reshape(16, RG)
                img[base + date, line] = pixels.astype(jnp.float32)

    def split(values, row):
        upper = values.astype(jnp.bfloat16)
        hi[pl.ds(row, 16), :] = upper
        lo[pl.ds(row, 16), :] = (values - upper.astype(jnp.float32)).astype(jnp.bfloat16)

    def power(half, carry):
        total = []
        for date in range(2):
            acc = jnp.zeros((ITEMS, RG), jnp.float32)
            for line in range(lines):
                re = img[2 * half + date, line, 0:8, :]
                im = img[2 * half + date, line, 8:16, :]
                acc = acc + (re * re + im * im)
            total.append(acc)
        split(jnp.concatenate(total, axis=0), pl.multiple_of(half * 16, 16))
        return carry

    lax.fori_loop(0, DATES // 2, power, 0)

    def cross(k, carry):
        a, b = epochs[0, k], epochs[1, k]
        acc_re = jnp.zeros((ITEMS, RG), jnp.float32)
        acc_im = jnp.zeros((ITEMS, RG), jnp.float32)
        for line in range(lines):
            re_a, im_a = img[a, line, 0:8, :], img[a, line, 8:16, :]
            re_b, im_b = img[b, line, 0:8, :], img[b, line, 8:16, :]
            acc_re = acc_re + (re_a * re_b + im_a * im_b)
            acc_im = acc_im + (im_a * re_b - re_a * im_b)
        split(jnp.concatenate([acc_re, acc_im], axis=0), pl.multiple_of(64 + k * 16, 16))
        return carry

    lax.fori_loop(0, PAIRS, cross, 0)
    return jnp.dot(hi[...], box[...], preferred_element_type=jnp.float32) + jnp.dot(
        lo[...], box[...], preferred_element_type=jnp.float32
    )


def early_kernel(epochs, own, one, two, three, box, sums, img, hi, lo):
    for part in range(2):
        sums[part] = add_lines(
            epochs, (own, one, two, three), part * ITEMS, SPLIT, box, img, hi, lo
        )


def late_kernel(epochs, own, one, two, three, box, early, table, out, img, hi, lo, sums):
    del table
    start = lax.rem(lax.axis_index("date"), 2) * HALF
    for part in range(2):
        total = add_lines(
            epochs, (own, one, two, three), part * ITEMS, LOOK_AZ - SPLIT, box, img, hi, lo
        )
        sums[...] = (total + early[part]) * SCALE
        for owner in range(4):
            rows = []
            for kk in range(4):
                k = owner * 4 + kk
                power_a = sums[pl.ds(pl.multiple_of(epochs[0, k] * 8, 8), 8), :]
                power_b = sums[pl.ds(pl.multiple_of(epochs[1, k] * 8, 8), 8), :]
                weight = 1.0 / jnp.sqrt((power_a + EPS) * (power_b + EPS))
                rows.append(sums[64 + k * 16 : 72 + k * 16, :] * weight)
                rows.append(sums[72 + k * 16 : 80 + k * 16, :] * weight)
            out[pl.ds(start + part * ITEMS, ITEMS), owner] = jnp.swapaxes(
                jnp.stack(rows, axis=0), 0, 1
            )


def looks(kernel, epochs, operands, out_shape, lines, scratch=()):
    work = lines * HALF * RG * (PAIRS * 8 + DATES * 4) + 4 * ROWS * RG * LCOL
    return pl.pallas_call(
        kernel,
        out_shape=out_shape,
        grid_spec=pltpu.PrefetchScalarGridSpec(
            num_scalar_prefetch=1,
            grid=(),
            in_specs=[VMEM if x.ndim > 1 else SMEM for x in operands],
            out_specs=jax.tree.map(lambda _: VMEM, out_shape),
            scratch_shapes=[
                pltpu.VMEM((DATES, lines, 16, RG), jnp.float32),
                pltpu.VMEM((ROWS, RG), jnp.bfloat16),
                pltpu.VMEM((ROWS, RG), jnp.bfloat16),
                *scratch,
            ],
        ),
        cost_estimate=pl.CostEstimate(
            flops=work, bytes_accessed=DATES * lines * 32 * RG * 2, transcendentals=0
        ),
        compiler_params=pltpu.CompilerParams(vmem_limit_bytes=24 << 20),
    )(epochs, *operands)


def place_kernel(table, got, out, rows):
    half = lax.div(lax.axis_index("tile"), HALF)
    for burst in range(32):
        position = table[burst]
        valid = jnp.where(position < table[32], 1.0, 0.0).astype(jnp.float32)
        base = pl.multiple_of(position * 16, 16)
        rows[pl.ds(base, 8), :] = got[burst, half] * valid
        rows[pl.ds(base + 8, 8), :] = got[burst, 2 + half] * valid
    for plane in range(8):
        for part in range(8):
            out[plane // 2, plane % 2, part * 8 : part * 8 + 8, :] = rows[
                pl.ds(part * 64 + plane, 8, stride=8), :
            ]


def on_device(complex_images, segment_position_map, usable_position_total, interferogram_epochs):
    images = complex_images[:, 0].transpose(0, 1, 3, 2, 4)
    epochs = interferogram_epochs.T
    table = jnp.concatenate([segment_position_map[0], usable_position_total])
    box = (
        jnp.arange(RG)[:, None] // LOOK_RG == jnp.arange(LCOL)[None, :]
    ).astype(jnp.bfloat16)

    early = meet(*cut(images, 0, SPLIT))
    late = meet(*cut(images, SPLIT, LOOK_AZ, early[3]))

    sums = looks(
        early_kernel,
        epochs,
        (*early, box),
        jax.ShapeDtypeStruct((2, ROWS, LCOL), jnp.float32),
        SPLIT,
    )
    gamma = looks(
        late_kernel,
        epochs,
        (*late, box, sums, table),
        jax.ShapeDtypeStruct((32, 4, 8, LCOL), jnp.float32),
        LOOK_AZ - SPLIT,
        (pltpu.VMEM((ROWS, LCOL), jnp.float32),),
    )
    got = lax.all_to_all(
        gamma.reshape(128, 8, LCOL), ("tile", "date"), split_axis=0, concat_axis=0, tiled=True
    ).reshape(32, 4, 8, LCOL)
    return pl.pallas_call(
        place_kernel,
        out_shape=jax.ShapeDtypeStruct((4, 2, 64, LCOL), jnp.float32),
        grid_spec=pltpu.PrefetchScalarGridSpec(
            num_scalar_prefetch=1,
            grid=(),
            in_specs=[VMEM],
            out_specs=VMEM,
            scratch_shapes=[pltpu.VMEM((512, LCOL), jnp.float32)],
        ),
        compiler_params=pltpu.CompilerParams(vmem_limit_bytes=4 << 20),
    )(table, got)


def solution(mesh):
    in_specs = (P("date", "tile", None, None, None, None), P("tile", None), P("tile"), P())
    out_specs = P("date", None, None, "tile")
    return jax.shard_map(
        on_device, mesh=mesh, in_specs=in_specs, out_specs=out_specs, check_vma=False
    )
```

time: 100 us -> 90.5 us (0.905)
  blocking collectives: 33.6 us -> 23.2 us
    all_to_all x1, blocking collectives: 33.6 us -> 23.2 us  [on_device(): lax.all_to_all(gamma.reshape(128, 8, LCOL), ('tile', 'date'), split_axis=...]
  transfers between devices with their start and end apart: 7 -> 6, of which waited for: 3 -> 3; matrix products, arithmetic and copies ran while one was open for 0% -> 0% of each run, Pallas kernels for 8% -> 8%
where the time goes in v6:
time: 90.5 us; the launch traced here: 90.3 us
  waiting for transfers between devices  42.2 us (47%)
  blocking collectives  23.2 us (26%)
  Pallas kernels  13.5 us (15%)
  starting transfers between devices  7.91 us (9%)
  local copies, waits for them, and re-layouts  2.4 us (3%)
    ppermute x2, waiting for transfers between devices, meet(): three = lax.ppermute(to1, 'date', ring(1))  23.8 us
    all_to_all x1, blocking collectives, on_device(): lax.all_to_all(gamma.reshape(128, 8, LCOL), ('tile', 'date'), split_axis=...  23.2 us
    ppermute x2, waiting for transfers between devices, meet(): two = lax.ppermute(to2, 'date', ring(2))  18.3 us
    pallas_call x2, Pallas kernels, looks(): pl.pallas_call(kernel, out_shape=out_shape, grid_spec=pltpu.PrefetchScala...  11.5 us
    ppermute x2, starting transfers between devices, meet(): one = lax.ppermute(to3, 'date', ring(3))  3 us
    ppermute x2, starting transfers between devices, meet(): three = lax.ppermute(to1, 'date', ring(1))  2.74 us
    unnamed x8, local copies, waits for them, and re-layouts  2.4 us
    ppermute x2, starting transfers between devices, meet(): two = lax.ppermute(to2, 'date', ring(2))  2.17 us
  transfers between devices with their start and end apart: 6, of which 3 were waited for; matrix products, arithmetic and copies ran while one was open for 0% of the time, Pallas kernels for 8%

profile of v6, /device:TPU:1, one launch (start us, length us, event | category | flops | bytes accessed | tf_op | source)
XLA Modules:
  0.0 90.3 jit_solution(202980046856025404)
XLA Ops:
  0.0 2.4 %copy-done = bf16[2,1,32,2,10,1920]{5,3,4,2,1,0:T(2,128)(2,1)S(1)} copy-done((bf16[2,1,32,2,10,1920]{5,3,4,2,1,0:T(2,128)(2,1)S(1)}, bf16[2,1,32,2,10,1920]{5,3,4,2,1,0:T(2,128)(2,1)}, u32[]{:S(2)}) %copy-start) | copy-done | bytes 4915224
  2.4 0.4 shard_map.46
  2.8 2.1 %collective-permute-start = (bf16[16,2,4,2,1920]{4,3,2,1,0:T(2,128)(2,1)S(1)}, bf16[16,2,4,2,1920]{4,3,2,1,0:T(2,128)(2,1)S(1)}, u32[]{:S(2)}, u32[]{:S(2)}) collective-permute-start(bf16[16,2,4,2,1920]{4,3,2,1,0:T(2,128)(2,1)S(1)} %get-tuple-element.13), channel_id=1, source_target_pairs={{0,1},{1,2},{2,3},{3,0},{4,5},{5,6},{6,7},{7,4},{8,9},{9,10},{10,1... | collective-permute-start | bytes 2949128 | tf_op jit(solution)/shard_map/ppermute | solution.py:65
  4.9 1.3 %collective-permute-start.4 = (bf16[16,2,4,2,1920]{4,3,2,1,0:T(2,128)(2,1)S(1)}, bf16[16,2,4,2,1920]{4,3,2,1,0:T(2,128)(2,1)S(1)}, u32[]{:S(2)}, u32[]{:S(2)}) collective-permute-start(bf16[16,2,4,2,1920]{4,3,2,1,0:T(2,128)(2,1)S(1)} %get-tuple-element.19), channel_id=1, source_target_pairs={{0,3},{1,0},{2,1},{3,2},{4,7},{5,4},{6,5},{7,6},{8,11},{9,8},{10,9... | collective-permute-start | bytes 2949128 | tf_op jit(solution)/shard_map/ppermute | solution.py:66
  6.3 1.6 %collective-permute-start.5 = (bf16[16,2,4,2,1920]{4,3,2,1,0:T(2,128)(2,1)S(1)}, bf16[16,2,4,2,1920]{4,3,2,1,0:T(2,128)(2,1)S(1)}, u32[]{:S(2)}, u32[]{:S(2)}) collective-permute-start(bf16[16,2,4,2,1920]{4,3,2,1,0:T(2,128)(2,1)S(1)} %get-tuple-element.20), channel_id=1, source_target_pairs={{0,2},{1,3},{2,0},{3,1},{4,6},{5,7},{6,4},{7,5},{8,10},{9,11},{10,... | collective-permute-start | bytes 2949128 | tf_op jit(solution)/shard_map/ppermute | solution.py:67
  7.9 19.3 %collective-permute-done.rest_0_.three = bf16[16,2,4,2,1920]{4,3,2,1,0:T(2,128)(2,1)S(1)} collective-permute-done((bf16[16,2,4,2,1920]{4,3,2,1,0:T(2,128)(2,1)S(1)}, bf16[16,2,4,2,1920]{4,3,2,1,0:T(2,128)(2,1)S(1)}, u32[]{:S(2)}, u32[]{:S(2)}) %collective-permute-start) | collective-permute-done | bytes 983072 | tf_op jit(solution)/shard_map/ppermute | solution.py:65
  27.2 0.0 copy-done.1
  27.2 0.2 shard_map.47
  27.4 1.7 %collective-permute-start.1 = (bf16[16,2,1,2,1920]{4,3,2,1,0:T(2,128)(2,1)S(1)}, bf16[16,2,1,2,1920]{4,3,2,1,0:T(2,128)(2,1)S(1)}, u32[]{:S(2)}, u32[]{:S(2)}) collective-permute-start(bf16[16,2,1,2,1920]{4,3,2,1,0:T(2,128)(2,1)S(1)} %get-tuple-element.15), channel_id=1, source_target_pairs={{0,3},{1,0},{2,1},{3,2},{4,7},{5,4},{6,5},{7,6},{8,11},{9,8},{10,9... | collective-permute-start | bytes 737288 | tf_op jit(solution)/shard_map/ppermute | solution.py:66
  29.1 0.5 collective-permute-start.2
  29.6 0.6 collective-permute-start.3
  30.3 0.3 fusion.box
  31.2 0.0 copy-done.3
  31.2 0.1 pad_add_fusion.table
  31.3 0.0 collective-permute-done.4.one
  31.3 18.3 %collective-permute-done.5.two = bf16[16,2,4,2,1920]{4,3,2,1,0:T(2,128)(2,1)S(1)} collective-permute-done((bf16[16,2,4,2,1920]{4,3,2,1,0:T(2,128)(2,1)S(1)}, bf16[16,2,4,2,1920]{4,3,2,1,0:T(2,128)(2,1)S(1)}, u32[]{:S(2)}, u32[]{:S(2)}) %collective-permute-start.5) | collective-permute-done | bytes 983072 | tf_op jit(solution)/shard_map/ppermute | solution.py:67
  49.7 0.0 copy-done.2
  49.7 7.0 %shard_map.48.early = f32[2,320,128]{2,1,0:T(8,128)S(1)} custom-call(s32[2,16]{1,0:T(2,128)S(1)} %bitcast.11, bf16[16,2,4,2,1920]{4,3,2,1,0:T(2,128)(2,1)S(1)} %get-tuple-element.18.own, bf16[16,2,4,2,1920]{4,3,2,1,0:T(2,128)(2,1)S(1)} %collective-permute-done.4.one, bf16[16,2,4,2,1920]{4,3,2,1,0:T(2,128)(2,1)S(1)} %collective-permute-done.5.two, ...), custom_call_target="tpu_custom_call" | custom-call | flops 334233600 | bytes 3932160 | tf_op jit(solution)/shard_map/pallas_call | solution.py:149
  56.7 0.0 collective-permute-done.1.one
  56.7 0.0 collective-permute-done.2.two
  56.7 4.5 %collective-permute-done.3.three = bf16[16,2,1,2,1920]{4,3,2,1,0:T(2,128)(2,1)S(1)} collective-permute-done((bf16[16,2,1,2,1920]{4,3,2,1,0:T(2,128)(2,1)S(1)}, bf16[16,2,1,2,1920]{4,3,2,1,0:T(2,128)(2,1)S(1)}, u32[]{:S(2)}, u32[]{:S(2)}) %collective-permute-start.3) | collective-permute-done | bytes 245792 | tf_op jit(solution)/shard_map/ppermute | solution.py:65
  61.2 4.5 %shard_map.49 = f32[32,4,8,128]{3,2,1,0:T(8,128)S(1)} custom-call(s32[2,16]{1,0:T(2,128)S(1)} %bitcast.12, bf16[16,2,1,2,1920]{4,3,2,1,0:T(2,128)(2,1)S(1)} %get-tuple-element.14.own, bf16[16,2,1,2,1920]{4,3,2,1,0:T(2,128)(2,1)S(1)} %collective-permute-done.1.one, bf16[16,2,1,2,1920]{4,3,2,1,0:T(2,128)(2,1)S(1)} %collective-permute-done.2.two, ...), custom_call_target="tpu_custom_call" | custom-call | flops 319488000 | bytes 983040 | tf_op jit(solution)/shard_map/pallas_call | solution.py:149
  65.8 23.2 %all_to_all.5 = f32[128,8,128]{2,1,0:T(8,128)S(1)} all-to-all(f32[128,8,128]{2,1,0:T(8,128)S(1)} %bitcast.9), channel_id=1, replica_groups=mesh['tile'=32,'date'=4] {'tile','date'}, dimensions={0} | all-to-all | bytes 1048576 | tf_op jit(solution)/shard_map/all_to_all | solution.py:212
  89.0 1.4 %shard_map.50 = f32[4,2,64,128]{3,2,1,0:T(8,128)} custom-call(s32[33]{0:T(128)S(1)} %pad_add_fusion.table, f32[32,4,8,128]{3,2,1,0:T(8,128)S(1)} %bitcast.10), custom_call_target="tpu_custom_call" | custom-call | tf_op jit(solution)/shard_map/pallas_call | solution.py:215
  (5 shorter events, 0.0 us)
Async XLA Ops:
  0.0 2.4 %copy-start = (bf16[2,1,32,2,10,1920]{5,3,4,2,1,0:T(2,128)(2,1)S(1)}, bf16[2,1,32,2,10,1920]{5,3,4,2,1,0:T(2,128)(2,1)}, u32[]{:S(2)}) copy-start(bf16[2,1,32,2,10,1920]{5,3,4,2,1,0:T(2,128)(2,1)} %param.4) | copy-start | bytes 14745604
  2.4 24.9 %copy-start.1 = (bf16[2,1,32,2,10,1920]{5,3,4,2,1,0:T(2,128)(2,1)S(1)}, bf16[2,1,32,2,10,1920]{5,3,4,2,1,0:T(2,128)(2,1)}, u32[]{:S(2)}) copy-start(bf16[2,1,32,2,10,1920]{5,3,4,2,1,0:T(2,128)(2,1)} %param.4) | copy-start | bytes 14745604
  2.4 28.8 %copy-start.3 = (s32[1,32]{1,0:T(1,128)S(1)}, s32[1,32]{1,0:T(1,128)}, u32[]{:S(2)}) copy-start(s32[1,32]{1,0:T(1,128)} %param.5) | copy-start | bytes 388
  2.4 47.3 %copy-start.2 = (s32[16,2]{0,1:T(2,128)S(1)}, s32[16,2]{0,1:T(2,128)}, u32[]{:S(2)}) copy-start(s32[16,2]{0,1:T(2,128)} %param.7) | copy-start | bytes 388
  2.8 24.4 %collective-permute-start = (bf16[16,2,4,2,1920]{4,3,2,1,0:T(2,128)(2,1)S(1)}, bf16[16,2,4,2,1920]{4,3,2,1,0:T(2,128)(2,1)S(1)}, u32[]{:S(2)}, u32[]{:S(2)}) collective-permute-start(bf16[16,2,4,2,1920]{4,3,2,1,0:T(2,128)(2,1)S(1)} %get-tuple-element.13), channel_id=1, source_target_pairs={{0,1},{1,2},{2,3},{3,0},{4,5},{5,6},{6,7},{7,4},{8,9},{9,10},{10,1... | collective-permute-start | bytes 2949128 | tf_op jit(solution)/shard_map/ppermute | solution.py:65
  4.9 26.4 %collective-permute-start.4 = (bf16[16,2,4,2,1920]{4,3,2,1,0:T(2,128)(2,1)S(1)}, bf16[16,2,4,2,1920]{4,3,2,1,0:T(2,128)(2,1)S(1)}, u32[]{:S(2)}, u32[]{:S(2)}) collective-permute-start(bf16[16,2,4,2,1920]{4,3,2,1,0:T(2,128)(2,1)S(1)} %get-tuple-element.19), channel_id=1, source_target_pairs={{0,3},{1,0},{2,1},{3,2},{4,7},{5,4},{6,5},{7,6},{8,11},{9,8},{10,9... | collective-permute-start | bytes 2949128 | tf_op jit(solution)/shard_map/ppermute | solution.py:66
  6.3 43.4 %collective-permute-start.5 = (bf16[16,2,4,2,1920]{4,3,2,1,0:T(2,128)(2,1)S(1)}, bf16[16,2,4,2,1920]{4,3,2,1,0:T(2,128)(2,1)S(1)}, u32[]{:S(2)}, u32[]{:S(2)}) collective-permute-start(bf16[16,2,4,2,1920]{4,3,2,1,0:T(2,128)(2,1)S(1)} %get-tuple-element.20), channel_id=1, source_target_pairs={{0,2},{1,3},{2,0},{3,1},{4,6},{5,7},{6,4},{7,5},{8,10},{9,11},{10,... | collective-permute-start | bytes 2949128 | tf_op jit(solution)/shard_map/ppermute | solution.py:67
  27.4 29.2 %collective-permute-start.1 = (bf16[16,2,1,2,1920]{4,3,2,1,0:T(2,128)(2,1)S(1)}, bf16[16,2,1,2,1920]{4,3,2,1,0:T(2,128)(2,1)S(1)}, u32[]{:S(2)}, u32[]{:S(2)}) collective-permute-start(bf16[16,2,1,2,1920]{4,3,2,1,0:T(2,128)(2,1)S(1)} %get-tuple-element.15), channel_id=1, source_target_pairs={{0,3},{1,0},{2,1},{3,2},{4,7},{5,4},{6,5},{7,6},{8,11},{9,8},{10,9... | collective-permute-start | bytes 737288 | tf_op jit(solution)/shard_map/ppermute | solution.py:66
  29.1 27.6 %collective-permute-start.2 = (bf16[16,2,1,2,1920]{4,3,2,1,0:T(2,128)(2,1)S(1)}, bf16[16,2,1,2,1920]{4,3,2,1,0:T(2,128)(2,1)S(1)}, u32[]{:S(2)}, u32[]{:S(2)}) collective-permute-start(bf16[16,2,1,2,1920]{4,3,2,1,0:T(2,128)(2,1)S(1)} %get-tuple-element.16), channel_id=1, source_target_pairs={{0,2},{1,3},{2,0},{3,1},{4,6},{5,7},{6,4},{7,5},{8,10},{9,11},{10,... | collective-permute-start | bytes 737288 | tf_op jit(solution)/shard_map/ppermute | solution.py:67
  29.6 31.6 %collective-permute-start.3 = (bf16[16,2,1,2,1920]{4,3,2,1,0:T(2,128)(2,1)S(1)}, bf16[16,2,1,2,1920]{4,3,2,1,0:T(2,128)(2,1)S(1)}, u32[]{:S(2)}, u32[]{:S(2)}) collective-permute-start(bf16[16,2,1,2,1920]{4,3,2,1,0:T(2,128)(2,1)S(1)} %get-tuple-element.17), channel_id=1, source_target_pairs={{0,1},{1,2},{2,3},{3,0},{4,5},{5,6},{6,7},{7,4},{8,9},{9,10},{10,1... | collective-permute-start | bytes 737288 | tf_op jit(solution)/shard_map/ppermute | solution.py:65

commit v7 on v6

--- a/solution.py
+++ b/solution.py
@@ -17,7 +17,7 @@
 RG = 1920
 LCOL = 128
 ROWS = 320
-SPLIT = 4
+SPLIT = 3
 HALF = 16
 
 VMEM = pl.BlockSpec(memory_space=pltpu.VMEM)
@@ -26,34 +26,41 @@
 ANYWHERE = pl.BlockSpec(memory_space=pl.ANY)
 
 
-def cut_kernel(low, high, images, *rest):
+def cut_kernel(parts, images, *rest):
     to1, to2, to3, own, sem = rest[-5:]
     group = lax.axis_index("date")
     copies = []
     for step, out in ((1, to1), (3, to3), (2, to2), (0, own)):
         taker = lax.rem(group + step, 4)
-        tiles = pl.ds(lax.rem(taker, 2) * HALF, HALF)
-        lines = pl.ds(lax.div(taker, 2) * LOOK_AZ + low, high - low)
-        for date in range(2):
-            copies.append(
-                pltpu.make_async_copy(
-                    images.at[date, tiles, lines], out.at[:, date], sem.at[len(copies)]
+        start, top = lax.rem(taker, 2) * HALF, lax.div(taker, 2) * LOOK_AZ
+        filled = 0
+        for first, low, high in parts:
+            tiles, lines = pl.ds(start + first, ITEMS), pl.ds(top + low, high - low)
+            slots = slice(filled, filled + high - low)
+            filled += high - low
+            for date in range(2):
+                copies.append(
+                    pltpu.make_async_copy(
+                        images.at[date, tiles, lines],
+                        out.at[:, date, slots],
+                        sem.at[len(copies)],
+                    )
                 )
-            )
-            copies[-1].start()
+                copies[-1].start()
     for copy in copies:
         copy.wait()
 
 
-def cut(images, low, high, after=None):
-    block = jax.ShapeDtypeStruct((HALF, 2, high - low, 2, RG), jnp.bfloat16)
+def cut(images, parts, after=None):
+    slots = sum(high - low for _, low, high in parts)
+    block = jax.ShapeDtypeStruct((ITEMS, 2, slots, 2, RG), jnp.bfloat16)
     operands = (images,) + (() if after is None else (after,))
     return pl.pallas_call(
-        functools.partial(cut_kernel, low, high),
+        functools.partial(cut_kernel, parts),
         out_shape=[block] * 4,
         in_specs=[HBM, ANYWHERE][: len(operands)],
         out_specs=[VMEM] * 4,
-        scratch_shapes=[pltpu.SemaphoreType.DMA((8,))],
+        scratch_shapes=[pltpu.SemaphoreType.DMA((8 * len(parts),))],
         compiler_params=pltpu.CompilerParams(vmem_limit_bytes=8 << 20),
     )(*operands)
 
@@ -68,14 +75,14 @@
     return own, one, two, three
 
 
-def add_lines(epochs, blocks, first, lines, box, img, hi, lo):
+def add_lines(epochs, blocks, low, high, box, img, hi, lo):
     group = lax.axis_index("date")
+    lines = high - low
     for step, block in enumerate(blocks):
         base = lax.rem(group + step, 4) * 2
         for date in range(2):
             for line in range(lines):
-                pixels = block[first : first + ITEMS, date, line]
-                pixels = jnp.swapaxes(pixels, 0, 1).reshape(16, RG)
+                pixels = jnp.swapaxes(block[:, date, low + line], 0, 1).reshape(16, RG)
                 img[base + date, line] = pixels.astype(jnp.float32)
 
     def split(values, row):
@@ -115,37 +122,37 @@
     )
 
 
-def early_kernel(epochs, own, one, two, three, box, sums, img, hi, lo):
-    for part in range(2):
-        sums[part] = add_lines(
-            epochs, (own, one, two, three), part * ITEMS, SPLIT, box, img, hi, lo
-        )
-
-
-def late_kernel(epochs, own, one, two, three, box, early, table, out, img, hi, lo, sums):
+def coherence(epochs, part, sums, out):
+    start = lax.rem(lax.axis_index("date"), 2) * HALF + part * ITEMS
+    for owner in range(4):
+        rows = []
+        for kk in range(4):
+            k = owner * 4 + kk
+            power_a = sums[pl.ds(pl.multiple_of(epochs[0, k] * 8, 8), 8), :]
+            power_b = sums[pl.ds(pl.multiple_of(epochs[1, k] * 8, 8), 8), :]
+            weight = 1.0 / jnp.sqrt((power_a + EPS) * (power_b + EPS))
+            rows.append(sums[64 + k * 16 : 72 + k * 16, :] * weight)
+            rows.append(sums[72 + k * 16 : 80 + k * 16, :] * weight)
+        out[pl.ds(start, ITEMS), owner] = jnp.swapaxes(jnp.stack(rows, axis=0), 0, 1)
+
+
+def early_kernel(epochs, own, one, two, three, box, out, later, img, hi, lo, sums):
+    blocks = (own, one, two, three)
+    sums[...] = add_lines(epochs, blocks, 0, LOOK_AZ, box, img, hi, lo) * SCALE
+    coherence(epochs, 0, sums, out)
+    later[...] = add_lines(epochs, blocks, LOOK_AZ, LOOK_AZ + SPLIT, box, img, hi, lo)
+
+
+def late_kernel(epochs, own, one, two, three, box, early, table, given, out, img, hi, lo, sums):
     del table
-    start = lax.rem(lax.axis_index("date"), 2) * HALF
-    for part in range(2):
-        total = add_lines(
-            epochs, (own, one, two, three), part * ITEMS, LOOK_AZ - SPLIT, box, img, hi, lo
-        )
-        sums[...] = (total + early[part]) * SCALE
-        for owner in range(4):
-            rows = []
-            for kk in range(4):
-                k = owner * 4 + kk
-                power_a = sums[pl.ds(pl.multiple_of(epochs[0, k] * 8, 8), 8), :]
-                power_b = sums[pl.ds(pl.multiple_of(epochs[1, k] * 8, 8), 8), :]
-                weight = 1.0 / jnp.sqrt((power_a + EPS) * (power_b + EPS))
-                rows.append(sums[64 + k * 16 : 72 + k * 16, :] * weight)
-                rows.append(sums[72 + k * 16 : 80 + k * 16, :] * weight)
-            out[pl.ds(start + part * ITEMS, ITEMS), owner] = jnp.swapaxes(
-                jnp.stack(rows, axis=0), 0, 1
-            )
-
-
-def looks(kernel, epochs, operands, out_shape, lines, scratch=()):
-    work = lines * HALF * RG * (PAIRS * 8 + DATES * 4) + 4 * ROWS * RG * LCOL
+    del given
+    total = add_lines(epochs, (own, one, two, three), 0, LOOK_AZ - SPLIT, box, img, hi, lo)
+    sums[...] = (total + early[...]) * SCALE
+    coherence(epochs, 1, sums, out)
+
+
+def looks(kernel, epochs, operands, out_shape, lines, aliases):
+    work = lines * ITEMS * RG * (PAIRS * 8 + DATES * 4) + 4 * ROWS * RG * LCOL
     return pl.pallas_call(
         kernel,
         out_shape=out_shape,
@@ -155,14 +162,15 @@
             in_specs=[VMEM if x.ndim > 1 else SMEM for x in operands],
             out_specs=jax.tree.map(lambda _: VMEM, out_shape),
             scratch_shapes=[
-                pltpu.VMEM((DATES, lines, 16, RG), jnp.float32),
+                pltpu.VMEM((DATES, min(lines, LOOK_AZ), 16, RG), jnp.float32),
                 pltpu.VMEM((ROWS, RG), jnp.bfloat16),
                 pltpu.VMEM((ROWS, RG), jnp.bfloat16),
-                *scratch,
+                pltpu.VMEM((ROWS, LCOL), jnp.float32),
             ],
         ),
+        input_output_aliases=aliases,
         cost_estimate=pl.CostEstimate(
-            flops=work, bytes_accessed=DATES * lines * 32 * RG * 2, transcendentals=0
+            flops=work, bytes_accessed=DATES * lines * 16 * RG * 2, transcendentals=0
         ),
         compiler_params=pltpu.CompilerParams(vmem_limit_bytes=24 << 20),
     )(epochs, *operands)
@@ -191,23 +199,16 @@
         jnp.arange(RG)[:, None] // LOOK_RG == jnp.arange(LCOL)[None, :]
     ).astype(jnp.bfloat16)
 
-    early = meet(*cut(images, 0, SPLIT))
-    late = meet(*cut(images, SPLIT, LOOK_AZ, early[3]))
-
-    sums = looks(
-        early_kernel,
-        epochs,
-        (*early, box),
-        jax.ShapeDtypeStruct((2, ROWS, LCOL), jnp.float32),
-        SPLIT,
+    early = meet(*cut(images, ((0, 0, LOOK_AZ), (ITEMS, 0, SPLIT))))
+    late = meet(*cut(images, ((ITEMS, SPLIT, LOOK_AZ),), early[3]))
+
+    shape = jax.ShapeDtypeStruct((32, 4, 8, LCOL), jnp.float32)
+    partial = jax.ShapeDtypeStruct((ROWS, LCOL), jnp.float32)
+    gamma, sums = looks(
+        early_kernel, epochs, (*early, box), (shape, partial), LOOK_AZ + SPLIT, {}
     )
     gamma = looks(
-        late_kernel,
-        epochs,
-        (*late, box, sums, table),
-        jax.ShapeDtypeStruct((32, 4, 8, LCOL), jnp.float32),
-        LOOK_AZ - SPLIT,
-        (pltpu.VMEM((ROWS, LCOL), jnp.float32),),
+        late_kernel, epochs, (*late, box, sums, table, gamma), shape, LOOK_AZ - SPLIT, {8: 0}
     )
     got = lax.all_to_all(
         gamma.reshape(128, 8, LCOL), ("tile", "date"), split_axis=0, concat_axis=0, tiled=True

time: 90.5 us -> 89.5 us (0.989)
  transfers between devices with their start and end apart: 6 -> 6, of which waited for: 3 -> 3; matrix products, arithmetic and copies ran while one was open for 0% -> 0% of each run, Pallas kernels for 8% -> 9%
where the time goes in v7:
time: 89.5 us; the launch traced here: 89.3 us
  waiting for transfers between devices  41.5 us (46%)
  blocking collectives  23.2 us (26%)
  Pallas kernels  13.2 us (15%)
  starting transfers between devices  7.91 us (9%)
  local copies, waits for them, and re-layouts  2.4 us (3%)
    all_to_all x1, blocking collectives, on_device(): lax.all_to_all(gamma.reshape(128, 8, LCOL), ('tile', 'date'), split_axis=...  23.2 us
    ppermute x2, waiting for transfers between devices, meet(): three = lax.ppermute(to1, 'date', ring(1))  23.2 us
    ppermute x2, waiting for transfers between devices, meet(): two = lax.ppermute(to2, 'date', ring(2))  18.3 us
    pallas_call x2, Pallas kernels, looks(): pl.pallas_call(kernel, out_shape=out_shape, grid_spec=pltpu.PrefetchScala...  11 us
    ppermute x2, starting transfers between devices, meet(): one = lax.ppermute(to3, 'date', ring(3))  3 us
    ppermute x2, starting transfers between devices, meet(): three = lax.ppermute(to1, 'date', ring(1))  2.74 us
    unnamed x8, local copies, waits for them, and re-layouts  2.4 us
    ppermute x2, starting transfers between devices, meet(): two = lax.ppermute(to2, 'date', ring(2))  2.17 us
  transfers between devices with their start and end apart: 6, of which 3 were waited for; matrix products, arithmetic and copies ran while one was open for 0% of the time, Pallas kernels for 9%

profile of v7, /device:TPU:1, one launch (start us, length us, event | category | flops | bytes accessed | tf_op | source)
XLA Modules:
  0.0 89.3 jit_solution(1765770040655991043)
XLA Ops:
  0.0 2.4 %copy-done = bf16[2,1,32,2,10,1920]{5,3,4,2,1,0:T(2,128)(2,1)S(1)} copy-done((bf16[2,1,32,2,10,1920]{5,3,4,2,1,0:T(2,128)(2,1)S(1)}, bf16[2,1,32,2,10,1920]{5,3,4,2,1,0:T(2,128)(2,1)}, u32[]{:S(2)}) %copy-start) | copy-done | bytes 4915224
  2.4 0.6 shard_map.46
  3.0 2.1 %collective-permute-start = (bf16[8,2,8,2,1920]{4,3,2,1,0:T(2,128)(2,1)S(1)}, bf16[8,2,8,2,1920]{4,3,2,1,0:T(2,128)(2,1)S(1)}, u32[]{:S(2)}, u32[]{:S(2)}) collective-permute-start(bf16[8,2,8,2,1920]{4,3,2,1,0:T(2,128)(2,1)S(1)} %get-tuple-element.15), channel_id=1, source_target_pairs={{0,1},{1,2},{2,3},{3,0},{4,5},{5,6},{6,7},{7,4},{8,9},{9,10},{10,1... | collective-permute-start | bytes 2949128 | tf_op jit(solution)/shard_map/ppermute | solution.py:72
  5.1 1.3 %collective-permute-start.4 = (bf16[8,2,8,2,1920]{4,3,2,1,0:T(2,128)(2,1)S(1)}, bf16[8,2,8,2,1920]{4,3,2,1,0:T(2,128)(2,1)S(1)}, u32[]{:S(2)}, u32[]{:S(2)}) collective-permute-start(bf16[8,2,8,2,1920]{4,3,2,1,0:T(2,128)(2,1)S(1)} %get-tuple-element.21), channel_id=1, source_target_pairs={{0,3},{1,0},{2,1},{3,2},{4,7},{5,4},{6,5},{7,6},{8,11},{9,8},{10,9... | collective-permute-start | bytes 2949128 | tf_op jit(solution)/shard_map/ppermute | solution.py:73
  6.5 1.6 %collective-permute-start.5 = (bf16[8,2,8,2,1920]{4,3,2,1,0:T(2,128)(2,1)S(1)}, bf16[8,2,8,2,1920]{4,3,2,1,0:T(2,128)(2,1)S(1)}, u32[]{:S(2)}, u32[]{:S(2)}) collective-permute-start(bf16[8,2,8,2,1920]{4,3,2,1,0:T(2,128)(2,1)S(1)} %get-tuple-element.22), channel_id=1, source_target_pairs={{0,2},{1,3},{2,0},{3,1},{4,6},{5,7},{6,4},{7,5},{8,10},{9,11},{10,... | collective-permute-start | bytes 2949128 | tf_op jit(solution)/shard_map/ppermute | solution.py:74
  8.1 19.3 %collective-permute-done.rest_0_.three = bf16[8,2,8,2,1920]{4,3,2,1,0:T(2,128)(2,1)S(1)} collective-permute-done((bf16[8,2,8,2,1920]{4,3,2,1,0:T(2,128)(2,1)S(1)}, bf16[8,2,8,2,1920]{4,3,2,1,0:T(2,128)(2,1)S(1)}, u32[]{:S(2)}, u32[]{:S(2)}) %collective-permute-start) | collective-permute-done | bytes 983072 | tf_op jit(solution)/shard_map/ppermute | solution.py:72
  27.4 0.0 copy-done.1
  27.4 0.2 shard_map.47
  27.7 1.7 %collective-permute-start.1 = (bf16[8,2,2,2,1920]{4,3,2,1,0:T(2,128)(2,1)S(1)}, bf16[8,2,2,2,1920]{4,3,2,1,0:T(2,128)(2,1)S(1)}, u32[]{:S(2)}, u32[]{:S(2)}) collective-permute-start(bf16[8,2,2,2,1920]{4,3,2,1,0:T(2,128)(2,1)S(1)} %get-tuple-element.17), channel_id=1, source_target_pairs={{0,3},{1,0},{2,1},{3,2},{4,7},{5,4},{6,5},{7,6},{8,11},{9,8},{10,9... | collective-permute-start | bytes 737288 | tf_op jit(solution)/shard_map/ppermute | solution.py:73
  29.3 0.5 collective-permute-start.2
  29.9 0.6 collective-permute-start.3
  30.5 0.3 fusion.box
  31.5 0.0 copy-done.3
  31.5 0.1 pad_add_fusion.table
  31.5 0.0 collective-permute-done.4.one
  31.5 18.3 %collective-permute-done.5.two = bf16[8,2,8,2,1920]{4,3,2,1,0:T(2,128)(2,1)S(1)} collective-permute-done((bf16[8,2,8,2,1920]{4,3,2,1,0:T(2,128)(2,1)S(1)}, bf16[8,2,8,2,1920]{4,3,2,1,0:T(2,128)(2,1)S(1)}, u32[]{:S(2)}, u32[]{:S(2)}) %collective-permute-start.5) | collective-permute-done | bytes 983072 | tf_op jit(solution)/shard_map/ppermute | solution.py:74
  49.8 0.0 copy-done.2
  49.8 7.7 %shard_map.48 = (f32[32,4,8,128]{3,2,1,0:T(8,128)S(1)}, f32[320,128]{1,0:T(8,128)S(1)}) custom-call(s32[2,16]{1,0:T(2,128)S(1)} %bitcast.11, bf16[8,2,8,2,1920]{4,3,2,1,0:T(2,128)(2,1)S(1)} %get-tuple-element.20.own, bf16[8,2,8,2,1920]{4,3,2,1,0:T(2,128)(2,1)S(1)} %collective-permute-done.4.one, bf16[8,2,8,2,1920]{4,3,2,1,0:T(2,128)(2,1)S(1)} %collective-permute-done.5.two, ...), custom_call_target="tpu_custom_call" | custom-call | flops 334233600 | bytes 3932160 | tf_op jit(solution)/shard_map/pallas_call | solution.py:156
  57.5 0.0 collective-permute-done.1.one
  57.5 0.0 collective-permute-done.2.two
  57.5 3.9 %collective-permute-done.3.three = bf16[8,2,2,2,1920]{4,3,2,1,0:T(2,128)(2,1)S(1)} collective-permute-done((bf16[8,2,2,2,1920]{4,3,2,1,0:T(2,128)(2,1)S(1)}, bf16[8,2,2,2,1920]{4,3,2,1,0:T(2,128)(2,1)S(1)}, u32[]{:S(2)}, u32[]{:S(2)}) %collective-permute-start.3) | collective-permute-done | bytes 245792 | tf_op jit(solution)/shard_map/ppermute | solution.py:72
  61.4 3.3 %shard_map.49 = f32[32,4,8,128]{3,2,1,0:T(8,128)S(1)} custom-call(s32[2,16]{1,0:T(2,128)S(1)} %bitcast.12, bf16[8,2,2,2,1920]{4,3,2,1,0:T(2,128)(2,1)S(1)} %get-tuple-element.16.own, bf16[8,2,2,2,1920]{4,3,2,1,0:T(2,128)(2,1)S(1)} %collective-permute-done.1.one, ...), custom_call_target="tpu_custom_call", output_to_operand_aliasing={{}: (8, {})} | custom-call | flops 319488000 | bytes 983040 | tf_op jit(solution)/shard_map/pallas_call | solution.py:156
  64.7 23.2 %all_to_all.5 = f32[128,8,128]{2,1,0:T(8,128)S(1)} all-to-all(f32[128,8,128]{2,1,0:T(8,128)S(1)} %bitcast.10), channel_id=1, replica_groups=mesh['tile'=32,'date'=4] {'tile','date'}, dimensions={0} | all-to-all | bytes 1048576 | tf_op jit(solution)/shard_map/all_to_all | solution.py:213
  87.9 1.4 %shard_map.50 = f32[4,2,64,128]{3,2,1,0:T(8,128)} custom-call(s32[33]{0:T(128)S(1)} %pad_add_fusion.table, f32[32,4,8,128]{3,2,1,0:T(8,128)S(1)} %bitcast.9), custom_call_target="tpu_custom_call" | custom-call | tf_op jit(solution)/shard_map/pallas_call | solution.py:216
  (5 shorter events, 0.0 us)
Async XLA Ops:
  0.0 2.4 %copy-start = (bf16[2,1,32,2,10,1920]{5,3,4,2,1,0:T(2,128)(2,1)S(1)}, bf16[2,1,32,2,10,1920]{5,3,4,2,1,0:T(2,128)(2,1)}, u32[]{:S(2)}) copy-start(bf16[2,1,32,2,10,1920]{5,3,4,2,1,0:T(2,128)(2,1)} %param.4) | copy-start | bytes 14745604
  2.4 25.0 %copy-start.1 = (bf16[2,1,32,2,10,1920]{5,3,4,2,1,0:T(2,128)(2,1)S(1)}, bf16[2,1,32,2,10,1920]{5,3,4,2,1,0:T(2,128)(2,1)}, u32[]{:S(2)}) copy-start(bf16[2,1,32,2,10,1920]{5,3,4,2,1,0:T(2,128)(2,1)} %param.4) | copy-start | bytes 14745604
  2.4 29.1 %copy-start.3 = (s32[1,32]{1,0:T(1,128)S(1)}, s32[1,32]{1,0:T(1,128)}, u32[]{:S(2)}) copy-start(s32[1,32]{1,0:T(1,128)} %param.5) | copy-start | bytes 388
  2.4 47.4 %copy-start.2 = (s32[16,2]{0,1:T(2,128)S(1)}, s32[16,2]{0,1:T(2,128)}, u32[]{:S(2)}) copy-start(s32[16,2]{0,1:T(2,128)} %param.7) | copy-start | bytes 388
  3.0 24.4 %collective-permute-start = (bf16[8,2,8,2,1920]{4,3,2,1,0:T(2,128)(2,1)S(1)}, bf16[8,2,8,2,1920]{4,3,2,1,0:T(2,128)(2,1)S(1)}, u32[]{:S(2)}, u32[]{:S(2)}) collective-permute-start(bf16[8,2,8,2,1920]{4,3,2,1,0:T(2,128)(2,1)S(1)} %get-tuple-element.15), channel_id=1, source_target_pairs={{0,1},{1,2},{2,3},{3,0},{4,5},{5,6},{6,7},{7,4},{8,9},{9,10},{10,1... | collective-permute-start | bytes 2949128 | tf_op jit(solution)/shard_map/ppermute | solution.py:72
  5.1 26.4 %collective-permute-start.4 = (bf16[8,2,8,2,1920]{4,3,2,1,0:T(2,128)(2,1)S(1)}, bf16[8,2,8,2,1920]{4,3,2,1,0:T(2,128)(2,1)S(1)}, u32[]{:S(2)}, u32[]{:S(2)}) collective-permute-start(bf16[8,2,8,2,1920]{4,3,2,1,0:T(2,128)(2,1)S(1)} %get-tuple-element.21), channel_id=1, source_target_pairs={{0,3},{1,0},{2,1},{3,2},{4,7},{5,4},{6,5},{7,6},{8,11},{9,8},{10,9... | collective-permute-start | bytes 2949128 | tf_op jit(solution)/shard_map/ppermute | solution.py:73
  6.5 43.4 %collective-permute-start.5 = (bf16[8,2,8,2,1920]{4,3,2,1,0:T(2,128)(2,1)S(1)}, bf16[8,2,8,2,1920]{4,3,2,1,0:T(2,128)(2,1)S(1)}, u32[]{:S(2)}, u32[]{:S(2)}) collective-permute-start(bf16[8,2,8,2,1920]{4,3,2,1,0:T(2,128)(2,1)S(1)} %get-tuple-element.22), channel_id=1, source_target_pairs={{0,2},{1,3},{2,0},{3,1},{4,6},{5,7},{6,4},{7,5},{8,10},{9,11},{10,... | collective-permute-start | bytes 2949128 | tf_op jit(solution)/shard_map/ppermute | solution.py:74
  27.7 29.8 %collective-permute-start.1 = (bf16[8,2,2,2,1920]{4,3,2,1,0:T(2,128)(2,1)S(1)}, bf16[8,2,2,2,1920]{4,3,2,1,0:T(2,128)(2,1)S(1)}, u32[]{:S(2)}, u32[]{:S(2)}) collective-permute-start(bf16[8,2,2,2,1920]{4,3,2,1,0:T(2,128)(2,1)S(1)} %get-tuple-element.17), channel_id=1, source_target_pairs={{0,3},{1,0},{2,1},{3,2},{4,7},{5,4},{6,5},{7,6},{8,11},{9,8},{10,9... | collective-permute-start | bytes 737288 | tf_op jit(solution)/shard_map/ppermute | solution.py:73
  29.3 28.2 %collective-permute-start.2 = (bf16[8,2,2,2,1920]{4,3,2,1,0:T(2,128)(2,1)S(1)}, bf16[8,2,2,2,1920]{4,3,2,1,0:T(2,128)(2,1)S(1)}, u32[]{:S(2)}, u32[]{:S(2)}) collective-permute-start(bf16[8,2,2,2,1920]{4,3,2,1,0:T(2,128)(2,1)S(1)} %get-tuple-element.18), channel_id=1, source_target_pairs={{0,2},{1,3},{2,0},{3,1},{4,6},{5,7},{6,4},{7,5},{8,10},{9,11},{10,... | collective-permute-start | bytes 737288 | tf_op jit(solution)/shard_map/ppermute | solution.py:74
  29.9 31.5 %collective-permute-start.3 = (bf16[8,2,2,2,1920]{4,3,2,1,0:T(2,128)(2,1)S(1)}, bf16[8,2,2,2,1920]{4,3,2,1,0:T(2,128)(2,1)S(1)}, u32[]{:S(2)}, u32[]{:S(2)}) collective-permute-start(bf16[8,2,2,2,1920]{4,3,2,1,0:T(2,128)(2,1)S(1)} %get-tuple-element.19), channel_id=1, source_target_pairs={{0,1},{1,2},{2,3},{3,0},{4,5},{5,6},{6,7},{7,4},{8,9},{9,10},{10,1... | collective-permute-start | bytes 737288 | tf_op jit(solution)/shard_map/ppermute | solution.py:72

commit v8 on v7

v8 whole, which is shorter than its diff:
```python
import functools

import jax
import jax.numpy as jnp
from jax import lax
from jax.experimental import pallas as pl
from jax.experimental.pallas import tpu as pltpu
from jax.sharding import PartitionSpec as P

LOOK_RG = 15
LOOK_AZ = 5
EPS = 1e-05
SCALE = 1.0 / (LOOK_AZ * LOOK_RG)
DATES = 8
PAIRS = 16
ITEMS = 8
RG = 1920
LCOL = 128
ROWS = 320
TILES = 32
MAIN = 896
WIDE = 1024
EARLY = ((0, 0, 5), (8, 0, 5), (16, 0, 5), (24, 0, 3))
LATE = ((24, 3, 5),)

VMEM = pl.BlockSpec(memory_space=pltpu.VMEM)
SMEM = pl.BlockSpec(memory_space=pltpu.SMEM)
HBM = pl.BlockSpec(memory_space=pltpu.HBM)
ANYWHERE = pl.BlockSpec(memory_space=pl.ANY)


def cut_kernel(parts, images, *rest):
    to1, to2, to3, own, sem = rest[-5:]
    group = lax.axis_index("date")
    copies = []
    for step, out in ((1, to1), (3, to3), (2, to2), (0, own)):
        taker = lax.rem(group + step, 4)
        top, left = lax.div(taker, 2) * LOOK_AZ, lax.rem(taker, 2) * WIDE
        filled = 0
        for first, low, high in parts:
            lines, slots = pl.ds(top + low, high - low), slice(filled, filled + high - low)
            filled += high - low
            for date in range(2):
                copies.append(
                    pltpu.make_async_copy(
                        images.at[
                            date,
                            first : first + ITEMS,
                            lines,
                            :,
                            pl.ds(pl.multiple_of(left, WIDE), MAIN),
                        ],
                        out.at[:, date, slots],
                        sem.at[len(copies)],
                    )
                )
                copies[-1].start()
    for copy in copies:
        copy.wait()


def cut(images, parts, after=None):
    slots = sum(high - low for _, low, high in parts)
    block = jax.ShapeDtypeStruct((ITEMS, 2, slots, 2, MAIN), jnp.bfloat16)
    operands = (images,) + (() if after is None else (after,))
    return pl.pallas_call(
        functools.partial(cut_kernel, parts),
        out_shape=[block] * 4,
        in_specs=[HBM, ANYWHERE][: len(operands)],
        out_specs=[VMEM] * 4,
        scratch_shapes=[pltpu.SemaphoreType.DMA((8 * len(parts),))],
        compiler_params=pltpu.CompilerParams(vmem_limit_bytes=8 << 20),
    )(*operands)


def cut_middle_kernel(images, to1, to2, to3, own, block, sem):
    copy = pltpu.make_async_copy(images.at[:, :, :, :, MAIN:WIDE], block, sem)
    copy.start()
    copy.wait()
    group = lax.axis_index("date")
    left = lax.broadcasted_iota(jnp.int32, (16, LCOL), 1) < 64
    for step, out in ((1, to1), (3, to3), (2, to2), (0, own)):
        taker = lax.rem(group + step, 4)
        top, half = lax.div(taker, 2) * LOOK_AZ, lax.rem(taker, 2)

        def pack(slot, carry, out=out, top=top, half=half):
            tiles = pl.ds(lax.div(slot, LOOK_AZ) * ITEMS, ITEMS)
            line = top + lax.rem(slot, LOOK_AZ)
            zero = block[0, tiles, line].reshape(16, LCOL).astype(jnp.float32)
            one = block[1, tiles, line].reshape(16, LCOL).astype(jnp.float32)
            first = jnp.where(left, zero, pltpu.roll(one, 64, 1))
            second = jnp.where(left, pltpu.roll(zero, 64, 1), one)
            packed = jnp.where(half == 0, first, second).astype(jnp.bfloat16)
            out[:, slot] = packed.reshape(ITEMS, 2, LCOL)
            return carry

        lax.fori_loop(0, TILES // ITEMS * LOOK_AZ, pack, 0)


def cut_middle(images):
    slots = TILES // ITEMS * LOOK_AZ
    return pl.pallas_call(
        cut_middle_kernel,
        out_shape=[jax.ShapeDtypeStruct((ITEMS, slots, 2, LCOL), jnp.bfloat16)] * 4,
        in_specs=[HBM],
        out_specs=[VMEM] * 4,
        scratch_shapes=[
            pltpu.VMEM((2, TILES, 2 * LOOK_AZ, 2, LCOL), jnp.bfloat16),
            pltpu.SemaphoreType.DMA,
        ],
        compiler_params=pltpu.CompilerParams(vmem_limit_bytes=8 << 20),
    )(images)


def meet(to1, to2, to3, own):
    def ring(step):
        return [(i, (i + step) % 4) for i in range(4)]

    three = lax.ppermute(to1, "date", ring(1))
    one = lax.ppermute(to3, "date", ring(3))
    two = lax.ppermute(to2, "date", ring(2))
    return own, one, two, three


def add_lines(epochs, mains, slot, middles, middle_slot, lines, box, img, hi, lo):
    group = lax.axis_index("date")
    left = lax.broadcasted_iota(jnp.int32, (16, LCOL), 1) < 64
    for step, (main, middle) in enumerate(zip(mains, middles)):
        base = lax.rem(group + step, 4) * 2
        for line in range(lines):
            for date in range(2):
                pixels = jnp.swapaxes(main[:, date, slot + line], 0, 1).reshape(16, MAIN)
                img[base + date, line, :, 0:MAIN] = pixels.astype(jnp.float32)
            packed = jnp.swapaxes(middle[:, middle_slot + line], 0, 1).reshape(16, LCOL)
            packed = packed.astype(jnp.float32)
            img[base, line, :, MAIN:WIDE] = jnp.where(left, packed, 0.0)
            img[base + 1, line, :, MAIN:WIDE] = jnp.where(left, pltpu.roll(packed, 64, 1), 0.0)

    def split(values, row):
        upper = values.astype(jnp.bfloat16)
        hi[pl.ds(row, 16), :] = upper
        lo[pl.ds(row, 16), :] = (values - upper.astype(jnp.float32)).astype(jnp.bfloat16)

    def power(half, carry):
        total = []
        for date in range(2):
            acc = jnp.zeros((ITEMS, WIDE), jnp.float32)
            for line in range(lines):
                re = img[2 * half + date, line, 0:8, :]
                im = img[2 * half + date, line, 8:16, :]
                acc = acc + (re * re + im * im)
            total.append(acc)
        split(jnp.concatenate(total, axis=0), pl.multiple_of(half * 16, 16))
        return carry

    lax.fori_loop(0, DATES // 2, power, 0)

    def cross(k, carry):
        a, b = epochs[0, k], epochs[1, k]
        acc_re = jnp.zeros((ITEMS, WIDE), jnp.float32)
        acc_im = jnp.zeros((ITEMS, WIDE), jnp.float32)
        for line in range(lines):
            re_a, im_a = img[a, line, 0:8, :], img[a, line, 8:16, :]
            re_b, im_b = img[b, line, 0:8, :], img[b, line, 8:16, :]
            acc_re = acc_re + (re_a * re_b + im_a * im_b)
            acc_im = acc_im + (im_a * re_b - re_a * im_b)
        split(jnp.concatenate([acc_re, acc_im], axis=0), pl.multiple_of(64 + k * 16, 16))
        return carry

    lax.fori_loop(0, PAIRS, cross, 0)
    return jnp.dot(hi[...], box[...], preferred_element_type=jnp.float32) + jnp.dot(
        lo[...], box[...], preferred_element_type=jnp.float32
    )


def coherence(epochs, part, sums, out):
    left = lax.broadcasted_iota(jnp.int32, (ITEMS, LCOL), 1) < 64
    for owner in range(4):
        rows = []
        for kk in range(4):
            k = owner * 4 + kk
            power_a = sums[pl.ds(pl.multiple_of(epochs[0, k] * 8, 8), 8), :]
            power_b = sums[pl.ds(pl.multiple_of(epochs[1, k] * 8, 8), 8), :]
            weight = 1.0 / jnp.sqrt((power_a + EPS) * (power_b + EPS))
            cross = jnp.where(
                left, sums[64 + k * 16 : 72 + k * 16, :], sums[72 + k * 16 : 80 + k * 16, :]
            )
            rows.append(cross * weight)
        out[part * ITEMS : (part + 1) * ITEMS, owner] = jnp.swapaxes(
            jnp.stack(rows, axis=0), 0, 1
        )


def early_kernel(epochs, *rest):
    mains, middles, (box, table, out, most, img, hi, lo, sums) = rest[:4], rest[4:8], rest[8:]
    del table
    slot = 0
    for part, (_, low, high) in enumerate(EARLY):
        total = add_lines(
            epochs, mains, slot, middles, part * LOOK_AZ + low, high - low, box, img, hi, lo
        )
        slot += high - low
        if high - low == LOOK_AZ:
            sums[...] = total * SCALE
            coherence(epochs, part, sums, out)
        else:
            most[...] = total


def late_kernel(epochs, *rest):
    mains, middles, (box, most, given, out, img, hi, lo, sums) = rest[:4], rest[4:8], rest[8:]
    del given
    ((_, low, high),) = LATE
    part = len(EARLY) - 1
    total = add_lines(
        epochs, mains, 0, middles, part * LOOK_AZ + low, high - low, box, img, hi, lo
    )
    sums[...] = (total + most[...]) * SCALE
    coherence(epochs, part, sums, out)


def looks(kernel, epochs, operands, out_shape, lines, aliases):
    work = lines * ITEMS * WIDE * (PAIRS * 8 + DATES * 4) + 4 * ROWS * WIDE * LCOL
    return pl.pallas_call(
        kernel,
        out_shape=out_shape,
        grid_spec=pltpu.PrefetchScalarGridSpec(
            num_scalar_prefetch=1,
            grid=(),
            in_specs=[VMEM if x.ndim > 1 else SMEM for x in operands],
            out_specs=jax.tree.map(lambda _: VMEM, out_shape),
            scratch_shapes=[
                pltpu.VMEM((DATES, min(lines, LOOK_AZ), 16, WIDE), jnp.float32),
                pltpu.VMEM((ROWS, WIDE), jnp.bfloat16),
                pltpu.VMEM((ROWS, WIDE), jnp.bfloat16),
                pltpu.VMEM((ROWS, LCOL), jnp.float32),
            ],
        ),
        input_output_aliases=aliases,
        cost_estimate=pl.CostEstimate(
            flops=work, bytes_accessed=DATES * lines * 16 * WIDE * 2, transcendentals=0
        ),
        compiler_params=pltpu.CompilerParams(vmem_limit_bytes=24 << 20),
    )(epochs, *operands)


def place_kernel(table, got, out, rows):
    lane = lax.broadcasted_iota(jnp.int32, (8, LCOL), 1) < 64
    row = lax.broadcasted_iota(jnp.int32, (8, LCOL), 0) < 4
    keep = lane == row
    for burst in range(TILES):
        position = table[burst]
        valid = jnp.where(position < table[TILES], 1.0, 0.0).astype(jnp.float32)
        base = pl.multiple_of(position * 16, 16)
        for look in range(2):
            halves = got[burst * 2 + look]
            crossed = pltpu.roll(pltpu.roll(halves, 64, 1), 4, 0)
            rows[pl.ds(base + look * 8, 8), :] = jnp.where(keep, halves, crossed) * valid
    for pair in range(4):
        for part in range(2):
            for eight in range(8):
                out[pair, part, eight * 8 : eight * 8 + 8, :] = rows[
                    pl.ds(eight * 64 + part * 4 + pair, 8, stride=8), :
                ]


def on_device(complex_images, segment_position_map, usable_position_total, interferogram_epochs):
    images = complex_images[:, 0].transpose(0, 1, 3, 2, 4)
    epochs = interferogram_epochs.T
    table = jnp.concatenate([segment_position_map[0], usable_position_total])

    half = lax.rem(lax.axis_index("date"), 2)
    lane = jnp.arange(WIDE)
    place = jnp.where(lane < MAIN, lane + 64 * half, lane - MAIN * half)
    look = jnp.where(lane < MAIN + 64, place // LOOK_RG, -1)
    box = (look[:, None] == jnp.arange(LCOL)[None, :] % 64).astype(jnp.bfloat16)

    early = meet(*cut(images, EARLY))
    middle = meet(*cut_middle(images))
    late = meet(*cut(images, LATE, early[3]))

    shape = jax.ShapeDtypeStruct((TILES, 4, 4, LCOL), jnp.float32)
    partial = jax.ShapeDtypeStruct((ROWS, LCOL), jnp.float32)
    gamma, most = looks(early_kernel, epochs, (*early, *middle, box, table), (shape, partial), 18, {})
    gamma = looks(late_kernel, epochs, (*late, *middle, box, most, gamma), shape, 2, {11: 0})
    got = lax.all_to_all(
        gamma.reshape(128, 4, LCOL), ("tile", "date"), split_axis=0, concat_axis=0, tiled=True
    ).reshape(64, 8, LCOL)
    return pl.pallas_call(
        place_kernel,
        out_shape=jax.ShapeDtypeStruct((4, 2, 64, LCOL), jnp.float32),
        grid_spec=pltpu.PrefetchScalarGridSpec(
            num_scalar_prefetch=1,
            grid=(),
            in_specs=[VMEM],
            out_specs=VMEM,
            scratch_shapes=[pltpu.VMEM((512, LCOL), jnp.float32)],
        ),
        compiler_params=pltpu.CompilerParams(vmem_limit_bytes=4 << 20),
    )(table, got)


def solution(mesh):
    in_specs = (P("date", "tile", None, None, None, None), P("tile", None), P("tile"), P())
    out_specs = P("date", None, None, "tile")
    return jax.shard_map(
        on_device, mesh=mesh, in_specs=in_specs, out_specs=out_specs, check_vma=False
    )
```

time: 89.5 us -> 98.2 us (1.097)
  Pallas kernels: 13.2 us -> 25.2 us
  waiting for transfers between devices: 41.5 us -> 32.6 us
  starting transfers between devices: 7.91 us -> 10.3 us
  local copies, waits for them, and re-layouts: 2.4 us -> 4.79 us
    ppermute x2 -> x3, waiting for transfers between devices: 0.01 us -> 20.3 us  [meet(): one = lax.ppermute(to3, 'date', ring(3))]
    ppermute x2 -> x3, waiting for transfers between devices: 18.3 us -> 0.01 us  [meet(): two = lax.ppermute(to2, 'date', ring(2))]
    ppermute x2 -> x3, waiting for transfers between devices: 23.2 us -> 12.3 us  [meet(): three = lax.ppermute(to1, 'date', ring(1))]
    pallas_call x0 -> x1, Pallas kernels: none -> 7.68 us  [cut_middle(): pl.pallas_call(cut_middle_kernel, out_shape=[jax.ShapeDtypeStruct((ITEMS,...]
    pallas_call x2, Pallas kernels: 11 us -> 13.5 us  [looks(): pl.pallas_call(kernel, out_shape=out_shape, grid_spec=pltpu.PrefetchScala...]
    unnamed x8, local copies, waits for them, and re-layouts: 2.4 us -> 4.79 us
    pallas_call x2, Pallas kernels: 0.84 us -> 2.59 us  [cut(): pl.pallas_call(functools.partial(cut_kernel, parts), out_shape=[block] *...]
    ppermute x2 -> x3, starting transfers between devices: 2.17 us -> 3.9 us  [meet(): two = lax.ppermute(to2, 'date', ring(2))]
  transfers between devices with their start and end apart: 6 -> 9, of which waited for: 3 -> 3; matrix products, arithmetic and copies ran while one was open for 0% -> 0% of each run, Pallas kernels for 9% -> 20%
where the time goes in v8:
time: 98.2 us; the launch traced here: 98 us
  waiting for transfers between devices  32.6 us (33%)
  Pallas kernels  25.2 us (26%)
  blocking collectives  24 us (24%)
  starting transfers between devices  10.3 us (10%)
  local copies, waits for them, and re-layouts  4.79 us (5%)
    all_to_all x1, blocking collectives, on_device(): lax.all_to_all(gamma.reshape(128, 4, LCOL), ('tile', 'date'), split_axis=...  24 us
    ppermute x3, waiting for transfers between devices, meet(): one = lax.ppermute(to3, 'date', ring(3))  20.3 us
    pallas_call x2, Pallas kernels, looks(): pl.pallas_call(kernel, out_shape=out_shape, grid_spec=pltpu.PrefetchScala...  13.5 us
    ppermute x3, waiting for transfers between devices, meet(): three = lax.ppermute(to1, 'date', ring(1))  12.3 us
    pallas_call x1, Pallas kernels, cut_middle(): pl.pallas_call(cut_middle_kernel, out_shape=[jax.ShapeDtypeStruct((ITEMS,...  7.68 us
    unnamed x8, local copies, waits for them, and re-layouts  4.79 us
    ppermute x3, starting transfers between devices, meet(): two = lax.ppermute(to2, 'date', ring(2))  3.9 us
    ppermute x3, starting transfers between devices, meet(): one = lax.ppermute(to3, 'date', ring(3))  3.64 us
  transfers between devices with their start and end apart: 9, of which 3 were waited for; matrix products, arithmetic and copies ran while one was open for 0% of the time, Pallas kernels for 20%

profile of v8, /device:TPU:1, one launch (start us, length us, event | category | flops | bytes accessed | tf_op | source)
XLA Modules:
  0.0 98.0 jit_solution(11800890899119709172)
XLA Ops:
  0.0 2.4 %copy-done = bf16[2,1,32,2,10,1920]{5,3,4,2,1,0:T(2,128)(2,1)S(1)} copy-done((bf16[2,1,32,2,10,1920]{5,3,4,2,1,0:T(2,128)(2,1)S(1)}, bf16[2,1,32,2,10,1920]{5,3,4,2,1,0:T(2,128)(2,1)}, u32[]{:S(2)}) %copy-start) | copy-done | bytes 4915224
  2.4 2.4 %shard_map.46 = (bf16[8,2,18,2,896]{4,3,2,1,0:T(2,128)(2,1)}, bf16[8,2,18,2,896]{4,3,2,1,0:T(2,128)(2,1)}, bf16[8,2,18,2,896]{4,3,2,1,0:T(2,128)(2,1)}, bf16[8,2,18,2,896]{4,3,2,1,0:T(2,128)(2,1)S(1)}) custom-call(bf16[2,32,10,2,1920]{4,3,2,1,0:T(2,128)(2,1)S(1)} %bitcast.7), custom_call_target="tpu_custom_call" | custom-call | tf_op jit(solution)/shard_map/pallas_call | solution.py:66
  4.8 2.1 %collective-permute-start = (bf16[8,2,18,2,896]{4,3,2,1,0:T(2,128)(2,1)}, bf16[8,2,18,2,896]{4,3,2,1,0:T(2,128)(2,1)S(1)}, u32[]{:S(2)}, u32[]{:S(2)}) collective-permute-start(bf16[8,2,18,2,896]{4,3,2,1,0:T(2,128)(2,1)} %get-tuple-element.19), channel_id=1, source_target_pairs={{0,1},{1,2},{2,3},{3,0},{4,5},{5,6},{6,7},{7,4},{8,9},{9,10},{10,1... | collective-permute-start | bytes 3096584 | tf_op jit(solution)/shard_map/ppermute | solution.py:119
  7.0 1.3 %collective-permute-start.7 = (bf16[8,2,18,2,896]{4,3,2,1,0:T(2,128)(2,1)}, bf16[8,2,18,2,896]{4,3,2,1,0:T(2,128)(2,1)S(1)}, u32[]{:S(2)}, u32[]{:S(2)}) collective-permute-start(bf16[8,2,18,2,896]{4,3,2,1,0:T(2,128)(2,1)} %get-tuple-element.29), channel_id=1, source_target_pairs={{0,3},{1,0},{2,1},{3,2},{4,7},{5,4},{6,5},{7,6},{8,11},{9,8},{10,9... | collective-permute-start | bytes 3096584 | tf_op jit(solution)/shard_map/ppermute | solution.py:120
  8.3 1.6 %collective-permute-start.8 = (bf16[8,2,18,2,896]{4,3,2,1,0:T(2,128)(2,1)}, bf16[8,2,18,2,896]{4,3,2,1,0:T(2,128)(2,1)}, u32[]{:S(2)}, u32[]{:S(2)}) collective-permute-start(bf16[8,2,18,2,896]{4,3,2,1,0:T(2,128)(2,1)} %get-tuple-element.30), channel_id=1, source_target_pairs={{0,2},{1,3},{2,0},{3,1},{4,6},{5,7},{6,4},{7,5},{8,10},{9,11},{10,... | collective-permute-start | bytes 3096584 | tf_op jit(solution)/shard_map/ppermute | solution.py:121
  10.0 7.7 %shard_map.48 = (bf16[8,20,2,128]{3,2,1,0:T(2,128)(2,1)S(1)}, bf16[8,20,2,128]{3,2,1,0:T(2,128)(2,1)S(1)}, bf16[8,20,2,128]{3,2,1,0:T(2,128)(2,1)}, bf16[8,20,2,128]{3,2,1,0:T(2,128)(2,1)S(1)}) custom-call(bf16[2,32,10,2,1920]{4,3,2,1,0:T(2,128)(2,1)S(1)} %bitcast.8), custom_call_target="tpu_custom_call" | custom-call | tf_op jit(solution)/shard_map/pallas_call | solution.py:102
  17.6 0.9 collective-permute-start.4
  18.6 1.2 %collective-permute-start.5 = (bf16[8,20,2,128]{3,2,1,0:T(2,128)(2,1)S(1)}, bf16[8,20,2,128]{3,2,1,0:T(2,128)(2,1)S(1)}, u32[]{:S(2)}, u32[]{:S(2)}) collective-permute-start(bf16[8,20,2,128]{3,2,1,0:T(2,128)(2,1)S(1)} %get-tuple-element.26), channel_id=1, source_target_pairs={{0,2},{1,3},{2,0},{3,1},{4,6},{5,7},{6,4},{7,5},{8,10},{9,11},{10,... | collective-permute-start | bytes 245768 | tf_op jit(solution)/shard_map/ppermute | solution.py:121
  19.8 10.7 %collective-permute-done.rest_0_.rest_3_ = bf16[8,2,18,2,896]{4,3,2,1,0:T(2,128)(2,1)S(1)} collective-permute-done((bf16[8,2,18,2,896]{4,3,2,1,0:T(2,128)(2,1)}, bf16[8,2,18,2,896]{4,3,2,1,0:T(2,128)(2,1)S(1)}, u32[]{:S(2)}, u32[]{:S(2)}) %collective-permute-start) | collective-permute-done | bytes 1032224 | tf_op jit(solution)/shard_map/ppermute | solution.py:119
  30.5 0.3 collective-permute-start.6
  30.8 0.2 compare_convert_fusion.rest_8_
  31.7 0.0 copy-start.1
  31.7 2.4 %copy-done.1 = bf16[2,1,32,2,10,1920]{5,3,4,2,1,0:T(2,128)(2,1)S(1)} copy-done((bf16[2,1,32,2,10,1920]{5,3,4,2,1,0:T(2,128)(2,1)S(1)}, bf16[2,1,32,2,10,1920]{5,3,4,2,1,0:T(2,128)(2,1)}, u32[]{:S(2)}) %copy-start.1) | copy-done | bytes 4915224
  34.1 0.2 shard_map.47
  34.3 20.3 %collective-permute-done.4.rest_5_ = bf16[8,20,2,128]{3,2,1,0:T(2,128)(2,1)S(1)} collective-permute-done((bf16[8,20,2,128]{3,2,1,0:T(2,128)(2,1)}, bf16[8,20,2,128]{3,2,1,0:T(2,128)(2,1)S(1)}, u32[]{:S(2)}, u32[]{:S(2)}) %collective-permute-start.4) | collective-permute-done | bytes 81952 | tf_op jit(solution)/shard_map/ppermute | solution.py:120
  54.5 1.4 %collective-permute-start.1 = (bf16[8,2,2,2,896]{4,3,2,1,0:T(2,128)(2,1)S(1)}, bf16[8,2,2,2,896]{4,3,2,1,0:T(2,128)(2,1)S(1)}, u32[]{:S(2)}, u32[]{:S(2)}) collective-permute-start(bf16[8,2,2,2,896]{4,3,2,1,0:T(2,128)(2,1)S(1)} %get-tuple-element.21), channel_id=1, source_target_pairs={{0,3},{1,0},{2,1},{3,2},{4,7},{5,4},{6,5},{7,6},{8,11},{9,8},{10,9... | collective-permute-start | bytes 344072 | tf_op jit(solution)/shard_map/ppermute | solution.py:120
  55.9 1.0 %collective-permute-start.2 = (bf16[8,2,2,2,896]{4,3,2,1,0:T(2,128)(2,1)S(1)}, bf16[8,2,2,2,896]{4,3,2,1,0:T(2,128)(2,1)S(1)}, u32[]{:S(2)}, u32[]{:S(2)}) collective-permute-start(bf16[8,2,2,2,896]{4,3,2,1,0:T(2,128)(2,1)S(1)} %get-tuple-element.22), channel_id=1, source_target_pairs={{0,2},{1,3},{2,0},{3,1},{4,6},{5,7},{6,4},{7,5},{8,10},{9,11},{10,... | collective-permute-start | bytes 344072 | tf_op jit(solution)/shard_map/ppermute | solution.py:121
  56.9 1.6 %collective-permute-done.6.rest_7_ = bf16[8,20,2,128]{3,2,1,0:T(2,128)(2,1)S(1)} collective-permute-done((bf16[8,20,2,128]{3,2,1,0:T(2,128)(2,1)S(1)}, bf16[8,20,2,128]{3,2,1,0:T(2,128)(2,1)S(1)}, u32[]{:S(2)}, u32[]{:S(2)}) %collective-permute-start.6) | collective-permute-done | bytes 81952 | tf_op jit(solution)/shard_map/ppermute | solution.py:119
  58.5 0.4 collective-permute-start.3
  58.9 0.1 pad_add_fusion.rest_9_.table
  59.0 11.6 %shard_map.49 = (f32[32,4,4,128]{3,2,1,0:T(4,128)S(1)}, f32[320,128]{1,0:T(8,128)S(1)}) custom-call(s32[2,16]{1,0:T(2,128)S(1)} %bitcast.12, bf16[8,2,18,2,896]{4,3,2,1,0:T(2,128)(2,1)S(1)} %get-tuple-element.28.rest_0_, bf16[8,2,18,2,896]{4,3,2,1,0:T(2,128)(2,1)S(1)} %collective-permute-done.7.rest_1_, ...), custom_call_target="tpu_custom_call" | custom-call | flops 191365120 | bytes 4718592 | tf_op jit(solution)/shard_map/pallas_call | solution.py:224
  70.6 2.0 %shard_map.50 = f32[32,4,4,128]{3,2,1,0:T(4,128)S(1)} custom-call(s32[2,16]{1,0:T(2,128)S(1)} %bitcast.13, bf16[8,2,2,2,896]{4,3,2,1,0:T(2,128)(2,1)S(1)} %get-tuple-element.20.rest_0_, bf16[8,2,2,2,896]{4,3,2,1,0:T(2,128)(2,1)S(1)} %collective-permute-done.1.rest_1_, ...), custom_call_target="tpu_custom_call", output_to_operand_aliasing={{}: (11, {})} | custom-call | flops 170393600 | bytes 524288 | tf_op jit(solution)/shard_map/pallas_call | solution.py:224
  72.5 24.0 %all_to_all.5 = f32[128,4,128]{2,1,0:T(4,128)S(1)} all-to-all(f32[128,4,128]{2,1,0:T(4,128)S(1)} %bitcast.11), channel_id=1, replica_groups=mesh['tile'=32,'date'=4] {'tile','date'}, dimensions={0} | all-to-all | bytes 524288 | tf_op jit(solution)/shard_map/all_to_all | solution.py:286
  96.5 1.4 %shard_map.51 = f32[4,2,64,128]{3,2,1,0:T(8,128)} custom-call(s32[33]{0:T(128)S(1)} %pad_add_fusion.rest_9_.table, f32[64,8,128]{2,1,0:T(8,128)S(1)} %bitcast.10), custom_call_target="tpu_custom_call" | custom-call | tf_op jit(solution)/shard_map/pallas_call | solution.py:289
  (13 shorter events, 0.0 us)
Async XLA Ops:
  0.0 2.4 %copy-start = (bf16[2,1,32,2,10,1920]{5,3,4,2,1,0:T(2,128)(2,1)S(1)}, bf16[2,1,32,2,10,1920]{5,3,4,2,1,0:T(2,128)(2,1)}, u32[]{:S(2)}) copy-start(bf16[2,1,32,2,10,1920]{5,3,4,2,1,0:T(2,128)(2,1)} %param.4) | copy-start | bytes 14745604
  4.8 25.7 %collective-permute-start = (bf16[8,2,18,2,896]{4,3,2,1,0:T(2,128)(2,1)}, bf16[8,2,18,2,896]{4,3,2,1,0:T(2,128)(2,1)S(1)}, u32[]{:S(2)}, u32[]{:S(2)}) collective-permute-start(bf16[8,2,18,2,896]{4,3,2,1,0:T(2,128)(2,1)} %get-tuple-element.19), channel_id=1, source_target_pairs={{0,1},{1,2},{2,3},{3,0},{4,5},{5,6},{6,7},{7,4},{8,9},{9,10},{10,1... | collective-permute-start | bytes 3096584 | tf_op jit(solution)/shard_map/ppermute | solution.py:119
  7.0 52.0 %collective-permute-start.7 = (bf16[8,2,18,2,896]{4,3,2,1,0:T(2,128)(2,1)}, bf16[8,2,18,2,896]{4,3,2,1,0:T(2,128)(2,1)S(1)}, u32[]{:S(2)}, u32[]{:S(2)}) collective-permute-start(bf16[8,2,18,2,896]{4,3,2,1,0:T(2,128)(2,1)} %get-tuple-element.29), channel_id=1, source_target_pairs={{0,3},{1,0},{2,1},{3,2},{4,7},{5,4},{6,5},{7,6},{8,11},{9,8},{10,9... | collective-permute-start | bytes 3096584 | tf_op jit(solution)/shard_map/ppermute | solution.py:120
  8.3 50.6 %copy-start.3 = (s32[1,32]{1,0:T(1,128)S(1)}, s32[1,32]{1,0:T(1,128)}, u32[]{:S(2)}) copy-start(s32[1,32]{1,0:T(1,128)} %param.5) | copy-start | bytes 388
  8.3 50.7 %copy-start.2 = (s32[16,2]{0,1:T(2,128)S(1)}, s32[16,2]{0,1:T(2,128)}, u32[]{:S(2)}) copy-start(s32[16,2]{0,1:T(2,128)} %param.7) | copy-start | bytes 388
  8.3 50.7 %collective-permute-start.8 = (bf16[8,2,18,2,896]{4,3,2,1,0:T(2,128)(2,1)}, bf16[8,2,18,2,896]{4,3,2,1,0:T(2,128)(2,1)}, u32[]{:S(2)}, u32[]{:S(2)}) collective-permute-start(bf16[8,2,18,2,896]{4,3,2,1,0:T(2,128)(2,1)} %get-tuple-element.30), channel_id=1, source_target_pairs={{0,2},{1,3},{2,0},{3,1},{4,6},{5,7},{6,4},{7,5},{8,10},{9,11},{10,... | collective-permute-start | bytes 3096584 | tf_op jit(solution)/shard_map/ppermute | solution.py:121
  17.6 36.9 %collective-permute-start.4 = (bf16[8,20,2,128]{3,2,1,0:T(2,128)(2,1)}, bf16[8,20,2,128]{3,2,1,0:T(2,128)(2,1)S(1)}, u32[]{:S(2)}, u32[]{:S(2)}) collective-permute-start(bf16[8,20,2,128]{3,2,1,0:T(2,128)(2,1)} %get-tuple-element.25), channel_id=1, source_target_pairs={{0,3},{1,0},{2,1},{3,2},{4,7},{5,4},{6,5},{7,6},{8,11},{9,8},{10,9... | collective-permute-start | bytes 245768 | tf_op jit(solution)/shard_map/ppermute | solution.py:120
  18.6 37.3 %collective-permute-start.5 = (bf16[8,20,2,128]{3,2,1,0:T(2,128)(2,1)S(1)}, bf16[8,20,2,128]{3,2,1,0:T(2,128)(2,1)S(1)}, u32[]{:S(2)}, u32[]{:S(2)}) collective-permute-start(bf16[8,20,2,128]{3,2,1,0:T(2,128)(2,1)S(1)} %get-tuple-element.26), channel_id=1, source_target_pairs={{0,2},{1,3},{2,0},{3,1},{4,6},{5,7},{6,4},{7,5},{8,10},{9,11},{10,... | collective-permute-start | bytes 245768 | tf_op jit(solution)/shard_map/ppermute | solution.py:121
  30.5 28.0 %collective-permute-start.6 = (bf16[8,20,2,128]{3,2,1,0:T(2,128)(2,1)S(1)}, bf16[8,20,2,128]{3,2,1,0:T(2,128)(2,1)S(1)}, u32[]{:S(2)}, u32[]{:S(2)}) collective-permute-start(bf16[8,20,2,128]{3,2,1,0:T(2,128)(2,1)S(1)} %get-tuple-element.27), channel_id=1, source_target_pairs={{0,1},{1,2},{2,3},{3,0},{4,5},{5,6},{6,7},{7,4},{8,9},{9,10},{10,1... | collective-permute-start | bytes 245768 | tf_op jit(solution)/shard_map/ppermute | solution.py:119
  31.7 2.4 %copy-start.1 = (bf16[2,1,32,2,10,1920]{5,3,4,2,1,0:T(2,128)(2,1)S(1)}, bf16[2,1,32,2,10,1920]{5,3,4,2,1,0:T(2,128)(2,1)}, u32[]{:S(2)}) copy-start(bf16[2,1,32,2,10,1920]{5,3,4,2,1,0:T(2,128)(2,1)} %param.4) | copy-start | bytes 14745604
  54.5 16.0 %collective-permute-start.1 = (bf16[8,2,2,2,896]{4,3,2,1,0:T(2,128)(2,1)S(1)}, bf16[8,2,2,2,896]{4,3,2,1,0:T(2,128)(2,1)S(1)}, u32[]{:S(2)}, u32[]{:S(2)}) collective-permute-start(bf16[8,2,2,2,896]{4,3,2,1,0:T(2,128)(2,1)S(1)} %get-tuple-element.21), channel_id=1, source_target_pairs={{0,3},{1,0},{2,1},{3,2},{4,7},{5,4},{6,5},{7,6},{8,11},{9,8},{10,9... | collective-permute-start | bytes 344072 | tf_op jit(solution)/shard_map/ppermute | solution.py:120
  55.9 14.6 %collective-permute-start.2 = (bf16[8,2,2,2,896]{4,3,2,1,0:T(2,128)(2,1)S(1)}, bf16[8,2,2,2,896]{4,3,2,1,0:T(2,128)(2,1)S(1)}, u32[]{:S(2)}, u32[]{:S(2)}) collective-permute-start(bf16[8,2,2,2,896]{4,3,2,1,0:T(2,128)(2,1)S(1)} %get-tuple-element.22), channel_id=1, source_target_pairs={{0,2},{1,3},{2,0},{3,1},{4,6},{5,7},{6,4},{7,5},{8,10},{9,11},{10,... | collective-permute-start | bytes 344072 | tf_op jit(solution)/shard_map/ppermute | solution.py:121
  58.5 12.0 %collective-permute-start.3 = (bf16[8,2,2,2,896]{4,3,2,1,0:T(2,128)(2,1)S(1)}, bf16[8,2,2,2,896]{4,3,2,1,0:T(2,128)(2,1)S(1)}, u32[]{:S(2)}, u32[]{:S(2)}) collective-permute-start(bf16[8,2,2,2,896]{4,3,2,1,0:T(2,128)(2,1)S(1)} %get-tuple-element.23), channel_id=1, source_target_pairs={{0,1},{1,2},{2,3},{3,0},{4,5},{5,6},{6,7},{7,4},{8,9},{9,10},{10,1... | collective-permute-start | bytes 344072 | tf_op jit(solution)/shard_map/ppermute | solution.py:119

commit v9 on v8

--- a/solution.py
+++ b/solution.py
@@ -20,8 +20,7 @@
 TILES = 32
 MAIN = 896
 WIDE = 1024
-EARLY = ((0, 0, 5), (8, 0, 5), (16, 0, 5), (24, 0, 3))
-LATE = ((24, 3, 5),)
+CHUNKS = (((0, 0, 5), (8, 0, 5)), ((16, 0, 5), (24, 0, 3)), ((24, 3, 5),))
 
 VMEM = pl.BlockSpec(memory_space=pltpu.VMEM)
 SMEM = pl.BlockSpec(memory_space=pltpu.SMEM)
@@ -73,7 +72,8 @@
     )(*operands)
 
 
-def cut_middle_kernel(images, to1, to2, to3, own, block, sem):
+def cut_middle_kernel(images, *rest):
+    to1, to2, to3, own, block, sem = rest[-6:]
     copy = pltpu.make_async_copy(images.at[:, :, :, :, MAIN:WIDE], block, sem)
     copy.start()
     copy.wait()
@@ -97,19 +97,19 @@
         lax.fori_loop(0, TILES // ITEMS * LOOK_AZ, pack, 0)
 
 
-def cut_middle(images):
+def cut_middle(images, after):
     slots = TILES // ITEMS * LOOK_AZ
     return pl.pallas_call(
         cut_middle_kernel,
         out_shape=[jax.ShapeDtypeStruct((ITEMS, slots, 2, LCOL), jnp.bfloat16)] * 4,
-        in_specs=[HBM],
+        in_specs=[HBM, ANYWHERE],
         out_specs=[VMEM] * 4,
         scratch_shapes=[
             pltpu.VMEM((2, TILES, 2 * LOOK_AZ, 2, LCOL), jnp.bfloat16),
             pltpu.SemaphoreType.DMA,
         ],
         compiler_params=pltpu.CompilerParams(vmem_limit_bytes=8 << 20),
-    )(images)
+    )(images, after)
 
 
 def meet(to1, to2, to3, own):
@@ -191,38 +191,39 @@
         )
 
 
-def early_kernel(epochs, *rest):
-    mains, middles, (box, table, out, most, img, hi, lo, sums) = rest[:4], rest[4:8], rest[8:]
-    del table
+def looks_kernel(chunk, epochs, *rest):
+    mains, middles, (box, *rest), work = rest[:4], rest[4:8], rest[8:-4], rest[-4:]
+    sums = work[-1]
+    if chunk == 0:
+        table, out = rest
+        del table
+    elif chunk == 1:
+        given, out, most = rest
+        del given
+    else:
+        most, given, out = rest
+        del given
     slot = 0
-    for part, (_, low, high) in enumerate(EARLY):
+    for first, low, high in CHUNKS[chunk]:
+        part = first // ITEMS
         total = add_lines(
-            epochs, mains, slot, middles, part * LOOK_AZ + low, high - low, box, img, hi, lo
+            epochs, mains, slot, middles, part * LOOK_AZ + low, high - low, box, *work[:-1]
         )
         slot += high - low
-        if high - low == LOOK_AZ:
+        if low > 0:
+            total = total + most[...]
+        if high < LOOK_AZ:
+            most[...] = total
+        else:
             sums[...] = total * SCALE
             coherence(epochs, part, sums, out)
-        else:
-            most[...] = total
-
-
-def late_kernel(epochs, *rest):
-    mains, middles, (box, most, given, out, img, hi, lo, sums) = rest[:4], rest[4:8], rest[8:]
-    del given
-    ((_, low, high),) = LATE
-    part = len(EARLY) - 1
-    total = add_lines(
-        epochs, mains, 0, middles, part * LOOK_AZ + low, high - low, box, img, hi, lo
-    )
-    sums[...] = (total + most[...]) * SCALE
-    coherence(epochs, part, sums, out)
-
-
-def looks(kernel, epochs, operands, out_shape, lines, aliases):
+
+
+def looks(chunk, epochs, operands, out_shape, aliases):
+    lines = sum(high - low for _, low, high in CHUNKS[chunk])
     work = lines * ITEMS * WIDE * (PAIRS * 8 + DATES * 4) + 4 * ROWS * WIDE * LCOL
     return pl.pallas_call(
-        kernel,
+        functools.partial(looks_kernel, chunk),
         out_shape=out_shape,
         grid_spec=pltpu.PrefetchScalarGridSpec(
             num_scalar_prefetch=1,
@@ -275,14 +276,17 @@
     look = jnp.where(lane < MAIN + 64, place // LOOK_RG, -1)
     box = (look[:, None] == jnp.arange(LCOL)[None, :] % 64).astype(jnp.bfloat16)
 
-    early = meet(*cut(images, EARLY))
-    middle = meet(*cut_middle(images))
-    late = meet(*cut(images, LATE, early[3]))
+    cut0 = cut(images, CHUNKS[0])
+    cut_between = cut_middle(images, cut0[1])
+    cut1 = cut(images, CHUNKS[1], cut_between[1])
+    chunk0, middle, chunk1 = meet(*cut0), meet(*cut_between), meet(*cut1)
+    chunk2 = meet(*cut(images, CHUNKS[2], chunk0[3]))
 
     shape = jax.ShapeDtypeStruct((TILES, 4, 4, LCOL), jnp.float32)
     partial = jax.ShapeDtypeStruct((ROWS, LCOL), jnp.float32)
-    gamma, most = looks(early_kernel, epochs, (*early, *middle, box, table), (shape, partial), 18, {})
-    gamma = looks(late_kernel, epochs, (*late, *middle, box, most, gamma), shape, 2, {11: 0})
+    gamma = looks(0, epochs, (*chunk0, *middle, box, table), shape, {})
+    gamma, most = looks(1, epochs, (*chunk1, *middle, box, gamma), (shape, partial), {10: 0})
+    gamma = looks(2, epochs, (*chunk2, *middle, box, most, gamma), shape, {11: 0})
     got = lax.all_to_all(
         gamma.reshape(128, 4, LCOL), ("tile", "date"), split_axis=0, concat_axis=0, tiled=True
     ).reshape(64, 8, LCOL)

time: 98.2 us -> 97.3 us (level)
  waiting for transfers between devices: 32.6 us -> 26.8 us
  starting transfers between devices: 10.3 us -> 14.8 us
  blocking collectives: 24 us -> 21.3 us
  local copies, waits for them, and re-layouts: 4.79 us -> 7.14 us
    ppermute x3 -> x4, waiting for transfers between devices: 20.3 us -> 0.01 us  [meet(): one = lax.ppermute(to3, 'date', ring(3))]
    ppermute x3 -> x4, waiting for transfers between devices: 0.01 us -> 12 us  [meet(): two = lax.ppermute(to2, 'date', ring(2))]
    ppermute x3 -> x4, starting transfers between devices: 3.64 us -> 6.35 us  [meet(): one = lax.ppermute(to3, 'date', ring(3))]
    all_to_all x1, blocking collectives: 24 us -> 21.3 us  [on_device(): lax.all_to_all(gamma.reshape(128, 4, LCOL), ('tile', 'date'), split_axis=...]
    ppermute x3 -> x4, waiting for transfers between devices: 12.3 us -> 14.7 us  [meet(): three = lax.ppermute(to1, 'date', ring(1))]
    unnamed x8 -> x16, local copies, waits for them, and re-layouts: 4.79 us -> 7.14 us
    ppermute x3 -> x4, starting transfers between devices: 2.8 us -> 4.06 us  [meet(): three = lax.ppermute(to1, 'date', ring(1))]
    pallas_call x2 -> x3, Pallas kernels: 13.5 us -> 14.6 us  [looks(): pl.pallas_call(functools.partial(looks_kernel, chunk), out_shape=out_shap...]
  transfers between devices with their start and end apart: 9 -> 12, of which waited for: 3 -> 3; matrix products, arithmetic and copies ran while one was open for 0% -> 0% of each run, Pallas kernels for 20% -> 22%
where the time goes in v9:
time: 97.3 us; the launch traced here: 97 us
  waiting for transfers between devices  26.8 us (28%)
  Pallas kernels  25.9 us (27%)
  blocking collectives  21.3 us (22%)
  starting transfers between devices  14.8 us (15%)
  local copies, waits for them, and re-layouts  7.14 us (7%)
    all_to_all x1, blocking collectives, on_device(): lax.all_to_all(gamma.reshape(128, 4, LCOL), ('tile', 'date'), split_axis=...  21.3 us
    ppermute x4, waiting for transfers between devices, meet(): three = lax.ppermute(to1, 'date', ring(1))  14.7 us
    pallas_call x3, Pallas kernels, looks(): pl.pallas_call(functools.partial(looks_kernel, chunk), out_shape=out_shap...  14.6 us
    ppermute x4, waiting for transfers between devices, meet(): two = lax.ppermute(to2, 'date', ring(2))  12 us
    unnamed x16, local copies, waits for them, and re-layouts  7.14 us
    pallas_call x1, Pallas kernels, cut_middle(): pl.pallas_call(cut_middle_kernel, out_shape=[jax.ShapeDtypeStruct((ITEMS,...  7.13 us
    ppermute x4, starting transfers between devices, meet(): one = lax.ppermute(to3, 'date', ring(3))  6.35 us
    ppermute x4, starting transfers between devices, meet(): two = lax.ppermute(to2, 'date', ring(2))  4.41 us
  transfers between devices with their start and end apart: 12, of which 3 were waited for; matrix products, arithmetic and copies ran while one was open for 0% of the time, Pallas kernels for 22%

profile of v9, /device:TPU:1, one launch (start us, length us, event | category | flops | bytes accessed | tf_op | source)
XLA Modules:
  0.0 97.0 jit_solution(10370341970297717108)
XLA Ops:
  0.0 2.4 %copy-done = bf16[2,1,32,2,10,1920]{5,3,4,2,1,0:T(2,128)(2,1)S(1)} copy-done((bf16[2,1,32,2,10,1920]{5,3,4,2,1,0:T(2,128)(2,1)S(1)}, bf16[2,1,32,2,10,1920]{5,3,4,2,1,0:T(2,128)(2,1)}, u32[]{:S(2)}) %copy-start) | copy-done | bytes 4915224
  2.4 1.5 %shard_map.46 = (bf16[8,2,10,2,896]{4,3,2,1,0:T(2,128)(2,1)}, bf16[8,2,10,2,896]{4,3,2,1,0:T(2,128)(2,1)S(1)}, bf16[8,2,10,2,896]{4,3,2,1,0:T(2,128)(2,1)}, bf16[8,2,10,2,896]{4,3,2,1,0:T(2,128)(2,1)S(1)}) custom-call(bf16[2,32,10,2,1920]{4,3,2,1,0:T(2,128)(2,1)S(1)} %bitcast.7), custom_call_target="tpu_custom_call" | custom-call | tf_op jit(solution)/shard_map/pallas_call | solution.py:65
  3.9 2.1 %collective-permute-start = (bf16[8,2,10,2,896]{4,3,2,1,0:T(2,128)(2,1)}, bf16[8,2,10,2,896]{4,3,2,1,0:T(2,128)(2,1)S(1)}, u32[]{:S(2)}, u32[]{:S(2)}) collective-permute-start(bf16[8,2,10,2,896]{4,3,2,1,0:T(2,128)(2,1)} %get-tuple-element.23), channel_id=1, source_target_pairs={{0,1},{1,2},{2,3},{3,0},{4,5},{5,6},{6,7},{7,4},{8,9},{9,10},{10,1... | collective-permute-start | bytes 1720328 | tf_op jit(solution)/shard_map/ppermute | solution.py:119
  6.0 2.5 %collective-permute-start.11 = (bf16[8,2,10,2,896]{4,3,2,1,0:T(2,128)(2,1)S(1)}, bf16[8,2,10,2,896]{4,3,2,1,0:T(2,128)(2,1)S(1)}, u32[]{:S(2)}, u32[]{:S(2)}) collective-permute-start(bf16[8,2,10,2,896]{4,3,2,1,0:T(2,128)(2,1)S(1)} %get-tuple-element.28.rest_0_), channel_id=1, source_target_pairs={{0,2},{1,3},{2,0},{3,1},{4,6},{5,7},{6,4},{7,5},{8,10},{9,11},{10,... | collective-permute-start | bytes 1720328 | tf_op jit(solution)/shard_map/ppermute | solution.py:121
  8.4 1.2 %collective-permute-start.10 = (bf16[8,2,10,2,896]{4,3,2,1,0:T(2,128)(2,1)}, bf16[8,2,10,2,896]{4,3,2,1,0:T(2,128)(2,1)S(1)}, u32[]{:S(2)}, u32[]{:S(2)}) collective-permute-start(bf16[8,2,10,2,896]{4,3,2,1,0:T(2,128)(2,1)} %get-tuple-element.38), channel_id=1, source_target_pairs={{0,3},{1,0},{2,1},{3,2},{4,7},{5,4},{6,5},{7,6},{8,11},{9,8},{10,9... | collective-permute-start | bytes 1720328 | tf_op jit(solution)/shard_map/ppermute | solution.py:120
  9.6 7.1 %shard_map.48 = (bf16[8,20,2,128]{3,2,1,0:T(2,128)(2,1)S(1)}, bf16[8,20,2,128]{3,2,1,0:T(2,128)(2,1)S(1)}, bf16[8,20,2,128]{3,2,1,0:T(2,128)(2,1)S(1)}, bf16[8,20,2,128]{3,2,1,0:T(2,128)(2,1)S(1)}) custom-call(bf16[2,32,10,2,1920]{4,3,2,1,0:T(2,128)(2,1)S(1)} %bitcast.8, bf16[8,2,10,2,896]{4,3,2,1,0:T(2,128)(2,1)S(1)} %get-tuple-element.28.rest_0_), custom_call_target="tpu_custom_call" | custom-call | tf_op jit(solution)/shard_map/pallas_call | solution.py:102
  16.9 2.6 %collective-permute-start.4 = (bf16[8,20,2,128]{3,2,1,0:T(2,128)(2,1)S(1)}, bf16[8,20,2,128]{3,2,1,0:T(2,128)(2,1)S(1)}, u32[]{:S(2)}, u32[]{:S(2)}) collective-permute-start(bf16[8,20,2,128]{3,2,1,0:T(2,128)(2,1)S(1)} %get-tuple-element.30), channel_id=1, source_target_pairs={{0,3},{1,0},{2,1},{3,2},{4,7},{5,4},{6,5},{7,6},{8,11},{9,8},{10,9... | collective-permute-start | bytes 245768 | tf_op jit(solution)/shard_map/ppermute | solution.py:120
  19.5 1.2 %shard_map.49 = (bf16[8,2,8,2,896]{4,3,2,1,0:T(2,128)(2,1)S(1)}, bf16[8,2,8,2,896]{4,3,2,1,0:T(2,128)(2,1)S(1)}, bf16[8,2,8,2,896]{4,3,2,1,0:T(2,128)(2,1)}, bf16[8,2,8,2,896]{4,3,2,1,0:T(2,128)(2,1)S(1)}) custom-call(bf16[2,32,10,2,1920]{4,3,2,1,0:T(2,128)(2,1)S(1)} %bitcast.9, bf16[8,20,2,128]{3,2,1,0:T(2,128)(2,1)S(1)} %get-tuple-element.31.rest_0_), custom_call_target="tpu_custom_call" | custom-call | tf_op jit(solution)/shard_map/pallas_call | solution.py:65
  21.5 0.8 copy-done.5
  22.2 0.8 copy-done.6
  23.0 12.0 %collective-permute-done.5.rest_6_ = bf16[8,20,2,128]{3,2,1,0:T(2,128)(2,1)S(1)} collective-permute-done((bf16[8,20,2,128]{3,2,1,0:T(2,128)(2,1)S(1)}, bf16[8,20,2,128]{3,2,1,0:T(2,128)(2,1)S(1)}, u32[]{:S(2)}, u32[]{:S(2)}) %collective-permute-start.5) | collective-permute-done | bytes 81952 | tf_op jit(solution)/shard_map/ppermute | solution.py:121
  35.1 1.1 %collective-permute-start.7 = (bf16[8,2,8,2,896]{4,3,2,1,0:T(2,128)(2,1)}, bf16[8,2,8,2,896]{4,3,2,1,0:T(2,128)(2,1)}, u32[]{:S(2)}, u32[]{:S(2)}) collective-permute-start(bf16[8,2,8,2,896]{4,3,2,1,0:T(2,128)(2,1)} %get-tuple-element.34), channel_id=1, source_target_pairs={{0,3},{1,0},{2,1},{3,2},{4,7},{5,4},{6,5},{7,6},{8,11},{9,8},{10,9... | collective-permute-start | bytes 1376264 | tf_op jit(solution)/shard_map/ppermute | solution.py:120
  37.3 4.0 %collective-permute-done.6.rest_7_ = bf16[8,20,2,128]{3,2,1,0:T(2,128)(2,1)S(1)} collective-permute-done((bf16[8,20,2,128]{3,2,1,0:T(2,128)(2,1)S(1)}, bf16[8,20,2,128]{3,2,1,0:T(2,128)(2,1)S(1)}, u32[]{:S(2)}, u32[]{:S(2)}) %collective-permute-start.6) | collective-permute-done | bytes 81952 | tf_op jit(solution)/shard_map/ppermute | solution.py:119
  41.4 0.8 collective-permute-start.8
  42.2 1.2 %collective-permute-start.9 = (bf16[8,2,8,2,896]{4,3,2,1,0:T(2,128)(2,1)}, bf16[8,2,8,2,896]{4,3,2,1,0:T(2,128)(2,1)S(1)}, u32[]{:S(2)}, u32[]{:S(2)}) collective-permute-start(bf16[8,2,8,2,896]{4,3,2,1,0:T(2,128)(2,1)} %copy-done.5), channel_id=1, source_target_pairs={{0,1},{1,2},{2,3},{3,0},{4,5},{5,6},{6,7},{7,4},{8,9},{9,10},{10,1... | collective-permute-start | bytes 1376264 | tf_op jit(solution)/shard_map/ppermute | solution.py:119
  43.6 2.4 %copy-done.1 = bf16[2,1,32,2,10,1920]{5,3,4,2,1,0:T(2,128)(2,1)S(1)} copy-done((bf16[2,1,32,2,10,1920]{5,3,4,2,1,0:T(2,128)(2,1)S(1)}, bf16[2,1,32,2,10,1920]{5,3,4,2,1,0:T(2,128)(2,1)}, u32[]{:S(2)}) %copy-start.1) | copy-done | bytes 4915224
  46.2 1.5 %collective-permute-start.1 = (bf16[8,2,2,2,896]{4,3,2,1,0:T(2,128)(2,1)S(1)}, bf16[8,2,2,2,896]{4,3,2,1,0:T(2,128)(2,1)S(1)}, u32[]{:S(2)}, u32[]{:S(2)}) collective-permute-start(bf16[8,2,2,2,896]{4,3,2,1,0:T(2,128)(2,1)S(1)} %get-tuple-element.25), channel_id=1, source_target_pairs={{0,3},{1,0},{2,1},{3,2},{4,7},{5,4},{6,5},{7,6},{8,11},{9,8},{10,9... | collective-permute-start | bytes 344072 | tf_op jit(solution)/shard_map/ppermute | solution.py:120
  47.7 0.9 collective-permute-start.2
  49.0 6.4 %shard_map.50.rest_9_ = f32[32,4,4,128]{3,2,1,0:T(4,128)S(1)} custom-call(s32[2,16]{1,0:T(2,128)S(1)} %bitcast.13, bf16[8,2,10,2,896]{4,3,2,1,0:T(2,128)(2,1)S(1)} %get-tuple-element.37.rest_0_, bf16[8,2,10,2,896]{4,3,2,1,0:T(2,128)(2,1)S(1)} %collective-permute-done.10.rest_1_, bf16[8,2,10,2,896]{4,3,2,1,0:T(2,128)(2,1)S(1)} %collective-permute-done.11.rest_2_, ...), custom_call_target="tpu_custom_call" | custom-call | flops 180879360 | bytes 2621440 | tf_op jit(solution)/shard_map/pallas_call | solution.py:225
  55.4 10.7 %collective-permute-done.9.rest_3_ = bf16[8,2,8,2,896]{4,3,2,1,0:T(2,128)(2,1)S(1)} collective-permute-done((bf16[8,2,8,2,896]{4,3,2,1,0:T(2,128)(2,1)}, bf16[8,2,8,2,896]{4,3,2,1,0:T(2,128)(2,1)S(1)}, u32[]{:S(2)}, u32[]{:S(2)}) %collective-permute-start.9) | collective-permute-done | bytes 458784 | tf_op jit(solution)/shard_map/ppermute | solution.py:119
  66.1 6.2 %shard_map.51 = (f32[32,4,4,128]{3,2,1,0:T(4,128)S(1)}, f32[320,128]{1,0:T(8,128)S(1)}) custom-call(s32[2,16]{1,0:T(2,128)S(1)} %bitcast.14, bf16[8,2,8,2,896]{4,3,2,1,0:T(2,128)(2,1)S(1)} %copy-done.3, bf16[8,2,8,2,896]{4,3,2,1,0:T(2,128)(2,1)} %collective-permute-done.7.rest_1_, ...), custom_call_target="tpu_custom_call", output_to_operand_aliasing={{0}: (10, {})} | custom-call | flops 178257920 | bytes 2097152 | tf_op jit(solution)/shard_map/pallas_call | solution.py:225
  72.3 2.0 %shard_map.52 = f32[32,4,4,128]{3,2,1,0:T(4,128)S(1)} custom-call(s32[2,16]{1,0:T(2,128)S(1)} %bitcast.15, bf16[8,2,2,2,896]{4,3,2,1,0:T(2,128)(2,1)S(1)} %get-tuple-element.24.rest_0_, bf16[8,2,2,2,896]{4,3,2,1,0:T(2,128)(2,1)S(1)} %collective-permute-done.1.rest_1_, ...), custom_call_target="tpu_custom_call", output_to_operand_aliasing={{}: (11, {})} | custom-call | flops 170393600 | bytes 524288 | tf_op jit(solution)/shard_map/pallas_call | solution.py:225
  74.3 21.3 %all_to_all.5 = f32[128,4,128]{2,1,0:T(4,128)S(1)} all-to-all(f32[128,4,128]{2,1,0:T(4,128)S(1)} %bitcast.11), channel_id=1, replica_groups=mesh['tile'=32,'date'=4] {'tile','date'}, dimensions={0} | all-to-all | bytes 524288 | tf_op jit(solution)/shard_map/all_to_all | solution.py:290
  95.6 1.4 %shard_map.53 = f32[4,2,64,128]{3,2,1,0:T(8,128)} custom-call(s32[33]{0:T(128)S(1)} %pad_add_fusion.rest_9_.table, f32[64,8,128]{2,1,0:T(8,128)S(1)} %bitcast.12), custom_call_target="tpu_custom_call" | custom-call | tf_op jit(solution)/shard_map/pallas_call | solution.py:293
  (29 shorter events, 2.2 us)
Async XLA Ops:
  0.0 2.4 %copy-start = (bf16[2,1,32,2,10,1920]{5,3,4,2,1,0:T(2,128)(2,1)S(1)}, bf16[2,1,32,2,10,1920]{5,3,4,2,1,0:T(2,128)(2,1)}, u32[]{:S(2)}) copy-start(bf16[2,1,32,2,10,1920]{5,3,4,2,1,0:T(2,128)(2,1)} %param.4) | copy-start | bytes 14745604
  3.9 38.3 %collective-permute-start = (bf16[8,2,10,2,896]{4,3,2,1,0:T(2,128)(2,1)}, bf16[8,2,10,2,896]{4,3,2,1,0:T(2,128)(2,1)S(1)}, u32[]{:S(2)}, u32[]{:S(2)}) collective-permute-start(bf16[8,2,10,2,896]{4,3,2,1,0:T(2,128)(2,1)} %get-tuple-element.23), channel_id=1, source_target_pairs={{0,1},{1,2},{2,3},{3,0},{4,5},{5,6},{6,7},{7,4},{8,9},{9,10},{10,1... | collective-permute-start | bytes 1720328 | tf_op jit(solution)/shard_map/ppermute | solution.py:119
  6.0 41.8 %collective-permute-start.11 = (bf16[8,2,10,2,896]{4,3,2,1,0:T(2,128)(2,1)S(1)}, bf16[8,2,10,2,896]{4,3,2,1,0:T(2,128)(2,1)S(1)}, u32[]{:S(2)}, u32[]{:S(2)}) collective-permute-start(bf16[8,2,10,2,896]{4,3,2,1,0:T(2,128)(2,1)S(1)} %get-tuple-element.28.rest_0_), channel_id=1, source_target_pairs={{0,2},{1,3},{2,0},{3,1},{4,6},{5,7},{6,4},{7,5},{8,10},{9,11},{10,... | collective-permute-start | bytes 1720328 | tf_op jit(solution)/shard_map/ppermute | solution.py:121
  8.4 40.2 %collective-permute-start.10 = (bf16[8,2,10,2,896]{4,3,2,1,0:T(2,128)(2,1)}, bf16[8,2,10,2,896]{4,3,2,1,0:T(2,128)(2,1)S(1)}, u32[]{:S(2)}, u32[]{:S(2)}) collective-permute-start(bf16[8,2,10,2,896]{4,3,2,1,0:T(2,128)(2,1)} %get-tuple-element.38), channel_id=1, source_target_pairs={{0,3},{1,0},{2,1},{3,2},{4,7},{5,4},{6,5},{7,6},{8,11},{9,8},{10,9... | collective-permute-start | bytes 1720328 | tf_op jit(solution)/shard_map/ppermute | solution.py:120
  16.7 18.3 %collective-permute-start.5 = (bf16[8,20,2,128]{3,2,1,0:T(2,128)(2,1)S(1)}, bf16[8,20,2,128]{3,2,1,0:T(2,128)(2,1)S(1)}, u32[]{:S(2)}, u32[]{:S(2)}) collective-permute-start(bf16[8,20,2,128]{3,2,1,0:T(2,128)(2,1)S(1)} %get-tuple-element.31.rest_0_), channel_id=1, source_target_pairs={{0,2},{1,3},{2,0},{3,1},{4,6},{5,7},{6,4},{7,5},{8,10},{9,11},{10,... | collective-permute-start | bytes 245768 | tf_op jit(solution)/shard_map/ppermute | solution.py:121
  16.9 32.0 %copy-start.7 = (s32[1,32]{1,0:T(1,128)S(1)}, s32[1,32]{1,0:T(1,128)}, u32[]{:S(2)}) copy-start(s32[1,32]{1,0:T(1,128)} %param.5) | copy-start | bytes 388
  16.9 32.0 %copy-start.4 = (s32[16,2]{0,1:T(2,128)S(1)}, s32[16,2]{0,1:T(2,128)}, u32[]{:S(2)}) copy-start(s32[16,2]{0,1:T(2,128)} %param.7) | copy-start | bytes 388
  16.9 19.9 %collective-permute-start.4 = (bf16[8,20,2,128]{3,2,1,0:T(2,128)(2,1)S(1)}, bf16[8,20,2,128]{3,2,1,0:T(2,128)(2,1)S(1)}, u32[]{:S(2)}, u32[]{:S(2)}) collective-permute-start(bf16[8,20,2,128]{3,2,1,0:T(2,128)(2,1)S(1)} %get-tuple-element.30), channel_id=1, source_target_pairs={{0,3},{1,0},{2,1},{3,2},{4,7},{5,4},{6,5},{7,6},{8,11},{9,8},{10,9... | collective-permute-start | bytes 245768 | tf_op jit(solution)/shard_map/ppermute | solution.py:120
  20.7 0.8 copy-start.2
  21.5 0.8 copy-start.5
  22.2 0.8 copy-start.6
  35.1 11.1 %collective-permute-start.7 = (bf16[8,2,8,2,896]{4,3,2,1,0:T(2,128)(2,1)}, bf16[8,2,8,2,896]{4,3,2,1,0:T(2,128)(2,1)}, u32[]{:S(2)}, u32[]{:S(2)}) collective-permute-start(bf16[8,2,8,2,896]{4,3,2,1,0:T(2,128)(2,1)} %get-tuple-element.34), channel_id=1, source_target_pairs={{0,3},{1,0},{2,1},{3,2},{4,7},{5,4},{6,5},{7,6},{8,11},{9,8},{10,9... | collective-permute-start | bytes 1376264 | tf_op jit(solution)/shard_map/ppermute | solution.py:120
  36.8 4.6 %collective-permute-start.6 = (bf16[8,20,2,128]{3,2,1,0:T(2,128)(2,1)S(1)}, bf16[8,20,2,128]{3,2,1,0:T(2,128)(2,1)S(1)}, u32[]{:S(2)}, u32[]{:S(2)}) collective-permute-start(bf16[8,20,2,128]{3,2,1,0:T(2,128)(2,1)S(1)} %get-tuple-element.32), channel_id=1, source_target_pairs={{0,1},{1,2},{2,3},{3,0},{4,5},{5,6},{6,7},{7,4},{8,9},{9,10},{10,1... | collective-permute-start | bytes 245768 | tf_op jit(solution)/shard_map/ppermute | solution.py:119
  41.4 14.0 %collective-permute-start.8 = (bf16[8,2,8,2,896]{4,3,2,1,0:T(2,128)(2,1)}, bf16[8,2,8,2,896]{4,3,2,1,0:T(2,128)(2,1)S(1)}, u32[]{:S(2)}, u32[]{:S(2)}) collective-permute-start(bf16[8,2,8,2,896]{4,3,2,1,0:T(2,128)(2,1)} %copy-done.6), channel_id=1, source_target_pairs={{0,2},{1,3},{2,0},{3,1},{4,6},{5,7},{6,4},{7,5},{8,10},{9,11},{10,... | collective-permute-start | bytes 1376264 | tf_op jit(solution)/shard_map/ppermute | solution.py:121
  42.2 23.9 %collective-permute-start.9 = (bf16[8,2,8,2,896]{4,3,2,1,0:T(2,128)(2,1)}, bf16[8,2,8,2,896]{4,3,2,1,0:T(2,128)(2,1)S(1)}, u32[]{:S(2)}, u32[]{:S(2)}) collective-permute-start(bf16[8,2,8,2,896]{4,3,2,1,0:T(2,128)(2,1)} %copy-done.5), channel_id=1, source_target_pairs={{0,1},{1,2},{2,3},{3,0},{4,5},{5,6},{6,7},{7,4},{8,9},{9,10},{10,1... | collective-permute-start | bytes 1376264 | tf_op jit(solution)/shard_map/ppermute | solution.py:119
  43.6 2.4 %copy-start.1 = (bf16[2,1,32,2,10,1920]{5,3,4,2,1,0:T(2,128)(2,1)S(1)}, bf16[2,1,32,2,10,1920]{5,3,4,2,1,0:T(2,128)(2,1)}, u32[]{:S(2)}) copy-start(bf16[2,1,32,2,10,1920]{5,3,4,2,1,0:T(2,128)(2,1)} %param.4) | copy-start | bytes 14745604
  46.0 20.0 %copy-start.3 = (bf16[8,2,8,2,896]{4,3,2,1,0:T(2,128)(2,1)S(1)}, bf16[8,2,8,2,896]{4,3,2,1,0:T(2,128)(2,1)}, u32[]{:S(2)}) copy-start(bf16[8,2,8,2,896]{4,3,2,1,0:T(2,128)(2,1)} %copy-done.2) | copy-start | bytes 1376260
  46.2 26.1 %collective-permute-start.1 = (bf16[8,2,2,2,896]{4,3,2,1,0:T(2,128)(2,1)S(1)}, bf16[8,2,2,2,896]{4,3,2,1,0:T(2,128)(2,1)S(1)}, u32[]{:S(2)}, u32[]{:S(2)}) collective-permute-start(bf16[8,2,2,2,896]{4,3,2,1,0:T(2,128)(2,1)S(1)} %get-tuple-element.25), channel_id=1, source_target_pairs={{0,3},{1,0},{2,1},{3,2},{4,7},{5,4},{6,5},{7,6},{8,11},{9,8},{10,9... | collective-permute-start | bytes 344072 | tf_op jit(solution)/shard_map/ppermute | solution.py:120
  47.7 24.6 %collective-permute-start.2 = (bf16[8,2,2,2,896]{4,3,2,1,0:T(2,128)(2,1)S(1)}, bf16[8,2,2,2,896]{4,3,2,1,0:T(2,128)(2,1)S(1)}, u32[]{:S(2)}, u32[]{:S(2)}) collective-permute-start(bf16[8,2,2,2,896]{4,3,2,1,0:T(2,128)(2,1)S(1)} %get-tuple-element.26), channel_id=1, source_target_pairs={{0,2},{1,3},{2,0},{3,1},{4,6},{5,7},{6,4},{7,5},{8,10},{9,11},{10,... | collective-permute-start | bytes 344072 | tf_op jit(solution)/shard_map/ppermute | solution.py:121
  48.7 23.6 %collective-permute-start.3 = (bf16[8,2,2,2,896]{4,3,2,1,0:T(2,128)(2,1)S(1)}, bf16[8,2,2,2,896]{4,3,2,1,0:T(2,128)(2,1)S(1)}, u32[]{:S(2)}, u32[]{:S(2)}) collective-permute-start(bf16[8,2,2,2,896]{4,3,2,1,0:T(2,128)(2,1)S(1)} %get-tuple-element.27), channel_id=1, source_target_pairs={{0,1},{1,2},{2,3},{3,0},{4,5},{5,6},{6,7},{7,4},{8,9},{9,10},{10,1... | collective-permute-start | bytes 344072 | tf_op jit(solution)/shard_map/ppermute | solution.py:119

commit v10 on v7

--- a/solution.py
+++ b/solution.py
@@ -17,7 +17,7 @@
 RG = 1920
 LCOL = 128
 ROWS = 320
-SPLIT = 3
+CHUNKS = ((0, 0, 5), (8, 0, 4), (8, 4, 5))
 HALF = 16
 
 VMEM = pl.BlockSpec(memory_space=pltpu.VMEM)
@@ -26,41 +26,36 @@
 ANYWHERE = pl.BlockSpec(memory_space=pl.ANY)
 
 
-def cut_kernel(parts, images, *rest):
+def cut_kernel(chunk, images, *rest):
     to1, to2, to3, own, sem = rest[-5:]
+    first, low, high = chunk
     group = lax.axis_index("date")
     copies = []
     for step, out in ((1, to1), (3, to3), (2, to2), (0, own)):
         taker = lax.rem(group + step, 4)
-        start, top = lax.rem(taker, 2) * HALF, lax.div(taker, 2) * LOOK_AZ
-        filled = 0
-        for first, low, high in parts:
-            tiles, lines = pl.ds(start + first, ITEMS), pl.ds(top + low, high - low)
-            slots = slice(filled, filled + high - low)
-            filled += high - low
-            for date in range(2):
-                copies.append(
-                    pltpu.make_async_copy(
-                        images.at[date, tiles, lines],
-                        out.at[:, date, slots],
-                        sem.at[len(copies)],
-                    )
+        tiles = pl.ds(lax.rem(taker, 2) * HALF + first, ITEMS)
+        lines = pl.ds(lax.div(taker, 2) * LOOK_AZ + low, high - low)
+        for date in range(2):
+            copies.append(
+                pltpu.make_async_copy(
+                    images.at[date, tiles, lines], out.at[:, date], sem.at[len(copies)]
                 )
-                copies[-1].start()
+            )
+            copies[-1].start()
     for copy in copies:
         copy.wait()
 
 
-def cut(images, parts, after=None):
-    slots = sum(high - low for _, low, high in parts)
-    block = jax.ShapeDtypeStruct((ITEMS, 2, slots, 2, RG), jnp.bfloat16)
+def cut(images, chunk, after=None):
+    _, low, high = chunk
+    block = jax.ShapeDtypeStruct((ITEMS, 2, high - low, 2, RG), jnp.bfloat16)
     operands = (images,) + (() if after is None else (after,))
     return pl.pallas_call(
-        functools.partial(cut_kernel, parts),
+        functools.partial(cut_kernel, chunk),
         out_shape=[block] * 4,
         in_specs=[HBM, ANYWHERE][: len(operands)],
         out_specs=[VMEM] * 4,
-        scratch_shapes=[pltpu.SemaphoreType.DMA((8 * len(parts),))],
+        scratch_shapes=[pltpu.SemaphoreType.DMA((8,))],
         compiler_params=pltpu.CompilerParams(vmem_limit_bytes=8 << 20),
     )(*operands)
 
@@ -75,14 +70,14 @@
     return own, one, two, three
 
 
-def add_lines(epochs, blocks, low, high, box, img, hi, lo):
+def add_lines(epochs, blocks, box, img, hi, lo):
     group = lax.axis_index("date")
-    lines = high - low
+    lines = blocks[0].shape[2]
     for step, block in enumerate(blocks):
         base = lax.rem(group + step, 4) * 2
         for date in range(2):
             for line in range(lines):
-                pixels = jnp.swapaxes(block[:, date, low + line], 0, 1).reshape(16, RG)
+                pixels = jnp.swapaxes(block[:, date, line], 0, 1).reshape(16, RG)
                 img[base + date, line] = pixels.astype(jnp.float32)
 
     def split(values, row):
@@ -136,22 +131,25 @@
         out[pl.ds(start, ITEMS), owner] = jnp.swapaxes(jnp.stack(rows, axis=0), 0, 1)
 
 
-def early_kernel(epochs, own, one, two, three, box, out, later, img, hi, lo, sums):
-    blocks = (own, one, two, three)
-    sums[...] = add_lines(epochs, blocks, 0, LOOK_AZ, box, img, hi, lo) * SCALE
+def whole_kernel(epochs, own, one, two, three, box, table, out, img, hi, lo, sums):
+    del table
+    sums[...] = add_lines(epochs, (own, one, two, three), box, img, hi, lo) * SCALE
     coherence(epochs, 0, sums, out)
-    later[...] = add_lines(epochs, blocks, LOOK_AZ, LOOK_AZ + SPLIT, box, img, hi, lo)
-
-
-def late_kernel(epochs, own, one, two, three, box, early, table, given, out, img, hi, lo, sums):
-    del table
+
+
+def most_kernel(epochs, own, one, two, three, box, after, later, img, hi, lo, sums):
+    del after, sums
+    later[...] = add_lines(epochs, (own, one, two, three), box, img, hi, lo)
+
+
+def last_kernel(epochs, own, one, two, three, box, most, given, out, img, hi, lo, sums):
     del given
-    total = add_lines(epochs, (own, one, two, three), 0, LOOK_AZ - SPLIT, box, img, hi, lo)
-    sums[...] = (total + early[...]) * SCALE
+    total = add_lines(epochs, (own, one, two, three), box, img, hi, lo)
+    sums[...] = (total + most[...]) * SCALE
     coherence(epochs, 1, sums, out)
 
 
-def looks(kernel, epochs, operands, out_shape, lines, aliases):
+def looks(kernel, epochs, operands, out_shape, lines, aliases={}):
     work = lines * ITEMS * RG * (PAIRS * 8 + DATES * 4) + 4 * ROWS * RG * LCOL
     return pl.pallas_call(
         kernel,
@@ -162,7 +160,7 @@
             in_specs=[VMEM if x.ndim > 1 else SMEM for x in operands],
             out_specs=jax.tree.map(lambda _: VMEM, out_shape),
             scratch_shapes=[
-                pltpu.VMEM((DATES, min(lines, LOOK_AZ), 16, RG), jnp.float32),
+                pltpu.VMEM((DATES, lines, 16, RG), jnp.float32),
                 pltpu.VMEM((ROWS, RG), jnp.bfloat16),
                 pltpu.VMEM((ROWS, RG), jnp.bfloat16),
                 pltpu.VMEM((ROWS, LCOL), jnp.float32),
@@ -199,17 +197,15 @@
         jnp.arange(RG)[:, None] // LOOK_RG == jnp.arange(LCOL)[None, :]
     ).astype(jnp.bfloat16)
 
-    early = meet(*cut(images, ((0, 0, LOOK_AZ), (ITEMS, 0, SPLIT))))
-    late = meet(*cut(images, ((ITEMS, SPLIT, LOOK_AZ),), early[3]))
+    first = meet(*cut(images, CHUNKS[0]))
+    second = meet(*cut(images, CHUNKS[1], first[3]))
+    third = meet(*cut(images, CHUNKS[2], first[2]))
 
     shape = jax.ShapeDtypeStruct((32, 4, 8, LCOL), jnp.float32)
     partial = jax.ShapeDtypeStruct((ROWS, LCOL), jnp.float32)
-    gamma, sums = looks(
-        early_kernel, epochs, (*early, box), (shape, partial), LOOK_AZ + SPLIT, {}
-    )
-    gamma = looks(
-        late_kernel, epochs, (*late, box, sums, table, gamma), shape, LOOK_AZ - SPLIT, {8: 0}
-    )
+    gamma = looks(whole_kernel, epochs, (*first, box, table), shape, 5)
+    most = looks(most_kernel, epochs, (*second, box, gamma), partial, 4)
+    gamma = looks(last_kernel, epochs, (*third, box, most, gamma), shape, 1, {7: 0})
     got = lax.all_to_all(
         gamma.reshape(128, 8, LCOL), ("tile", "date"), split_axis=0, concat_axis=0, tiled=True
     ).reshape(32, 4, 8, LCOL)

time: 89.5 us -> 91.4 us (1.021)
  waiting for transfers between devices: 41.5 us -> 36.4 us
  starting transfers between devices: 7.91 us -> 11.3 us
  blocking collectives: 23.2 us -> 26.5 us
    ppermute x2 -> x3, waiting for transfers between devices: 0.01 us -> 8.82 us  [meet(): one = lax.ppermute(to3, 'date', ring(3))]
    ppermute x2 -> x3, waiting for transfers between devices: 18.3 us -> 10.2 us  [meet(): two = lax.ppermute(to2, 'date', ring(2))]
    ppermute x2 -> x3, waiting for transfers between devices: 23.2 us -> 17.4 us  [meet(): three = lax.ppermute(to1, 'date', ring(1))]
    all_to_all x1, blocking collectives: 23.2 us -> 26.5 us  [on_device(): lax.all_to_all(gamma.reshape(128, 8, LCOL), ('tile', 'date'), split_axis=...]
    ppermute x2 -> x3, starting transfers between devices: 2.17 us -> 4.85 us  [meet(): two = lax.ppermute(to2, 'date', ring(2))]
    ppermute x2 -> x3, starting transfers between devices: 2.74 us -> 3.53 us  [meet(): three = lax.ppermute(to1, 'date', ring(1))]
    pallas_call x2 -> x3, Pallas kernels: 11 us -> 11.2 us  [looks(): pl.pallas_call(kernel, out_shape=out_shape, grid_spec=pltpu.PrefetchScala...]
    ppermute x2 -> x3, starting transfers between devices: 3 us -> 2.88 us  [meet(): one = lax.ppermute(to3, 'date', ring(3))]
  transfers between devices with their start and end apart: 6 -> 9, of which waited for: 3 -> 5; matrix products, arithmetic and copies ran while one was open for 0% -> 0% of each run, Pallas kernels for 9% -> 10%
where the time goes in v10:
time: 91.4 us; the launch traced here: 91.2 us
  waiting for transfers between devices  36.4 us (40%)
  blocking collectives  26.5 us (29%)
  Pallas kernels  13.5 us (15%)
  starting transfers between devices  11.3 us (12%)
  local copies, waits for them, and re-layouts  2.4 us (3%)
    all_to_all x1, blocking collectives, on_device(): lax.all_to_all(gamma.reshape(128, 8, LCOL), ('tile', 'date'), split_axis=...  26.5 us
    ppermute x3, waiting for transfers between devices, meet(): three = lax.ppermute(to1, 'date', ring(1))  17.4 us
    pallas_call x3, Pallas kernels, looks(): pl.pallas_call(kernel, out_shape=out_shape, grid_spec=pltpu.PrefetchScala...  11.2 us
    ppermute x3, waiting for transfers between devices, meet(): two = lax.ppermute(to2, 'date', ring(2))  10.2 us
    ppermute x3, waiting for transfers between devices, meet(): one = lax.ppermute(to3, 'date', ring(3))  8.82 us
    ppermute x3, starting transfers between devices, meet(): two = lax.ppermute(to2, 'date', ring(2))  4.85 us
    ppermute x3, starting transfers between devices, meet(): three = lax.ppermute(to1, 'date', ring(1))  3.53 us
    ppermute x3, starting transfers between devices, meet(): one = lax.ppermute(to3, 'date', ring(3))  2.88 us
  transfers between devices with their start and end apart: 9, of which 5 were waited for; matrix products, arithmetic and copies ran while one was open for 0% of the time, Pallas kernels for 10%

profile of v10, /device:TPU:1, one launch (start us, length us, event | category | flops | bytes accessed | tf_op | source)
XLA Modules:
  0.0 91.2 jit_solution(8907229683392324171)
XLA Ops:
  0.0 2.4 %copy-done = bf16[2,1,32,2,10,1920]{5,3,4,2,1,0:T(2,128)(2,1)S(1)} copy-done((bf16[2,1,32,2,10,1920]{5,3,4,2,1,0:T(2,128)(2,1)S(1)}, bf16[2,1,32,2,10,1920]{5,3,4,2,1,0:T(2,128)(2,1)}, u32[]{:S(2)}) %copy-start) | copy-done | bytes 4915224
  2.4 0.3 shard_map.46
  2.7 2.1 %collective-permute-start.4 = (bf16[8,2,5,2,1920]{4,3,2,1,0:T(2,128)(2,1)S(1)}, bf16[8,2,5,2,1920]{4,3,2,1,0:T(2,128)(2,1)S(1)}, u32[]{:S(2)}, u32[]{:S(2)}) collective-permute-start(bf16[8,2,5,2,1920]{4,3,2,1,0:T(2,128)(2,1)S(1)} %get-tuple-element.22), channel_id=1, source_target_pairs={{0,1},{1,2},{2,3},{3,0},{4,5},{5,6},{6,7},{7,4},{8,9},{9,10},{10,1... | collective-permute-start | bytes 1843208 | tf_op jit(solution)/shard_map/ppermute | solution.py:67
  4.8 2.5 %collective-permute-start = (bf16[8,2,5,2,1920]{4,3,2,1,0:T(2,128)(2,1)S(1)}, bf16[8,2,5,2,1920]{4,3,2,1,0:T(2,128)(2,1)S(1)}, u32[]{:S(2)}, u32[]{:S(2)}) collective-permute-start(bf16[8,2,5,2,1920]{4,3,2,1,0:T(2,128)(2,1)S(1)} %get-tuple-element.17), channel_id=1, source_target_pairs={{0,2},{1,3},{2,0},{3,1},{4,6},{5,7},{6,4},{7,5},{8,10},{9,11},{10,... | collective-permute-start | bytes 1843208 | tf_op jit(solution)/shard_map/ppermute | solution.py:69
  7.3 1.2 %collective-permute-start.8 = (bf16[8,2,5,2,1920]{4,3,2,1,0:T(2,128)(2,1)S(1)}, bf16[8,2,5,2,1920]{4,3,2,1,0:T(2,128)(2,1)S(1)}, u32[]{:S(2)}, u32[]{:S(2)}) collective-permute-start(bf16[8,2,5,2,1920]{4,3,2,1,0:T(2,128)(2,1)S(1)} %get-tuple-element.28), channel_id=1, source_target_pairs={{0,3},{1,0},{2,1},{3,2},{4,7},{5,4},{6,5},{7,6},{8,11},{9,8},{10,9... | collective-permute-start | bytes 1843208 | tf_op jit(solution)/shard_map/ppermute | solution.py:68
  8.4 10.8 %collective-permute-done.4.rest_0_.three = bf16[8,2,5,2,1920]{4,3,2,1,0:T(2,128)(2,1)S(1)} collective-permute-done((bf16[8,2,5,2,1920]{4,3,2,1,0:T(2,128)(2,1)S(1)}, bf16[8,2,5,2,1920]{4,3,2,1,0:T(2,128)(2,1)S(1)}, u32[]{:S(2)}, u32[]{:S(2)}) %collective-permute-start.4) | collective-permute-done | bytes 614432 | tf_op jit(solution)/shard_map/ppermute | solution.py:67
  19.2 0.4 shard_map.48
  19.6 1.7 %collective-permute-start.5 = (bf16[8,2,4,2,1920]{4,3,2,1,0:T(2,128)(2,1)S(1)}, bf16[8,2,4,2,1920]{4,3,2,1,0:T(2,128)(2,1)S(1)}, u32[]{:S(2)}, u32[]{:S(2)}) collective-permute-start(bf16[8,2,4,2,1920]{4,3,2,1,0:T(2,128)(2,1)S(1)} %get-tuple-element.24), channel_id=1, source_target_pairs={{0,3},{1,0},{2,1},{3,2},{4,7},{5,4},{6,5},{7,6},{8,11},{9,8},{10,9... | collective-permute-start | bytes 1474568 | tf_op jit(solution)/shard_map/ppermute | solution.py:68
  21.9 0.6 collective-permute-start.6
  22.5 0.6 collective-permute-start.7
  23.2 0.3 fusion.box
  23.5 10.2 %collective-permute-done.rest_0_.two = bf16[8,2,5,2,1920]{4,3,2,1,0:T(2,128)(2,1)S(1)} collective-permute-done((bf16[8,2,5,2,1920]{4,3,2,1,0:T(2,128)(2,1)S(1)}, bf16[8,2,5,2,1920]{4,3,2,1,0:T(2,128)(2,1)S(1)}, u32[]{:S(2)}, u32[]{:S(2)}) %collective-permute-start) | collective-permute-done | bytes 614432 | tf_op jit(solution)/shard_map/ppermute | solution.py:69
  33.7 0.2 shard_map.47
  33.9 0.1 collective-permute-start.1
  34.0 1.8 %collective-permute-start.2 = (bf16[8,2,1,2,1920]{4,3,2,1,0:T(2,128)(2,1)S(1)}, bf16[8,2,1,2,1920]{4,3,2,1,0:T(2,128)(2,1)S(1)}, u32[]{:S(2)}, u32[]{:S(2)}) collective-permute-start(bf16[8,2,1,2,1920]{4,3,2,1,0:T(2,128)(2,1)S(1)} %get-tuple-element.20), channel_id=1, source_target_pairs={{0,2},{1,3},{2,0},{3,1},{4,6},{5,7},{6,4},{7,5},{8,10},{9,11},{10,... | collective-permute-start | bytes 368648 | tf_op jit(solution)/shard_map/ppermute | solution.py:69
  35.8 8.8 %collective-permute-done.5.one = bf16[8,2,4,2,1920]{4,3,2,1,0:T(2,128)(2,1)S(1)} collective-permute-done((bf16[8,2,4,2,1920]{4,3,2,1,0:T(2,128)(2,1)S(1)}, bf16[8,2,4,2,1920]{4,3,2,1,0:T(2,128)(2,1)S(1)}, u32[]{:S(2)}, u32[]{:S(2)}) %collective-permute-start.5) | collective-permute-done | bytes 491552 | tf_op jit(solution)/shard_map/ppermute | solution.py:68
  44.6 0.8 collective-permute-start.3
  45.5 5.2 %shard_map.49.after.given = f32[32,4,8,128]{3,2,1,0:T(8,128)S(1)} custom-call(s32[2,16]{1,0:T(2,128)S(1)} %bitcast.12, bf16[8,2,5,2,1920]{4,3,2,1,0:T(2,128)(2,1)S(1)} %get-tuple-element.27.own, bf16[8,2,5,2,1920]{4,3,2,1,0:T(2,128)(2,1)S(1)} %collective-permute-done.8.one, bf16[8,2,5,2,1920]{4,3,2,1,0:T(2,128)(2,1)S(1)} %collective-permute-done.rest_0_.two, ...), custom_call_target="tpu_custom_call" | custom-call | flops 326860800 | bytes 2457600 | tf_op jit(solution)/shard_map/pallas_call | solution.py:154
  50.7 6.1 %collective-permute-done.7.three = bf16[8,2,4,2,1920]{4,3,2,1,0:T(2,128)(2,1)S(1)} collective-permute-done((bf16[8,2,4,2,1920]{4,3,2,1,0:T(2,128)(2,1)S(1)}, bf16[8,2,4,2,1920]{4,3,2,1,0:T(2,128)(2,1)S(1)}, u32[]{:S(2)}, u32[]{:S(2)}) %collective-permute-start.7) | collective-permute-done | bytes 491552 | tf_op jit(solution)/shard_map/ppermute | solution.py:67
  56.8 3.8 %shard_map.50.most = f32[320,128]{1,0:T(8,128)S(1)} custom-call(s32[2,16]{1,0:T(2,128)S(1)} %bitcast.13, bf16[8,2,4,2,1920]{4,3,2,1,0:T(2,128)(2,1)S(1)} %get-tuple-element.23.own, bf16[8,2,4,2,1920]{4,3,2,1,0:T(2,128)(2,1)S(1)} %collective-permute-done.5.one, bf16[8,2,4,2,1920]{4,3,2,1,0:T(2,128)(2,1)S(1)} %collective-permute-done.6.two, ...), custom_call_target="tpu_custom_call" | custom-call | flops 324403200 | bytes 1966080 | tf_op jit(solution)/shard_map/pallas_call | solution.py:154
  60.6 0.4 collective-permute-done.3.three
  61.1 2.3 %shard_map.51 = f32[32,4,8,128]{3,2,1,0:T(8,128)S(1)} custom-call(s32[2,16]{1,0:T(2,128)S(1)} %bitcast.14, bf16[8,2,1,2,1920]{4,3,2,1,0:T(2,128)(2,1)S(1)} %get-tuple-element.18.own, bf16[8,2,1,2,1920]{4,3,2,1,0:T(2,128)(2,1)S(1)} %collective-permute-done.1.one, ...), custom_call_target="tpu_custom_call", output_to_operand_aliasing={{}: (7, {})} | custom-call | flops 317030400 | bytes 491520 | tf_op jit(solution)/shard_map/pallas_call | solution.py:154
  63.4 26.5 %all_to_all.5 = f32[128,8,128]{2,1,0:T(8,128)S(1)} all-to-all(f32[128,8,128]{2,1,0:T(8,128)S(1)} %bitcast.10), channel_id=1, replica_groups=mesh['tile'=32,'date'=4] {'tile','date'}, dimensions={0} | all-to-all | bytes 1048576 | tf_op jit(solution)/shard_map/all_to_all | solution.py:209
  89.8 1.4 %shard_map.52 = f32[4,2,64,128]{3,2,1,0:T(8,128)} custom-call(s32[33]{0:T(128)S(1)} %pad_add_fusion.table, f32[32,4,8,128]{3,2,1,0:T(8,128)S(1)} %bitcast.11), custom_call_target="tpu_custom_call" | custom-call | tf_op jit(solution)/shard_map/pallas_call | solution.py:212
  (13 shorter events, 0.1 us)
Async XLA Ops:
  0.0 2.4 %copy-start = (bf16[2,1,32,2,10,1920]{5,3,4,2,1,0:T(2,128)(2,1)S(1)}, bf16[2,1,32,2,10,1920]{5,3,4,2,1,0:T(2,128)(2,1)}, u32[]{:S(2)}) copy-start(bf16[2,1,32,2,10,1920]{5,3,4,2,1,0:T(2,128)(2,1)} %param.4) | copy-start | bytes 14745604
  2.4 31.3 %copy-start.1 = (bf16[2,1,32,2,10,1920]{5,3,4,2,1,0:T(2,128)(2,1)S(1)}, bf16[2,1,32,2,10,1920]{5,3,4,2,1,0:T(2,128)(2,1)}, u32[]{:S(2)}) copy-start(bf16[2,1,32,2,10,1920]{5,3,4,2,1,0:T(2,128)(2,1)} %param.4) | copy-start | bytes 14745604
  2.7 16.5 %collective-permute-start.4 = (bf16[8,2,5,2,1920]{4,3,2,1,0:T(2,128)(2,1)S(1)}, bf16[8,2,5,2,1920]{4,3,2,1,0:T(2,128)(2,1)S(1)}, u32[]{:S(2)}, u32[]{:S(2)}) collective-permute-start(bf16[8,2,5,2,1920]{4,3,2,1,0:T(2,128)(2,1)S(1)} %get-tuple-element.22), channel_id=1, source_target_pairs={{0,1},{1,2},{2,3},{3,0},{4,5},{5,6},{6,7},{7,4},{8,9},{9,10},{10,1... | collective-permute-start | bytes 1843208 | tf_op jit(solution)/shard_map/ppermute | solution.py:67
  4.8 28.9 %collective-permute-start = (bf16[8,2,5,2,1920]{4,3,2,1,0:T(2,128)(2,1)S(1)}, bf16[8,2,5,2,1920]{4,3,2,1,0:T(2,128)(2,1)S(1)}, u32[]{:S(2)}, u32[]{:S(2)}) collective-permute-start(bf16[8,2,5,2,1920]{4,3,2,1,0:T(2,128)(2,1)S(1)} %get-tuple-element.17), channel_id=1, source_target_pairs={{0,2},{1,3},{2,0},{3,1},{4,6},{5,7},{6,4},{7,5},{8,10},{9,11},{10,... | collective-permute-start | bytes 1843208 | tf_op jit(solution)/shard_map/ppermute | solution.py:69
  7.3 38.1 %copy-start.3 = (s32[1,32]{1,0:T(1,128)S(1)}, s32[1,32]{1,0:T(1,128)}, u32[]{:S(2)}) copy-start(s32[1,32]{1,0:T(1,128)} %param.5) | copy-start | bytes 388
  7.3 38.2 %copy-start.2 = (s32[16,2]{0,1:T(2,128)S(1)}, s32[16,2]{0,1:T(2,128)}, u32[]{:S(2)}) copy-start(s32[16,2]{0,1:T(2,128)} %param.7) | copy-start | bytes 388
  7.3 26.7 %collective-permute-start.8 = (bf16[8,2,5,2,1920]{4,3,2,1,0:T(2,128)(2,1)S(1)}, bf16[8,2,5,2,1920]{4,3,2,1,0:T(2,128)(2,1)S(1)}, u32[]{:S(2)}, u32[]{:S(2)}) collective-permute-start(bf16[8,2,5,2,1920]{4,3,2,1,0:T(2,128)(2,1)S(1)} %get-tuple-element.28), channel_id=1, source_target_pairs={{0,3},{1,0},{2,1},{3,2},{4,7},{5,4},{6,5},{7,6},{8,11},{9,8},{10,9... | collective-permute-start | bytes 1843208 | tf_op jit(solution)/shard_map/ppermute | solution.py:68
  19.6 25.0 %collective-permute-start.5 = (bf16[8,2,4,2,1920]{4,3,2,1,0:T(2,128)(2,1)S(1)}, bf16[8,2,4,2,1920]{4,3,2,1,0:T(2,128)(2,1)S(1)}, u32[]{:S(2)}, u32[]{:S(2)}) collective-permute-start(bf16[8,2,4,2,1920]{4,3,2,1,0:T(2,128)(2,1)S(1)} %get-tuple-element.24), channel_id=1, source_target_pairs={{0,3},{1,0},{2,1},{3,2},{4,7},{5,4},{6,5},{7,6},{8,11},{9,8},{10,9... | collective-permute-start | bytes 1474568 | tf_op jit(solution)/shard_map/ppermute | solution.py:68
  21.9 28.7 %collective-permute-start.6 = (bf16[8,2,4,2,1920]{4,3,2,1,0:T(2,128)(2,1)S(1)}, bf16[8,2,4,2,1920]{4,3,2,1,0:T(2,128)(2,1)S(1)}, u32[]{:S(2)}, u32[]{:S(2)}) collective-permute-start(bf16[8,2,4,2,1920]{4,3,2,1,0:T(2,128)(2,1)S(1)} %get-tuple-element.25), channel_id=1, source_target_pairs={{0,2},{1,3},{2,0},{3,1},{4,6},{5,7},{6,4},{7,5},{8,10},{9,11},{10,... | collective-permute-start | bytes 1474568 | tf_op jit(solution)/shard_map/ppermute | solution.py:69
  22.5 34.3 %collective-permute-start.7 = (bf16[8,2,4,2,1920]{4,3,2,1,0:T(2,128)(2,1)S(1)}, bf16[8,2,4,2,1920]{4,3,2,1,0:T(2,128)(2,1)S(1)}, u32[]{:S(2)}, u32[]{:S(2)}) collective-permute-start(bf16[8,2,4,2,1920]{4,3,2,1,0:T(2,128)(2,1)S(1)} %get-tuple-element.26), channel_id=1, source_target_pairs={{0,1},{1,2},{2,3},{3,0},{4,5},{5,6},{6,7},{7,4},{8,9},{9,10},{10,1... | collective-permute-start | bytes 1474568 | tf_op jit(solution)/shard_map/ppermute | solution.py:67
  33.9 26.7 %collective-permute-start.1 = (bf16[8,2,1,2,1920]{4,3,2,1,0:T(2,128)(2,1)S(1)}, bf16[8,2,1,2,1920]{4,3,2,1,0:T(2,128)(2,1)S(1)}, u32[]{:S(2)}, u32[]{:S(2)}) collective-permute-start(bf16[8,2,1,2,1920]{4,3,2,1,0:T(2,128)(2,1)S(1)} %get-tuple-element.19), channel_id=1, source_target_pairs={{0,3},{1,0},{2,1},{3,2},{4,7},{5,4},{6,5},{7,6},{8,11},{9,8},{10,9... | collective-permute-start | bytes 368648 | tf_op jit(solution)/shard_map/ppermute | solution.py:68
  34.0 26.6 %collective-permute-start.2 = (bf16[8,2,1,2,1920]{4,3,2,1,0:T(2,128)(2,1)S(1)}, bf16[8,2,1,2,1920]{4,3,2,1,0:T(2,128)(2,1)S(1)}, u32[]{:S(2)}, u32[]{:S(2)}) collective-permute-start(bf16[8,2,1,2,1920]{4,3,2,1,0:T(2,128)(2,1)S(1)} %get-tuple-element.20), channel_id=1, source_target_pairs={{0,2},{1,3},{2,0},{3,1},{4,6},{5,7},{6,4},{7,5},{8,10},{9,11},{10,... | collective-permute-start | bytes 368648 | tf_op jit(solution)/shard_map/ppermute | solution.py:69
  44.6 16.5 %collective-permute-start.3 = (bf16[8,2,1,2,1920]{4,3,2,1,0:T(2,128)(2,1)S(1)}, bf16[8,2,1,2,1920]{4,3,2,1,0:T(2,128)(2,1)S(1)}, u32[]{:S(2)}, u32[]{:S(2)}) collective-permute-start(bf16[8,2,1,2,1920]{4,3,2,1,0:T(2,128)(2,1)S(1)} %get-tuple-element.21), channel_id=1, source_target_pairs={{0,1},{1,2},{2,3},{3,0},{4,5},{5,6},{6,7},{7,4},{8,9},{9,10},{10,1... | collective-permute-start | bytes 368648 | tf_op jit(solution)/shard_map/ppermute | solution.py:67

commit v11 on v10

--- a/solution.py
+++ b/solution.py
@@ -199,11 +199,11 @@
 
     first = meet(*cut(images, CHUNKS[0]))
     second = meet(*cut(images, CHUNKS[1], first[3]))
-    third = meet(*cut(images, CHUNKS[2], first[2]))
 
     shape = jax.ShapeDtypeStruct((32, 4, 8, LCOL), jnp.float32)
     partial = jax.ShapeDtypeStruct((ROWS, LCOL), jnp.float32)
     gamma = looks(whole_kernel, epochs, (*first, box, table), shape, 5)
+    third = meet(*cut(images, CHUNKS[2], gamma))
     most = looks(most_kernel, epochs, (*second, box, gamma), partial, 4)
     gamma = looks(last_kernel, epochs, (*third, box, most, gamma), shape, 1, {7: 0})
     got = lax.all_to_all(

time: 91.4 us -> 88.1 us (0.964)
  blocking collectives: 26.5 us -> 23.1 us
    ppermute x3, waiting for transfers between devices: 8.82 us -> 2.78 us  [meet(): one = lax.ppermute(to3, 'date', ring(3))]
    ppermute x3, waiting for transfers between devices: 17.4 us -> 23.2 us  [meet(): three = lax.ppermute(to1, 'date', ring(1))]
    all_to_all x1, blocking collectives: 26.5 us -> 23.1 us  [on_device(): lax.all_to_all(gamma.reshape(128, 8, LCOL), ('tile', 'date'), split_axis=...]
    ppermute x3, starting transfers between devices: 4.85 us -> 3.41 us  [meet(): two = lax.ppermute(to2, 'date', ring(2))]
    ppermute x3, starting transfers between devices: 2.88 us -> 4.17 us  [meet(): one = lax.ppermute(to3, 'date', ring(3))]
  transfers between devices with their start and end apart: 9 -> 9, of which waited for: 5 -> 5; matrix products, arithmetic and copies ran while one was open for 0% -> 0% of each run, Pallas kernels for 10% -> 11%
where the time goes in v11:
time: 88.1 us; the launch traced here: 88 us
  waiting for transfers between devices  36.9 us (42%)
  blocking collectives  23.1 us (26%)
  Pallas kernels  13.8 us (16%)
  starting transfers between devices  10.5 us (12%)
  local copies, waits for them, and re-layouts  2.42 us (3%)
    ppermute x3, waiting for transfers between devices, meet(): three = lax.ppermute(to1, 'date', ring(1))  23.2 us
    all_to_all x1, blocking collectives, on_device(): lax.all_to_all(gamma.reshape(128, 8, LCOL), ('tile', 'date'), split_axis=...  23.1 us
    pallas_call x3, Pallas kernels, looks(): pl.pallas_call(kernel, out_shape=out_shape, grid_spec=pltpu.PrefetchScala...  11.6 us
    ppermute x3, waiting for transfers between devices, meet(): two = lax.ppermute(to2, 'date', ring(2))  11 us
    ppermute x3, starting transfers between devices, meet(): one = lax.ppermute(to3, 'date', ring(3))  4.17 us
    ppermute x3, starting transfers between devices, meet(): two = lax.ppermute(to2, 'date', ring(2))  3.41 us
    ppermute x3, starting transfers between devices, meet(): three = lax.ppermute(to1, 'date', ring(1))  2.92 us
    ppermute x3, waiting for transfers between devices, meet(): one = lax.ppermute(to3, 'date', ring(3))  2.78 us
  transfers between devices with their start and end apart: 9, of which 5 were waited for; matrix products, arithmetic and copies ran while one was open for 0% of the time, Pallas kernels for 11%

profile of v11, /device:TPU:1, one launch (start us, length us, event | category | flops | bytes accessed | tf_op | source)
XLA Modules:
  0.0 88.0 jit_solution(13712718027272376591)
XLA Ops:
  0.0 2.4 %copy-done = bf16[2,1,32,2,10,1920]{5,3,4,2,1,0:T(2,128)(2,1)S(1)} copy-done((bf16[2,1,32,2,10,1920]{5,3,4,2,1,0:T(2,128)(2,1)S(1)}, bf16[2,1,32,2,10,1920]{5,3,4,2,1,0:T(2,128)(2,1)}, u32[]{:S(2)}) %copy-start) | copy-done | bytes 4915224
  2.4 0.3 shard_map.46
  2.7 2.1 %collective-permute-start.2 = (bf16[8,2,5,2,1920]{4,3,2,1,0:T(2,128)(2,1)S(1)}, bf16[8,2,5,2,1920]{4,3,2,1,0:T(2,128)(2,1)S(1)}, u32[]{:S(2)}, u32[]{:S(2)}) collective-permute-start(bf16[8,2,5,2,1920]{4,3,2,1,0:T(2,128)(2,1)S(1)} %get-tuple-element.20), channel_id=1, source_target_pairs={{0,1},{1,2},{2,3},{3,0},{4,5},{5,6},{6,7},{7,4},{8,9},{9,10},{10,1... | collective-permute-start | bytes 1843208 | tf_op jit(solution)/shard_map/ppermute | solution.py:67
  4.8 1.3 %collective-permute-start = (bf16[8,2,5,2,1920]{4,3,2,1,0:T(2,128)(2,1)S(1)}, bf16[8,2,5,2,1920]{4,3,2,1,0:T(2,128)(2,1)S(1)}, u32[]{:S(2)}, u32[]{:S(2)}) collective-permute-start(bf16[8,2,5,2,1920]{4,3,2,1,0:T(2,128)(2,1)S(1)} %get-tuple-element.18), channel_id=1, source_target_pairs={{0,3},{1,0},{2,1},{3,2},{4,7},{5,4},{6,5},{7,6},{8,11},{9,8},{10,9... | collective-permute-start | bytes 1843208 | tf_op jit(solution)/shard_map/ppermute | solution.py:68
  6.2 1.6 %collective-permute-start.1 = (bf16[8,2,5,2,1920]{4,3,2,1,0:T(2,128)(2,1)S(1)}, bf16[8,2,5,2,1920]{4,3,2,1,0:T(2,128)(2,1)S(1)}, u32[]{:S(2)}, u32[]{:S(2)}) collective-permute-start(bf16[8,2,5,2,1920]{4,3,2,1,0:T(2,128)(2,1)S(1)} %get-tuple-element.19), channel_id=1, source_target_pairs={{0,2},{1,3},{2,0},{3,1},{4,6},{5,7},{6,4},{7,5},{8,10},{9,11},{10,... | collective-permute-start | bytes 1843208 | tf_op jit(solution)/shard_map/ppermute | solution.py:69
  8.6 10.7 %collective-permute-done.2.three.rest_0_ = bf16[8,2,5,2,1920]{4,3,2,1,0:T(2,128)(2,1)S(1)} collective-permute-done((bf16[8,2,5,2,1920]{4,3,2,1,0:T(2,128)(2,1)S(1)}, bf16[8,2,5,2,1920]{4,3,2,1,0:T(2,128)(2,1)S(1)}, u32[]{:S(2)}, u32[]{:S(2)}) %collective-permute-start.2) | collective-permute-done | bytes 614432 | tf_op jit(solution)/shard_map/ppermute | solution.py:67
  19.2 0.4 shard_map.49
  19.7 1.7 %collective-permute-start.6 = (bf16[8,2,4,2,1920]{4,3,2,1,0:T(2,128)(2,1)S(1)}, bf16[8,2,4,2,1920]{4,3,2,1,0:T(2,128)(2,1)S(1)}, u32[]{:S(2)}, u32[]{:S(2)}) collective-permute-start(bf16[8,2,4,2,1920]{4,3,2,1,0:T(2,128)(2,1)S(1)} %get-tuple-element.26), channel_id=1, source_target_pairs={{0,3},{1,0},{2,1},{3,2},{4,7},{5,4},{6,5},{7,6},{8,11},{9,8},{10,9... | collective-permute-start | bytes 1474568 | tf_op jit(solution)/shard_map/ppermute | solution.py:68
  21.3 0.5 collective-permute-start.7
  21.8 0.6 collective-permute-start.8
  22.5 0.3 fusion.box
  22.8 11.0 %collective-permute-done.1.two = bf16[8,2,5,2,1920]{4,3,2,1,0:T(2,128)(2,1)S(1)} collective-permute-done((bf16[8,2,5,2,1920]{4,3,2,1,0:T(2,128)(2,1)S(1)}, bf16[8,2,5,2,1920]{4,3,2,1,0:T(2,128)(2,1)S(1)}, u32[]{:S(2)}, u32[]{:S(2)}) %collective-permute-start.1) | collective-permute-done | bytes 614432 | tf_op jit(solution)/shard_map/ppermute | solution.py:69
  33.8 5.5 %shard_map.47.rest_0_.after.given = f32[32,4,8,128]{3,2,1,0:T(8,128)S(1)} custom-call(s32[2,16]{1,0:T(2,128)S(1)} %bitcast.12, bf16[8,2,5,2,1920]{4,3,2,1,0:T(2,128)(2,1)S(1)} %get-tuple-element.17.own, bf16[8,2,5,2,1920]{4,3,2,1,0:T(2,128)(2,1)S(1)} %collective-permute-done.one, bf16[8,2,5,2,1920]{4,3,2,1,0:T(2,128)(2,1)S(1)} %collective-permute-done.1.two, ...), custom_call_target="tpu_custom_call" | custom-call | flops 326860800 | bytes 2457600 | tf_op jit(solution)/shard_map/pallas_call | solution.py:154
  39.3 0.2 shard_map.48
  39.5 1.2 %collective-permute-start.3 = (bf16[8,2,1,2,1920]{4,3,2,1,0:T(2,128)(2,1)S(1)}, bf16[8,2,1,2,1920]{4,3,2,1,0:T(2,128)(2,1)S(1)}, u32[]{:S(2)}, u32[]{:S(2)}) collective-permute-start(bf16[8,2,1,2,1920]{4,3,2,1,0:T(2,128)(2,1)S(1)} %get-tuple-element.22), channel_id=1, source_target_pairs={{0,3},{1,0},{2,1},{3,2},{4,7},{5,4},{6,5},{7,6},{8,11},{9,8},{10,9... | collective-permute-start | bytes 368648 | tf_op jit(solution)/shard_map/ppermute | solution.py:68
  40.6 1.2 %collective-permute-start.4 = (bf16[8,2,1,2,1920]{4,3,2,1,0:T(2,128)(2,1)S(1)}, bf16[8,2,1,2,1920]{4,3,2,1,0:T(2,128)(2,1)S(1)}, u32[]{:S(2)}, u32[]{:S(2)}) collective-permute-start(bf16[8,2,1,2,1920]{4,3,2,1,0:T(2,128)(2,1)S(1)} %get-tuple-element.23), channel_id=1, source_target_pairs={{0,2},{1,3},{2,0},{3,1},{4,6},{5,7},{6,4},{7,5},{8,10},{9,11},{10,... | collective-permute-start | bytes 368648 | tf_op jit(solution)/shard_map/ppermute | solution.py:69
  41.9 2.8 %collective-permute-done.6.one = bf16[8,2,4,2,1920]{4,3,2,1,0:T(2,128)(2,1)S(1)} collective-permute-done((bf16[8,2,4,2,1920]{4,3,2,1,0:T(2,128)(2,1)S(1)}, bf16[8,2,4,2,1920]{4,3,2,1,0:T(2,128)(2,1)S(1)}, u32[]{:S(2)}, u32[]{:S(2)}) %collective-permute-start.6) | collective-permute-done | bytes 491552 | tf_op jit(solution)/shard_map/ppermute | solution.py:68
  44.6 0.2 collective-permute-start.5
  44.8 12.0 %collective-permute-done.8.three = bf16[8,2,4,2,1920]{4,3,2,1,0:T(2,128)(2,1)S(1)} collective-permute-done((bf16[8,2,4,2,1920]{4,3,2,1,0:T(2,128)(2,1)S(1)}, bf16[8,2,4,2,1920]{4,3,2,1,0:T(2,128)(2,1)S(1)}, u32[]{:S(2)}, u32[]{:S(2)}) %collective-permute-start.8) | collective-permute-done | bytes 491552 | tf_op jit(solution)/shard_map/ppermute | solution.py:67
  56.8 3.8 %shard_map.50.most = f32[320,128]{1,0:T(8,128)S(1)} custom-call(s32[2,16]{1,0:T(2,128)S(1)} %bitcast.13, bf16[8,2,4,2,1920]{4,3,2,1,0:T(2,128)(2,1)S(1)} %get-tuple-element.25.own, bf16[8,2,4,2,1920]{4,3,2,1,0:T(2,128)(2,1)S(1)} %collective-permute-done.6.one, bf16[8,2,4,2,1920]{4,3,2,1,0:T(2,128)(2,1)S(1)} %collective-permute-done.7.two, ...), custom_call_target="tpu_custom_call" | custom-call | flops 324403200 | bytes 1966080 | tf_op jit(solution)/shard_map/pallas_call | solution.py:154
  60.6 0.5 collective-permute-done.5.three
  61.2 2.3 %shard_map.51 = f32[32,4,8,128]{3,2,1,0:T(8,128)S(1)} custom-call(s32[2,16]{1,0:T(2,128)S(1)} %bitcast.14, bf16[8,2,1,2,1920]{4,3,2,1,0:T(2,128)(2,1)S(1)} %get-tuple-element.21.own, bf16[8,2,1,2,1920]{4,3,2,1,0:T(2,128)(2,1)S(1)} %collective-permute-done.3.one, ...), custom_call_target="tpu_custom_call", output_to_operand_aliasing={{}: (7, {})} | custom-call | flops 317030400 | bytes 491520 | tf_op jit(solution)/shard_map/pallas_call | solution.py:154
  63.5 23.1 %all_to_all.5 = f32[128,8,128]{2,1,0:T(8,128)S(1)} all-to-all(f32[128,8,128]{2,1,0:T(8,128)S(1)} %bitcast.10), channel_id=1, replica_groups=mesh['tile'=32,'date'=4] {'tile','date'}, dimensions={0} | all-to-all | bytes 1048576 | tf_op jit(solution)/shard_map/all_to_all | solution.py:209
  86.6 1.4 %shard_map.52 = f32[4,2,64,128]{3,2,1,0:T(8,128)} custom-call(s32[33]{0:T(128)S(1)} %pad_add_fusion.table, f32[32,4,8,128]{3,2,1,0:T(8,128)S(1)} %bitcast.11), custom_call_target="tpu_custom_call" | custom-call | tf_op jit(solution)/shard_map/pallas_call | solution.py:212
  (13 shorter events, 0.1 us)
Async XLA Ops:
  0.0 8.5 %copy-start.3 = (s32[1,32]{1,0:T(1,128)S(1)}, s32[1,32]{1,0:T(1,128)}, u32[]{:S(2)}) copy-start(s32[1,32]{1,0:T(1,128)} %param.5) | copy-start | bytes 388
  0.0 2.4 %copy-start = (bf16[2,1,32,2,10,1920]{5,3,4,2,1,0:T(2,128)(2,1)S(1)}, bf16[2,1,32,2,10,1920]{5,3,4,2,1,0:T(2,128)(2,1)}, u32[]{:S(2)}) copy-start(bf16[2,1,32,2,10,1920]{5,3,4,2,1,0:T(2,128)(2,1)} %param.4) | copy-start | bytes 14745604
  2.4 16.8 %copy-start.1 = (bf16[2,1,32,2,10,1920]{5,3,4,2,1,0:T(2,128)(2,1)S(1)}, bf16[2,1,32,2,10,1920]{5,3,4,2,1,0:T(2,128)(2,1)}, u32[]{:S(2)}) copy-start(bf16[2,1,32,2,10,1920]{5,3,4,2,1,0:T(2,128)(2,1)} %param.4) | copy-start | bytes 14745604
  2.4 31.3 %copy-start.2 = (s32[16,2]{0,1:T(2,128)S(1)}, s32[16,2]{0,1:T(2,128)}, u32[]{:S(2)}) copy-start(s32[16,2]{0,1:T(2,128)} %param.7) | copy-start | bytes 388
  2.7 16.5 %collective-permute-start.2 = (bf16[8,2,5,2,1920]{4,3,2,1,0:T(2,128)(2,1)S(1)}, bf16[8,2,5,2,1920]{4,3,2,1,0:T(2,128)(2,1)S(1)}, u32[]{:S(2)}, u32[]{:S(2)}) collective-permute-start(bf16[8,2,5,2,1920]{4,3,2,1,0:T(2,128)(2,1)S(1)} %get-tuple-element.20), channel_id=1, source_target_pairs={{0,1},{1,2},{2,3},{3,0},{4,5},{5,6},{6,7},{7,4},{8,9},{9,10},{10,1... | collective-permute-start | bytes 1843208 | tf_op jit(solution)/shard_map/ppermute | solution.py:67
  4.8 18.0 %collective-permute-start = (bf16[8,2,5,2,1920]{4,3,2,1,0:T(2,128)(2,1)S(1)}, bf16[8,2,5,2,1920]{4,3,2,1,0:T(2,128)(2,1)S(1)}, u32[]{:S(2)}, u32[]{:S(2)}) collective-permute-start(bf16[8,2,5,2,1920]{4,3,2,1,0:T(2,128)(2,1)S(1)} %get-tuple-element.18), channel_id=1, source_target_pairs={{0,3},{1,0},{2,1},{3,2},{4,7},{5,4},{6,5},{7,6},{8,11},{9,8},{10,9... | collective-permute-start | bytes 1843208 | tf_op jit(solution)/shard_map/ppermute | solution.py:68
  6.2 27.6 %collective-permute-start.1 = (bf16[8,2,5,2,1920]{4,3,2,1,0:T(2,128)(2,1)S(1)}, bf16[8,2,5,2,1920]{4,3,2,1,0:T(2,128)(2,1)S(1)}, u32[]{:S(2)}, u32[]{:S(2)}) collective-permute-start(bf16[8,2,5,2,1920]{4,3,2,1,0:T(2,128)(2,1)S(1)} %get-tuple-element.19), channel_id=1, source_target_pairs={{0,2},{1,3},{2,0},{3,1},{4,6},{5,7},{6,4},{7,5},{8,10},{9,11},{10,... | collective-permute-start | bytes 1843208 | tf_op jit(solution)/shard_map/ppermute | solution.py:69
  19.7 25.0 %collective-permute-start.6 = (bf16[8,2,4,2,1920]{4,3,2,1,0:T(2,128)(2,1)S(1)}, bf16[8,2,4,2,1920]{4,3,2,1,0:T(2,128)(2,1)S(1)}, u32[]{:S(2)}, u32[]{:S(2)}) collective-permute-start(bf16[8,2,4,2,1920]{4,3,2,1,0:T(2,128)(2,1)S(1)} %get-tuple-element.26), channel_id=1, source_target_pairs={{0,3},{1,0},{2,1},{3,2},{4,7},{5,4},{6,5},{7,6},{8,11},{9,8},{10,9... | collective-permute-start | bytes 1474568 | tf_op jit(solution)/shard_map/ppermute | solution.py:68
  21.3 23.5 %collective-permute-start.7 = (bf16[8,2,4,2,1920]{4,3,2,1,0:T(2,128)(2,1)S(1)}, bf16[8,2,4,2,1920]{4,3,2,1,0:T(2,128)(2,1)S(1)}, u32[]{:S(2)}, u32[]{:S(2)}) collective-permute-start(bf16[8,2,4,2,1920]{4,3,2,1,0:T(2,128)(2,1)S(1)} %get-tuple-element.27), channel_id=1, source_target_pairs={{0,2},{1,3},{2,0},{3,1},{4,6},{5,7},{6,4},{7,5},{8,10},{9,11},{10,... | collective-permute-start | bytes 1474568 | tf_op jit(solution)/shard_map/ppermute | solution.py:69
  21.8 35.0 %collective-permute-start.8 = (bf16[8,2,4,2,1920]{4,3,2,1,0:T(2,128)(2,1)S(1)}, bf16[8,2,4,2,1920]{4,3,2,1,0:T(2,128)(2,1)S(1)}, u32[]{:S(2)}, u32[]{:S(2)}) collective-permute-start(bf16[8,2,4,2,1920]{4,3,2,1,0:T(2,128)(2,1)S(1)} %get-tuple-element.28), channel_id=1, source_target_pairs={{0,1},{1,2},{2,3},{3,0},{4,5},{5,6},{6,7},{7,4},{8,9},{9,10},{10,1... | collective-permute-start | bytes 1474568 | tf_op jit(solution)/shard_map/ppermute | solution.py:67
  39.5 21.2 %collective-permute-start.3 = (bf16[8,2,1,2,1920]{4,3,2,1,0:T(2,128)(2,1)S(1)}, bf16[8,2,1,2,1920]{4,3,2,1,0:T(2,128)(2,1)S(1)}, u32[]{:S(2)}, u32[]{:S(2)}) collective-permute-start(bf16[8,2,1,2,1920]{4,3,2,1,0:T(2,128)(2,1)S(1)} %get-tuple-element.22), channel_id=1, source_target_pairs={{0,3},{1,0},{2,1},{3,2},{4,7},{5,4},{6,5},{7,6},{8,11},{9,8},{10,9... | collective-permute-start | bytes 368648 | tf_op jit(solution)/shard_map/ppermute | solution.py:68
  40.6 20.0 %collective-permute-start.4 = (bf16[8,2,1,2,1920]{4,3,2,1,0:T(2,128)(2,1)S(1)}, bf16[8,2,1,2,1920]{4,3,2,1,0:T(2,128)(2,1)S(1)}, u32[]{:S(2)}, u32[]{:S(2)}) collective-permute-start(bf16[8,2,1,2,1920]{4,3,2,1,0:T(2,128)(2,1)S(1)} %get-tuple-element.23), channel_id=1, source_target_pairs={{0,2},{1,3},{2,0},{3,1},{4,6},{5,7},{6,4},{7,5},{8,10},{9,11},{10,... | collective-permute-start | bytes 368648 | tf_op jit(solution)/shard_map/ppermute | solution.py:69
  44.6 16.5 %collective-permute-start.5 = (bf16[8,2,1,2,1920]{4,3,2,1,0:T(2,128)(2,1)S(1)}, bf16[8,2,1,2,1920]{4,3,2,1,0:T(2,128)(2,1)S(1)}, u32[]{:S(2)}, u32[]{:S(2)}) collective-permute-start(bf16[8,2,1,2,1920]{4,3,2,1,0:T(2,128)(2,1)S(1)} %get-tuple-element.24), channel_id=1, source_target_pairs={{0,1},{1,2},{2,3},{3,0},{4,5},{5,6},{6,7},{7,4},{8,9},{9,10},{10,1... | collective-permute-start | bytes 368648 | tf_op jit(solution)/shard_map/ppermute | solution.py:67

commit v12 on v11

--- a/solution.py
+++ b/solution.py
@@ -26,12 +26,12 @@
 ANYWHERE = pl.BlockSpec(memory_space=pl.ANY)
 
 
-def cut_kernel(chunk, images, *rest):
-    to1, to2, to3, own, sem = rest[-5:]
+def cut_kernel(chunk, steps, images, *rest):
+    *outs, sem = rest[-1 - len(steps) :]
     first, low, high = chunk
     group = lax.axis_index("date")
     copies = []
-    for step, out in ((1, to1), (3, to3), (2, to2), (0, own)):
+    for step, out in zip(steps, outs):
         taker = lax.rem(group + step, 4)
         tiles = pl.ds(lax.rem(taker, 2) * HALF + first, ITEMS)
         lines = pl.ds(lax.div(taker, 2) * LOOK_AZ + low, high - low)
@@ -46,17 +46,17 @@
         copy.wait()
 
 
-def cut(images, chunk, after=None):
+def cut(images, chunk, after=None, steps=(1, 2, 3, 0), limit=8):
     _, low, high = chunk
     block = jax.ShapeDtypeStruct((ITEMS, 2, high - low, 2, RG), jnp.bfloat16)
     operands = (images,) + (() if after is None else (after,))
     return pl.pallas_call(
-        functools.partial(cut_kernel, chunk),
-        out_shape=[block] * 4,
+        functools.partial(cut_kernel, chunk, steps),
+        out_shape=[block] * len(steps),
         in_specs=[HBM, ANYWHERE][: len(operands)],
-        out_specs=[VMEM] * 4,
-        scratch_shapes=[pltpu.SemaphoreType.DMA((8,))],
-        compiler_params=pltpu.CompilerParams(vmem_limit_bytes=8 << 20),
+        out_specs=[VMEM] * len(steps),
+        scratch_shapes=[pltpu.SemaphoreType.DMA((2 * len(steps),))],
+        compiler_params=pltpu.CompilerParams(vmem_limit_bytes=limit << 20),
     )(*operands)
 
 
@@ -197,7 +197,12 @@
         jnp.arange(RG)[:, None] // LOOK_RG == jnp.arange(LCOL)[None, :]
     ).astype(jnp.bfloat16)
 
-    first = meet(*cut(images, CHUNKS[0]))
+    (to1,) = cut(images, CHUNKS[0], None, (1,), 56)
+    (to3,) = cut(images, CHUNKS[0], None, (3,), 56)
+    (to2,) = cut(images, CHUNKS[0], None, (2,), 56)
+    _, one, two, three = meet(to1, to2, to3, to1)
+    (own,) = cut(images, CHUNKS[0], three, (0,))
+    first = (own, one, two, three)
     second = meet(*cut(images, CHUNKS[1], first[3]))
 
     shape = jax.ShapeDtypeStruct((32, 4, 8, LCOL), jnp.float32)

time: 88.1 us -> 90.2 us (1.024)
  waiting for transfers between devices: 36.9 us -> 29.4 us
  Pallas kernels: 13.8 us -> 19.4 us
  starting transfers between devices: 10.5 us -> 13.9 us
  blocking collectives: 23.1 us -> 26.2 us
  local copies, waits for them, and re-layouts: 2.42 us -> 0.02 us
    ppermute x3, waiting for transfers between devices: 23.2 us -> 17.2 us  [meet(): three = lax.ppermute(to1, 'date', ring(1))]
    pallas_call x3 -> x6, Pallas kernels: 0.88 us -> 6.56 us  [cut(): pl.pallas_call(functools.partial(cut_kernel, chunk, steps), out_shape=[bl...]
    all_to_all x1, blocking collectives: 23.1 us -> 26.2 us  [on_device(): lax.all_to_all(gamma.reshape(128, 8, LCOL), ('tile', 'date'), split_axis=...]
    unnamed x8, local copies, waits for them, and re-layouts: 2.42 us -> 0.02 us
    ppermute x3, starting transfers between devices: 4.17 us -> 6.24 us  [meet(): one = lax.ppermute(to3, 'date', ring(3))]
    ppermute x3, waiting for transfers between devices: 2.78 us -> 1.34 us  [meet(): one = lax.ppermute(to3, 'date', ring(3))]
    ppermute x3, starting transfers between devices: 2.92 us -> 4.15 us  [meet(): three = lax.ppermute(to1, 'date', ring(1))]
  transfers between devices with their start and end apart: 9 -> 9, of which waited for: 5 -> 4; matrix products, arithmetic and copies ran while one was open for 0% -> 0% of each run, Pallas kernels for 11% -> 15%
where the time goes in v12:
time: 90.2 us; the launch traced here: 90.1 us
  waiting for transfers between devices  29.4 us (33%)
  blocking collectives  26.2 us (29%)
  Pallas kernels  19.4 us (22%)
  starting transfers between devices  13.9 us (15%)
    all_to_all x1, blocking collectives, on_device(): lax.all_to_all(gamma.reshape(128, 8, LCOL), ('tile', 'date'), split_axis=...  26.2 us
    ppermute x3, waiting for transfers between devices, meet(): three = lax.ppermute(to1, 'date', ring(1))  17.2 us
    pallas_call x3, Pallas kernels, looks(): pl.pallas_call(kernel, out_shape=out_shape, grid_spec=pltpu.PrefetchScala...  11.5 us
    ppermute x3, waiting for transfers between devices, meet(): two = lax.ppermute(to2, 'date', ring(2))  10.9 us
    pallas_call x6, Pallas kernels, cut(): pl.pallas_call(functools.partial(cut_kernel, chunk, steps), out_shape=[bl...  6.56 us
    ppermute x3, starting transfers between devices, meet(): one = lax.ppermute(to3, 'date', ring(3))  6.24 us
    ppermute x3, starting transfers between devices, meet(): three = lax.ppermute(to1, 'date', ring(1))  4.15 us
    ppermute x3, starting transfers between devices, meet(): two = lax.ppermute(to2, 'date', ring(2))  3.49 us
  transfers between devices with their start and end apart: 9, of which 4 were waited for; matrix products, arithmetic and copies ran while one was open for 0% of the time, Pallas kernels for 15%

profile of v12, /device:TPU:1, one launch (start us, length us, event | category | flops | bytes accessed | tf_op | source)
XLA Modules:
  0.0 90.1 jit_solution(6160420034872059842)
XLA Ops:
  0.0 2.1 %shard_map.46 = bf16[8,2,5,2,1920]{4,3,2,1,0:T(2,128)(2,1)} custom-call(bf16[2,32,10,2,1920]{4,3,2,1,0:T(2,128)(2,1)} %bitcast.7), custom_call_target="tpu_custom_call" | custom-call | tf_op jit(solution)/shard_map/pallas_call | solution.py:53
  2.1 2.1 %collective-permute-start = (bf16[8,2,5,2,1920]{4,3,2,1,0:T(2,128)(2,1)}, bf16[8,2,5,2,1920]{4,3,2,1,0:T(2,128)(2,1)S(1)}, u32[]{:S(2)}, u32[]{:S(2)}) collective-permute-start(bf16[8,2,5,2,1920]{4,3,2,1,0:T(2,128)(2,1)} %shard_map.46), channel_id=1, source_target_pairs={{0,1},{1,2},{2,3},{3,0},{4,5},{5,6},{6,7},{7,4},{8,9},{9,10},{10,1... | collective-permute-start | bytes 1843208 | tf_op jit(solution)/shard_map/ppermute | solution.py:67
  4.2 1.9 %shard_map.48 = bf16[8,2,5,2,1920]{4,3,2,1,0:T(2,128)(2,1)} custom-call(bf16[2,32,10,2,1920]{4,3,2,1,0:T(2,128)(2,1)} %bitcast.8), custom_call_target="tpu_custom_call" | custom-call | tf_op jit(solution)/shard_map/pallas_call | solution.py:53
  6.1 1.4 %collective-permute-start.1 = (bf16[8,2,5,2,1920]{4,3,2,1,0:T(2,128)(2,1)}, bf16[8,2,5,2,1920]{4,3,2,1,0:T(2,128)(2,1)S(1)}, u32[]{:S(2)}, u32[]{:S(2)}) collective-permute-start(bf16[8,2,5,2,1920]{4,3,2,1,0:T(2,128)(2,1)} %shard_map.48), channel_id=1, source_target_pairs={{0,3},{1,0},{2,1},{3,2},{4,7},{5,4},{6,5},{7,6},{8,11},{9,8},{10,9... | collective-permute-start | bytes 1843208 | tf_op jit(solution)/shard_map/ppermute | solution.py:68
  7.6 1.9 %shard_map.49 = bf16[8,2,5,2,1920]{4,3,2,1,0:T(2,128)(2,1)} custom-call(bf16[2,32,10,2,1920]{4,3,2,1,0:T(2,128)(2,1)} %bitcast.9), custom_call_target="tpu_custom_call" | custom-call | tf_op jit(solution)/shard_map/pallas_call | solution.py:53
  9.5 1.7 %collective-permute-start.2 = (bf16[8,2,5,2,1920]{4,3,2,1,0:T(2,128)(2,1)}, bf16[8,2,5,2,1920]{4,3,2,1,0:T(2,128)(2,1)S(1)}, u32[]{:S(2)}, u32[]{:S(2)}) collective-permute-start(bf16[8,2,5,2,1920]{4,3,2,1,0:T(2,128)(2,1)} %shard_map.49), channel_id=1, source_target_pairs={{0,2},{1,3},{2,0},{3,1},{4,6},{5,7},{6,4},{7,5},{8,10},{9,11},{10,... | collective-permute-start | bytes 1843208 | tf_op jit(solution)/shard_map/ppermute | solution.py:69
  11.9 6.9 %collective-permute-done.rest_0_.three = bf16[8,2,5,2,1920]{4,3,2,1,0:T(2,128)(2,1)S(1)} collective-permute-done((bf16[8,2,5,2,1920]{4,3,2,1,0:T(2,128)(2,1)}, bf16[8,2,5,2,1920]{4,3,2,1,0:T(2,128)(2,1)S(1)}, u32[]{:S(2)}, u32[]{:S(2)}) %collective-permute-start) | collective-permute-done | bytes 614432 | tf_op jit(solution)/shard_map/ppermute | solution.py:67
  18.8 0.4 shard_map.52
  19.2 1.7 %collective-permute-start.6 = (bf16[8,2,4,2,1920]{4,3,2,1,0:T(2,128)(2,1)S(1)}, bf16[8,2,4,2,1920]{4,3,2,1,0:T(2,128)(2,1)S(1)}, u32[]{:S(2)}, u32[]{:S(2)}) collective-permute-start(bf16[8,2,4,2,1920]{4,3,2,1,0:T(2,128)(2,1)S(1)} %get-tuple-element.18), channel_id=1, source_target_pairs={{0,3},{1,0},{2,1},{3,2},{4,7},{5,4},{6,5},{7,6},{8,11},{9,8},{10,9... | collective-permute-start | bytes 1474568 | tf_op jit(solution)/shard_map/ppermute | solution.py:68
  20.9 0.5 collective-permute-start.7
  21.4 0.6 collective-permute-start.8
  22.0 0.3 fusion.box
  22.5 10.9 %collective-permute-done.2.two = bf16[8,2,5,2,1920]{4,3,2,1,0:T(2,128)(2,1)S(1)} collective-permute-done((bf16[8,2,5,2,1920]{4,3,2,1,0:T(2,128)(2,1)}, bf16[8,2,5,2,1920]{4,3,2,1,0:T(2,128)(2,1)S(1)}, u32[]{:S(2)}, u32[]{:S(2)}) %collective-permute-start.2) | collective-permute-done | bytes 614432 | tf_op jit(solution)/shard_map/ppermute | solution.py:69
  33.3 5.4 %shard_map.50.rest_0_.after.given = f32[32,4,8,128]{3,2,1,0:T(8,128)S(1)} custom-call(s32[2,16]{1,0:T(2,128)S(1)} %bitcast.17, bf16[8,2,5,2,1920]{4,3,2,1,0:T(2,128)(2,1)S(1)} %shard_map.47.own, bf16[8,2,5,2,1920]{4,3,2,1,0:T(2,128)(2,1)S(1)} %collective-permute-done.1.one, bf16[8,2,5,2,1920]{4,3,2,1,0:T(2,128)(2,1)S(1)} %collective-permute-done.2.two, ...), custom_call_target="tpu_custom_call" | custom-call | flops 326860800 | bytes 2457600 | tf_op jit(solution)/shard_map/pallas_call | solution.py:154
  38.8 0.2 shard_map.51
  39.0 3.2 %collective-permute-start.3 = (bf16[8,2,1,2,1920]{4,3,2,1,0:T(2,128)(2,1)S(1)}, bf16[8,2,1,2,1920]{4,3,2,1,0:T(2,128)(2,1)S(1)}, u32[]{:S(2)}, u32[]{:S(2)}) collective-permute-start(bf16[8,2,1,2,1920]{4,3,2,1,0:T(2,128)(2,1)S(1)} %get-tuple-element.14), channel_id=1, source_target_pairs={{0,3},{1,0},{2,1},{3,2},{4,7},{5,4},{6,5},{7,6},{8,11},{9,8},{10,9... | collective-permute-start | bytes 368648 | tf_op jit(solution)/shard_map/ppermute | solution.py:68
  42.1 1.2 %collective-permute-start.4 = (bf16[8,2,1,2,1920]{4,3,2,1,0:T(2,128)(2,1)S(1)}, bf16[8,2,1,2,1920]{4,3,2,1,0:T(2,128)(2,1)S(1)}, u32[]{:S(2)}, u32[]{:S(2)}) collective-permute-start(bf16[8,2,1,2,1920]{4,3,2,1,0:T(2,128)(2,1)S(1)} %get-tuple-element.15), channel_id=1, source_target_pairs={{0,2},{1,3},{2,0},{3,1},{4,6},{5,7},{6,4},{7,5},{8,10},{9,11},{10,... | collective-permute-start | bytes 368648 | tf_op jit(solution)/shard_map/ppermute | solution.py:69
  43.4 1.3 %collective-permute-done.6.one = bf16[8,2,4,2,1920]{4,3,2,1,0:T(2,128)(2,1)S(1)} collective-permute-done((bf16[8,2,4,2,1920]{4,3,2,1,0:T(2,128)(2,1)S(1)}, bf16[8,2,4,2,1920]{4,3,2,1,0:T(2,128)(2,1)S(1)}, u32[]{:S(2)}, u32[]{:S(2)}) %collective-permute-start.6) | collective-permute-done | bytes 491552 | tf_op jit(solution)/shard_map/ppermute | solution.py:68
  44.7 1.4 %collective-permute-start.5 = (bf16[8,2,1,2,1920]{4,3,2,1,0:T(2,128)(2,1)S(1)}, bf16[8,2,1,2,1920]{4,3,2,1,0:T(2,128)(2,1)S(1)}, u32[]{:S(2)}, u32[]{:S(2)}) collective-permute-start(bf16[8,2,1,2,1920]{4,3,2,1,0:T(2,128)(2,1)S(1)} %get-tuple-element.16), channel_id=1, source_target_pairs={{0,1},{1,2},{2,3},{3,0},{4,5},{5,6},{6,7},{7,4},{8,9},{9,10},{10,1... | collective-permute-start | bytes 368648 | tf_op jit(solution)/shard_map/ppermute | solution.py:67
  46.1 10.3 %collective-permute-done.8.three = bf16[8,2,4,2,1920]{4,3,2,1,0:T(2,128)(2,1)S(1)} collective-permute-done((bf16[8,2,4,2,1920]{4,3,2,1,0:T(2,128)(2,1)S(1)}, bf16[8,2,4,2,1920]{4,3,2,1,0:T(2,128)(2,1)S(1)}, u32[]{:S(2)}, u32[]{:S(2)}) %collective-permute-start.8) | collective-permute-done | bytes 491552 | tf_op jit(solution)/shard_map/ppermute | solution.py:67
  56.4 3.8 %shard_map.53.most = f32[320,128]{1,0:T(8,128)S(1)} custom-call(s32[2,16]{1,0:T(2,128)S(1)} %bitcast.18, bf16[8,2,4,2,1920]{4,3,2,1,0:T(2,128)(2,1)S(1)} %get-tuple-element.17.own, bf16[8,2,4,2,1920]{4,3,2,1,0:T(2,128)(2,1)S(1)} %collective-permute-done.6.one, bf16[8,2,4,2,1920]{4,3,2,1,0:T(2,128)(2,1)S(1)} %collective-permute-done.7.two, ...), custom_call_target="tpu_custom_call" | custom-call | flops 324403200 | bytes 1966080 | tf_op jit(solution)/shard_map/pallas_call | solution.py:154
  60.2 2.3 %shard_map.54 = f32[32,4,8,128]{3,2,1,0:T(8,128)S(1)} custom-call(s32[2,16]{1,0:T(2,128)S(1)} %bitcast.19, bf16[8,2,1,2,1920]{4,3,2,1,0:T(2,128)(2,1)S(1)} %get-tuple-element.13.own, bf16[8,2,1,2,1920]{4,3,2,1,0:T(2,128)(2,1)S(1)} %collective-permute-done.3.one, ...), custom_call_target="tpu_custom_call", output_to_operand_aliasing={{}: (7, {})} | custom-call | flops 317030400 | bytes 491520 | tf_op jit(solution)/shard_map/pallas_call | solution.py:154
  62.5 26.2 %all_to_all.5 = f32[128,8,128]{2,1,0:T(8,128)S(1)} all-to-all(f32[128,8,128]{2,1,0:T(8,128)S(1)} %bitcast.15), channel_id=1, replica_groups=mesh['tile'=32,'date'=4] {'tile','date'}, dimensions={0} | all-to-all | bytes 1048576 | tf_op jit(solution)/shard_map/all_to_all | solution.py:214
  88.7 1.4 %shard_map.55 = f32[4,2,64,128]{3,2,1,0:T(8,128)} custom-call(s32[33]{0:T(128)S(1)} %pad_add_fusion.table, f32[32,4,8,128]{3,2,1,0:T(8,128)S(1)} %bitcast.16), custom_call_target="tpu_custom_call" | custom-call | tf_op jit(solution)/shard_map/pallas_call | solution.py:217
  (17 shorter events, 0.2 us)
Async XLA Ops:
  0.0 18.8 %slice-start = ((s8[4915200]{0:T(1024)(128)(4,1)}), s8[4194304]{0:T(1024)(128)(4,1)S(1)}, s32[]{:S(2)}) async-start(s8[4915200]{0:T(1024)(128)(4,1)} %bitcast.10), calls=%async_computation.1 | async-start | bytes 8388608
  2.1 9.8 %copy-start.1 = (s32[1,32]{1,0:T(1,128)S(1)}, s32[1,32]{1,0:T(1,128)}, u32[]{:S(2)}) copy-start(s32[1,32]{1,0:T(1,128)} %param.5) | copy-start | bytes 388
  2.1 16.7 %slice-start.1 = ((s8[4915200]{0:T(1024)(128)(4,1)}), s8[720896]{0:T(1024)(128)(4,1)S(1)}, s32[]{:S(2)}) async-start(s8[4915200]{0:T(1024)(128)(4,1)} %bitcast.10), calls=%async_computation.2 | async-start | bytes 1441792
  2.1 16.7 %collective-permute-start = (bf16[8,2,5,2,1920]{4,3,2,1,0:T(2,128)(2,1)}, bf16[8,2,5,2,1920]{4,3,2,1,0:T(2,128)(2,1)S(1)}, u32[]{:S(2)}, u32[]{:S(2)}) collective-permute-start(bf16[8,2,5,2,1920]{4,3,2,1,0:T(2,128)(2,1)} %shard_map.46), channel_id=1, source_target_pairs={{0,1},{1,2},{2,3},{3,0},{4,5},{5,6},{6,7},{7,4},{8,9},{9,10},{10,1... | collective-permute-start | bytes 1843208 | tf_op jit(solution)/shard_map/ppermute | solution.py:67
  6.1 16.3 %collective-permute-start.1 = (bf16[8,2,5,2,1920]{4,3,2,1,0:T(2,128)(2,1)}, bf16[8,2,5,2,1920]{4,3,2,1,0:T(2,128)(2,1)S(1)}, u32[]{:S(2)}, u32[]{:S(2)}) collective-permute-start(bf16[8,2,5,2,1920]{4,3,2,1,0:T(2,128)(2,1)} %shard_map.48), channel_id=1, source_target_pairs={{0,3},{1,0},{2,1},{3,2},{4,7},{5,4},{6,5},{7,6},{8,11},{9,8},{10,9... | collective-permute-start | bytes 1843208 | tf_op jit(solution)/shard_map/ppermute | solution.py:68
  9.5 23.9 %collective-permute-start.2 = (bf16[8,2,5,2,1920]{4,3,2,1,0:T(2,128)(2,1)}, bf16[8,2,5,2,1920]{4,3,2,1,0:T(2,128)(2,1)S(1)}, u32[]{:S(2)}, u32[]{:S(2)}) collective-permute-start(bf16[8,2,5,2,1920]{4,3,2,1,0:T(2,128)(2,1)} %shard_map.49), channel_id=1, source_target_pairs={{0,2},{1,3},{2,0},{3,1},{4,6},{5,7},{6,4},{7,5},{8,10},{9,11},{10,... | collective-permute-start | bytes 1843208 | tf_op jit(solution)/shard_map/ppermute | solution.py:69
  11.9 21.4 %copy-start = (s32[16,2]{0,1:T(2,128)S(1)}, s32[16,2]{0,1:T(2,128)}, u32[]{:S(2)}) copy-start(s32[16,2]{0,1:T(2,128)} %param.7) | copy-start | bytes 388
  19.2 25.4 %collective-permute-start.6 = (bf16[8,2,4,2,1920]{4,3,2,1,0:T(2,128)(2,1)S(1)}, bf16[8,2,4,2,1920]{4,3,2,1,0:T(2,128)(2,1)S(1)}, u32[]{:S(2)}, u32[]{:S(2)}) collective-permute-start(bf16[8,2,4,2,1920]{4,3,2,1,0:T(2,128)(2,1)S(1)} %get-tuple-element.18), channel_id=1, source_target_pairs={{0,3},{1,0},{2,1},{3,2},{4,7},{5,4},{6,5},{7,6},{8,11},{9,8},{10,9... | collective-permute-start | bytes 1474568 | tf_op jit(solution)/shard_map/ppermute | solution.py:68
  20.9 25.2 %collective-permute-start.7 = (bf16[8,2,4,2,1920]{4,3,2,1,0:T(2,128)(2,1)S(1)}, bf16[8,2,4,2,1920]{4,3,2,1,0:T(2,128)(2,1)S(1)}, u32[]{:S(2)}, u32[]{:S(2)}) collective-permute-start(bf16[8,2,4,2,1920]{4,3,2,1,0:T(2,128)(2,1)S(1)} %get-tuple-element.19), channel_id=1, source_target_pairs={{0,2},{1,3},{2,0},{3,1},{4,6},{5,7},{6,4},{7,5},{8,10},{9,11},{10,... | collective-permute-start | bytes 1474568 | tf_op jit(solution)/shard_map/ppermute | solution.py:69
  21.4 35.0 %collective-permute-start.8 = (bf16[8,2,4,2,1920]{4,3,2,1,0:T(2,128)(2,1)S(1)}, bf16[8,2,4,2,1920]{4,3,2,1,0:T(2,128)(2,1)S(1)}, u32[]{:S(2)}, u32[]{:S(2)}) collective-permute-start(bf16[8,2,4,2,1920]{4,3,2,1,0:T(2,128)(2,1)S(1)} %get-tuple-element.20), channel_id=1, source_target_pairs={{0,1},{1,2},{2,3},{3,0},{4,5},{5,6},{6,7},{7,4},{8,9},{9,10},{10,1... | collective-permute-start | bytes 1474568 | tf_op jit(solution)/shard_map/ppermute | solution.py:67
  39.0 21.3 %collective-permute-start.3 = (bf16[8,2,1,2,1920]{4,3,2,1,0:T(2,128)(2,1)S(1)}, bf16[8,2,1,2,1920]{4,3,2,1,0:T(2,128)(2,1)S(1)}, u32[]{:S(2)}, u32[]{:S(2)}) collective-permute-start(bf16[8,2,1,2,1920]{4,3,2,1,0:T(2,128)(2,1)S(1)} %get-tuple-element.14), channel_id=1, source_target_pairs={{0,3},{1,0},{2,1},{3,2},{4,7},{5,4},{6,5},{7,6},{8,11},{9,8},{10,9... | collective-permute-start | bytes 368648 | tf_op jit(solution)/shard_map/ppermute | solution.py:68
  42.1 18.1 %collective-permute-start.4 = (bf16[8,2,1,2,1920]{4,3,2,1,0:T(2,128)(2,1)S(1)}, bf16[8,2,1,2,1920]{4,3,2,1,0:T(2,128)(2,1)S(1)}, u32[]{:S(2)}, u32[]{:S(2)}) collective-permute-start(bf16[8,2,1,2,1920]{4,3,2,1,0:T(2,128)(2,1)S(1)} %get-tuple-element.15), channel_id=1, source_target_pairs={{0,2},{1,3},{2,0},{3,1},{4,6},{5,7},{6,4},{7,5},{8,10},{9,11},{10,... | collective-permute-start | bytes 368648 | tf_op jit(solution)/shard_map/ppermute | solution.py:69
  44.7 15.5 %collective-permute-start.5 = (bf16[8,2,1,2,1920]{4,3,2,1,0:T(2,128)(2,1)S(1)}, bf16[8,2,1,2,1920]{4,3,2,1,0:T(2,128)(2,1)S(1)}, u32[]{:S(2)}, u32[]{:S(2)}) collective-permute-start(bf16[8,2,1,2,1920]{4,3,2,1,0:T(2,128)(2,1)S(1)} %get-tuple-element.16), channel_id=1, source_target_pairs={{0,1},{1,2},{2,3},{3,0},{4,5},{5,6},{6,7},{7,4},{8,9},{9,10},{10,1... | collective-permute-start | bytes 368648 | tf_op jit(solution)/shard_map/ppermute | solution.py:67

commit v13 on v12

--- a/solution.py
+++ b/solution.py
@@ -33,15 +33,18 @@
     copies = []
     for step, out in zip(steps, outs):
         taker = lax.rem(group + step, 4)
-        tiles = pl.ds(lax.rem(taker, 2) * HALF + first, ITEMS)
+        start = lax.rem(taker, 2) * HALF + first
         lines = pl.ds(lax.div(taker, 2) * LOOK_AZ + low, high - low)
-        for date in range(2):
-            copies.append(
-                pltpu.make_async_copy(
-                    images.at[date, tiles, lines], out.at[:, date], sem.at[len(copies)]
+        for tile in range(ITEMS):
+            for date in range(2):
+                copies.append(
+                    pltpu.make_async_copy(
+                        images.at[date, start + tile, lines],
+                        out.at[tile, date],
+                        sem.at[len(copies)],
+                    )
                 )
-            )
-            copies[-1].start()
+                copies[-1].start()
     for copy in copies:
         copy.wait()
 
@@ -55,7 +58,7 @@
         out_shape=[block] * len(steps),
         in_specs=[HBM, ANYWHERE][: len(operands)],
         out_specs=[VMEM] * len(steps),
-        scratch_shapes=[pltpu.SemaphoreType.DMA((2 * len(steps),))],
+        scratch_shapes=[pltpu.SemaphoreType.DMA((2 * ITEMS * len(steps),))],
         compiler_params=pltpu.CompilerParams(vmem_limit_bytes=limit << 20),
     )(*operands)
 

time: 90.2 us -> 90 us (level)
  Pallas kernels: 19.4 us -> 24.1 us
  waiting for transfers between devices: 29.4 us -> 25.7 us
  blocking collectives: 26.2 us -> 24.8 us
    pallas_call x6, Pallas kernels: 6.56 us -> 11.3 us  [cut(): pl.pallas_call(functools.partial(cut_kernel, chunk, steps), out_shape=[bl...]
    ppermute x3, waiting for transfers between devices: 10.9 us -> 7.32 us  [meet(): two = lax.ppermute(to2, 'date', ring(2))]
    all_to_all x1, blocking collectives: 26.2 us -> 24.8 us  [on_device(): lax.all_to_all(gamma.reshape(128, 8, LCOL), ('tile', 'date'), split_axis=...]
  transfers between devices with their start and end apart: 9 -> 9, of which waited for: 4 -> 5; matrix products, arithmetic and copies ran while one was open for 0% -> 0% of each run, Pallas kernels for 15% -> 20%
where the time goes in v13:
time: 90 us; the launch traced here: 89.8 us
  waiting for transfers between devices  25.7 us (29%)
  blocking collectives  24.8 us (28%)
  Pallas kernels  24.1 us (27%)
  starting transfers between devices  13.9 us (15%)
    all_to_all x1, blocking collectives, on_device(): lax.all_to_all(gamma.reshape(128, 8, LCOL), ('tile', 'date'), split_axis=...  24.8 us
    ppermute x3, waiting for transfers between devices, meet(): three = lax.ppermute(to1, 'date', ring(1))  16.4 us
    pallas_call x3, Pallas kernels, looks(): pl.pallas_call(kernel, out_shape=out_shape, grid_spec=pltpu.PrefetchScala...  11.5 us
    pallas_call x6, Pallas kernels, cut(): pl.pallas_call(functools.partial(cut_kernel, chunk, steps), out_shape=[bl...  11.3 us
    ppermute x3, waiting for transfers between devices, meet(): two = lax.ppermute(to2, 'date', ring(2))  7.32 us
    ppermute x3, starting transfers between devices, meet(): one = lax.ppermute(to3, 'date', ring(3))  6.33 us
    ppermute x3, starting transfers between devices, meet(): three = lax.ppermute(to1, 'date', ring(1))  4.04 us
    ppermute x3, starting transfers between devices, meet(): two = lax.ppermute(to2, 'date', ring(2))  3.5 us
  transfers between devices with their start and end apart: 9, of which 5 were waited for; matrix products, arithmetic and copies ran while one was open for 0% of the time, Pallas kernels for 20%

profile of v13, /device:TPU:1, one launch (start us, length us, event | category | flops | bytes accessed | tf_op | source)
XLA Modules:
  0.0 89.8 jit_solution(12076343621948563705)
XLA Ops:
  0.0 2.2 %shard_map.46 = bf16[8,2,5,2,1920]{4,3,2,1,0:T(2,128)(2,1)} custom-call(bf16[2,32,10,2,1920]{4,3,2,1,0:T(2,128)(2,1)} %bitcast.7), custom_call_target="tpu_custom_call" | custom-call | tf_op jit(solution)/shard_map/pallas_call | solution.py:56
  2.2 2.1 %collective-permute-start = (bf16[8,2,5,2,1920]{4,3,2,1,0:T(2,128)(2,1)}, bf16[8,2,5,2,1920]{4,3,2,1,0:T(2,128)(2,1)S(1)}, u32[]{:S(2)}, u32[]{:S(2)}) collective-permute-start(bf16[8,2,5,2,1920]{4,3,2,1,0:T(2,128)(2,1)} %shard_map.46), channel_id=1, source_target_pairs={{0,1},{1,2},{2,3},{3,0},{4,5},{5,6},{6,7},{7,4},{8,9},{9,10},{10,1... | collective-permute-start | bytes 1843208 | tf_op jit(solution)/shard_map/ppermute | solution.py:70
  4.3 2.0 %shard_map.48 = bf16[8,2,5,2,1920]{4,3,2,1,0:T(2,128)(2,1)} custom-call(bf16[2,32,10,2,1920]{4,3,2,1,0:T(2,128)(2,1)} %bitcast.8), custom_call_target="tpu_custom_call" | custom-call | tf_op jit(solution)/shard_map/pallas_call | solution.py:56
  6.3 1.4 %collective-permute-start.1 = (bf16[8,2,5,2,1920]{4,3,2,1,0:T(2,128)(2,1)}, bf16[8,2,5,2,1920]{4,3,2,1,0:T(2,128)(2,1)S(1)}, u32[]{:S(2)}, u32[]{:S(2)}) collective-permute-start(bf16[8,2,5,2,1920]{4,3,2,1,0:T(2,128)(2,1)} %shard_map.48), channel_id=1, source_target_pairs={{0,3},{1,0},{2,1},{3,2},{4,7},{5,4},{6,5},{7,6},{8,11},{9,8},{10,9... | collective-permute-start | bytes 1843208 | tf_op jit(solution)/shard_map/ppermute | solution.py:71
  7.8 2.0 %shard_map.49 = bf16[8,2,5,2,1920]{4,3,2,1,0:T(2,128)(2,1)} custom-call(bf16[2,32,10,2,1920]{4,3,2,1,0:T(2,128)(2,1)} %bitcast.9), custom_call_target="tpu_custom_call" | custom-call | tf_op jit(solution)/shard_map/pallas_call | solution.py:56
  9.8 1.7 %collective-permute-start.2 = (bf16[8,2,5,2,1920]{4,3,2,1,0:T(2,128)(2,1)}, bf16[8,2,5,2,1920]{4,3,2,1,0:T(2,128)(2,1)S(1)}, u32[]{:S(2)}, u32[]{:S(2)}) collective-permute-start(bf16[8,2,5,2,1920]{4,3,2,1,0:T(2,128)(2,1)} %shard_map.49), channel_id=1, source_target_pairs={{0,2},{1,3},{2,0},{3,1},{4,6},{5,7},{6,4},{7,5},{8,10},{9,11},{10,... | collective-permute-start | bytes 1843208 | tf_op jit(solution)/shard_map/ppermute | solution.py:72
  12.3 6.7 %collective-permute-done.rest_0_.three = bf16[8,2,5,2,1920]{4,3,2,1,0:T(2,128)(2,1)S(1)} collective-permute-done((bf16[8,2,5,2,1920]{4,3,2,1,0:T(2,128)(2,1)}, bf16[8,2,5,2,1920]{4,3,2,1,0:T(2,128)(2,1)S(1)}, u32[]{:S(2)}, u32[]{:S(2)}) %collective-permute-start) | collective-permute-done | bytes 614432 | tf_op jit(solution)/shard_map/ppermute | solution.py:70
  18.9 3.1 %shard_map.52 = (bf16[8,2,4,2,1920]{4,3,2,1,0:T(2,128)(2,1)S(1)}, bf16[8,2,4,2,1920]{4,3,2,1,0:T(2,128)(2,1)S(1)}, bf16[8,2,4,2,1920]{4,3,2,1,0:T(2,128)(2,1)S(1)}, bf16[8,2,4,2,1920]{4,3,2,1,0:T(2,128)(2,1)S(1)}) custom-call(bf16[2,32,10,2,1920]{4,3,2,1,0:T(2,128)(2,1)S(1)} %bitcast.12, bf16[8,2,5,2,1920]{4,3,2,1,0:T(2,128)(2,1)S(1)} %collective-permute-done.rest_0_.three), custom_call_target="tpu_custom_call" | custom-call | tf_op jit(solution)/shard_map/pallas_call | solution.py:56
  22.0 1.7 %collective-permute-start.6 = (bf16[8,2,4,2,1920]{4,3,2,1,0:T(2,128)(2,1)S(1)}, bf16[8,2,4,2,1920]{4,3,2,1,0:T(2,128)(2,1)S(1)}, u32[]{:S(2)}, u32[]{:S(2)}) collective-permute-start(bf16[8,2,4,2,1920]{4,3,2,1,0:T(2,128)(2,1)S(1)} %get-tuple-element.18), channel_id=1, source_target_pairs={{0,3},{1,0},{2,1},{3,2},{4,7},{5,4},{6,5},{7,6},{8,11},{9,8},{10,9... | collective-permute-start | bytes 1474568 | tf_op jit(solution)/shard_map/ppermute | solution.py:71
  24.2 0.6 collective-permute-start.8
  25.1 0.9 %shard_map.47.own = bf16[8,2,5,2,1920]{4,3,2,1,0:T(2,128)(2,1)S(1)} custom-call(bf16[2,32,10,2,1920]{4,3,2,1,0:T(2,128)(2,1)S(1)} %bitcast.13, bf16[8,2,5,2,1920]{4,3,2,1,0:T(2,128)(2,1)S(1)} %collective-permute-done.rest_0_.three), custom_call_target="tpu_custom_call" | custom-call | tf_op jit(solution)/shard_map/pallas_call | solution.py:56
  26.1 7.3 %collective-permute-done.2.two = bf16[8,2,5,2,1920]{4,3,2,1,0:T(2,128)(2,1)S(1)} collective-permute-done((bf16[8,2,5,2,1920]{4,3,2,1,0:T(2,128)(2,1)}, bf16[8,2,5,2,1920]{4,3,2,1,0:T(2,128)(2,1)S(1)}, u32[]{:S(2)}, u32[]{:S(2)}) %collective-permute-start.2) | collective-permute-done | bytes 614432 | tf_op jit(solution)/shard_map/ppermute | solution.py:72
  33.4 5.4 %shard_map.50.rest_0_.after.given = f32[32,4,8,128]{3,2,1,0:T(8,128)S(1)} custom-call(s32[2,16]{1,0:T(2,128)S(1)} %bitcast.17, bf16[8,2,5,2,1920]{4,3,2,1,0:T(2,128)(2,1)S(1)} %shard_map.47.own, bf16[8,2,5,2,1920]{4,3,2,1,0:T(2,128)(2,1)S(1)} %collective-permute-done.1.one, bf16[8,2,5,2,1920]{4,3,2,1,0:T(2,128)(2,1)S(1)} %collective-permute-done.2.two, ...), custom_call_target="tpu_custom_call" | custom-call | flops 326860800 | bytes 2457600 | tf_op jit(solution)/shard_map/pallas_call | solution.py:157
  38.9 1.1 %shard_map.51 = (bf16[8,2,1,2,1920]{4,3,2,1,0:T(2,128)(2,1)S(1)}, bf16[8,2,1,2,1920]{4,3,2,1,0:T(2,128)(2,1)S(1)}, bf16[8,2,1,2,1920]{4,3,2,1,0:T(2,128)(2,1)S(1)}, bf16[8,2,1,2,1920]{4,3,2,1,0:T(2,128)(2,1)S(1)}) custom-call(bf16[2,32,10,2,1920]{4,3,2,1,0:T(2,128)(2,1)S(1)} %bitcast.14, f32[32,4,8,128]{3,2,1,0:T(8,128)S(1)} %shard_map.50.rest_0_.after.given), custom_call_target="tpu_custom_call" | custom-call | tf_op jit(solution)/shard_map/pallas_call | solution.py:56
  40.0 3.3 %collective-permute-start.3 = (bf16[8,2,1,2,1920]{4,3,2,1,0:T(2,128)(2,1)S(1)}, bf16[8,2,1,2,1920]{4,3,2,1,0:T(2,128)(2,1)S(1)}, u32[]{:S(2)}, u32[]{:S(2)}) collective-permute-start(bf16[8,2,1,2,1920]{4,3,2,1,0:T(2,128)(2,1)S(1)} %get-tuple-element.14), channel_id=1, source_target_pairs={{0,3},{1,0},{2,1},{3,2},{4,7},{5,4},{6,5},{7,6},{8,11},{9,8},{10,9... | collective-permute-start | bytes 368648 | tf_op jit(solution)/shard_map/ppermute | solution.py:71
  43.2 1.2 %collective-permute-start.4 = (bf16[8,2,1,2,1920]{4,3,2,1,0:T(2,128)(2,1)S(1)}, bf16[8,2,1,2,1920]{4,3,2,1,0:T(2,128)(2,1)S(1)}, u32[]{:S(2)}, u32[]{:S(2)}) collective-permute-start(bf16[8,2,1,2,1920]{4,3,2,1,0:T(2,128)(2,1)S(1)} %get-tuple-element.15), channel_id=1, source_target_pairs={{0,2},{1,3},{2,0},{3,1},{4,6},{5,7},{6,4},{7,5},{8,10},{9,11},{10,... | collective-permute-start | bytes 368648 | tf_op jit(solution)/shard_map/ppermute | solution.py:72
  44.5 2.0 %collective-permute-done.6.one = bf16[8,2,4,2,1920]{4,3,2,1,0:T(2,128)(2,1)S(1)} collective-permute-done((bf16[8,2,4,2,1920]{4,3,2,1,0:T(2,128)(2,1)S(1)}, bf16[8,2,4,2,1920]{4,3,2,1,0:T(2,128)(2,1)S(1)}, u32[]{:S(2)}, u32[]{:S(2)}) %collective-permute-start.6) | collective-permute-done | bytes 491552 | tf_op jit(solution)/shard_map/ppermute | solution.py:71
  46.4 1.3 %collective-permute-start.5 = (bf16[8,2,1,2,1920]{4,3,2,1,0:T(2,128)(2,1)S(1)}, bf16[8,2,1,2,1920]{4,3,2,1,0:T(2,128)(2,1)S(1)}, u32[]{:S(2)}, u32[]{:S(2)}) collective-permute-start(bf16[8,2,1,2,1920]{4,3,2,1,0:T(2,128)(2,1)S(1)} %get-tuple-element.16), channel_id=1, source_target_pairs={{0,1},{1,2},{2,3},{3,0},{4,5},{5,6},{6,7},{7,4},{8,9},{9,10},{10,1... | collective-permute-start | bytes 368648 | tf_op jit(solution)/shard_map/ppermute | solution.py:70
  47.7 8.8 %collective-permute-done.8.three = bf16[8,2,4,2,1920]{4,3,2,1,0:T(2,128)(2,1)S(1)} collective-permute-done((bf16[8,2,4,2,1920]{4,3,2,1,0:T(2,128)(2,1)S(1)}, bf16[8,2,4,2,1920]{4,3,2,1,0:T(2,128)(2,1)S(1)}, u32[]{:S(2)}, u32[]{:S(2)}) %collective-permute-start.8) | collective-permute-done | bytes 491552 | tf_op jit(solution)/shard_map/ppermute | solution.py:70
  56.5 3.8 %shard_map.53.most = f32[320,128]{1,0:T(8,128)S(1)} custom-call(s32[2,16]{1,0:T(2,128)S(1)} %bitcast.18, bf16[8,2,4,2,1920]{4,3,2,1,0:T(2,128)(2,1)S(1)} %get-tuple-element.17.own, bf16[8,2,4,2,1920]{4,3,2,1,0:T(2,128)(2,1)S(1)} %collective-permute-done.6.one, bf16[8,2,4,2,1920]{4,3,2,1,0:T(2,128)(2,1)S(1)} %collective-permute-done.7.two, ...), custom_call_target="tpu_custom_call" | custom-call | flops 324403200 | bytes 1966080 | tf_op jit(solution)/shard_map/pallas_call | solution.py:157
  60.3 0.9 %collective-permute-done.5.three = bf16[8,2,1,2,1920]{4,3,2,1,0:T(2,128)(2,1)S(1)} collective-permute-done((bf16[8,2,1,2,1920]{4,3,2,1,0:T(2,128)(2,1)S(1)}, bf16[8,2,1,2,1920]{4,3,2,1,0:T(2,128)(2,1)S(1)}, u32[]{:S(2)}, u32[]{:S(2)}) %collective-permute-start.5) | collective-permute-done | bytes 122912 | tf_op jit(solution)/shard_map/ppermute | solution.py:70
  61.3 2.3 %shard_map.54 = f32[32,4,8,128]{3,2,1,0:T(8,128)S(1)} custom-call(s32[2,16]{1,0:T(2,128)S(1)} %bitcast.19, bf16[8,2,1,2,1920]{4,3,2,1,0:T(2,128)(2,1)S(1)} %get-tuple-element.13.own, bf16[8,2,1,2,1920]{4,3,2,1,0:T(2,128)(2,1)S(1)} %collective-permute-done.3.one, ...), custom_call_target="tpu_custom_call", output_to_operand_aliasing={{}: (7, {})} | custom-call | flops 317030400 | bytes 491520 | tf_op jit(solution)/shard_map/pallas_call | solution.py:157
  63.6 24.8 %all_to_all.5 = f32[128,8,128]{2,1,0:T(8,128)S(1)} all-to-all(f32[128,8,128]{2,1,0:T(8,128)S(1)} %bitcast.15), channel_id=1, replica_groups=mesh['tile'=32,'date'=4] {'tile','date'}, dimensions={0} | all-to-all | bytes 1048576 | tf_op jit(solution)/shard_map/all_to_all | solution.py:217
  88.4 1.3 %shard_map.55 = f32[4,2,64,128]{3,2,1,0:T(8,128)} custom-call(s32[33]{0:T(128)S(1)} %pad_add_fusion.table, f32[32,4,8,128]{3,2,1,0:T(8,128)S(1)} %bitcast.16), custom_call_target="tpu_custom_call" | custom-call | tf_op jit(solution)/shard_map/pallas_call | solution.py:220
  (17 shorter events, 1.0 us)
Async XLA Ops:
  0.0 18.9 %slice-start = ((s8[4915200]{0:T(1024)(128)(4,1)}), s8[4194304]{0:T(1024)(128)(4,1)S(1)}, s32[]{:S(2)}) async-start(s8[4915200]{0:T(1024)(128)(4,1)} %bitcast.10), calls=%async_computation.1 | async-start | bytes 8388608
  2.2 10.0 %copy-start.1 = (s32[1,32]{1,0:T(1,128)S(1)}, s32[1,32]{1,0:T(1,128)}, u32[]{:S(2)}) copy-start(s32[1,32]{1,0:T(1,128)} %param.5) | copy-start | bytes 388
  2.2 16.7 %slice-start.1 = ((s8[4915200]{0:T(1024)(128)(4,1)}), s8[720896]{0:T(1024)(128)(4,1)S(1)}, s32[]{:S(2)}) async-start(s8[4915200]{0:T(1024)(128)(4,1)} %bitcast.10), calls=%async_computation.2 | async-start | bytes 1441792
  2.2 16.7 %collective-permute-start = (bf16[8,2,5,2,1920]{4,3,2,1,0:T(2,128)(2,1)}, bf16[8,2,5,2,1920]{4,3,2,1,0:T(2,128)(2,1)S(1)}, u32[]{:S(2)}, u32[]{:S(2)}) collective-permute-start(bf16[8,2,5,2,1920]{4,3,2,1,0:T(2,128)(2,1)} %shard_map.46), channel_id=1, source_target_pairs={{0,1},{1,2},{2,3},{3,0},{4,5},{5,6},{6,7},{7,4},{8,9},{9,10},{10,1... | collective-permute-start | bytes 1843208 | tf_op jit(solution)/shard_map/ppermute | solution.py:70
  6.3 19.8 %collective-permute-start.1 = (bf16[8,2,5,2,1920]{4,3,2,1,0:T(2,128)(2,1)}, bf16[8,2,5,2,1920]{4,3,2,1,0:T(2,128)(2,1)S(1)}, u32[]{:S(2)}, u32[]{:S(2)}) collective-permute-start(bf16[8,2,5,2,1920]{4,3,2,1,0:T(2,128)(2,1)} %shard_map.48), channel_id=1, source_target_pairs={{0,3},{1,0},{2,1},{3,2},{4,7},{5,4},{6,5},{7,6},{8,11},{9,8},{10,9... | collective-permute-start | bytes 1843208 | tf_op jit(solution)/shard_map/ppermute | solution.py:71
  9.8 23.7 %collective-permute-start.2 = (bf16[8,2,5,2,1920]{4,3,2,1,0:T(2,128)(2,1)}, bf16[8,2,5,2,1920]{4,3,2,1,0:T(2,128)(2,1)S(1)}, u32[]{:S(2)}, u32[]{:S(2)}) collective-permute-start(bf16[8,2,5,2,1920]{4,3,2,1,0:T(2,128)(2,1)} %shard_map.49), channel_id=1, source_target_pairs={{0,2},{1,3},{2,0},{3,1},{4,6},{5,7},{6,4},{7,5},{8,10},{9,11},{10,... | collective-permute-start | bytes 1843208 | tf_op jit(solution)/shard_map/ppermute | solution.py:72
  12.3 21.2 %copy-start = (s32[16,2]{0,1:T(2,128)S(1)}, s32[16,2]{0,1:T(2,128)}, u32[]{:S(2)}) copy-start(s32[16,2]{0,1:T(2,128)} %param.7) | copy-start | bytes 388
  22.0 24.4 %collective-permute-start.6 = (bf16[8,2,4,2,1920]{4,3,2,1,0:T(2,128)(2,1)S(1)}, bf16[8,2,4,2,1920]{4,3,2,1,0:T(2,128)(2,1)S(1)}, u32[]{:S(2)}, u32[]{:S(2)}) collective-permute-start(bf16[8,2,4,2,1920]{4,3,2,1,0:T(2,128)(2,1)S(1)} %get-tuple-element.18), channel_id=1, source_target_pairs={{0,3},{1,0},{2,1},{3,2},{4,7},{5,4},{6,5},{7,6},{8,11},{9,8},{10,9... | collective-permute-start | bytes 1474568 | tf_op jit(solution)/shard_map/ppermute | solution.py:71
  23.7 24.1 %collective-permute-start.7 = (bf16[8,2,4,2,1920]{4,3,2,1,0:T(2,128)(2,1)S(1)}, bf16[8,2,4,2,1920]{4,3,2,1,0:T(2,128)(2,1)S(1)}, u32[]{:S(2)}, u32[]{:S(2)}) collective-permute-start(bf16[8,2,4,2,1920]{4,3,2,1,0:T(2,128)(2,1)S(1)} %get-tuple-element.19), channel_id=1, source_target_pairs={{0,2},{1,3},{2,0},{3,1},{4,6},{5,7},{6,4},{7,5},{8,10},{9,11},{10,... | collective-permute-start | bytes 1474568 | tf_op jit(solution)/shard_map/ppermute | solution.py:72
  24.2 32.3 %collective-permute-start.8 = (bf16[8,2,4,2,1920]{4,3,2,1,0:T(2,128)(2,1)S(1)}, bf16[8,2,4,2,1920]{4,3,2,1,0:T(2,128)(2,1)S(1)}, u32[]{:S(2)}, u32[]{:S(2)}) collective-permute-start(bf16[8,2,4,2,1920]{4,3,2,1,0:T(2,128)(2,1)S(1)} %get-tuple-element.20), channel_id=1, source_target_pairs={{0,1},{1,2},{2,3},{3,0},{4,5},{5,6},{6,7},{7,4},{8,9},{9,10},{10,1... | collective-permute-start | bytes 1474568 | tf_op jit(solution)/shard_map/ppermute | solution.py:70
  40.0 20.4 %collective-permute-start.3 = (bf16[8,2,1,2,1920]{4,3,2,1,0:T(2,128)(2,1)S(1)}, bf16[8,2,1,2,1920]{4,3,2,1,0:T(2,128)(2,1)S(1)}, u32[]{:S(2)}, u32[]{:S(2)}) collective-permute-start(bf16[8,2,1,2,1920]{4,3,2,1,0:T(2,128)(2,1)S(1)} %get-tuple-element.14), channel_id=1, source_target_pairs={{0,3},{1,0},{2,1},{3,2},{4,7},{5,4},{6,5},{7,6},{8,11},{9,8},{10,9... | collective-permute-start | bytes 368648 | tf_op jit(solution)/shard_map/ppermute | solution.py:71
  43.2 17.1 %collective-permute-start.4 = (bf16[8,2,1,2,1920]{4,3,2,1,0:T(2,128)(2,1)S(1)}, bf16[8,2,1,2,1920]{4,3,2,1,0:T(2,128)(2,1)S(1)}, u32[]{:S(2)}, u32[]{:S(2)}) collective-permute-start(bf16[8,2,1,2,1920]{4,3,2,1,0:T(2,128)(2,1)S(1)} %get-tuple-element.15), channel_id=1, source_target_pairs={{0,2},{1,3},{2,0},{3,1},{4,6},{5,7},{6,4},{7,5},{8,10},{9,11},{10,... | collective-permute-start | bytes 368648 | tf_op jit(solution)/shard_map/ppermute | solution.py:72
  46.4 14.8 %collective-permute-start.5 = (bf16[8,2,1,2,1920]{4,3,2,1,0:T(2,128)(2,1)S(1)}, bf16[8,2,1,2,1920]{4,3,2,1,0:T(2,128)(2,1)S(1)}, u32[]{:S(2)}, u32[]{:S(2)}) collective-permute-start(bf16[8,2,1,2,1920]{4,3,2,1,0:T(2,128)(2,1)S(1)} %get-tuple-element.16), channel_id=1, source_target_pairs={{0,1},{1,2},{2,3},{3,0},{4,5},{5,6},{6,7},{7,4},{8,9},{9,10},{10,1... | collective-permute-start | bytes 368648 | tf_op jit(solution)/shard_map/ppermute | solution.py:70

commit v14 on v11

--- a/solution.py
+++ b/solution.py
@@ -70,7 +70,7 @@
     return own, one, two, three
 
 
-def add_lines(epochs, blocks, box, img, hi, lo):
+def add_lines(epochs, blocks, box, img, terms):
     group = lax.axis_index("date")
     lines = blocks[0].shape[2]
     for step, block in enumerate(blocks):
@@ -82,8 +82,10 @@
 
     def split(values, row):
         upper = values.astype(jnp.bfloat16)
-        hi[pl.ds(row, 16), :] = upper
-        lo[pl.ds(row, 16), :] = (values - upper.astype(jnp.float32)).astype(jnp.bfloat16)
+        terms[pl.ds(row, 16), :] = upper
+        terms[pl.ds(ROWS + row, 16), :] = (values - upper.astype(jnp.float32)).astype(
+            jnp.bfloat16
+        )
 
     def power(half, carry):
         total = []
@@ -112,9 +114,8 @@
         return carry
 
     lax.fori_loop(0, PAIRS, cross, 0)
-    return jnp.dot(hi[...], box[...], preferred_element_type=jnp.float32) + jnp.dot(
-        lo[...], box[...], preferred_element_type=jnp.float32
-    )
+    both = jnp.dot(terms[...], box[...], preferred_element_type=jnp.float32)
+    return both[:ROWS] + both[ROWS:]
 
 
 def coherence(epochs, part, sums, out):
@@ -131,20 +132,20 @@
         out[pl.ds(start, ITEMS), owner] = jnp.swapaxes(jnp.stack(rows, axis=0), 0, 1)
 
 
-def whole_kernel(epochs, own, one, two, three, box, table, out, img, hi, lo, sums):
+def whole_kernel(epochs, own, one, two, three, box, table, out, img, terms, sums):
     del table
-    sums[...] = add_lines(epochs, (own, one, two, three), box, img, hi, lo) * SCALE
+    sums[...] = add_lines(epochs, (own, one, two, three), box, img, terms) * SCALE
     coherence(epochs, 0, sums, out)
 
 
-def most_kernel(epochs, own, one, two, three, box, after, later, img, hi, lo, sums):
+def most_kernel(epochs, own, one, two, three, box, after, later, img, terms, sums):
     del after, sums
-    later[...] = add_lines(epochs, (own, one, two, three), box, img, hi, lo)
-
-
-def last_kernel(epochs, own, one, two, three, box, most, given, out, img, hi, lo, sums):
+    later[...] = add_lines(epochs, (own, one, two, three), box, img, terms)
+
+
+def last_kernel(epochs, own, one, two, three, box, most, given, out, img, terms, sums):
     del given
-    total = add_lines(epochs, (own, one, two, three), box, img, hi, lo)
+    total = add_lines(epochs, (own, one, two, three), box, img, terms)
     sums[...] = (total + most[...]) * SCALE
     coherence(epochs, 1, sums, out)
 
@@ -161,8 +162,7 @@
             out_specs=jax.tree.map(lambda _: VMEM, out_shape),
             scratch_shapes=[
                 pltpu.VMEM((DATES, lines, 16, RG), jnp.float32),
-                pltpu.VMEM((ROWS, RG), jnp.bfloat16),
-                pltpu.VMEM((ROWS, RG), jnp.bfloat16),
+                pltpu.VMEM((2 * ROWS, RG), jnp.bfloat16),
                 pltpu.VMEM((ROWS, LCOL), jnp.float32),
             ],
         ),

time: 88.1 us -> 88.2 us (level)
  no operation moved by 1% of the time
where the time goes in v14:
time: 88.2 us; the launch traced here: 88 us
  waiting for transfers between devices  37.2 us (42%)
  blocking collectives  23.1 us (26%)
  Pallas kernels  13.6 us (15%)
  starting transfers between devices  10.5 us (12%)
  local copies, waits for them, and re-layouts  2.42 us (3%)
    ppermute x3, waiting for transfers between devices, meet(): three = lax.ppermute(to1, 'date', ring(1))  23.2 us
    all_to_all x1, blocking collectives, on_device(): lax.all_to_all(gamma.reshape(128, 8, LCOL), ('tile', 'date'), split_axis=...  23.1 us
    pallas_call x3, Pallas kernels, looks(): pl.pallas_call(kernel, out_shape=out_shape, grid_spec=pltpu.PrefetchScala...  11.4 us
    ppermute x3, waiting for transfers between devices, meet(): two = lax.ppermute(to2, 'date', ring(2))  11 us
    ppermute x3, starting transfers between devices, meet(): one = lax.ppermute(to3, 'date', ring(3))  4.17 us
    ppermute x3, starting transfers between devices, meet(): two = lax.ppermute(to2, 'date', ring(2))  3.41 us
    ppermute x3, waiting for transfers between devices, meet(): one = lax.ppermute(to3, 'date', ring(3))  3.05 us
    ppermute x3, starting transfers between devices, meet(): three = lax.ppermute(to1, 'date', ring(1))  2.92 us
  transfers between devices with their start and end apart: 9, of which 5 were waited for; matrix products, arithmetic and copies ran while one was open for 0% of the time, Pallas kernels for 11%

profile of v14, /device:TPU:1, one launch (start us, length us, event | category | flops | bytes accessed | tf_op | source)
XLA Modules:
  0.0 88.0 jit_solution(394245016241176407)
XLA Ops:
  0.0 2.4 %copy-done = bf16[2,1,32,2,10,1920]{5,3,4,2,1,0:T(2,128)(2,1)S(1)} copy-done((bf16[2,1,32,2,10,1920]{5,3,4,2,1,0:T(2,128)(2,1)S(1)}, bf16[2,1,32,2,10,1920]{5,3,4,2,1,0:T(2,128)(2,1)}, u32[]{:S(2)}) %copy-start) | copy-done | bytes 4915224
  2.4 0.3 shard_map.46
  2.7 2.1 %collective-permute-start.2 = (bf16[8,2,5,2,1920]{4,3,2,1,0:T(2,128)(2,1)S(1)}, bf16[8,2,5,2,1920]{4,3,2,1,0:T(2,128)(2,1)S(1)}, u32[]{:S(2)}, u32[]{:S(2)}) collective-permute-start(bf16[8,2,5,2,1920]{4,3,2,1,0:T(2,128)(2,1)S(1)} %get-tuple-element.20), channel_id=1, source_target_pairs={{0,1},{1,2},{2,3},{3,0},{4,5},{5,6},{6,7},{7,4},{8,9},{9,10},{10,1... | collective-permute-start | bytes 1843208 | tf_op jit(solution)/shard_map/ppermute | solution.py:67
  4.8 1.3 %collective-permute-start = (bf16[8,2,5,2,1920]{4,3,2,1,0:T(2,128)(2,1)S(1)}, bf16[8,2,5,2,1920]{4,3,2,1,0:T(2,128)(2,1)S(1)}, u32[]{:S(2)}, u32[]{:S(2)}) collective-permute-start(bf16[8,2,5,2,1920]{4,3,2,1,0:T(2,128)(2,1)S(1)} %get-tuple-element.18), channel_id=1, source_target_pairs={{0,3},{1,0},{2,1},{3,2},{4,7},{5,4},{6,5},{7,6},{8,11},{9,8},{10,9... | collective-permute-start | bytes 1843208 | tf_op jit(solution)/shard_map/ppermute | solution.py:68
  6.2 1.6 %collective-permute-start.1 = (bf16[8,2,5,2,1920]{4,3,2,1,0:T(2,128)(2,1)S(1)}, bf16[8,2,5,2,1920]{4,3,2,1,0:T(2,128)(2,1)S(1)}, u32[]{:S(2)}, u32[]{:S(2)}) collective-permute-start(bf16[8,2,5,2,1920]{4,3,2,1,0:T(2,128)(2,1)S(1)} %get-tuple-element.19), channel_id=1, source_target_pairs={{0,2},{1,3},{2,0},{3,1},{4,6},{5,7},{6,4},{7,5},{8,10},{9,11},{10,... | collective-permute-start | bytes 1843208 | tf_op jit(solution)/shard_map/ppermute | solution.py:69
  8.6 10.7 %collective-permute-done.2.three.rest_0_ = bf16[8,2,5,2,1920]{4,3,2,1,0:T(2,128)(2,1)S(1)} collective-permute-done((bf16[8,2,5,2,1920]{4,3,2,1,0:T(2,128)(2,1)S(1)}, bf16[8,2,5,2,1920]{4,3,2,1,0:T(2,128)(2,1)S(1)}, u32[]{:S(2)}, u32[]{:S(2)}) %collective-permute-start.2) | collective-permute-done | bytes 614432 | tf_op jit(solution)/shard_map/ppermute | solution.py:67
  19.2 0.4 shard_map.49
  19.7 1.7 %collective-permute-start.6 = (bf16[8,2,4,2,1920]{4,3,2,1,0:T(2,128)(2,1)S(1)}, bf16[8,2,4,2,1920]{4,3,2,1,0:T(2,128)(2,1)S(1)}, u32[]{:S(2)}, u32[]{:S(2)}) collective-permute-start(bf16[8,2,4,2,1920]{4,3,2,1,0:T(2,128)(2,1)S(1)} %get-tuple-element.26), channel_id=1, source_target_pairs={{0,3},{1,0},{2,1},{3,2},{4,7},{5,4},{6,5},{7,6},{8,11},{9,8},{10,9... | collective-permute-start | bytes 1474568 | tf_op jit(solution)/shard_map/ppermute | solution.py:68
  21.3 0.5 collective-permute-start.7
  21.8 0.6 collective-permute-start.8
  22.5 0.3 fusion.box
  22.8 11.0 %collective-permute-done.1.two = bf16[8,2,5,2,1920]{4,3,2,1,0:T(2,128)(2,1)S(1)} collective-permute-done((bf16[8,2,5,2,1920]{4,3,2,1,0:T(2,128)(2,1)S(1)}, bf16[8,2,5,2,1920]{4,3,2,1,0:T(2,128)(2,1)S(1)}, u32[]{:S(2)}, u32[]{:S(2)}) %collective-permute-start.1) | collective-permute-done | bytes 614432 | tf_op jit(solution)/shard_map/ppermute | solution.py:69
  33.8 5.2 %shard_map.47.rest_0_.after.given = f32[32,4,8,128]{3,2,1,0:T(8,128)S(1)} custom-call(s32[2,16]{1,0:T(2,128)S(1)} %bitcast.12, bf16[8,2,5,2,1920]{4,3,2,1,0:T(2,128)(2,1)S(1)} %get-tuple-element.17.own, bf16[8,2,5,2,1920]{4,3,2,1,0:T(2,128)(2,1)S(1)} %collective-permute-done.one, bf16[8,2,5,2,1920]{4,3,2,1,0:T(2,128)(2,1)S(1)} %collective-permute-done.1.two, ...), custom_call_target="tpu_custom_call" | custom-call | flops 326860800 | bytes 2457600 | tf_op jit(solution)/shard_map/pallas_call | solution.py:155
  39.0 0.2 shard_map.48
  39.2 1.2 %collective-permute-start.3 = (bf16[8,2,1,2,1920]{4,3,2,1,0:T(2,128)(2,1)S(1)}, bf16[8,2,1,2,1920]{4,3,2,1,0:T(2,128)(2,1)S(1)}, u32[]{:S(2)}, u32[]{:S(2)}) collective-permute-start(bf16[8,2,1,2,1920]{4,3,2,1,0:T(2,128)(2,1)S(1)} %get-tuple-element.22), channel_id=1, source_target_pairs={{0,3},{1,0},{2,1},{3,2},{4,7},{5,4},{6,5},{7,6},{8,11},{9,8},{10,9... | collective-permute-start | bytes 368648 | tf_op jit(solution)/shard_map/ppermute | solution.py:68
  40.4 1.2 %collective-permute-start.4 = (bf16[8,2,1,2,1920]{4,3,2,1,0:T(2,128)(2,1)S(1)}, bf16[8,2,1,2,1920]{4,3,2,1,0:T(2,128)(2,1)S(1)}, u32[]{:S(2)}, u32[]{:S(2)}) collective-permute-start(bf16[8,2,1,2,1920]{4,3,2,1,0:T(2,128)(2,1)S(1)} %get-tuple-element.23), channel_id=1, source_target_pairs={{0,2},{1,3},{2,0},{3,1},{4,6},{5,7},{6,4},{7,5},{8,10},{9,11},{10,... | collective-permute-start | bytes 368648 | tf_op jit(solution)/shard_map/ppermute | solution.py:69
  41.6 3.0 %collective-permute-done.6.one = bf16[8,2,4,2,1920]{4,3,2,1,0:T(2,128)(2,1)S(1)} collective-permute-done((bf16[8,2,4,2,1920]{4,3,2,1,0:T(2,128)(2,1)S(1)}, bf16[8,2,4,2,1920]{4,3,2,1,0:T(2,128)(2,1)S(1)}, u32[]{:S(2)}, u32[]{:S(2)}) %collective-permute-start.6) | collective-permute-done | bytes 491552 | tf_op jit(solution)/shard_map/ppermute | solution.py:68
  44.6 0.2 collective-permute-start.5
  44.8 12.0 %collective-permute-done.8.three = bf16[8,2,4,2,1920]{4,3,2,1,0:T(2,128)(2,1)S(1)} collective-permute-done((bf16[8,2,4,2,1920]{4,3,2,1,0:T(2,128)(2,1)S(1)}, bf16[8,2,4,2,1920]{4,3,2,1,0:T(2,128)(2,1)S(1)}, u32[]{:S(2)}, u32[]{:S(2)}) %collective-permute-start.8) | collective-permute-done | bytes 491552 | tf_op jit(solution)/shard_map/ppermute | solution.py:67
  56.8 3.8 %shard_map.50.most = f32[320,128]{1,0:T(8,128)S(1)} custom-call(s32[2,16]{1,0:T(2,128)S(1)} %bitcast.13, bf16[8,2,4,2,1920]{4,3,2,1,0:T(2,128)(2,1)S(1)} %get-tuple-element.25.own, bf16[8,2,4,2,1920]{4,3,2,1,0:T(2,128)(2,1)S(1)} %collective-permute-done.6.one, bf16[8,2,4,2,1920]{4,3,2,1,0:T(2,128)(2,1)S(1)} %collective-permute-done.7.two, ...), custom_call_target="tpu_custom_call" | custom-call | flops 324403200 | bytes 1966080 | tf_op jit(solution)/shard_map/pallas_call | solution.py:155
  60.6 0.5 collective-permute-done.5.three
  61.2 2.3 %shard_map.51 = f32[32,4,8,128]{3,2,1,0:T(8,128)S(1)} custom-call(s32[2,16]{1,0:T(2,128)S(1)} %bitcast.14, bf16[8,2,1,2,1920]{4,3,2,1,0:T(2,128)(2,1)S(1)} %get-tuple-element.21.own, bf16[8,2,1,2,1920]{4,3,2,1,0:T(2,128)(2,1)S(1)} %collective-permute-done.3.one, ...), custom_call_target="tpu_custom_call", output_to_operand_aliasing={{}: (7, {})} | custom-call | flops 317030400 | bytes 491520 | tf_op jit(solution)/shard_map/pallas_call | solution.py:155
  63.5 23.1 %all_to_all.5 = f32[128,8,128]{2,1,0:T(8,128)S(1)} all-to-all(f32[128,8,128]{2,1,0:T(8,128)S(1)} %bitcast.10), channel_id=1, replica_groups=mesh['tile'=32,'date'=4] {'tile','date'}, dimensions={0} | all-to-all | bytes 1048576 | tf_op jit(solution)/shard_map/all_to_all | solution.py:209
  86.7 1.4 %shard_map.52 = f32[4,2,64,128]{3,2,1,0:T(8,128)} custom-call(s32[33]{0:T(128)S(1)} %pad_add_fusion.table, f32[32,4,8,128]{3,2,1,0:T(8,128)S(1)} %bitcast.11), custom_call_target="tpu_custom_call" | custom-call | tf_op jit(solution)/shard_map/pallas_call | solution.py:212
  (13 shorter events, 0.1 us)
Async XLA Ops:
  0.0 8.5 %copy-start.3 = (s32[1,32]{1,0:T(1,128)S(1)}, s32[1,32]{1,0:T(1,128)}, u32[]{:S(2)}) copy-start(s32[1,32]{1,0:T(1,128)} %param.5) | copy-start | bytes 388
  0.0 2.4 %copy-start = (bf16[2,1,32,2,10,1920]{5,3,4,2,1,0:T(2,128)(2,1)S(1)}, bf16[2,1,32,2,10,1920]{5,3,4,2,1,0:T(2,128)(2,1)}, u32[]{:S(2)}) copy-start(bf16[2,1,32,2,10,1920]{5,3,4,2,1,0:T(2,128)(2,1)} %param.4) | copy-start | bytes 14745604
  2.4 16.8 %copy-start.1 = (bf16[2,1,32,2,10,1920]{5,3,4,2,1,0:T(2,128)(2,1)S(1)}, bf16[2,1,32,2,10,1920]{5,3,4,2,1,0:T(2,128)(2,1)}, u32[]{:S(2)}) copy-start(bf16[2,1,32,2,10,1920]{5,3,4,2,1,0:T(2,128)(2,1)} %param.4) | copy-start | bytes 14745604
  2.4 31.3 %copy-start.2 = (s32[16,2]{0,1:T(2,128)S(1)}, s32[16,2]{0,1:T(2,128)}, u32[]{:S(2)}) copy-start(s32[16,2]{0,1:T(2,128)} %param.7) | copy-start | bytes 388
  2.7 16.5 %collective-permute-start.2 = (bf16[8,2,5,2,1920]{4,3,2,1,0:T(2,128)(2,1)S(1)}, bf16[8,2,5,2,1920]{4,3,2,1,0:T(2,128)(2,1)S(1)}, u32[]{:S(2)}, u32[]{:S(2)}) collective-permute-start(bf16[8,2,5,2,1920]{4,3,2,1,0:T(2,128)(2,1)S(1)} %get-tuple-element.20), channel_id=1, source_target_pairs={{0,1},{1,2},{2,3},{3,0},{4,5},{5,6},{6,7},{7,4},{8,9},{9,10},{10,1... | collective-permute-start | bytes 1843208 | tf_op jit(solution)/shard_map/ppermute | solution.py:67
  4.8 18.0 %collective-permute-start = (bf16[8,2,5,2,1920]{4,3,2,1,0:T(2,128)(2,1)S(1)}, bf16[8,2,5,2,1920]{4,3,2,1,0:T(2,128)(2,1)S(1)}, u32[]{:S(2)}, u32[]{:S(2)}) collective-permute-start(bf16[8,2,5,2,1920]{4,3,2,1,0:T(2,128)(2,1)S(1)} %get-tuple-element.18), channel_id=1, source_target_pairs={{0,3},{1,0},{2,1},{3,2},{4,7},{5,4},{6,5},{7,6},{8,11},{9,8},{10,9... | collective-permute-start | bytes 1843208 | tf_op jit(solution)/shard_map/ppermute | solution.py:68
  6.2 27.6 %collective-permute-start.1 = (bf16[8,2,5,2,1920]{4,3,2,1,0:T(2,128)(2,1)S(1)}, bf16[8,2,5,2,1920]{4,3,2,1,0:T(2,128)(2,1)S(1)}, u32[]{:S(2)}, u32[]{:S(2)}) collective-permute-start(bf16[8,2,5,2,1920]{4,3,2,1,0:T(2,128)(2,1)S(1)} %get-tuple-element.19), channel_id=1, source_target_pairs={{0,2},{1,3},{2,0},{3,1},{4,6},{5,7},{6,4},{7,5},{8,10},{9,11},{10,... | collective-permute-start | bytes 1843208 | tf_op jit(solution)/shard_map/ppermute | solution.py:69
  19.7 25.0 %collective-permute-start.6 = (bf16[8,2,4,2,1920]{4,3,2,1,0:T(2,128)(2,1)S(1)}, bf16[8,2,4,2,1920]{4,3,2,1,0:T(2,128)(2,1)S(1)}, u32[]{:S(2)}, u32[]{:S(2)}) collective-permute-start(bf16[8,2,4,2,1920]{4,3,2,1,0:T(2,128)(2,1)S(1)} %get-tuple-element.26), channel_id=1, source_target_pairs={{0,3},{1,0},{2,1},{3,2},{4,7},{5,4},{6,5},{7,6},{8,11},{9,8},{10,9... | collective-permute-start | bytes 1474568 | tf_op jit(solution)/shard_map/ppermute | solution.py:68
  21.3 23.5 %collective-permute-start.7 = (bf16[8,2,4,2,1920]{4,3,2,1,0:T(2,128)(2,1)S(1)}, bf16[8,2,4,2,1920]{4,3,2,1,0:T(2,128)(2,1)S(1)}, u32[]{:S(2)}, u32[]{:S(2)}) collective-permute-start(bf16[8,2,4,2,1920]{4,3,2,1,0:T(2,128)(2,1)S(1)} %get-tuple-element.27), channel_id=1, source_target_pairs={{0,2},{1,3},{2,0},{3,1},{4,6},{5,7},{6,4},{7,5},{8,10},{9,11},{10,... | collective-permute-start | bytes 1474568 | tf_op jit(solution)/shard_map/ppermute | solution.py:69
  21.8 35.0 %collective-permute-start.8 = (bf16[8,2,4,2,1920]{4,3,2,1,0:T(2,128)(2,1)S(1)}, bf16[8,2,4,2,1920]{4,3,2,1,0:T(2,128)(2,1)S(1)}, u32[]{:S(2)}, u32[]{:S(2)}) collective-permute-start(bf16[8,2,4,2,1920]{4,3,2,1,0:T(2,128)(2,1)S(1)} %get-tuple-element.28), channel_id=1, source_target_pairs={{0,1},{1,2},{2,3},{3,0},{4,5},{5,6},{6,7},{7,4},{8,9},{9,10},{10,1... | collective-permute-start | bytes 1474568 | tf_op jit(solution)/shard_map/ppermute | solution.py:67
  39.2 21.4 %collective-permute-start.3 = (bf16[8,2,1,2,1920]{4,3,2,1,0:T(2,128)(2,1)S(1)}, bf16[8,2,1,2,1920]{4,3,2,1,0:T(2,128)(2,1)S(1)}, u32[]{:S(2)}, u32[]{:S(2)}) collective-permute-start(bf16[8,2,1,2,1920]{4,3,2,1,0:T(2,128)(2,1)S(1)} %get-tuple-element.22), channel_id=1, source_target_pairs={{0,3},{1,0},{2,1},{3,2},{4,7},{5,4},{6,5},{7,6},{8,11},{9,8},{10,9... | collective-permute-start | bytes 368648 | tf_op jit(solution)/shard_map/ppermute | solution.py:68
  40.4 20.3 %collective-permute-start.4 = (bf16[8,2,1,2,1920]{4,3,2,1,0:T(2,128)(2,1)S(1)}, bf16[8,2,1,2,1920]{4,3,2,1,0:T(2,128)(2,1)S(1)}, u32[]{:S(2)}, u32[]{:S(2)}) collective-permute-start(bf16[8,2,1,2,1920]{4,3,2,1,0:T(2,128)(2,1)S(1)} %get-tuple-element.23), channel_id=1, source_target_pairs={{0,2},{1,3},{2,0},{3,1},{4,6},{5,7},{6,4},{7,5},{8,10},{9,11},{10,... | collective-permute-start | bytes 368648 | tf_op jit(solution)/shard_map/ppermute | solution.py:69
  44.6 16.5 %collective-permute-start.5 = (bf16[8,2,1,2,1920]{4,3,2,1,0:T(2,128)(2,1)S(1)}, bf16[8,2,1,2,1920]{4,3,2,1,0:T(2,128)(2,1)S(1)}, u32[]{:S(2)}, u32[]{:S(2)}) collective-permute-start(bf16[8,2,1,2,1920]{4,3,2,1,0:T(2,128)(2,1)S(1)} %get-tuple-element.24), channel_id=1, source_target_pairs={{0,1},{1,2},{2,3},{3,0},{4,5},{5,6},{6,7},{7,4},{8,9},{9,10},{10,1... | collective-permute-start | bytes 368648 | tf_op jit(solution)/shard_map/ppermute | solution.py:67

commit v15 on v9

--- a/solution.py
+++ b/solution.py
@@ -20,7 +20,7 @@
 TILES = 32
 MAIN = 896
 WIDE = 1024
-CHUNKS = (((0, 0, 5), (8, 0, 5)), ((16, 0, 5), (24, 0, 3)), ((24, 3, 5),))
+CHUNKS = (((0, 0, 5), (8, 0, 5)), ((16, 0, 5), (24, 0, 4)), ((24, 4, 5),))
 
 VMEM = pl.BlockSpec(memory_space=pltpu.VMEM)
 SMEM = pl.BlockSpec(memory_space=pltpu.SMEM)
@@ -28,12 +28,25 @@
 ANYWHERE = pl.BlockSpec(memory_space=pl.ANY)
 
 
-def cut_kernel(parts, images, *rest):
-    to1, to2, to3, own, sem = rest[-5:]
+def slots_of(parts):
+    return sum(high - low for _, low, high in parts)
+
+
+def cut_kernel(parts, middle, images, *rest):
+    to1, to2, to3, own, block, middle_sem, sem = rest[-7:]
+    if middle:
+        first = parts[0][0]
+        fetch = pltpu.make_async_copy(
+            images.at[:, first : first + 2 * ITEMS, :, :, MAIN:WIDE], block, middle_sem
+        )
+        fetch.start()
     group = lax.axis_index("date")
+    takers = [
+        (lax.rem(group + step, 4), out)
+        for step, out in ((1, to1), (3, to3), (2, to2), (0, own))
+    ]
     copies = []
-    for step, out in ((1, to1), (3, to3), (2, to2), (0, own)):
-        taker = lax.rem(group + step, 4)
+    for taker, out in takers:
         top, left = lax.div(taker, 2) * LOOK_AZ, lax.rem(taker, 2) * WIDE
         filled = 0
         for first, low, high in parts:
@@ -54,62 +67,48 @@
                     )
                 )
                 copies[-1].start()
+    if middle:
+        fetch.wait()
     for copy in copies:
         copy.wait()
-
-
-def cut(images, parts, after=None):
-    slots = sum(high - low for _, low, high in parts)
-    block = jax.ShapeDtypeStruct((ITEMS, 2, slots, 2, MAIN), jnp.bfloat16)
+    if middle:
+        source = lax.broadcasted_iota(jnp.int32, (LCOL, LCOL), 0)
+        lane = lax.broadcasted_iota(jnp.int32, (LCOL, LCOL), 1)
+        rows = 2 * ITEMS * LOOK_AZ * 2
+        for taker, out in takers:
+            top, half = lax.div(taker, 2) * LOOK_AZ, lax.rem(taker, 2)
+            packed = jnp.zeros((rows, LCOL), jnp.float32)
+            for date in range(2):
+                moved = lane + 64 * half - 64 * date
+                pick = jnp.where((source == moved) & ((lane < 64) == (date == 0)), 1.0, 0.0)
+                samples = block[date, :, pl.ds(top, LOOK_AZ)].reshape(rows, LCOL)
+                packed = packed + jnp.dot(
+                    samples, pick.astype(jnp.bfloat16), preferred_element_type=jnp.float32
+                )
+            packed = packed.astype(jnp.bfloat16).reshape(2 * ITEMS, LOOK_AZ, 2, LCOL)
+            for index in range(2 * LOOK_AZ):
+                part, line = index // LOOK_AZ, index % LOOK_AZ
+                lanes = slice(index % 7 * LCOL, (index % 7 + 1) * LCOL)
+                out[:, index // 7, slots_of(parts), :, lanes] = packed[
+                    part * ITEMS : (part + 1) * ITEMS, line
+                ]
+
+
+def cut(images, parts, middle, after=None):
+    block = jax.ShapeDtypeStruct((ITEMS, 2, slots_of(parts) + middle, 2, MAIN), jnp.bfloat16)
     operands = (images,) + (() if after is None else (after,))
     return pl.pallas_call(
-        functools.partial(cut_kernel, parts),
+        functools.partial(cut_kernel, parts, middle),
         out_shape=[block] * 4,
         in_specs=[HBM, ANYWHERE][: len(operands)],
         out_specs=[VMEM] * 4,
-        scratch_shapes=[pltpu.SemaphoreType.DMA((8 * len(parts),))],
+        scratch_shapes=[
+            pltpu.VMEM((2, 2 * ITEMS, 2 * LOOK_AZ, 2, LCOL), jnp.bfloat16),
+            pltpu.SemaphoreType.DMA,
+            pltpu.SemaphoreType.DMA((8 * len(parts),)),
+        ],
         compiler_params=pltpu.CompilerParams(vmem_limit_bytes=8 << 20),
     )(*operands)
-
-
-def cut_middle_kernel(images, *rest):
-    to1, to2, to3, own, block, sem = rest[-6:]
-    copy = pltpu.make_async_copy(images.at[:, :, :, :, MAIN:WIDE], block, sem)
-    copy.start()
-    copy.wait()
-    group = lax.axis_index("date")
-    left = lax.broadcasted_iota(jnp.int32, (16, LCOL), 1) < 64
-    for step, out in ((1, to1), (3, to3), (2, to2), (0, own)):
-        taker = lax.rem(group + step, 4)
-        top, half = lax.div(taker, 2) * LOOK_AZ, lax.rem(taker, 2)
-
-        def pack(slot, carry, out=out, top=top, half=half):
-            tiles = pl.ds(lax.div(slot, LOOK_AZ) * ITEMS, ITEMS)
-            line = top + lax.rem(slot, LOOK_AZ)
-            zero = block[0, tiles, line].reshape(16, LCOL).astype(jnp.float32)
-            one = block[1, tiles, line].reshape(16, LCOL).astype(jnp.float32)
-            first = jnp.where(left, zero, pltpu.roll(one, 64, 1))
-            second = jnp.where(left, pltpu.roll(zero, 64, 1), one)
-            packed = jnp.where(half == 0, first, second).astype(jnp.bfloat16)
-            out[:, slot] = packed.reshape(ITEMS, 2, LCOL)
-            return carry
-
-        lax.fori_loop(0, TILES // ITEMS * LOOK_AZ, pack, 0)
-
-
-def cut_middle(images, after):
-    slots = TILES // ITEMS * LOOK_AZ
-    return pl.pallas_call(
-        cut_middle_kernel,
-        out_shape=[jax.ShapeDtypeStruct((ITEMS, slots, 2, LCOL), jnp.bfloat16)] * 4,
-        in_specs=[HBM, ANYWHERE],
-        out_specs=[VMEM] * 4,
-        scratch_shapes=[
-            pltpu.VMEM((2, TILES, 2 * LOOK_AZ, 2, LCOL), jnp.bfloat16),
-            pltpu.SemaphoreType.DMA,
-        ],
-        compiler_params=pltpu.CompilerParams(vmem_limit_bytes=8 << 20),
-    )(images, after)
 
 
 def meet(to1, to2, to3, own):
@@ -122,7 +121,7 @@
     return own, one, two, three
 
 
-def add_lines(epochs, mains, slot, middles, middle_slot, lines, box, img, hi, lo):
+def add_lines(epochs, mains, slot, middles, spare, index, lines, box, img, hi, lo):
     group = lax.axis_index("date")
     left = lax.broadcasted_iota(jnp.int32, (16, LCOL), 1) < 64
     for step, (main, middle) in enumerate(zip(mains, middles)):
@@ -131,7 +130,9 @@
             for date in range(2):
                 pixels = jnp.swapaxes(main[:, date, slot + line], 0, 1).reshape(16, MAIN)
                 img[base + date, line, :, 0:MAIN] = pixels.astype(jnp.float32)
-            packed = jnp.swapaxes(middle[:, middle_slot + line], 0, 1).reshape(16, LCOL)
+            lanes = slice((index + line) % 7 * LCOL, ((index + line) % 7 + 1) * LCOL)
+            packed = middle[:, (index + line) // 7, spare, :, lanes]
+            packed = jnp.swapaxes(packed, 0, 1).reshape(16, LCOL)
             packed = packed.astype(jnp.float32)
             img[base, line, :, MAIN:WIDE] = jnp.where(left, packed, 0.0)
             img[base + 1, line, :, MAIN:WIDE] = jnp.where(left, pltpu.roll(packed, 64, 1), 0.0)
@@ -192,22 +193,30 @@
 
 
 def looks_kernel(chunk, epochs, *rest):
-    mains, middles, (box, *rest), work = rest[:4], rest[4:8], rest[8:-4], rest[-4:]
-    sums = work[-1]
+    mains, rest, (img, hi, lo, sums) = rest[:4], rest[4:-4], rest[-4:]
+    middles = mains
     if chunk == 0:
-        table, out = rest
-        del table
+        box, _, out = rest
     elif chunk == 1:
-        given, out, most = rest
-        del given
+        box, _, out, most = rest
     else:
-        most, given, out = rest
-        del given
+        middles, (box, most, _, out) = rest[:4], rest[4:]
+    spare = slots_of(CHUNKS[min(chunk, 1)])
     slot = 0
     for first, low, high in CHUNKS[chunk]:
         part = first // ITEMS
         total = add_lines(
-            epochs, mains, slot, middles, part * LOOK_AZ + low, high - low, box, *work[:-1]
+            epochs,
+            mains,
+            slot,
+            middles,
+            spare,
+            part % 2 * LOOK_AZ + low,
+            high - low,
+            box,
+            img,
+            hi,
+            lo,
         )
         slot += high - low
         if low > 0:
@@ -276,17 +285,15 @@
     look = jnp.where(lane < MAIN + 64, place // LOOK_RG, -1)
     box = (look[:, None] == jnp.arange(LCOL)[None, :] % 64).astype(jnp.bfloat16)
 
-    cut0 = cut(images, CHUNKS[0])
-    cut_between = cut_middle(images, cut0[1])
-    cut1 = cut(images, CHUNKS[1], cut_between[1])
-    chunk0, middle, chunk1 = meet(*cut0), meet(*cut_between), meet(*cut1)
-    chunk2 = meet(*cut(images, CHUNKS[2], chunk0[3]))
+    chunk0 = meet(*cut(images, CHUNKS[0], 1))
+    chunk1 = meet(*cut(images, CHUNKS[1], 1, chunk0[3]))
 
     shape = jax.ShapeDtypeStruct((TILES, 4, 4, LCOL), jnp.float32)
     partial = jax.ShapeDtypeStruct((ROWS, LCOL), jnp.float32)
-    gamma = looks(0, epochs, (*chunk0, *middle, box, table), shape, {})
-    gamma, most = looks(1, epochs, (*chunk1, *middle, box, gamma), (shape, partial), {10: 0})
-    gamma = looks(2, epochs, (*chunk2, *middle, box, most, gamma), shape, {11: 0})
+    gamma = looks(0, epochs, (*chunk0, box, table), shape, {})
+    chunk2 = meet(*cut(images, CHUNKS[2], 0, gamma))
+    gamma, most = looks(1, epochs, (*chunk1, box, gamma), (shape, partial), {6: 0})
+    gamma = looks(2, epochs, (*chunk2, *chunk1, box, most, gamma), shape, {11: 0})
     got = lax.all_to_all(
         gamma.reshape(128, 4, LCOL), ("tile", "date"), split_axis=0, concat_axis=0, tiled=True
     ).reshape(64, 8, LCOL)

time: 97.3 us -> 92.3 us (0.949)
  Pallas kernels: 25.9 us -> 17.8 us
  waiting for transfers between devices: 26.8 us -> 34.2 us
  local copies, waits for them, and re-layouts: 7.14 us -> 4.8 us
  starting transfers between devices: 14.8 us -> 13.1 us
    ppermute x4 -> x3, waiting for transfers between devices: 14.7 us -> 22 us  [meet(): three = lax.ppermute(to1, 'date', ring(1))]
    pallas_call x4 -> x3, Pallas kernels: 9.9 us -> 2.85 us  [cut(): pl.pallas_call(functools.partial(cut_kernel, parts, middle), out_shape=[b...]
    ppermute x4 -> x3, waiting for transfers between devices: 0.01 us -> 3.66 us  [meet(): one = lax.ppermute(to3, 'date', ring(3))]
    ppermute x4 -> x3, waiting for transfers between devices: 12 us -> 8.51 us  [meet(): two = lax.ppermute(to2, 'date', ring(2))]
    unnamed x16 -> x10, local copies, waits for them, and re-layouts: 7.14 us -> 4.8 us
    ppermute x4 -> x3, starting transfers between devices: 6.35 us -> 4.17 us  [meet(): one = lax.ppermute(to3, 'date', ring(3))]
    ppermute x4 -> x3, starting transfers between devices: 4.06 us -> 5.56 us  [meet(): three = lax.ppermute(to1, 'date', ring(1))]
    pallas_call x3, Pallas kernels: 14.6 us -> 13.5 us  [looks(): pl.pallas_call(functools.partial(looks_kernel, chunk), out_shape=out_shap...]
  transfers between devices with their start and end apart: 12 -> 9, of which waited for: 3 -> 4; matrix products, arithmetic and copies ran while one was open for 0% -> 0% of each run, Pallas kernels for 22% -> 14%
where the time goes in v15:
time: 92.3 us; the launch traced here: 92.1 us
  waiting for transfers between devices  34.2 us (37%)
  blocking collectives  21.1 us (23%)
  Pallas kernels  17.8 us (19%)
  starting transfers between devices  13.1 us (14%)
  local copies, waits for them, and re-layouts  4.8 us (5%)
    ppermute x3, waiting for transfers between devices, meet(): three = lax.ppermute(to1, 'date', ring(1))  22 us
    all_to_all x1, blocking collectives, on_device(): lax.all_to_all(gamma.reshape(128, 4, LCOL), ('tile', 'date'), split_axis=...  21.1 us
    pallas_call x3, Pallas kernels, looks(): pl.pallas_call(functools.partial(looks_kernel, chunk), out_shape=out_shap...  13.5 us
    ppermute x3, waiting for transfers between devices, meet(): two = lax.ppermute(to2, 'date', ring(2))  8.51 us
    ppermute x3, starting transfers between devices, meet(): three = lax.ppermute(to1, 'date', ring(1))  5.56 us
    unnamed x10, local copies, waits for them, and re-layouts  4.8 us
    ppermute x3, starting transfers between devices, meet(): one = lax.ppermute(to3, 'date', ring(3))  4.17 us
    ppermute x3, waiting for transfers between devices, meet(): one = lax.ppermute(to3, 'date', ring(3))  3.66 us
  transfers between devices with their start and end apart: 9, of which 4 were waited for; matrix products, arithmetic and copies ran while one was open for 0% of the time, Pallas kernels for 14%

profile of v15, /device:TPU:1, one launch (start us, length us, event | category | flops | bytes accessed | tf_op | source)
XLA Modules:
  0.0 92.1 jit_solution(15813889271184201404)
XLA Ops:
  0.0 2.4 %copy-done = bf16[2,1,32,2,10,1920]{5,3,4,2,1,0:T(2,128)(2,1)S(1)} copy-done((bf16[2,1,32,2,10,1920]{5,3,4,2,1,0:T(2,128)(2,1)S(1)}, bf16[2,1,32,2,10,1920]{5,3,4,2,1,0:T(2,128)(2,1)}, u32[]{:S(2)}) %copy-start) | copy-done | bytes 4915224
  2.4 1.9 %shard_map.46 = (bf16[8,2,11,2,896]{4,3,2,1,0:T(2,128)(2,1)}, bf16[8,2,11,2,896]{4,3,2,1,0:T(2,128)(2,1)S(1)}, bf16[8,2,11,2,896]{4,3,2,1,0:T(2,128)(2,1)}, bf16[8,2,11,2,896]{4,3,2,1,0:T(2,128)(2,1)S(1)}) custom-call(bf16[2,32,10,2,1920]{4,3,2,1,0:T(2,128)(2,1)S(1)} %bitcast.7), custom_call_target="tpu_custom_call" | custom-call | tf_op jit(solution)/shard_map/pallas_call | solution.py:100
  4.3 2.1 %collective-permute-start.2 = (bf16[8,2,11,2,896]{4,3,2,1,0:T(2,128)(2,1)}, bf16[8,2,11,2,896]{4,3,2,1,0:T(2,128)(2,1)S(1)}, u32[]{:S(2)}, u32[]{:S(2)}) collective-permute-start(bf16[8,2,11,2,896]{4,3,2,1,0:T(2,128)(2,1)} %get-tuple-element.22), channel_id=1, source_target_pairs={{0,1},{1,2},{2,3},{3,0},{4,5},{5,6},{6,7},{7,4},{8,9},{9,10},{10,1... | collective-permute-start | bytes 1892360 | tf_op jit(solution)/shard_map/ppermute | solution.py:118
  6.4 1.4 %collective-permute-start = (bf16[8,2,11,2,896]{4,3,2,1,0:T(2,128)(2,1)}, bf16[8,2,11,2,896]{4,3,2,1,0:T(2,128)(2,1)S(1)}, u32[]{:S(2)}, u32[]{:S(2)}) collective-permute-start(bf16[8,2,11,2,896]{4,3,2,1,0:T(2,128)(2,1)} %get-tuple-element.20), channel_id=1, source_target_pairs={{0,3},{1,0},{2,1},{3,2},{4,7},{5,4},{6,5},{7,6},{8,11},{9,8},{10,9... | collective-permute-start | bytes 1892360 | tf_op jit(solution)/shard_map/ppermute | solution.py:119
  7.7 1.6 %collective-permute-start.1 = (bf16[8,2,11,2,896]{4,3,2,1,0:T(2,128)(2,1)S(1)}, bf16[8,2,11,2,896]{4,3,2,1,0:T(2,128)(2,1)S(1)}, u32[]{:S(2)}, u32[]{:S(2)}) collective-permute-start(bf16[8,2,11,2,896]{4,3,2,1,0:T(2,128)(2,1)S(1)} %get-tuple-element.21), channel_id=1, source_target_pairs={{0,2},{1,3},{2,0},{3,1},{4,6},{5,7},{6,4},{7,5},{8,10},{9,11},{10,... | collective-permute-start | bytes 1892360 | tf_op jit(solution)/shard_map/ppermute | solution.py:120
  10.0 11.3 %collective-permute-done.2.rest_3_.rest_0_ = bf16[8,2,11,2,896]{4,3,2,1,0:T(2,128)(2,1)S(1)} collective-permute-done((bf16[8,2,11,2,896]{4,3,2,1,0:T(2,128)(2,1)}, bf16[8,2,11,2,896]{4,3,2,1,0:T(2,128)(2,1)S(1)}, u32[]{:S(2)}, u32[]{:S(2)}) %collective-permute-start.2) | collective-permute-done | bytes 630816 | tf_op jit(solution)/shard_map/ppermute | solution.py:118
  21.3 2.4 %copy-done.1 = bf16[2,1,32,2,10,1920]{5,3,4,2,1,0:T(2,128)(2,1)S(1)} copy-done((bf16[2,1,32,2,10,1920]{5,3,4,2,1,0:T(2,128)(2,1)S(1)}, bf16[2,1,32,2,10,1920]{5,3,4,2,1,0:T(2,128)(2,1)}, u32[]{:S(2)}) %copy-start.1) | copy-done | bytes 4915224
  23.7 0.8 shard_map.49
  24.6 1.7 %collective-permute-start.6 = (bf16[8,2,10,2,896]{4,3,2,1,0:T(2,128)(2,1)S(1)}, bf16[8,2,10,2,896]{4,3,2,1,0:T(2,128)(2,1)S(1)}, u32[]{:S(2)}, u32[]{:S(2)}) collective-permute-start(bf16[8,2,10,2,896]{4,3,2,1,0:T(2,128)(2,1)S(1)} %get-tuple-element.28), channel_id=1, source_target_pairs={{0,3},{1,0},{2,1},{3,2},{4,7},{5,4},{6,5},{7,6},{8,11},{9,8},{10,9... | collective-permute-start | bytes 1720328 | tf_op jit(solution)/shard_map/ppermute | solution.py:119
  26.2 0.5 collective-permute-start.7
  26.8 0.6 collective-permute-start.8
  27.5 0.2 compare_convert_fusion.rest_4_.rest_8_
  27.7 8.5 %collective-permute-done.1.rest_2_ = bf16[8,2,11,2,896]{4,3,2,1,0:T(2,128)(2,1)S(1)} collective-permute-done((bf16[8,2,11,2,896]{4,3,2,1,0:T(2,128)(2,1)S(1)}, bf16[8,2,11,2,896]{4,3,2,1,0:T(2,128)(2,1)S(1)}, u32[]{:S(2)}, u32[]{:S(2)}) %collective-permute-start.1) | collective-permute-done | bytes 630816 | tf_op jit(solution)/shard_map/ppermute | solution.py:120
  36.2 6.4 %shard_map.47.rest_0_.rest_5_ = f32[32,4,4,128]{3,2,1,0:T(4,128)S(1)} custom-call(s32[2,16]{1,0:T(2,128)S(1)} %bitcast.12, bf16[8,2,11,2,896]{4,3,2,1,0:T(2,128)(2,1)S(1)} %get-tuple-element.19.rest_0_, bf16[8,2,11,2,896]{4,3,2,1,0:T(2,128)(2,1)S(1)} %collective-permute-done.rest_1_, bf16[8,2,11,2,896]{4,3,2,1,0:T(2,128)(2,1)S(1)} %collective-permute-done.1.rest_2_, ...), custom_call_target="tpu_custom_call" | custom-call | flops 180879360 | bytes 2621440 | tf_op jit(solution)/shard_map/pallas_call | solution.py:234
  42.6 0.2 shard_map.48
  42.8 1.2 %collective-permute-start.3 = (bf16[8,2,1,2,896]{4,3,2,1,0:T(2,128)(2,1)S(1)}, bf16[8,2,1,2,896]{4,3,2,1,0:T(2,128)(2,1)S(1)}, u32[]{:S(2)}, u32[]{:S(2)}) collective-permute-start(bf16[8,2,1,2,896]{4,3,2,1,0:T(2,128)(2,1)S(1)} %get-tuple-element.24), channel_id=1, source_target_pairs={{0,3},{1,0},{2,1},{3,2},{4,7},{5,4},{6,5},{7,6},{8,11},{9,8},{10,9... | collective-permute-start | bytes 172040 | tf_op jit(solution)/shard_map/ppermute | solution.py:119
  44.0 1.2 %collective-permute-start.4 = (bf16[8,2,1,2,896]{4,3,2,1,0:T(2,128)(2,1)S(1)}, bf16[8,2,1,2,896]{4,3,2,1,0:T(2,128)(2,1)S(1)}, u32[]{:S(2)}, u32[]{:S(2)}) collective-permute-start(bf16[8,2,1,2,896]{4,3,2,1,0:T(2,128)(2,1)S(1)} %get-tuple-element.25), channel_id=1, source_target_pairs={{0,2},{1,3},{2,0},{3,1},{4,6},{5,7},{6,4},{7,5},{8,10},{9,11},{10,... | collective-permute-start | bytes 172040 | tf_op jit(solution)/shard_map/ppermute | solution.py:120
  45.2 3.7 %collective-permute-done.6.rest_1_.rest_5_ = bf16[8,2,10,2,896]{4,3,2,1,0:T(2,128)(2,1)S(1)} collective-permute-done((bf16[8,2,10,2,896]{4,3,2,1,0:T(2,128)(2,1)S(1)}, bf16[8,2,10,2,896]{4,3,2,1,0:T(2,128)(2,1)S(1)}, u32[]{:S(2)}, u32[]{:S(2)}) %collective-permute-start.6) | collective-permute-done | bytes 573472 | tf_op jit(solution)/shard_map/ppermute | solution.py:119
  48.8 2.8 %collective-permute-start.5 = (bf16[8,2,1,2,896]{4,3,2,1,0:T(2,128)(2,1)S(1)}, bf16[8,2,1,2,896]{4,3,2,1,0:T(2,128)(2,1)S(1)}, u32[]{:S(2)}, u32[]{:S(2)}) collective-permute-start(bf16[8,2,1,2,896]{4,3,2,1,0:T(2,128)(2,1)S(1)} %get-tuple-element.26), channel_id=1, source_target_pairs={{0,1},{1,2},{2,3},{3,0},{4,5},{5,6},{6,7},{7,4},{8,9},{9,10},{10,1... | collective-permute-start | bytes 172040 | tf_op jit(solution)/shard_map/ppermute | solution.py:118
  51.7 10.7 %collective-permute-done.8.rest_3_.rest_7_ = bf16[8,2,10,2,896]{4,3,2,1,0:T(2,128)(2,1)S(1)} collective-permute-done((bf16[8,2,10,2,896]{4,3,2,1,0:T(2,128)(2,1)S(1)}, bf16[8,2,10,2,896]{4,3,2,1,0:T(2,128)(2,1)S(1)}, u32[]{:S(2)}, u32[]{:S(2)}) %collective-permute-start.8) | collective-permute-done | bytes 573472 | tf_op jit(solution)/shard_map/ppermute | solution.py:118
  62.4 5.4 %shard_map.50 = (f32[32,4,4,128]{3,2,1,0:T(4,128)S(1)}, f32[320,128]{1,0:T(8,128)S(1)}) custom-call(s32[2,16]{1,0:T(2,128)S(1)} %bitcast.13, bf16[8,2,10,2,896]{4,3,2,1,0:T(2,128)(2,1)S(1)} %get-tuple-element.27.rest_0_.rest_4_, bf16[8,2,10,2,896]{4,3,2,1,0:T(2,128)(2,1)S(1)} %collective-permute-done.6.rest_1_.rest_5_, ...), custom_call_target="tpu_custom_call", output_to_operand_aliasing={{0}: (6, {})} | custom-call | flops 179568640 | bytes 2359296 | tf_op jit(solution)/shard_map/pallas_call | solution.py:234
  67.9 1.7 %shard_map.51 = f32[32,4,4,128]{3,2,1,0:T(4,128)S(1)} custom-call(s32[2,16]{1,0:T(2,128)S(1)} %bitcast.14, bf16[8,2,1,2,896]{4,3,2,1,0:T(2,128)(2,1)S(1)} %get-tuple-element.23.rest_0_, bf16[8,2,1,2,896]{4,3,2,1,0:T(2,128)(2,1)S(1)} %collective-permute-done.3.rest_1_, ...), custom_call_target="tpu_custom_call", output_to_operand_aliasing={{}: (11, {})} | custom-call | flops 169082880 | bytes 262144 | tf_op jit(solution)/shard_map/pallas_call | solution.py:234
  69.5 21.1 %all_to_all.5 = f32[128,4,128]{2,1,0:T(4,128)S(1)} all-to-all(f32[128,4,128]{2,1,0:T(4,128)S(1)} %bitcast.10), channel_id=1, replica_groups=mesh['tile'=32,'date'=4] {'tile','date'}, dimensions={0} | all-to-all | bytes 524288 | tf_op jit(solution)/shard_map/all_to_all | solution.py:297
  90.6 1.4 %shard_map.52 = f32[4,2,64,128]{3,2,1,0:T(8,128)} custom-call(s32[33]{0:T(128)S(1)} %pad_add_fusion.rest_5_.table, f32[64,8,128]{2,1,0:T(8,128)S(1)} %bitcast.11), custom_call_target="tpu_custom_call" | custom-call | tf_op jit(solution)/shard_map/pallas_call | solution.py:300
  (16 shorter events, 0.1 us)
Async XLA Ops:
  0.0 2.4 %copy-start = (bf16[2,1,32,2,10,1920]{5,3,4,2,1,0:T(2,128)(2,1)S(1)}, bf16[2,1,32,2,10,1920]{5,3,4,2,1,0:T(2,128)(2,1)}, u32[]{:S(2)}) copy-start(bf16[2,1,32,2,10,1920]{5,3,4,2,1,0:T(2,128)(2,1)} %param.4) | copy-start | bytes 14745604
  2.4 25.0 %copy-start.4 = (s32[1,32]{1,0:T(1,128)S(1)}, s32[1,32]{1,0:T(1,128)}, u32[]{:S(2)}) copy-start(s32[1,32]{1,0:T(1,128)} %param.5) | copy-start | bytes 388
  2.4 33.8 %copy-start.3 = (s32[16,2]{0,1:T(2,128)S(1)}, s32[16,2]{0,1:T(2,128)}, u32[]{:S(2)}) copy-start(s32[16,2]{0,1:T(2,128)} %param.7) | copy-start | bytes 388
  4.3 17.1 %collective-permute-start.2 = (bf16[8,2,11,2,896]{4,3,2,1,0:T(2,128)(2,1)}, bf16[8,2,11,2,896]{4,3,2,1,0:T(2,128)(2,1)S(1)}, u32[]{:S(2)}, u32[]{:S(2)}) collective-permute-start(bf16[8,2,11,2,896]{4,3,2,1,0:T(2,128)(2,1)} %get-tuple-element.22), channel_id=1, source_target_pairs={{0,1},{1,2},{2,3},{3,0},{4,5},{5,6},{6,7},{7,4},{8,9},{9,10},{10,1... | collective-permute-start | bytes 1892360 | tf_op jit(solution)/shard_map/ppermute | solution.py:118
  6.4 21.3 %collective-permute-start = (bf16[8,2,11,2,896]{4,3,2,1,0:T(2,128)(2,1)}, bf16[8,2,11,2,896]{4,3,2,1,0:T(2,128)(2,1)S(1)}, u32[]{:S(2)}, u32[]{:S(2)}) collective-permute-start(bf16[8,2,11,2,896]{4,3,2,1,0:T(2,128)(2,1)} %get-tuple-element.20), channel_id=1, source_target_pairs={{0,3},{1,0},{2,1},{3,2},{4,7},{5,4},{6,5},{7,6},{8,11},{9,8},{10,9... | collective-permute-start | bytes 1892360 | tf_op jit(solution)/shard_map/ppermute | solution.py:119
  7.7 28.5 %collective-permute-start.1 = (bf16[8,2,11,2,896]{4,3,2,1,0:T(2,128)(2,1)S(1)}, bf16[8,2,11,2,896]{4,3,2,1,0:T(2,128)(2,1)S(1)}, u32[]{:S(2)}, u32[]{:S(2)}) collective-permute-start(bf16[8,2,11,2,896]{4,3,2,1,0:T(2,128)(2,1)S(1)} %get-tuple-element.21), channel_id=1, source_target_pairs={{0,2},{1,3},{2,0},{3,1},{4,6},{5,7},{6,4},{7,5},{8,10},{9,11},{10,... | collective-permute-start | bytes 1892360 | tf_op jit(solution)/shard_map/ppermute | solution.py:120
  21.3 2.4 %copy-start.1 = (bf16[2,1,32,2,10,1920]{5,3,4,2,1,0:T(2,128)(2,1)S(1)}, bf16[2,1,32,2,10,1920]{5,3,4,2,1,0:T(2,128)(2,1)}, u32[]{:S(2)}) copy-start(bf16[2,1,32,2,10,1920]{5,3,4,2,1,0:T(2,128)(2,1)} %param.4) | copy-start | bytes 14745604
  23.7 18.9 %copy-start.2 = (bf16[2,1,32,2,10,1920]{5,3,4,2,1,0:T(2,128)(2,1)S(1)}, bf16[2,1,32,2,10,1920]{5,3,4,2,1,0:T(2,128)(2,1)}, u32[]{:S(2)}) copy-start(bf16[2,1,32,2,10,1920]{5,3,4,2,1,0:T(2,128)(2,1)} %param.4) | copy-start | bytes 14745604
  24.6 24.3 %collective-permute-start.6 = (bf16[8,2,10,2,896]{4,3,2,1,0:T(2,128)(2,1)S(1)}, bf16[8,2,10,2,896]{4,3,2,1,0:T(2,128)(2,1)S(1)}, u32[]{:S(2)}, u32[]{:S(2)}) collective-permute-start(bf16[8,2,10,2,896]{4,3,2,1,0:T(2,128)(2,1)S(1)} %get-tuple-element.28), channel_id=1, source_target_pairs={{0,3},{1,0},{2,1},{3,2},{4,7},{5,4},{6,5},{7,6},{8,11},{9,8},{10,9... | collective-permute-start | bytes 1720328 | tf_op jit(solution)/shard_map/ppermute | solution.py:119
  26.2 25.4 %collective-permute-start.7 = (bf16[8,2,10,2,896]{4,3,2,1,0:T(2,128)(2,1)S(1)}, bf16[8,2,10,2,896]{4,3,2,1,0:T(2,128)(2,1)S(1)}, u32[]{:S(2)}, u32[]{:S(2)}) collective-permute-start(bf16[8,2,10,2,896]{4,3,2,1,0:T(2,128)(2,1)S(1)} %get-tuple-element.29), channel_id=1, source_target_pairs={{0,2},{1,3},{2,0},{3,1},{4,6},{5,7},{6,4},{7,5},{8,10},{9,11},{10,... | collective-permute-start | bytes 1720328 | tf_op jit(solution)/shard_map/ppermute | solution.py:120
  26.8 35.6 %collective-permute-start.8 = (bf16[8,2,10,2,896]{4,3,2,1,0:T(2,128)(2,1)S(1)}, bf16[8,2,10,2,896]{4,3,2,1,0:T(2,128)(2,1)S(1)}, u32[]{:S(2)}, u32[]{:S(2)}) collective-permute-start(bf16[8,2,10,2,896]{4,3,2,1,0:T(2,128)(2,1)S(1)} %get-tuple-element.30), channel_id=1, source_target_pairs={{0,1},{1,2},{2,3},{3,0},{4,5},{5,6},{6,7},{7,4},{8,9},{9,10},{10,1... | collective-permute-start | bytes 1720328 | tf_op jit(solution)/shard_map/ppermute | solution.py:118
  42.8 25.0 %collective-permute-start.3 = (bf16[8,2,1,2,896]{4,3,2,1,0:T(2,128)(2,1)S(1)}, bf16[8,2,1,2,896]{4,3,2,1,0:T(2,128)(2,1)S(1)}, u32[]{:S(2)}, u32[]{:S(2)}) collective-permute-start(bf16[8,2,1,2,896]{4,3,2,1,0:T(2,128)(2,1)S(1)} %get-tuple-element.24), channel_id=1, source_target_pairs={{0,3},{1,0},{2,1},{3,2},{4,7},{5,4},{6,5},{7,6},{8,11},{9,8},{10,9... | collective-permute-start | bytes 172040 | tf_op jit(solution)/shard_map/ppermute | solution.py:119
  44.0 23.9 %collective-permute-start.4 = (bf16[8,2,1,2,896]{4,3,2,1,0:T(2,128)(2,1)S(1)}, bf16[8,2,1,2,896]{4,3,2,1,0:T(2,128)(2,1)S(1)}, u32[]{:S(2)}, u32[]{:S(2)}) collective-permute-start(bf16[8,2,1,2,896]{4,3,2,1,0:T(2,128)(2,1)S(1)} %get-tuple-element.25), channel_id=1, source_target_pairs={{0,2},{1,3},{2,0},{3,1},{4,6},{5,7},{6,4},{7,5},{8,10},{9,11},{10,... | collective-permute-start | bytes 172040 | tf_op jit(solution)/shard_map/ppermute | solution.py:120
  48.8 19.0 %collective-permute-start.5 = (bf16[8,2,1,2,896]{4,3,2,1,0:T(2,128)(2,1)S(1)}, bf16[8,2,1,2,896]{4,3,2,1,0:T(2,128)(2,1)S(1)}, u32[]{:S(2)}, u32[]{:S(2)}) collective-permute-start(bf16[8,2,1,2,896]{4,3,2,1,0:T(2,128)(2,1)S(1)} %get-tuple-element.26), channel_id=1, source_target_pairs={{0,1},{1,2},{2,3},{3,0},{4,5},{5,6},{6,7},{7,4},{8,9},{9,10},{10,1... | collective-permute-start | bytes 172040 | tf_op jit(solution)/shard_map/ppermute | solution.py:118

commit v16 on v15

--- a/solution.py
+++ b/solution.py
@@ -286,7 +286,7 @@
     box = (look[:, None] == jnp.arange(LCOL)[None, :] % 64).astype(jnp.bfloat16)
 
     chunk0 = meet(*cut(images, CHUNKS[0], 1))
-    chunk1 = meet(*cut(images, CHUNKS[1], 1, chunk0[3]))
+    chunk1 = meet(*cut(images, CHUNKS[1], 1, chunk0[0]))
 
     shape = jax.ShapeDtypeStruct((TILES, 4, 4, LCOL), jnp.float32)
     partial = jax.ShapeDtypeStruct((ROWS, LCOL), jnp.float32)

time: 92.3 us -> 94.5 us (1.024)
  starting transfers between devices: 13.1 us -> 9.35 us
  waiting for transfers between devices: 34.2 us -> 37.2 us
  Pallas kernels: 17.8 us -> 19.6 us
    ppermute x3, waiting for transfers between devices: 8.51 us -> 1.92 us  [meet(): two = lax.ppermute(to2, 'date', ring(2))]
    ppermute x3, waiting for transfers between devices: 22 us -> 28.6 us  [meet(): three = lax.ppermute(to1, 'date', ring(1))]
    ppermute x3, starting transfers between devices: 5.56 us -> 1.47 us  [meet(): three = lax.ppermute(to1, 'date', ring(1))]
    ppermute x3, waiting for transfers between devices: 3.66 us -> 6.69 us  [meet(): one = lax.ppermute(to3, 'date', ring(3))]
    ppermute x3, starting transfers between devices: 4.17 us -> 5.52 us  [meet(): one = lax.ppermute(to3, 'date', ring(3))]
    pallas_call x3, Pallas kernels: 2.85 us -> 3.97 us  [cut(): pl.pallas_call(functools.partial(cut_kernel, parts, middle), out_shape=[b...]
    ppermute x3, starting transfers between devices: 3.4 us -> 2.36 us  [meet(): two = lax.ppermute(to2, 'date', ring(2))]
  transfers between devices with their start and end apart: 9 -> 9, of which waited for: 4 -> 4; matrix products, arithmetic and copies ran while one was open for 0% -> 0% of each run, Pallas kernels for 14% -> 15%
where the time goes in v16:
time: 94.5 us; the launch traced here: 94.3 us
  waiting for transfers between devices  37.2 us (39%)
  blocking collectives  21.4 us (23%)
  Pallas kernels  19.6 us (21%)
  starting transfers between devices  9.35 us (10%)
  local copies, waits for them, and re-layouts  5.6 us (6%)
    ppermute x3, waiting for transfers between devices, meet(): three = lax.ppermute(to1, 'date', ring(1))  28.6 us
    all_to_all x1, blocking collectives, on_device(): lax.all_to_all(gamma.reshape(128, 4, LCOL), ('tile', 'date'), split_axis=...  21.4 us
    pallas_call x3, Pallas kernels, looks(): pl.pallas_call(functools.partial(looks_kernel, chunk), out_shape=out_shap...  14.2 us
    ppermute x3, waiting for transfers between devices, meet(): one = lax.ppermute(to3, 'date', ring(3))  6.69 us
    unnamed x10, local copies, waits for them, and re-layouts  5.6 us
    ppermute x3, starting transfers between devices, meet(): one = lax.ppermute(to3, 'date', ring(3))  5.52 us
    pallas_call x3, Pallas kernels, cut(): pl.pallas_call(functools.partial(cut_kernel, parts, middle), out_shape=[b...  3.97 us
    ppermute x3, starting transfers between devices, meet(): two = lax.ppermute(to2, 'date', ring(2))  2.36 us
  transfers between devices with their start and end apart: 9, of which 4 were waited for; matrix products, arithmetic and copies ran while one was open for 0% of the time, Pallas kernels for 15%

profile of v16, /device:TPU:1, one launch (start us, length us, event | category | flops | bytes accessed | tf_op | source)
XLA Modules:
  0.0 94.3 jit_solution(10701599037941981961)
XLA Ops:
  0.0 2.4 %copy-done = bf16[2,1,32,2,10,1920]{5,3,4,2,1,0:T(2,128)(2,1)S(1)} copy-done((bf16[2,1,32,2,10,1920]{5,3,4,2,1,0:T(2,128)(2,1)S(1)}, bf16[2,1,32,2,10,1920]{5,3,4,2,1,0:T(2,128)(2,1)}, u32[]{:S(2)}) %copy-start) | copy-done | bytes 4915224
  2.4 2.1 %shard_map.46 = (bf16[8,2,11,2,896]{4,3,2,1,0:T(2,128)(2,1)}, bf16[8,2,11,2,896]{4,3,2,1,0:T(2,128)(2,1)}, bf16[8,2,11,2,896]{4,3,2,1,0:T(2,128)(2,1)}, bf16[8,2,11,2,896]{4,3,2,1,0:T(2,128)(2,1)S(1)}) custom-call(bf16[2,32,10,2,1920]{4,3,2,1,0:T(2,128)(2,1)S(1)} %bitcast.7), custom_call_target="tpu_custom_call" | custom-call | tf_op jit(solution)/shard_map/pallas_call | solution.py:100
  4.5 3.4 %collective-permute-start = (bf16[8,2,11,2,896]{4,3,2,1,0:T(2,128)(2,1)}, bf16[8,2,11,2,896]{4,3,2,1,0:T(2,128)(2,1)S(1)}, u32[]{:S(2)}, u32[]{:S(2)}) collective-permute-start(bf16[8,2,11,2,896]{4,3,2,1,0:T(2,128)(2,1)} %get-tuple-element.20), channel_id=1, source_target_pairs={{0,3},{1,0},{2,1},{3,2},{4,7},{5,4},{6,5},{7,6},{8,11},{9,8},{10,9... | collective-permute-start | bytes 1892360 | tf_op jit(solution)/shard_map/ppermute | solution.py:119
  7.9 0.5 collective-permute-start.1
  8.4 0.6 collective-permute-start.2
  9.0 1.8 %shard_map.49 = (bf16[8,2,10,2,896]{4,3,2,1,0:T(2,128)(2,1)S(1)}, bf16[8,2,10,2,896]{4,3,2,1,0:T(2,128)(2,1)}, bf16[8,2,10,2,896]{4,3,2,1,0:T(2,128)(2,1)}, bf16[8,2,10,2,896]{4,3,2,1,0:T(2,128)(2,1)S(1)}) custom-call(bf16[2,32,10,2,1920]{4,3,2,1,0:T(2,128)(2,1)S(1)} %bitcast.8, bf16[8,2,11,2,896]{4,3,2,1,0:T(2,128)(2,1)S(1)} %get-tuple-element.19.rest_0_), custom_call_target="tpu_custom_call" | custom-call | tf_op jit(solution)/shard_map/pallas_call | solution.py:100
  10.8 0.8 copy-done.3
  11.6 2.1 %collective-permute-start.6 = (bf16[8,2,10,2,896]{4,3,2,1,0:T(2,128)(2,1)}, bf16[8,2,10,2,896]{4,3,2,1,0:T(2,128)(2,1)S(1)}, u32[]{:S(2)}, u32[]{:S(2)}) collective-permute-start(bf16[8,2,10,2,896]{4,3,2,1,0:T(2,128)(2,1)} %get-tuple-element.28), channel_id=1, source_target_pairs={{0,3},{1,0},{2,1},{3,2},{4,7},{5,4},{6,5},{7,6},{8,11},{9,8},{10,9... | collective-permute-start | bytes 1720328 | tf_op jit(solution)/shard_map/ppermute | solution.py:119
  13.7 1.2 %collective-permute-start.7 = (bf16[8,2,10,2,896]{4,3,2,1,0:T(2,128)(2,1)}, bf16[8,2,10,2,896]{4,3,2,1,0:T(2,128)(2,1)S(1)}, u32[]{:S(2)}, u32[]{:S(2)}) collective-permute-start(bf16[8,2,10,2,896]{4,3,2,1,0:T(2,128)(2,1)} %get-tuple-element.29), channel_id=1, source_target_pairs={{0,2},{1,3},{2,0},{3,1},{4,6},{5,7},{6,4},{7,5},{8,10},{9,11},{10,... | collective-permute-start | bytes 1720328 | tf_op jit(solution)/shard_map/ppermute | solution.py:120
  15.6 6.7 %collective-permute-done.rest_1_ = bf16[8,2,11,2,896]{4,3,2,1,0:T(2,128)(2,1)S(1)} collective-permute-done((bf16[8,2,11,2,896]{4,3,2,1,0:T(2,128)(2,1)}, bf16[8,2,11,2,896]{4,3,2,1,0:T(2,128)(2,1)S(1)}, u32[]{:S(2)}, u32[]{:S(2)}) %collective-permute-start) | collective-permute-done | bytes 630816 | tf_op jit(solution)/shard_map/ppermute | solution.py:119
  22.3 0.1 pad_add_fusion.rest_5_.table
  22.3 0.2 compare_convert_fusion.rest_4_.rest_8_
  22.6 1.9 %collective-permute-done.1.rest_2_ = bf16[8,2,11,2,896]{4,3,2,1,0:T(2,128)(2,1)} collective-permute-done((bf16[8,2,11,2,896]{4,3,2,1,0:T(2,128)(2,1)}, bf16[8,2,11,2,896]{4,3,2,1,0:T(2,128)(2,1)}, u32[]{:S(2)}, u32[]{:S(2)}) %collective-permute-start.1) | collective-permute-done | bytes 630816 | tf_op jit(solution)/shard_map/ppermute | solution.py:120
  24.5 16.2 %collective-permute-done.2.rest_3_ = bf16[8,2,11,2,896]{4,3,2,1,0:T(2,128)(2,1)} collective-permute-done((bf16[8,2,11,2,896]{4,3,2,1,0:T(2,128)(2,1)}, bf16[8,2,11,2,896]{4,3,2,1,0:T(2,128)(2,1)}, u32[]{:S(2)}, u32[]{:S(2)}) %collective-permute-start.2) | collective-permute-done | bytes 630816 | tf_op jit(solution)/shard_map/ppermute | solution.py:118
  40.6 7.1 %shard_map.47.rest_0_.rest_5_ = f32[32,4,4,128]{3,2,1,0:T(4,128)S(1)} custom-call(s32[2,16]{1,0:T(2,128)S(1)} %bitcast.12, bf16[8,2,11,2,896]{4,3,2,1,0:T(2,128)(2,1)S(1)} %get-tuple-element.19.rest_0_, bf16[8,2,11,2,896]{4,3,2,1,0:T(2,128)(2,1)S(1)} %collective-permute-done.rest_1_, bf16[8,2,11,2,896]{4,3,2,1,0:T(2,128)(2,1)} %collective-permute-done.1.rest_2_, ...), custom_call_target="tpu_custom_call" | custom-call | flops 180879360 | bytes 2621440 | tf_op jit(solution)/shard_map/pallas_call | solution.py:234
  47.8 2.4 %copy-done.1 = bf16[2,1,32,2,10,1920]{5,3,4,2,1,0:T(2,128)(2,1)S(1)} copy-done((bf16[2,1,32,2,10,1920]{5,3,4,2,1,0:T(2,128)(2,1)S(1)}, bf16[2,1,32,2,10,1920]{5,3,4,2,1,0:T(2,128)(2,1)}, u32[]{:S(2)}) %copy-start.1) | copy-done | bytes 4915224
  50.2 0.1 shard_map.48
  50.4 0.6 collective-permute-start.4
  51.0 0.9 collective-permute-start.5
  51.9 12.4 %collective-permute-done.8.rest_3_.rest_7_ = bf16[8,2,10,2,896]{4,3,2,1,0:T(2,128)(2,1)S(1)} collective-permute-done((bf16[8,2,10,2,896]{4,3,2,1,0:T(2,128)(2,1)}, bf16[8,2,10,2,896]{4,3,2,1,0:T(2,128)(2,1)S(1)}, u32[]{:S(2)}, u32[]{:S(2)}) %collective-permute-start.8) | collective-permute-done | bytes 573472 | tf_op jit(solution)/shard_map/ppermute | solution.py:118
  64.3 5.4 %shard_map.50 = (f32[32,4,4,128]{3,2,1,0:T(4,128)S(1)}, f32[320,128]{1,0:T(8,128)S(1)}) custom-call(s32[2,16]{1,0:T(2,128)S(1)} %bitcast.13, bf16[8,2,10,2,896]{4,3,2,1,0:T(2,128)(2,1)S(1)} %get-tuple-element.27.rest_0_.rest_4_, bf16[8,2,10,2,896]{4,3,2,1,0:T(2,128)(2,1)S(1)} %collective-permute-done.6.rest_1_.rest_5_, ...), custom_call_target="tpu_custom_call", output_to_operand_aliasing={{0}: (6, {})} | custom-call | flops 179568640 | bytes 2359296 | tf_op jit(solution)/shard_map/pallas_call | solution.py:234
  69.8 1.7 %shard_map.51 = f32[32,4,4,128]{3,2,1,0:T(4,128)S(1)} custom-call(s32[2,16]{1,0:T(2,128)S(1)} %bitcast.14, bf16[8,2,1,2,896]{4,3,2,1,0:T(2,128)(2,1)S(1)} %get-tuple-element.23.rest_0_, bf16[8,2,1,2,896]{4,3,2,1,0:T(2,128)(2,1)S(1)} %collective-permute-done.3.rest_1_, ...), custom_call_target="tpu_custom_call", output_to_operand_aliasing={{}: (11, {})} | custom-call | flops 169082880 | bytes 262144 | tf_op jit(solution)/shard_map/pallas_call | solution.py:234
  71.4 21.4 %all_to_all.5 = f32[128,4,128]{2,1,0:T(4,128)S(1)} all-to-all(f32[128,4,128]{2,1,0:T(4,128)S(1)} %bitcast.10), channel_id=1, replica_groups=mesh['tile'=32,'date'=4] {'tile','date'}, dimensions={0} | all-to-all | bytes 524288 | tf_op jit(solution)/shard_map/all_to_all | solution.py:297
  92.9 1.4 %shard_map.52 = f32[4,2,64,128]{3,2,1,0:T(8,128)} custom-call(s32[33]{0:T(128)S(1)} %pad_add_fusion.rest_5_.table, f32[64,8,128]{2,1,0:T(8,128)S(1)} %bitcast.11), custom_call_target="tpu_custom_call" | custom-call | tf_op jit(solution)/shard_map/pallas_call | solution.py:300
  (16 shorter events, 0.1 us)
Async XLA Ops:
  0.0 2.4 %copy-start = (bf16[2,1,32,2,10,1920]{5,3,4,2,1,0:T(2,128)(2,1)S(1)}, bf16[2,1,32,2,10,1920]{5,3,4,2,1,0:T(2,128)(2,1)}, u32[]{:S(2)}) copy-start(bf16[2,1,32,2,10,1920]{5,3,4,2,1,0:T(2,128)(2,1)} %param.4) | copy-start | bytes 14745604
  2.4 19.9 %copy-start.4 = (s32[1,32]{1,0:T(1,128)S(1)}, s32[1,32]{1,0:T(1,128)}, u32[]{:S(2)}) copy-start(s32[1,32]{1,0:T(1,128)} %param.5) | copy-start | bytes 388
  2.4 38.3 %copy-start.2 = (s32[16,2]{0,1:T(2,128)S(1)}, s32[16,2]{0,1:T(2,128)}, u32[]{:S(2)}) copy-start(s32[16,2]{0,1:T(2,128)} %param.7) | copy-start | bytes 388
  4.5 17.8 %collective-permute-start = (bf16[8,2,11,2,896]{4,3,2,1,0:T(2,128)(2,1)}, bf16[8,2,11,2,896]{4,3,2,1,0:T(2,128)(2,1)S(1)}, u32[]{:S(2)}, u32[]{:S(2)}) collective-permute-start(bf16[8,2,11,2,896]{4,3,2,1,0:T(2,128)(2,1)} %get-tuple-element.20), channel_id=1, source_target_pairs={{0,3},{1,0},{2,1},{3,2},{4,7},{5,4},{6,5},{7,6},{8,11},{9,8},{10,9... | collective-permute-start | bytes 1892360 | tf_op jit(solution)/shard_map/ppermute | solution.py:119
  7.9 16.6 %collective-permute-start.1 = (bf16[8,2,11,2,896]{4,3,2,1,0:T(2,128)(2,1)}, bf16[8,2,11,2,896]{4,3,2,1,0:T(2,128)(2,1)}, u32[]{:S(2)}, u32[]{:S(2)}) collective-permute-start(bf16[8,2,11,2,896]{4,3,2,1,0:T(2,128)(2,1)} %get-tuple-element.21), channel_id=1, source_target_pairs={{0,2},{1,3},{2,0},{3,1},{4,6},{5,7},{6,4},{7,5},{8,10},{9,11},{10,... | collective-permute-start | bytes 1892360 | tf_op jit(solution)/shard_map/ppermute | solution.py:120
  8.4 32.3 %collective-permute-start.2 = (bf16[8,2,11,2,896]{4,3,2,1,0:T(2,128)(2,1)}, bf16[8,2,11,2,896]{4,3,2,1,0:T(2,128)(2,1)}, u32[]{:S(2)}, u32[]{:S(2)}) collective-permute-start(bf16[8,2,11,2,896]{4,3,2,1,0:T(2,128)(2,1)} %get-tuple-element.22), channel_id=1, source_target_pairs={{0,1},{1,2},{2,3},{3,0},{4,5},{5,6},{6,7},{7,4},{8,9},{9,10},{10,1... | collective-permute-start | bytes 1892360 | tf_op jit(solution)/shard_map/ppermute | solution.py:118
  10.8 0.8 copy-start.3
  11.6 39.4 %collective-permute-start.6 = (bf16[8,2,10,2,896]{4,3,2,1,0:T(2,128)(2,1)}, bf16[8,2,10,2,896]{4,3,2,1,0:T(2,128)(2,1)S(1)}, u32[]{:S(2)}, u32[]{:S(2)}) collective-permute-start(bf16[8,2,10,2,896]{4,3,2,1,0:T(2,128)(2,1)} %get-tuple-element.28), channel_id=1, source_target_pairs={{0,3},{1,0},{2,1},{3,2},{4,7},{5,4},{6,5},{7,6},{8,11},{9,8},{10,9... | collective-permute-start | bytes 1720328 | tf_op jit(solution)/shard_map/ppermute | solution.py:119
  13.7 38.2 %collective-permute-start.7 = (bf16[8,2,10,2,896]{4,3,2,1,0:T(2,128)(2,1)}, bf16[8,2,10,2,896]{4,3,2,1,0:T(2,128)(2,1)S(1)}, u32[]{:S(2)}, u32[]{:S(2)}) collective-permute-start(bf16[8,2,10,2,896]{4,3,2,1,0:T(2,128)(2,1)} %get-tuple-element.29), channel_id=1, source_target_pairs={{0,2},{1,3},{2,0},{3,1},{4,6},{5,7},{6,4},{7,5},{8,10},{9,11},{10,... | collective-permute-start | bytes 1720328 | tf_op jit(solution)/shard_map/ppermute | solution.py:120
  22.2 42.1 %collective-permute-start.8 = (bf16[8,2,10,2,896]{4,3,2,1,0:T(2,128)(2,1)}, bf16[8,2,10,2,896]{4,3,2,1,0:T(2,128)(2,1)S(1)}, u32[]{:S(2)}, u32[]{:S(2)}) collective-permute-start(bf16[8,2,10,2,896]{4,3,2,1,0:T(2,128)(2,1)} %copy-done.3), channel_id=1, source_target_pairs={{0,1},{1,2},{2,3},{3,0},{4,5},{5,6},{6,7},{7,4},{8,9},{9,10},{10,1... | collective-permute-start | bytes 1720328 | tf_op jit(solution)/shard_map/ppermute | solution.py:118
  47.8 2.4 %copy-start.1 = (bf16[2,1,32,2,10,1920]{5,3,4,2,1,0:T(2,128)(2,1)S(1)}, bf16[2,1,32,2,10,1920]{5,3,4,2,1,0:T(2,128)(2,1)}, u32[]{:S(2)}) copy-start(bf16[2,1,32,2,10,1920]{5,3,4,2,1,0:T(2,128)(2,1)} %param.4) | copy-start | bytes 14745604
  50.3 19.4 %collective-permute-start.3 = (bf16[8,2,1,2,896]{4,3,2,1,0:T(2,128)(2,1)S(1)}, bf16[8,2,1,2,896]{4,3,2,1,0:T(2,128)(2,1)S(1)}, u32[]{:S(2)}, u32[]{:S(2)}) collective-permute-start(bf16[8,2,1,2,896]{4,3,2,1,0:T(2,128)(2,1)S(1)} %get-tuple-element.24), channel_id=1, source_target_pairs={{0,3},{1,0},{2,1},{3,2},{4,7},{5,4},{6,5},{7,6},{8,11},{9,8},{10,9... | collective-permute-start | bytes 172040 | tf_op jit(solution)/shard_map/ppermute | solution.py:119
  50.4 19.3 %collective-permute-start.4 = (bf16[8,2,1,2,896]{4,3,2,1,0:T(2,128)(2,1)S(1)}, bf16[8,2,1,2,896]{4,3,2,1,0:T(2,128)(2,1)S(1)}, u32[]{:S(2)}, u32[]{:S(2)}) collective-permute-start(bf16[8,2,1,2,896]{4,3,2,1,0:T(2,128)(2,1)S(1)} %get-tuple-element.25), channel_id=1, source_target_pairs={{0,2},{1,3},{2,0},{3,1},{4,6},{5,7},{6,4},{7,5},{8,10},{9,11},{10,... | collective-permute-start | bytes 172040 | tf_op jit(solution)/shard_map/ppermute | solution.py:120
  51.0 18.7 %collective-permute-start.5 = (bf16[8,2,1,2,896]{4,3,2,1,0:T(2,128)(2,1)S(1)}, bf16[8,2,1,2,896]{4,3,2,1,0:T(2,128)(2,1)S(1)}, u32[]{:S(2)}, u32[]{:S(2)}) collective-permute-start(bf16[8,2,1,2,896]{4,3,2,1,0:T(2,128)(2,1)S(1)} %get-tuple-element.26), channel_id=1, source_target_pairs={{0,1},{1,2},{2,3},{3,0},{4,5},{5,6},{6,7},{7,4},{8,9},{9,10},{10,1... | collective-permute-start | bytes 172040 | tf_op jit(solution)/shard_map/ppermute | solution.py:118

commit v17 on v11

--- a/solution.py
+++ b/solution.py
@@ -97,7 +97,7 @@
         split(jnp.concatenate(total, axis=0), pl.multiple_of(half * 16, 16))
         return carry
 
-    lax.fori_loop(0, DATES // 2, power, 0)
+    lax.fori_loop(0, DATES // 2, power, 0, unroll=True)
 
     def cross(k, carry):
         a, b = epochs[0, k], epochs[1, k]
@@ -111,7 +111,7 @@
         split(jnp.concatenate([acc_re, acc_im], axis=0), pl.multiple_of(64 + k * 16, 16))
         return carry
 
-    lax.fori_loop(0, PAIRS, cross, 0)
+    lax.fori_loop(0, PAIRS, cross, 0, unroll=4)
     return jnp.dot(hi[...], box[...], preferred_element_type=jnp.float32) + jnp.dot(
         lo[...], box[...], preferred_element_type=jnp.float32
     )

time: 88.1 us -> 88.1 us (level)
  no operation moved by 1% of the time
where the time goes in v17:
time: 88.1 us; the launch traced here: 88 us
  waiting for transfers between devices  37.2 us (42%)
  blocking collectives  23.1 us (26%)
  Pallas kernels  13.5 us (15%)
  starting transfers between devices  10.5 us (12%)
  local copies, waits for them, and re-layouts  2.42 us (3%)
    ppermute x3, waiting for transfers between devices, meet(): three = lax.ppermute(to1, 'date', ring(1))  23.2 us
    all_to_all x1, blocking collectives, on_device(): lax.all_to_all(gamma.reshape(128, 8, LCOL), ('tile', 'date'), split_axis=...  23.1 us
    pallas_call x3, Pallas kernels, looks(): pl.pallas_call(kernel, out_shape=out_shape, grid_spec=pltpu.PrefetchScala...  11.3 us
    ppermute x3, waiting for transfers between devices, meet(): two = lax.ppermute(to2, 'date', ring(2))  11 us
    ppermute x3, starting transfers between devices, meet(): one = lax.ppermute(to3, 'date', ring(3))  4.17 us
    ppermute x3, starting transfers between devices, meet(): two = lax.ppermute(to2, 'date', ring(2))  3.4 us
    ppermute x3, waiting for transfers between devices, meet(): one = lax.ppermute(to3, 'date', ring(3))  3.02 us
    ppermute x3, starting transfers between devices, meet(): three = lax.ppermute(to1, 'date', ring(1))  2.92 us
  transfers between devices with their start and end apart: 9, of which 5 were waited for; matrix products, arithmetic and copies ran while one was open for 0% of the time, Pallas kernels for 11%

profile of v17, /device:TPU:1, one launch (start us, length us, event | category | flops | bytes accessed | tf_op | source)
XLA Modules:
  0.0 88.0 jit_solution(6286678118746114804)
XLA Ops:
  0.0 2.4 %copy-done = bf16[2,1,32,2,10,1920]{5,3,4,2,1,0:T(2,128)(2,1)S(1)} copy-done((bf16[2,1,32,2,10,1920]{5,3,4,2,1,0:T(2,128)(2,1)S(1)}, bf16[2,1,32,2,10,1920]{5,3,4,2,1,0:T(2,128)(2,1)}, u32[]{:S(2)}) %copy-start) | copy-done | bytes 4915224
  2.4 0.3 shard_map.46
  2.7 2.1 %collective-permute-start.2 = (bf16[8,2,5,2,1920]{4,3,2,1,0:T(2,128)(2,1)S(1)}, bf16[8,2,5,2,1920]{4,3,2,1,0:T(2,128)(2,1)S(1)}, u32[]{:S(2)}, u32[]{:S(2)}) collective-permute-start(bf16[8,2,5,2,1920]{4,3,2,1,0:T(2,128)(2,1)S(1)} %get-tuple-element.20), channel_id=1, source_target_pairs={{0,1},{1,2},{2,3},{3,0},{4,5},{5,6},{6,7},{7,4},{8,9},{9,10},{10,1... | collective-permute-start | bytes 1843208 | tf_op jit(solution)/shard_map/ppermute | solution.py:67
  4.8 1.3 %collective-permute-start = (bf16[8,2,5,2,1920]{4,3,2,1,0:T(2,128)(2,1)S(1)}, bf16[8,2,5,2,1920]{4,3,2,1,0:T(2,128)(2,1)S(1)}, u32[]{:S(2)}, u32[]{:S(2)}) collective-permute-start(bf16[8,2,5,2,1920]{4,3,2,1,0:T(2,128)(2,1)S(1)} %get-tuple-element.18), channel_id=1, source_target_pairs={{0,3},{1,0},{2,1},{3,2},{4,7},{5,4},{6,5},{7,6},{8,11},{9,8},{10,9... | collective-permute-start | bytes 1843208 | tf_op jit(solution)/shard_map/ppermute | solution.py:68
  6.2 1.6 %collective-permute-start.1 = (bf16[8,2,5,2,1920]{4,3,2,1,0:T(2,128)(2,1)S(1)}, bf16[8,2,5,2,1920]{4,3,2,1,0:T(2,128)(2,1)S(1)}, u32[]{:S(2)}, u32[]{:S(2)}) collective-permute-start(bf16[8,2,5,2,1920]{4,3,2,1,0:T(2,128)(2,1)S(1)} %get-tuple-element.19), channel_id=1, source_target_pairs={{0,2},{1,3},{2,0},{3,1},{4,6},{5,7},{6,4},{7,5},{8,10},{9,11},{10,... | collective-permute-start | bytes 1843208 | tf_op jit(solution)/shard_map/ppermute | solution.py:69
  8.6 10.7 %collective-permute-done.2.three.rest_0_ = bf16[8,2,5,2,1920]{4,3,2,1,0:T(2,128)(2,1)S(1)} collective-permute-done((bf16[8,2,5,2,1920]{4,3,2,1,0:T(2,128)(2,1)S(1)}, bf16[8,2,5,2,1920]{4,3,2,1,0:T(2,128)(2,1)S(1)}, u32[]{:S(2)}, u32[]{:S(2)}) %collective-permute-start.2) | collective-permute-done | bytes 614432 | tf_op jit(solution)/shard_map/ppermute | solution.py:67
  19.2 0.4 shard_map.49
  19.7 1.7 %collective-permute-start.6 = (bf16[8,2,4,2,1920]{4,3,2,1,0:T(2,128)(2,1)S(1)}, bf16[8,2,4,2,1920]{4,3,2,1,0:T(2,128)(2,1)S(1)}, u32[]{:S(2)}, u32[]{:S(2)}) collective-permute-start(bf16[8,2,4,2,1920]{4,3,2,1,0:T(2,128)(2,1)S(1)} %get-tuple-element.26), channel_id=1, source_target_pairs={{0,3},{1,0},{2,1},{3,2},{4,7},{5,4},{6,5},{7,6},{8,11},{9,8},{10,9... | collective-permute-start | bytes 1474568 | tf_op jit(solution)/shard_map/ppermute | solution.py:68
  21.3 0.5 collective-permute-start.7
  21.8 0.6 collective-permute-start.8
  22.5 0.3 fusion.box
  22.8 11.0 %collective-permute-done.1.two = bf16[8,2,5,2,1920]{4,3,2,1,0:T(2,128)(2,1)S(1)} collective-permute-done((bf16[8,2,5,2,1920]{4,3,2,1,0:T(2,128)(2,1)S(1)}, bf16[8,2,5,2,1920]{4,3,2,1,0:T(2,128)(2,1)S(1)}, u32[]{:S(2)}, u32[]{:S(2)}) %collective-permute-start.1) | collective-permute-done | bytes 614432 | tf_op jit(solution)/shard_map/ppermute | solution.py:69
  33.8 5.3 %shard_map.47.rest_0_.after.given = f32[32,4,8,128]{3,2,1,0:T(8,128)S(1)} custom-call(s32[2,16]{1,0:T(2,128)S(1)} %bitcast.12, bf16[8,2,5,2,1920]{4,3,2,1,0:T(2,128)(2,1)S(1)} %get-tuple-element.17.own, bf16[8,2,5,2,1920]{4,3,2,1,0:T(2,128)(2,1)S(1)} %collective-permute-done.one, bf16[8,2,5,2,1920]{4,3,2,1,0:T(2,128)(2,1)S(1)} %collective-permute-done.1.two, ...), custom_call_target="tpu_custom_call" | custom-call | flops 326860800 | bytes 2457600 | tf_op jit(solution)/shard_map/pallas_call | solution.py:154
  39.0 0.2 shard_map.48
  39.2 1.2 %collective-permute-start.3 = (bf16[8,2,1,2,1920]{4,3,2,1,0:T(2,128)(2,1)S(1)}, bf16[8,2,1,2,1920]{4,3,2,1,0:T(2,128)(2,1)S(1)}, u32[]{:S(2)}, u32[]{:S(2)}) collective-permute-start(bf16[8,2,1,2,1920]{4,3,2,1,0:T(2,128)(2,1)S(1)} %get-tuple-element.22), channel_id=1, source_target_pairs={{0,3},{1,0},{2,1},{3,2},{4,7},{5,4},{6,5},{7,6},{8,11},{9,8},{10,9... | collective-permute-start | bytes 368648 | tf_op jit(solution)/shard_map/ppermute | solution.py:68
  40.4 1.2 %collective-permute-start.4 = (bf16[8,2,1,2,1920]{4,3,2,1,0:T(2,128)(2,1)S(1)}, bf16[8,2,1,2,1920]{4,3,2,1,0:T(2,128)(2,1)S(1)}, u32[]{:S(2)}, u32[]{:S(2)}) collective-permute-start(bf16[8,2,1,2,1920]{4,3,2,1,0:T(2,128)(2,1)S(1)} %get-tuple-element.23), channel_id=1, source_target_pairs={{0,2},{1,3},{2,0},{3,1},{4,6},{5,7},{6,4},{7,5},{8,10},{9,11},{10,... | collective-permute-start | bytes 368648 | tf_op jit(solution)/shard_map/ppermute | solution.py:69
  41.6 3.0 %collective-permute-done.6.one = bf16[8,2,4,2,1920]{4,3,2,1,0:T(2,128)(2,1)S(1)} collective-permute-done((bf16[8,2,4,2,1920]{4,3,2,1,0:T(2,128)(2,1)S(1)}, bf16[8,2,4,2,1920]{4,3,2,1,0:T(2,128)(2,1)S(1)}, u32[]{:S(2)}, u32[]{:S(2)}) %collective-permute-start.6) | collective-permute-done | bytes 491552 | tf_op jit(solution)/shard_map/ppermute | solution.py:68
  44.6 0.2 collective-permute-start.5
  44.8 12.0 %collective-permute-done.8.three = bf16[8,2,4,2,1920]{4,3,2,1,0:T(2,128)(2,1)S(1)} collective-permute-done((bf16[8,2,4,2,1920]{4,3,2,1,0:T(2,128)(2,1)S(1)}, bf16[8,2,4,2,1920]{4,3,2,1,0:T(2,128)(2,1)S(1)}, u32[]{:S(2)}, u32[]{:S(2)}) %collective-permute-start.8) | collective-permute-done | bytes 491552 | tf_op jit(solution)/shard_map/ppermute | solution.py:67
  56.8 3.7 %shard_map.50.most = f32[320,128]{1,0:T(8,128)S(1)} custom-call(s32[2,16]{1,0:T(2,128)S(1)} %bitcast.13, bf16[8,2,4,2,1920]{4,3,2,1,0:T(2,128)(2,1)S(1)} %get-tuple-element.25.own, bf16[8,2,4,2,1920]{4,3,2,1,0:T(2,128)(2,1)S(1)} %collective-permute-done.6.one, bf16[8,2,4,2,1920]{4,3,2,1,0:T(2,128)(2,1)S(1)} %collective-permute-done.7.two, ...), custom_call_target="tpu_custom_call" | custom-call | flops 324403200 | bytes 1966080 | tf_op jit(solution)/shard_map/pallas_call | solution.py:154
  60.6 0.6 collective-permute-done.5.three
  61.2 2.3 %shard_map.51 = f32[32,4,8,128]{3,2,1,0:T(8,128)S(1)} custom-call(s32[2,16]{1,0:T(2,128)S(1)} %bitcast.14, bf16[8,2,1,2,1920]{4,3,2,1,0:T(2,128)(2,1)S(1)} %get-tuple-element.21.own, bf16[8,2,1,2,1920]{4,3,2,1,0:T(2,128)(2,1)S(1)} %collective-permute-done.3.one, ...), custom_call_target="tpu_custom_call", output_to_operand_aliasing={{}: (7, {})} | custom-call | flops 317030400 | bytes 491520 | tf_op jit(solution)/shard_map/pallas_call | solution.py:154
  63.5 23.1 %all_to_all.5 = f32[128,8,128]{2,1,0:T(8,128)S(1)} all-to-all(f32[128,8,128]{2,1,0:T(8,128)S(1)} %bitcast.10), channel_id=1, replica_groups=mesh['tile'=32,'date'=4] {'tile','date'}, dimensions={0} | all-to-all | bytes 1048576 | tf_op jit(solution)/shard_map/all_to_all | solution.py:209
  86.6 1.4 %shard_map.52 = f32[4,2,64,128]{3,2,1,0:T(8,128)} custom-call(s32[33]{0:T(128)S(1)} %pad_add_fusion.table, f32[32,4,8,128]{3,2,1,0:T(8,128)S(1)} %bitcast.11), custom_call_target="tpu_custom_call" | custom-call | tf_op jit(solution)/shard_map/pallas_call | solution.py:212
  (13 shorter events, 0.1 us)
Async XLA Ops:
  0.0 8.5 %copy-start.3 = (s32[1,32]{1,0:T(1,128)S(1)}, s32[1,32]{1,0:T(1,128)}, u32[]{:S(2)}) copy-start(s32[1,32]{1,0:T(1,128)} %param.5) | copy-start | bytes 388
  0.0 2.4 %copy-start = (bf16[2,1,32,2,10,1920]{5,3,4,2,1,0:T(2,128)(2,1)S(1)}, bf16[2,1,32,2,10,1920]{5,3,4,2,1,0:T(2,128)(2,1)}, u32[]{:S(2)}) copy-start(bf16[2,1,32,2,10,1920]{5,3,4,2,1,0:T(2,128)(2,1)} %param.4) | copy-start | bytes 14745604
  2.4 16.8 %copy-start.1 = (bf16[2,1,32,2,10,1920]{5,3,4,2,1,0:T(2,128)(2,1)S(1)}, bf16[2,1,32,2,10,1920]{5,3,4,2,1,0:T(2,128)(2,1)}, u32[]{:S(2)}) copy-start(bf16[2,1,32,2,10,1920]{5,3,4,2,1,0:T(2,128)(2,1)} %param.4) | copy-start | bytes 14745604
  2.4 31.3 %copy-start.2 = (s32[16,2]{0,1:T(2,128)S(1)}, s32[16,2]{0,1:T(2,128)}, u32[]{:S(2)}) copy-start(s32[16,2]{0,1:T(2,128)} %param.7) | copy-start | bytes 388
  2.7 16.5 %collective-permute-start.2 = (bf16[8,2,5,2,1920]{4,3,2,1,0:T(2,128)(2,1)S(1)}, bf16[8,2,5,2,1920]{4,3,2,1,0:T(2,128)(2,1)S(1)}, u32[]{:S(2)}, u32[]{:S(2)}) collective-permute-start(bf16[8,2,5,2,1920]{4,3,2,1,0:T(2,128)(2,1)S(1)} %get-tuple-element.20), channel_id=1, source_target_pairs={{0,1},{1,2},{2,3},{3,0},{4,5},{5,6},{6,7},{7,4},{8,9},{9,10},{10,1... | collective-permute-start | bytes 1843208 | tf_op jit(solution)/shard_map/ppermute | solution.py:67
  4.8 18.0 %collective-permute-start = (bf16[8,2,5,2,1920]{4,3,2,1,0:T(2,128)(2,1)S(1)}, bf16[8,2,5,2,1920]{4,3,2,1,0:T(2,128)(2,1)S(1)}, u32[]{:S(2)}, u32[]{:S(2)}) collective-permute-start(bf16[8,2,5,2,1920]{4,3,2,1,0:T(2,128)(2,1)S(1)} %get-tuple-element.18), channel_id=1, source_target_pairs={{0,3},{1,0},{2,1},{3,2},{4,7},{5,4},{6,5},{7,6},{8,11},{9,8},{10,9... | collective-permute-start | bytes 1843208 | tf_op jit(solution)/shard_map/ppermute | solution.py:68
  6.2 27.6 %collective-permute-start.1 = (bf16[8,2,5,2,1920]{4,3,2,1,0:T(2,128)(2,1)S(1)}, bf16[8,2,5,2,1920]{4,3,2,1,0:T(2,128)(2,1)S(1)}, u32[]{:S(2)}, u32[]{:S(2)}) collective-permute-start(bf16[8,2,5,2,1920]{4,3,2,1,0:T(2,128)(2,1)S(1)} %get-tuple-element.19), channel_id=1, source_target_pairs={{0,2},{1,3},{2,0},{3,1},{4,6},{5,7},{6,4},{7,5},{8,10},{9,11},{10,... | collective-permute-start | bytes 1843208 | tf_op jit(solution)/shard_map/ppermute | solution.py:69
  19.7 25.0 %collective-permute-start.6 = (bf16[8,2,4,2,1920]{4,3,2,1,0:T(2,128)(2,1)S(1)}, bf16[8,2,4,2,1920]{4,3,2,1,0:T(2,128)(2,1)S(1)}, u32[]{:S(2)}, u32[]{:S(2)}) collective-permute-start(bf16[8,2,4,2,1920]{4,3,2,1,0:T(2,128)(2,1)S(1)} %get-tuple-element.26), channel_id=1, source_target_pairs={{0,3},{1,0},{2,1},{3,2},{4,7},{5,4},{6,5},{7,6},{8,11},{9,8},{10,9... | collective-permute-start | bytes 1474568 | tf_op jit(solution)/shard_map/ppermute | solution.py:68
  21.3 23.5 %collective-permute-start.7 = (bf16[8,2,4,2,1920]{4,3,2,1,0:T(2,128)(2,1)S(1)}, bf16[8,2,4,2,1920]{4,3,2,1,0:T(2,128)(2,1)S(1)}, u32[]{:S(2)}, u32[]{:S(2)}) collective-permute-start(bf16[8,2,4,2,1920]{4,3,2,1,0:T(2,128)(2,1)S(1)} %get-tuple-element.27), channel_id=1, source_target_pairs={{0,2},{1,3},{2,0},{3,1},{4,6},{5,7},{6,4},{7,5},{8,10},{9,11},{10,... | collective-permute-start | bytes 1474568 | tf_op jit(solution)/shard_map/ppermute | solution.py:69
  21.8 35.0 %collective-permute-start.8 = (bf16[8,2,4,2,1920]{4,3,2,1,0:T(2,128)(2,1)S(1)}, bf16[8,2,4,2,1920]{4,3,2,1,0:T(2,128)(2,1)S(1)}, u32[]{:S(2)}, u32[]{:S(2)}) collective-permute-start(bf16[8,2,4,2,1920]{4,3,2,1,0:T(2,128)(2,1)S(1)} %get-tuple-element.28), channel_id=1, source_target_pairs={{0,1},{1,2},{2,3},{3,0},{4,5},{5,6},{6,7},{7,4},{8,9},{9,10},{10,1... | collective-permute-start | bytes 1474568 | tf_op jit(solution)/shard_map/ppermute | solution.py:67
  39.2 21.4 %collective-permute-start.3 = (bf16[8,2,1,2,1920]{4,3,2,1,0:T(2,128)(2,1)S(1)}, bf16[8,2,1,2,1920]{4,3,2,1,0:T(2,128)(2,1)S(1)}, u32[]{:S(2)}, u32[]{:S(2)}) collective-permute-start(bf16[8,2,1,2,1920]{4,3,2,1,0:T(2,128)(2,1)S(1)} %get-tuple-element.22), channel_id=1, source_target_pairs={{0,3},{1,0},{2,1},{3,2},{4,7},{5,4},{6,5},{7,6},{8,11},{9,8},{10,9... | collective-permute-start | bytes 368648 | tf_op jit(solution)/shard_map/ppermute | solution.py:68
  40.4 20.2 %collective-permute-start.4 = (bf16[8,2,1,2,1920]{4,3,2,1,0:T(2,128)(2,1)S(1)}, bf16[8,2,1,2,1920]{4,3,2,1,0:T(2,128)(2,1)S(1)}, u32[]{:S(2)}, u32[]{:S(2)}) collective-permute-start(bf16[8,2,1,2,1920]{4,3,2,1,0:T(2,128)(2,1)S(1)} %get-tuple-element.23), channel_id=1, source_target_pairs={{0,2},{1,3},{2,0},{3,1},{4,6},{5,7},{6,4},{7,5},{8,10},{9,11},{10,... | collective-permute-start | bytes 368648 | tf_op jit(solution)/shard_map/ppermute | solution.py:69
  44.6 16.5 %collective-permute-start.5 = (bf16[8,2,1,2,1920]{4,3,2,1,0:T(2,128)(2,1)S(1)}, bf16[8,2,1,2,1920]{4,3,2,1,0:T(2,128)(2,1)S(1)}, u32[]{:S(2)}, u32[]{:S(2)}) collective-permute-start(bf16[8,2,1,2,1920]{4,3,2,1,0:T(2,128)(2,1)S(1)} %get-tuple-element.24), channel_id=1, source_target_pairs={{0,1},{1,2},{2,3},{3,0},{4,5},{5,6},{6,7},{7,4},{8,9},{9,10},{10,1... | collective-permute-start | bytes 368648 | tf_op jit(solution)/shard_map/ppermute | solution.py:67

commit v18 on v11

--- a/solution.py
+++ b/solution.py
@@ -128,7 +128,7 @@
             weight = 1.0 / jnp.sqrt((power_a + EPS) * (power_b + EPS))
             rows.append(sums[64 + k * 16 : 72 + k * 16, :] * weight)
             rows.append(sums[72 + k * 16 : 80 + k * 16, :] * weight)
-        out[pl.ds(start, ITEMS), owner] = jnp.swapaxes(jnp.stack(rows, axis=0), 0, 1)
+        out[owner, pl.ds(start, ITEMS)] = jnp.swapaxes(jnp.stack(rows, axis=0), 0, 1)
 
 
 def whole_kernel(epochs, own, one, two, three, box, table, out, img, hi, lo, sums):
@@ -180,8 +180,8 @@
         position = table[burst]
         valid = jnp.where(position < table[32], 1.0, 0.0).astype(jnp.float32)
         base = pl.multiple_of(position * 16, 16)
-        rows[pl.ds(base, 8), :] = got[burst, half] * valid
-        rows[pl.ds(base + 8, 8), :] = got[burst, 2 + half] * valid
+        rows[pl.ds(base, 8), :] = got[half, burst] * valid
+        rows[pl.ds(base + 8, 8), :] = got[2 + half, burst] * valid
     for plane in range(8):
         for part in range(8):
             out[plane // 2, plane % 2, part * 8 : part * 8 + 8, :] = rows[
@@ -200,15 +200,15 @@
     first = meet(*cut(images, CHUNKS[0]))
     second = meet(*cut(images, CHUNKS[1], first[3]))
 
-    shape = jax.ShapeDtypeStruct((32, 4, 8, LCOL), jnp.float32)
+    shape = jax.ShapeDtypeStruct((4, 32, 8, LCOL), jnp.float32)
     partial = jax.ShapeDtypeStruct((ROWS, LCOL), jnp.float32)
     gamma = looks(whole_kernel, epochs, (*first, box, table), shape, 5)
     third = meet(*cut(images, CHUNKS[2], gamma))
     most = looks(most_kernel, epochs, (*second, box, gamma), partial, 4)
     gamma = looks(last_kernel, epochs, (*third, box, most, gamma), shape, 1, {7: 0})
     got = lax.all_to_all(
-        gamma.reshape(128, 8, LCOL), ("tile", "date"), split_axis=0, concat_axis=0, tiled=True
-    ).reshape(32, 4, 8, LCOL)
+        gamma.reshape(128, 8, LCOL), ("date", "tile"), split_axis=0, concat_axis=0, tiled=True
+    ).reshape(4, 32, 8, LCOL)
     return pl.pallas_call(
         place_kernel,
         out_shape=jax.ShapeDtypeStruct((4, 2, 64, LCOL), jnp.float32),

time: 88.1 us -> 87.7 us (level)
  no operation moved by 1% of the time
where the time goes in v18:
time: 87.7 us; the launch traced here: 87.5 us
  waiting for transfers between devices  37.1 us (42%)
  blocking collectives  22.7 us (26%)
  Pallas kernels  13.7 us (16%)
  starting transfers between devices  10.5 us (12%)
  local copies, waits for them, and re-layouts  2.42 us (3%)
    ppermute x3, waiting for transfers between devices, meet(): three = lax.ppermute(to1, 'date', ring(1))  23.2 us
    all_to_all x1, blocking collectives, on_device(): lax.all_to_all(gamma.reshape(128, 8, LCOL), ('date', 'tile'), split_axis=...  22.7 us
    pallas_call x3, Pallas kernels, looks(): pl.pallas_call(kernel, out_shape=out_shape, grid_spec=pltpu.PrefetchScala...  11.4 us
    ppermute x3, waiting for transfers between devices, meet(): two = lax.ppermute(to2, 'date', ring(2))  11 us
    ppermute x3, starting transfers between devices, meet(): one = lax.ppermute(to3, 'date', ring(3))  4.17 us
    ppermute x3, starting transfers between devices, meet(): two = lax.ppermute(to2, 'date', ring(2))  3.41 us
    ppermute x3, waiting for transfers between devices, meet(): one = lax.ppermute(to3, 'date', ring(3))  2.92 us
    ppermute x3, starting transfers between devices, meet(): three = lax.ppermute(to1, 'date', ring(1))  2.92 us
  transfers between devices with their start and end apart: 9, of which 5 were waited for; matrix products, arithmetic and copies ran while one was open for 0% of the time, Pallas kernels for 11%

profile of v18, /device:TPU:1, one launch (start us, length us, event | category | flops | bytes accessed | tf_op | source)
XLA Modules:
  0.0 87.5 jit_solution(14551556366547091103)
XLA Ops:
  0.0 2.4 %copy-done = bf16[2,1,32,2,10,1920]{5,3,4,2,1,0:T(2,128)(2,1)S(1)} copy-done((bf16[2,1,32,2,10,1920]{5,3,4,2,1,0:T(2,128)(2,1)S(1)}, bf16[2,1,32,2,10,1920]{5,3,4,2,1,0:T(2,128)(2,1)}, u32[]{:S(2)}) %copy-start) | copy-done | bytes 4915224
  2.4 0.3 shard_map.46
  2.7 2.1 %collective-permute-start.2 = (bf16[8,2,5,2,1920]{4,3,2,1,0:T(2,128)(2,1)S(1)}, bf16[8,2,5,2,1920]{4,3,2,1,0:T(2,128)(2,1)S(1)}, u32[]{:S(2)}, u32[]{:S(2)}) collective-permute-start(bf16[8,2,5,2,1920]{4,3,2,1,0:T(2,128)(2,1)S(1)} %get-tuple-element.20), channel_id=1, source_target_pairs={{0,1},{1,2},{2,3},{3,0},{4,5},{5,6},{6,7},{7,4},{8,9},{9,10},{10,1... | collective-permute-start | bytes 1843208 | tf_op jit(solution)/shard_map/ppermute | solution.py:67
  4.8 1.3 %collective-permute-start = (bf16[8,2,5,2,1920]{4,3,2,1,0:T(2,128)(2,1)S(1)}, bf16[8,2,5,2,1920]{4,3,2,1,0:T(2,128)(2,1)S(1)}, u32[]{:S(2)}, u32[]{:S(2)}) collective-permute-start(bf16[8,2,5,2,1920]{4,3,2,1,0:T(2,128)(2,1)S(1)} %get-tuple-element.18), channel_id=1, source_target_pairs={{0,3},{1,0},{2,1},{3,2},{4,7},{5,4},{6,5},{7,6},{8,11},{9,8},{10,9... | collective-permute-start | bytes 1843208 | tf_op jit(solution)/shard_map/ppermute | solution.py:68
  6.2 1.6 %collective-permute-start.1 = (bf16[8,2,5,2,1920]{4,3,2,1,0:T(2,128)(2,1)S(1)}, bf16[8,2,5,2,1920]{4,3,2,1,0:T(2,128)(2,1)S(1)}, u32[]{:S(2)}, u32[]{:S(2)}) collective-permute-start(bf16[8,2,5,2,1920]{4,3,2,1,0:T(2,128)(2,1)S(1)} %get-tuple-element.19), channel_id=1, source_target_pairs={{0,2},{1,3},{2,0},{3,1},{4,6},{5,7},{6,4},{7,5},{8,10},{9,11},{10,... | collective-permute-start | bytes 1843208 | tf_op jit(solution)/shard_map/ppermute | solution.py:69
  8.6 10.7 %collective-permute-done.2.three.rest_0_ = bf16[8,2,5,2,1920]{4,3,2,1,0:T(2,128)(2,1)S(1)} collective-permute-done((bf16[8,2,5,2,1920]{4,3,2,1,0:T(2,128)(2,1)S(1)}, bf16[8,2,5,2,1920]{4,3,2,1,0:T(2,128)(2,1)S(1)}, u32[]{:S(2)}, u32[]{:S(2)}) %collective-permute-start.2) | collective-permute-done | bytes 614432 | tf_op jit(solution)/shard_map/ppermute | solution.py:67
  19.2 0.4 shard_map.49
  19.7 1.7 %collective-permute-start.6 = (bf16[8,2,4,2,1920]{4,3,2,1,0:T(2,128)(2,1)S(1)}, bf16[8,2,4,2,1920]{4,3,2,1,0:T(2,128)(2,1)S(1)}, u32[]{:S(2)}, u32[]{:S(2)}) collective-permute-start(bf16[8,2,4,2,1920]{4,3,2,1,0:T(2,128)(2,1)S(1)} %get-tuple-element.26), channel_id=1, source_target_pairs={{0,3},{1,0},{2,1},{3,2},{4,7},{5,4},{6,5},{7,6},{8,11},{9,8},{10,9... | collective-permute-start | bytes 1474568 | tf_op jit(solution)/shard_map/ppermute | solution.py:68
  21.3 0.5 collective-permute-start.7
  21.8 0.6 collective-permute-start.8
  22.5 0.3 fusion.box
  22.8 11.0 %collective-permute-done.1.two = bf16[8,2,5,2,1920]{4,3,2,1,0:T(2,128)(2,1)S(1)} collective-permute-done((bf16[8,2,5,2,1920]{4,3,2,1,0:T(2,128)(2,1)S(1)}, bf16[8,2,5,2,1920]{4,3,2,1,0:T(2,128)(2,1)S(1)}, u32[]{:S(2)}, u32[]{:S(2)}) %collective-permute-start.1) | collective-permute-done | bytes 614432 | tf_op jit(solution)/shard_map/ppermute | solution.py:69
  33.8 5.4 %shard_map.47.rest_0_.after.given = f32[4,32,8,128]{3,2,1,0:T(8,128)S(1)} custom-call(s32[2,16]{1,0:T(2,128)S(1)} %bitcast.12, bf16[8,2,5,2,1920]{4,3,2,1,0:T(2,128)(2,1)S(1)} %get-tuple-element.17.own, bf16[8,2,5,2,1920]{4,3,2,1,0:T(2,128)(2,1)S(1)} %collective-permute-done.one, bf16[8,2,5,2,1920]{4,3,2,1,0:T(2,128)(2,1)S(1)} %collective-permute-done.1.two, ...), custom_call_target="tpu_custom_call" | custom-call | flops 326860800 | bytes 2457600 | tf_op jit(solution)/shard_map/pallas_call | solution.py:154
  39.1 0.2 shard_map.48
  39.3 1.2 %collective-permute-start.3 = (bf16[8,2,1,2,1920]{4,3,2,1,0:T(2,128)(2,1)S(1)}, bf16[8,2,1,2,1920]{4,3,2,1,0:T(2,128)(2,1)S(1)}, u32[]{:S(2)}, u32[]{:S(2)}) collective-permute-start(bf16[8,2,1,2,1920]{4,3,2,1,0:T(2,128)(2,1)S(1)} %get-tuple-element.22), channel_id=1, source_target_pairs={{0,3},{1,0},{2,1},{3,2},{4,7},{5,4},{6,5},{7,6},{8,11},{9,8},{10,9... | collective-permute-start | bytes 368648 | tf_op jit(solution)/shard_map/ppermute | solution.py:68
  40.5 1.2 %collective-permute-start.4 = (bf16[8,2,1,2,1920]{4,3,2,1,0:T(2,128)(2,1)S(1)}, bf16[8,2,1,2,1920]{4,3,2,1,0:T(2,128)(2,1)S(1)}, u32[]{:S(2)}, u32[]{:S(2)}) collective-permute-start(bf16[8,2,1,2,1920]{4,3,2,1,0:T(2,128)(2,1)S(1)} %get-tuple-element.23), channel_id=1, source_target_pairs={{0,2},{1,3},{2,0},{3,1},{4,6},{5,7},{6,4},{7,5},{8,10},{9,11},{10,... | collective-permute-start | bytes 368648 | tf_op jit(solution)/shard_map/ppermute | solution.py:69
  41.7 2.9 %collective-permute-done.6.one = bf16[8,2,4,2,1920]{4,3,2,1,0:T(2,128)(2,1)S(1)} collective-permute-done((bf16[8,2,4,2,1920]{4,3,2,1,0:T(2,128)(2,1)S(1)}, bf16[8,2,4,2,1920]{4,3,2,1,0:T(2,128)(2,1)S(1)}, u32[]{:S(2)}, u32[]{:S(2)}) %collective-permute-start.6) | collective-permute-done | bytes 491552 | tf_op jit(solution)/shard_map/ppermute | solution.py:68
  44.6 0.2 collective-permute-start.5
  44.8 12.0 %collective-permute-done.8.three = bf16[8,2,4,2,1920]{4,3,2,1,0:T(2,128)(2,1)S(1)} collective-permute-done((bf16[8,2,4,2,1920]{4,3,2,1,0:T(2,128)(2,1)S(1)}, bf16[8,2,4,2,1920]{4,3,2,1,0:T(2,128)(2,1)S(1)}, u32[]{:S(2)}, u32[]{:S(2)}) %collective-permute-start.8) | collective-permute-done | bytes 491552 | tf_op jit(solution)/shard_map/ppermute | solution.py:67
  56.8 3.8 %shard_map.50.most = f32[320,128]{1,0:T(8,128)S(1)} custom-call(s32[2,16]{1,0:T(2,128)S(1)} %bitcast.13, bf16[8,2,4,2,1920]{4,3,2,1,0:T(2,128)(2,1)S(1)} %get-tuple-element.25.own, bf16[8,2,4,2,1920]{4,3,2,1,0:T(2,128)(2,1)S(1)} %collective-permute-done.6.one, bf16[8,2,4,2,1920]{4,3,2,1,0:T(2,128)(2,1)S(1)} %collective-permute-done.7.two, ...), custom_call_target="tpu_custom_call" | custom-call | flops 324403200 | bytes 1966080 | tf_op jit(solution)/shard_map/pallas_call | solution.py:154
  60.6 0.5 collective-permute-done.5.three
  61.2 2.3 %shard_map.51 = f32[4,32,8,128]{3,2,1,0:T(8,128)S(1)} custom-call(s32[2,16]{1,0:T(2,128)S(1)} %bitcast.14, bf16[8,2,1,2,1920]{4,3,2,1,0:T(2,128)(2,1)S(1)} %get-tuple-element.21.own, bf16[8,2,1,2,1920]{4,3,2,1,0:T(2,128)(2,1)S(1)} %collective-permute-done.3.one, ...), custom_call_target="tpu_custom_call", output_to_operand_aliasing={{}: (7, {})} | custom-call | flops 317030400 | bytes 491520 | tf_op jit(solution)/shard_map/pallas_call | solution.py:154
  63.5 22.7 %all_to_all.5 = f32[128,8,128]{2,1,0:T(8,128)S(1)} all-to-all(f32[128,8,128]{2,1,0:T(8,128)S(1)} %bitcast.10), channel_id=1, replica_groups=mesh['tile'=32,'date'=4] {'date','tile'}, dimensions={0} | all-to-all | bytes 1048576 | tf_op jit(solution)/shard_map/all_to_all | solution.py:209
  86.2 1.4 %shard_map.52 = f32[4,2,64,128]{3,2,1,0:T(8,128)} custom-call(s32[33]{0:T(128)S(1)} %pad_add_fusion.table, f32[4,32,8,128]{3,2,1,0:T(8,128)S(1)} %bitcast.11), custom_call_target="tpu_custom_call" | custom-call | tf_op jit(solution)/shard_map/pallas_call | solution.py:212
  (13 shorter events, 0.1 us)
Async XLA Ops:
  0.0 8.5 %copy-start.3 = (s32[1,32]{1,0:T(1,128)S(1)}, s32[1,32]{1,0:T(1,128)}, u32[]{:S(2)}) copy-start(s32[1,32]{1,0:T(1,128)} %param.5) | copy-start | bytes 388
  0.0 2.4 %copy-start = (bf16[2,1,32,2,10,1920]{5,3,4,2,1,0:T(2,128)(2,1)S(1)}, bf16[2,1,32,2,10,1920]{5,3,4,2,1,0:T(2,128)(2,1)}, u32[]{:S(2)}) copy-start(bf16[2,1,32,2,10,1920]{5,3,4,2,1,0:T(2,128)(2,1)} %param.4) | copy-start | bytes 14745604
  2.4 16.8 %copy-start.1 = (bf16[2,1,32,2,10,1920]{5,3,4,2,1,0:T(2,128)(2,1)S(1)}, bf16[2,1,32,2,10,1920]{5,3,4,2,1,0:T(2,128)(2,1)}, u32[]{:S(2)}) copy-start(bf16[2,1,32,2,10,1920]{5,3,4,2,1,0:T(2,128)(2,1)} %param.4) | copy-start | bytes 14745604
  2.4 31.3 %copy-start.2 = (s32[16,2]{0,1:T(2,128)S(1)}, s32[16,2]{0,1:T(2,128)}, u32[]{:S(2)}) copy-start(s32[16,2]{0,1:T(2,128)} %param.7) | copy-start | bytes 388
  2.7 16.5 %collective-permute-start.2 = (bf16[8,2,5,2,1920]{4,3,2,1,0:T(2,128)(2,1)S(1)}, bf16[8,2,5,2,1920]{4,3,2,1,0:T(2,128)(2,1)S(1)}, u32[]{:S(2)}, u32[]{:S(2)}) collective-permute-start(bf16[8,2,5,2,1920]{4,3,2,1,0:T(2,128)(2,1)S(1)} %get-tuple-element.20), channel_id=1, source_target_pairs={{0,1},{1,2},{2,3},{3,0},{4,5},{5,6},{6,7},{7,4},{8,9},{9,10},{10,1... | collective-permute-start | bytes 1843208 | tf_op jit(solution)/shard_map/ppermute | solution.py:67
  4.8 18.0 %collective-permute-start = (bf16[8,2,5,2,1920]{4,3,2,1,0:T(2,128)(2,1)S(1)}, bf16[8,2,5,2,1920]{4,3,2,1,0:T(2,128)(2,1)S(1)}, u32[]{:S(2)}, u32[]{:S(2)}) collective-permute-start(bf16[8,2,5,2,1920]{4,3,2,1,0:T(2,128)(2,1)S(1)} %get-tuple-element.18), channel_id=1, source_target_pairs={{0,3},{1,0},{2,1},{3,2},{4,7},{5,4},{6,5},{7,6},{8,11},{9,8},{10,9... | collective-permute-start | bytes 1843208 | tf_op jit(solution)/shard_map/ppermute | solution.py:68
  6.2 27.6 %collective-permute-start.1 = (bf16[8,2,5,2,1920]{4,3,2,1,0:T(2,128)(2,1)S(1)}, bf16[8,2,5,2,1920]{4,3,2,1,0:T(2,128)(2,1)S(1)}, u32[]{:S(2)}, u32[]{:S(2)}) collective-permute-start(bf16[8,2,5,2,1920]{4,3,2,1,0:T(2,128)(2,1)S(1)} %get-tuple-element.19), channel_id=1, source_target_pairs={{0,2},{1,3},{2,0},{3,1},{4,6},{5,7},{6,4},{7,5},{8,10},{9,11},{10,... | collective-permute-start | bytes 1843208 | tf_op jit(solution)/shard_map/ppermute | solution.py:69
  19.7 25.0 %collective-permute-start.6 = (bf16[8,2,4,2,1920]{4,3,2,1,0:T(2,128)(2,1)S(1)}, bf16[8,2,4,2,1920]{4,3,2,1,0:T(2,128)(2,1)S(1)}, u32[]{:S(2)}, u32[]{:S(2)}) collective-permute-start(bf16[8,2,4,2,1920]{4,3,2,1,0:T(2,128)(2,1)S(1)} %get-tuple-element.26), channel_id=1, source_target_pairs={{0,3},{1,0},{2,1},{3,2},{4,7},{5,4},{6,5},{7,6},{8,11},{9,8},{10,9... | collective-permute-start | bytes 1474568 | tf_op jit(solution)/shard_map/ppermute | solution.py:68
  21.3 23.5 %collective-permute-start.7 = (bf16[8,2,4,2,1920]{4,3,2,1,0:T(2,128)(2,1)S(1)}, bf16[8,2,4,2,1920]{4,3,2,1,0:T(2,128)(2,1)S(1)}, u32[]{:S(2)}, u32[]{:S(2)}) collective-permute-start(bf16[8,2,4,2,1920]{4,3,2,1,0:T(2,128)(2,1)S(1)} %get-tuple-element.27), channel_id=1, source_target_pairs={{0,2},{1,3},{2,0},{3,1},{4,6},{5,7},{6,4},{7,5},{8,10},{9,11},{10,... | collective-permute-start | bytes 1474568 | tf_op jit(solution)/shard_map/ppermute | solution.py:69
  21.8 35.0 %collective-permute-start.8 = (bf16[8,2,4,2,1920]{4,3,2,1,0:T(2,128)(2,1)S(1)}, bf16[8,2,4,2,1920]{4,3,2,1,0:T(2,128)(2,1)S(1)}, u32[]{:S(2)}, u32[]{:S(2)}) collective-permute-start(bf16[8,2,4,2,1920]{4,3,2,1,0:T(2,128)(2,1)S(1)} %get-tuple-element.28), channel_id=1, source_target_pairs={{0,1},{1,2},{2,3},{3,0},{4,5},{5,6},{6,7},{7,4},{8,9},{9,10},{10,1... | collective-permute-start | bytes 1474568 | tf_op jit(solution)/shard_map/ppermute | solution.py:67
  39.3 21.3 %collective-permute-start.3 = (bf16[8,2,1,2,1920]{4,3,2,1,0:T(2,128)(2,1)S(1)}, bf16[8,2,1,2,1920]{4,3,2,1,0:T(2,128)(2,1)S(1)}, u32[]{:S(2)}, u32[]{:S(2)}) collective-permute-start(bf16[8,2,1,2,1920]{4,3,2,1,0:T(2,128)(2,1)S(1)} %get-tuple-element.22), channel_id=1, source_target_pairs={{0,3},{1,0},{2,1},{3,2},{4,7},{5,4},{6,5},{7,6},{8,11},{9,8},{10,9... | collective-permute-start | bytes 368648 | tf_op jit(solution)/shard_map/ppermute | solution.py:68
  40.5 20.2 %collective-permute-start.4 = (bf16[8,2,1,2,1920]{4,3,2,1,0:T(2,128)(2,1)S(1)}, bf16[8,2,1,2,1920]{4,3,2,1,0:T(2,128)(2,1)S(1)}, u32[]{:S(2)}, u32[]{:S(2)}) collective-permute-start(bf16[8,2,1,2,1920]{4,3,2,1,0:T(2,128)(2,1)S(1)} %get-tuple-element.23), channel_id=1, source_target_pairs={{0,2},{1,3},{2,0},{3,1},{4,6},{5,7},{6,4},{7,5},{8,10},{9,11},{10,... | collective-permute-start | bytes 368648 | tf_op jit(solution)/shard_map/ppermute | solution.py:69
  44.6 16.5 %collective-permute-start.5 = (bf16[8,2,1,2,1920]{4,3,2,1,0:T(2,128)(2,1)S(1)}, bf16[8,2,1,2,1920]{4,3,2,1,0:T(2,128)(2,1)S(1)}, u32[]{:S(2)}, u32[]{:S(2)}) collective-permute-start(bf16[8,2,1,2,1920]{4,3,2,1,0:T(2,128)(2,1)S(1)} %get-tuple-element.24), channel_id=1, source_target_pairs={{0,1},{1,2},{2,3},{3,0},{4,5},{5,6},{6,7},{7,4},{8,9},{9,10},{10,1... | collective-permute-start | bytes 368648 | tf_op jit(solution)/shard_map/ppermute | solution.py:67

commit v19 on v18

--- a/solution.py
+++ b/solution.py
@@ -125,7 +125,7 @@
             k = owner * 4 + kk
             power_a = sums[pl.ds(pl.multiple_of(epochs[0, k] * 8, 8), 8), :]
             power_b = sums[pl.ds(pl.multiple_of(epochs[1, k] * 8, 8), 8), :]
-            weight = 1.0 / jnp.sqrt((power_a + EPS) * (power_b + EPS))
+            weight = lax.rsqrt((power_a + EPS) * (power_b + EPS))
             rows.append(sums[64 + k * 16 : 72 + k * 16, :] * weight)
             rows.append(sums[72 + k * 16 : 80 + k * 16, :] * weight)
         out[owner, pl.ds(start, ITEMS)] = jnp.swapaxes(jnp.stack(rows, axis=0), 0, 1)
@@ -176,16 +176,21 @@
 
 def place_kernel(table, got, out, rows):
     half = lax.div(lax.axis_index("tile"), HALF)
-    for burst in range(32):
-        position = table[burst]
-        valid = jnp.where(position < table[32], 1.0, 0.0).astype(jnp.float32)
-        base = pl.multiple_of(position * 16, 16)
-        rows[pl.ds(base, 8), :] = got[half, burst] * valid
-        rows[pl.ds(base + 8, 8), :] = got[2 + half, burst] * valid
-    for plane in range(8):
-        for part in range(8):
-            out[plane // 2, plane % 2, part * 8 : part * 8 + 8, :] = rows[
-                pl.ds(part * 64 + plane, 8, stride=8), :
+    pair = pl.program_id(0)
+
+    @pl.when(pair == 0)
+    def _():
+        for burst in range(32):
+            position = table[burst]
+            valid = jnp.where(position < table[32], 1.0, 0.0).astype(jnp.float32)
+            base = pl.multiple_of(position * 16, 16)
+            rows[pl.ds(base, 8), :] = got[half, burst] * valid
+            rows[pl.ds(base + 8, 8), :] = got[2 + half, burst] * valid
+
+    for part in range(2):
+        for eight in range(8):
+            out[0, part, eight * 8 : eight * 8 + 8, :] = rows[
+                pl.ds(eight * 64 + pair * 2 + part, 8, stride=8), :
             ]
 
 
@@ -214,9 +219,9 @@
         out_shape=jax.ShapeDtypeStruct((4, 2, 64, LCOL), jnp.float32),
         grid_spec=pltpu.PrefetchScalarGridSpec(
             num_scalar_prefetch=1,
-            grid=(),
+            grid=(4,),
             in_specs=[VMEM],
-            out_specs=VMEM,
+            out_specs=pl.BlockSpec((1, 2, 64, LCOL), lambda pair, table: (pair, 0, 0, 0)),
             scratch_shapes=[pltpu.VMEM((512, LCOL), jnp.float32)],
         ),
         compiler_params=pltpu.CompilerParams(vmem_limit_bytes=4 << 20),

time: 87.7 us -> 88.2 us (level)
  no operation moved by 1% of the time
where the time goes in v19:
time: 88.2 us; the launch traced here: 88.1 us
  waiting for transfers between devices  36.9 us (42%)
  blocking collectives  22.7 us (26%)
  Pallas kernels  14.4 us (16%)
  starting transfers between devices  10.5 us (12%)
  local copies, waits for them, and re-layouts  2.42 us (3%)
    ppermute x3, waiting for transfers between devices, meet(): three = lax.ppermute(to1, 'date', ring(1))  23.2 us
    all_to_all x1, blocking collectives, on_device(): lax.all_to_all(gamma.reshape(128, 8, LCOL), ('date', 'tile'), split_axis=...  22.7 us
    pallas_call x3, Pallas kernels, looks(): pl.pallas_call(kernel, out_shape=out_shape, grid_spec=pltpu.PrefetchScala...  11.6 us
    ppermute x3, waiting for transfers between devices, meet(): two = lax.ppermute(to2, 'date', ring(2))  11 us
    ppermute x3, starting transfers between devices, meet(): one = lax.ppermute(to3, 'date', ring(3))  4.17 us
    ppermute x3, starting transfers between devices, meet(): two = lax.ppermute(to2, 'date', ring(2))  3.41 us
    ppermute x3, starting transfers between devices, meet(): three = lax.ppermute(to1, 'date', ring(1))  2.92 us
    ppermute x3, waiting for transfers between devices, meet(): one = lax.ppermute(to3, 'date', ring(3))  2.79 us
  transfers between devices with their start and end apart: 9, of which 5 were waited for; matrix products, arithmetic and copies ran while one was open for 0% of the time, Pallas kernels for 11%

profile of v19, /device:TPU:1, one launch (start us, length us, event | category | flops | bytes accessed | tf_op | source)
XLA Modules:
  0.0 88.1 jit_solution(1688814116054338370)
XLA Ops:
  0.0 2.4 %copy-done = bf16[2,1,32,2,10,1920]{5,3,4,2,1,0:T(2,128)(2,1)S(1)} copy-done((bf16[2,1,32,2,10,1920]{5,3,4,2,1,0:T(2,128)(2,1)S(1)}, bf16[2,1,32,2,10,1920]{5,3,4,2,1,0:T(2,128)(2,1)}, u32[]{:S(2)}) %copy-start) | copy-done | bytes 4915224
  2.4 0.3 shard_map.46
  2.7 2.1 %collective-permute-start.2 = (bf16[8,2,5,2,1920]{4,3,2,1,0:T(2,128)(2,1)S(1)}, bf16[8,2,5,2,1920]{4,3,2,1,0:T(2,128)(2,1)S(1)}, u32[]{:S(2)}, u32[]{:S(2)}) collective-permute-start(bf16[8,2,5,2,1920]{4,3,2,1,0:T(2,128)(2,1)S(1)} %get-tuple-element.20), channel_id=1, source_target_pairs={{0,1},{1,2},{2,3},{3,0},{4,5},{5,6},{6,7},{7,4},{8,9},{9,10},{10,1... | collective-permute-start | bytes 1843208 | tf_op jit(solution)/shard_map/ppermute | solution.py:67
  4.8 1.3 %collective-permute-start = (bf16[8,2,5,2,1920]{4,3,2,1,0:T(2,128)(2,1)S(1)}, bf16[8,2,5,2,1920]{4,3,2,1,0:T(2,128)(2,1)S(1)}, u32[]{:S(2)}, u32[]{:S(2)}) collective-permute-start(bf16[8,2,5,2,1920]{4,3,2,1,0:T(2,128)(2,1)S(1)} %get-tuple-element.18), channel_id=1, source_target_pairs={{0,3},{1,0},{2,1},{3,2},{4,7},{5,4},{6,5},{7,6},{8,11},{9,8},{10,9... | collective-permute-start | bytes 1843208 | tf_op jit(solution)/shard_map/ppermute | solution.py:68
  6.2 1.6 %collective-permute-start.1 = (bf16[8,2,5,2,1920]{4,3,2,1,0:T(2,128)(2,1)S(1)}, bf16[8,2,5,2,1920]{4,3,2,1,0:T(2,128)(2,1)S(1)}, u32[]{:S(2)}, u32[]{:S(2)}) collective-permute-start(bf16[8,2,5,2,1920]{4,3,2,1,0:T(2,128)(2,1)S(1)} %get-tuple-element.19), channel_id=1, source_target_pairs={{0,2},{1,3},{2,0},{3,1},{4,6},{5,7},{6,4},{7,5},{8,10},{9,11},{10,... | collective-permute-start | bytes 1843208 | tf_op jit(solution)/shard_map/ppermute | solution.py:69
  8.6 10.7 %collective-permute-done.2.three.rest_0_ = bf16[8,2,5,2,1920]{4,3,2,1,0:T(2,128)(2,1)S(1)} collective-permute-done((bf16[8,2,5,2,1920]{4,3,2,1,0:T(2,128)(2,1)S(1)}, bf16[8,2,5,2,1920]{4,3,2,1,0:T(2,128)(2,1)S(1)}, u32[]{:S(2)}, u32[]{:S(2)}) %collective-permute-start.2) | collective-permute-done | bytes 614432 | tf_op jit(solution)/shard_map/ppermute | solution.py:67
  19.2 0.4 shard_map.49
  19.7 1.7 %collective-permute-start.6 = (bf16[8,2,4,2,1920]{4,3,2,1,0:T(2,128)(2,1)S(1)}, bf16[8,2,4,2,1920]{4,3,2,1,0:T(2,128)(2,1)S(1)}, u32[]{:S(2)}, u32[]{:S(2)}) collective-permute-start(bf16[8,2,4,2,1920]{4,3,2,1,0:T(2,128)(2,1)S(1)} %get-tuple-element.26), channel_id=1, source_target_pairs={{0,3},{1,0},{2,1},{3,2},{4,7},{5,4},{6,5},{7,6},{8,11},{9,8},{10,9... | collective-permute-start | bytes 1474568 | tf_op jit(solution)/shard_map/ppermute | solution.py:68
  21.3 0.5 collective-permute-start.7
  21.8 0.6 collective-permute-start.8
  22.5 0.3 fusion.box
  22.8 11.0 %collective-permute-done.1.two = bf16[8,2,5,2,1920]{4,3,2,1,0:T(2,128)(2,1)S(1)} collective-permute-done((bf16[8,2,5,2,1920]{4,3,2,1,0:T(2,128)(2,1)S(1)}, bf16[8,2,5,2,1920]{4,3,2,1,0:T(2,128)(2,1)S(1)}, u32[]{:S(2)}, u32[]{:S(2)}) %collective-permute-start.1) | collective-permute-done | bytes 614432 | tf_op jit(solution)/shard_map/ppermute | solution.py:69
  33.8 5.5 %shard_map.47.rest_0_.after.given = f32[4,32,8,128]{3,2,1,0:T(8,128)S(1)} custom-call(s32[2,16]{1,0:T(2,128)S(1)} %bitcast.12, bf16[8,2,5,2,1920]{4,3,2,1,0:T(2,128)(2,1)S(1)} %get-tuple-element.17.own, bf16[8,2,5,2,1920]{4,3,2,1,0:T(2,128)(2,1)S(1)} %collective-permute-done.one, bf16[8,2,5,2,1920]{4,3,2,1,0:T(2,128)(2,1)S(1)} %collective-permute-done.1.two, ...), custom_call_target="tpu_custom_call" | custom-call | flops 326860800 | bytes 2457600 | tf_op jit(solution)/shard_map/pallas_call | solution.py:154
  39.3 0.2 shard_map.48
  39.4 1.2 %collective-permute-start.3 = (bf16[8,2,1,2,1920]{4,3,2,1,0:T(2,128)(2,1)S(1)}, bf16[8,2,1,2,1920]{4,3,2,1,0:T(2,128)(2,1)S(1)}, u32[]{:S(2)}, u32[]{:S(2)}) collective-permute-start(bf16[8,2,1,2,1920]{4,3,2,1,0:T(2,128)(2,1)S(1)} %get-tuple-element.22), channel_id=1, source_target_pairs={{0,3},{1,0},{2,1},{3,2},{4,7},{5,4},{6,5},{7,6},{8,11},{9,8},{10,9... | collective-permute-start | bytes 368648 | tf_op jit(solution)/shard_map/ppermute | solution.py:68
  40.6 1.2 %collective-permute-start.4 = (bf16[8,2,1,2,1920]{4,3,2,1,0:T(2,128)(2,1)S(1)}, bf16[8,2,1,2,1920]{4,3,2,1,0:T(2,128)(2,1)S(1)}, u32[]{:S(2)}, u32[]{:S(2)}) collective-permute-start(bf16[8,2,1,2,1920]{4,3,2,1,0:T(2,128)(2,1)S(1)} %get-tuple-element.23), channel_id=1, source_target_pairs={{0,2},{1,3},{2,0},{3,1},{4,6},{5,7},{6,4},{7,5},{8,10},{9,11},{10,... | collective-permute-start | bytes 368648 | tf_op jit(solution)/shard_map/ppermute | solution.py:69
  41.9 2.8 %collective-permute-done.6.one = bf16[8,2,4,2,1920]{4,3,2,1,0:T(2,128)(2,1)S(1)} collective-permute-done((bf16[8,2,4,2,1920]{4,3,2,1,0:T(2,128)(2,1)S(1)}, bf16[8,2,4,2,1920]{4,3,2,1,0:T(2,128)(2,1)S(1)}, u32[]{:S(2)}, u32[]{:S(2)}) %collective-permute-start.6) | collective-permute-done | bytes 491552 | tf_op jit(solution)/shard_map/ppermute | solution.py:68
  44.6 0.2 collective-permute-start.5
  44.8 12.0 %collective-permute-done.8.three = bf16[8,2,4,2,1920]{4,3,2,1,0:T(2,128)(2,1)S(1)} collective-permute-done((bf16[8,2,4,2,1920]{4,3,2,1,0:T(2,128)(2,1)S(1)}, bf16[8,2,4,2,1920]{4,3,2,1,0:T(2,128)(2,1)S(1)}, u32[]{:S(2)}, u32[]{:S(2)}) %collective-permute-start.8) | collective-permute-done | bytes 491552 | tf_op jit(solution)/shard_map/ppermute | solution.py:67
  56.8 3.8 %shard_map.50.most = f32[320,128]{1,0:T(8,128)S(1)} custom-call(s32[2,16]{1,0:T(2,128)S(1)} %bitcast.13, bf16[8,2,4,2,1920]{4,3,2,1,0:T(2,128)(2,1)S(1)} %get-tuple-element.25.own, bf16[8,2,4,2,1920]{4,3,2,1,0:T(2,128)(2,1)S(1)} %collective-permute-done.6.one, bf16[8,2,4,2,1920]{4,3,2,1,0:T(2,128)(2,1)S(1)} %collective-permute-done.7.two, ...), custom_call_target="tpu_custom_call" | custom-call | flops 324403200 | bytes 1966080 | tf_op jit(solution)/shard_map/pallas_call | solution.py:154
  60.6 0.5 collective-permute-done.5.three
  61.2 2.3 %shard_map.51 = f32[4,32,8,128]{3,2,1,0:T(8,128)S(1)} custom-call(s32[2,16]{1,0:T(2,128)S(1)} %bitcast.14, bf16[8,2,1,2,1920]{4,3,2,1,0:T(2,128)(2,1)S(1)} %get-tuple-element.21.own, bf16[8,2,1,2,1920]{4,3,2,1,0:T(2,128)(2,1)S(1)} %collective-permute-done.3.one, ...), custom_call_target="tpu_custom_call", output_to_operand_aliasing={{}: (7, {})} | custom-call | flops 317030400 | bytes 491520 | tf_op jit(solution)/shard_map/pallas_call | solution.py:154
  63.5 22.7 %all_to_all.5 = f32[128,8,128]{2,1,0:T(8,128)S(1)} all-to-all(f32[128,8,128]{2,1,0:T(8,128)S(1)} %bitcast.10), channel_id=1, replica_groups=mesh['tile'=32,'date'=4] {'date','tile'}, dimensions={0} | all-to-all | bytes 1048576 | tf_op jit(solution)/shard_map/all_to_all | solution.py:214
  86.1 1.9 %shard_map.52 = f32[4,2,64,128]{3,2,1,0:T(8,128)} custom-call(s32[33]{0:T(128)S(1)} %pad_add_fusion.table, f32[4,32,8,128]{3,2,1,0:T(8,128)S(1)} %bitcast.11), custom_call_target="tpu_custom_call" | custom-call | tf_op jit(solution)/shard_map/pallas_call | solution.py:217
  (13 shorter events, 0.1 us)
Async XLA Ops:
  0.0 8.5 %copy-start.3 = (s32[1,32]{1,0:T(1,128)S(1)}, s32[1,32]{1,0:T(1,128)}, u32[]{:S(2)}) copy-start(s32[1,32]{1,0:T(1,128)} %param.5) | copy-start | bytes 388
  0.0 2.4 %copy-start = (bf16[2,1,32,2,10,1920]{5,3,4,2,1,0:T(2,128)(2,1)S(1)}, bf16[2,1,32,2,10,1920]{5,3,4,2,1,0:T(2,128)(2,1)}, u32[]{:S(2)}) copy-start(bf16[2,1,32,2,10,1920]{5,3,4,2,1,0:T(2,128)(2,1)} %param.4) | copy-start | bytes 14745604
  2.4 16.8 %copy-start.1 = (bf16[2,1,32,2,10,1920]{5,3,4,2,1,0:T(2,128)(2,1)S(1)}, bf16[2,1,32,2,10,1920]{5,3,4,2,1,0:T(2,128)(2,1)}, u32[]{:S(2)}) copy-start(bf16[2,1,32,2,10,1920]{5,3,4,2,1,0:T(2,128)(2,1)} %param.4) | copy-start | bytes 14745604
  2.4 31.3 %copy-start.2 = (s32[16,2]{0,1:T(2,128)S(1)}, s32[16,2]{0,1:T(2,128)}, u32[]{:S(2)}) copy-start(s32[16,2]{0,1:T(2,128)} %param.7) | copy-start | bytes 388
  2.7 16.5 %collective-permute-start.2 = (bf16[8,2,5,2,1920]{4,3,2,1,0:T(2,128)(2,1)S(1)}, bf16[8,2,5,2,1920]{4,3,2,1,0:T(2,128)(2,1)S(1)}, u32[]{:S(2)}, u32[]{:S(2)}) collective-permute-start(bf16[8,2,5,2,1920]{4,3,2,1,0:T(2,128)(2,1)S(1)} %get-tuple-element.20), channel_id=1, source_target_pairs={{0,1},{1,2},{2,3},{3,0},{4,5},{5,6},{6,7},{7,4},{8,9},{9,10},{10,1... | collective-permute-start | bytes 1843208 | tf_op jit(solution)/shard_map/ppermute | solution.py:67
  4.8 18.0 %collective-permute-start = (bf16[8,2,5,2,1920]{4,3,2,1,0:T(2,128)(2,1)S(1)}, bf16[8,2,5,2,1920]{4,3,2,1,0:T(2,128)(2,1)S(1)}, u32[]{:S(2)}, u32[]{:S(2)}) collective-permute-start(bf16[8,2,5,2,1920]{4,3,2,1,0:T(2,128)(2,1)S(1)} %get-tuple-element.18), channel_id=1, source_target_pairs={{0,3},{1,0},{2,1},{3,2},{4,7},{5,4},{6,5},{7,6},{8,11},{9,8},{10,9... | collective-permute-start | bytes 1843208 | tf_op jit(solution)/shard_map/ppermute | solution.py:68
  6.2 27.6 %collective-permute-start.1 = (bf16[8,2,5,2,1920]{4,3,2,1,0:T(2,128)(2,1)S(1)}, bf16[8,2,5,2,1920]{4,3,2,1,0:T(2,128)(2,1)S(1)}, u32[]{:S(2)}, u32[]{:S(2)}) collective-permute-start(bf16[8,2,5,2,1920]{4,3,2,1,0:T(2,128)(2,1)S(1)} %get-tuple-element.19), channel_id=1, source_target_pairs={{0,2},{1,3},{2,0},{3,1},{4,6},{5,7},{6,4},{7,5},{8,10},{9,11},{10,... | collective-permute-start | bytes 1843208 | tf_op jit(solution)/shard_map/ppermute | solution.py:69
  19.7 25.0 %collective-permute-start.6 = (bf16[8,2,4,2,1920]{4,3,2,1,0:T(2,128)(2,1)S(1)}, bf16[8,2,4,2,1920]{4,3,2,1,0:T(2,128)(2,1)S(1)}, u32[]{:S(2)}, u32[]{:S(2)}) collective-permute-start(bf16[8,2,4,2,1920]{4,3,2,1,0:T(2,128)(2,1)S(1)} %get-tuple-element.26), channel_id=1, source_target_pairs={{0,3},{1,0},{2,1},{3,2},{4,7},{5,4},{6,5},{7,6},{8,11},{9,8},{10,9... | collective-permute-start | bytes 1474568 | tf_op jit(solution)/shard_map/ppermute | solution.py:68
  21.3 23.5 %collective-permute-start.7 = (bf16[8,2,4,2,1920]{4,3,2,1,0:T(2,128)(2,1)S(1)}, bf16[8,2,4,2,1920]{4,3,2,1,0:T(2,128)(2,1)S(1)}, u32[]{:S(2)}, u32[]{:S(2)}) collective-permute-start(bf16[8,2,4,2,1920]{4,3,2,1,0:T(2,128)(2,1)S(1)} %get-tuple-element.27), channel_id=1, source_target_pairs={{0,2},{1,3},{2,0},{3,1},{4,6},{5,7},{6,4},{7,5},{8,10},{9,11},{10,... | collective-permute-start | bytes 1474568 | tf_op jit(solution)/shard_map/ppermute | solution.py:69
  21.8 35.0 %collective-permute-start.8 = (bf16[8,2,4,2,1920]{4,3,2,1,0:T(2,128)(2,1)S(1)}, bf16[8,2,4,2,1920]{4,3,2,1,0:T(2,128)(2,1)S(1)}, u32[]{:S(2)}, u32[]{:S(2)}) collective-permute-start(bf16[8,2,4,2,1920]{4,3,2,1,0:T(2,128)(2,1)S(1)} %get-tuple-element.28), channel_id=1, source_target_pairs={{0,1},{1,2},{2,3},{3,0},{4,5},{5,6},{6,7},{7,4},{8,9},{9,10},{10,1... | collective-permute-start | bytes 1474568 | tf_op jit(solution)/shard_map/ppermute | solution.py:67
  39.4 21.2 %collective-permute-start.3 = (bf16[8,2,1,2,1920]{4,3,2,1,0:T(2,128)(2,1)S(1)}, bf16[8,2,1,2,1920]{4,3,2,1,0:T(2,128)(2,1)S(1)}, u32[]{:S(2)}, u32[]{:S(2)}) collective-permute-start(bf16[8,2,1,2,1920]{4,3,2,1,0:T(2,128)(2,1)S(1)} %get-tuple-element.22), channel_id=1, source_target_pairs={{0,3},{1,0},{2,1},{3,2},{4,7},{5,4},{6,5},{7,6},{8,11},{9,8},{10,9... | collective-permute-start | bytes 368648 | tf_op jit(solution)/shard_map/ppermute | solution.py:68
  40.6 20.0 %collective-permute-start.4 = (bf16[8,2,1,2,1920]{4,3,2,1,0:T(2,128)(2,1)S(1)}, bf16[8,2,1,2,1920]{4,3,2,1,0:T(2,128)(2,1)S(1)}, u32[]{:S(2)}, u32[]{:S(2)}) collective-permute-start(bf16[8,2,1,2,1920]{4,3,2,1,0:T(2,128)(2,1)S(1)} %get-tuple-element.23), channel_id=1, source_target_pairs={{0,2},{1,3},{2,0},{3,1},{4,6},{5,7},{6,4},{7,5},{8,10},{9,11},{10,... | collective-permute-start | bytes 368648 | tf_op jit(solution)/shard_map/ppermute | solution.py:69
  44.6 16.5 %collective-permute-start.5 = (bf16[8,2,1,2,1920]{4,3,2,1,0:T(2,128)(2,1)S(1)}, bf16[8,2,1,2,1920]{4,3,2,1,0:T(2,128)(2,1)S(1)}, u32[]{:S(2)}, u32[]{:S(2)}) collective-permute-start(bf16[8,2,1,2,1920]{4,3,2,1,0:T(2,128)(2,1)S(1)} %get-tuple-element.24), channel_id=1, source_target_pairs={{0,1},{1,2},{2,3},{3,0},{4,5},{5,6},{6,7},{7,4},{8,9},{9,10},{10,1... | collective-permute-start | bytes 368648 | tf_op jit(solution)/shard_map/ppermute | solution.py:67

commit v20 on v18

--- a/solution.py
+++ b/solution.py
@@ -125,7 +125,7 @@
             k = owner * 4 + kk
             power_a = sums[pl.ds(pl.multiple_of(epochs[0, k] * 8, 8), 8), :]
             power_b = sums[pl.ds(pl.multiple_of(epochs[1, k] * 8, 8), 8), :]
-            weight = 1.0 / jnp.sqrt((power_a + EPS) * (power_b + EPS))
+            weight = lax.rsqrt((power_a + EPS) * (power_b + EPS))
             rows.append(sums[64 + k * 16 : 72 + k * 16, :] * weight)
             rows.append(sums[72 + k * 16 : 80 + k * 16, :] * weight)
         out[owner, pl.ds(start, ITEMS)] = jnp.swapaxes(jnp.stack(rows, axis=0), 0, 1)

time: 87.7 us -> 87.6 us (level)
  no operation moved by 1% of the time
where the time goes in v20:
time: 87.6 us; the launch traced here: 87.5 us
  waiting for transfers between devices  37.1 us (42%)
  blocking collectives  22.7 us (26%)
  Pallas kernels  13.7 us (16%)
  starting transfers between devices  10.5 us (12%)
  local copies, waits for them, and re-layouts  2.42 us (3%)
    ppermute x3, waiting for transfers between devices, meet(): three = lax.ppermute(to1, 'date', ring(1))  23.2 us
    all_to_all x1, blocking collectives, on_device(): lax.all_to_all(gamma.reshape(128, 8, LCOL), ('date', 'tile'), split_axis=...  22.7 us
    pallas_call x3, Pallas kernels, looks(): pl.pallas_call(kernel, out_shape=out_shape, grid_spec=pltpu.PrefetchScala...  11.4 us
    ppermute x3, waiting for transfers between devices, meet(): two = lax.ppermute(to2, 'date', ring(2))  11 us
    ppermute x3, starting transfers between devices, meet(): one = lax.ppermute(to3, 'date', ring(3))  4.17 us
    ppermute x3, starting transfers between devices, meet(): two = lax.ppermute(to2, 'date', ring(2))  3.41 us
    ppermute x3, waiting for transfers between devices, meet(): one = lax.ppermute(to3, 'date', ring(3))  2.94 us
    ppermute x3, starting transfers between devices, meet(): three = lax.ppermute(to1, 'date', ring(1))  2.92 us
  transfers between devices with their start and end apart: 9, of which 5 were waited for; matrix products, arithmetic and copies ran while one was open for 0% of the time, Pallas kernels for 11%

profile of v20, /device:TPU:1, one launch (start us, length us, event | category | flops | bytes accessed | tf_op | source)
XLA Modules:
  0.0 87.5 jit_solution(11275172879682855485)
XLA Ops:
  0.0 2.4 %copy-done = bf16[2,1,32,2,10,1920]{5,3,4,2,1,0:T(2,128)(2,1)S(1)} copy-done((bf16[2,1,32,2,10,1920]{5,3,4,2,1,0:T(2,128)(2,1)S(1)}, bf16[2,1,32,2,10,1920]{5,3,4,2,1,0:T(2,128)(2,1)}, u32[]{:S(2)}) %copy-start) | copy-done | bytes 4915224
  2.4 0.3 shard_map.46
  2.7 2.1 %collective-permute-start.2 = (bf16[8,2,5,2,1920]{4,3,2,1,0:T(2,128)(2,1)S(1)}, bf16[8,2,5,2,1920]{4,3,2,1,0:T(2,128)(2,1)S(1)}, u32[]{:S(2)}, u32[]{:S(2)}) collective-permute-start(bf16[8,2,5,2,1920]{4,3,2,1,0:T(2,128)(2,1)S(1)} %get-tuple-element.20), channel_id=1, source_target_pairs={{0,1},{1,2},{2,3},{3,0},{4,5},{5,6},{6,7},{7,4},{8,9},{9,10},{10,1... | collective-permute-start | bytes 1843208 | tf_op jit(solution)/shard_map/ppermute | solution.py:67
  4.8 1.3 %collective-permute-start = (bf16[8,2,5,2,1920]{4,3,2,1,0:T(2,128)(2,1)S(1)}, bf16[8,2,5,2,1920]{4,3,2,1,0:T(2,128)(2,1)S(1)}, u32[]{:S(2)}, u32[]{:S(2)}) collective-permute-start(bf16[8,2,5,2,1920]{4,3,2,1,0:T(2,128)(2,1)S(1)} %get-tuple-element.18), channel_id=1, source_target_pairs={{0,3},{1,0},{2,1},{3,2},{4,7},{5,4},{6,5},{7,6},{8,11},{9,8},{10,9... | collective-permute-start | bytes 1843208 | tf_op jit(solution)/shard_map/ppermute | solution.py:68
  6.2 1.6 %collective-permute-start.1 = (bf16[8,2,5,2,1920]{4,3,2,1,0:T(2,128)(2,1)S(1)}, bf16[8,2,5,2,1920]{4,3,2,1,0:T(2,128)(2,1)S(1)}, u32[]{:S(2)}, u32[]{:S(2)}) collective-permute-start(bf16[8,2,5,2,1920]{4,3,2,1,0:T(2,128)(2,1)S(1)} %get-tuple-element.19), channel_id=1, source_target_pairs={{0,2},{1,3},{2,0},{3,1},{4,6},{5,7},{6,4},{7,5},{8,10},{9,11},{10,... | collective-permute-start | bytes 1843208 | tf_op jit(solution)/shard_map/ppermute | solution.py:69
  8.6 10.7 %collective-permute-done.2.three.rest_0_ = bf16[8,2,5,2,1920]{4,3,2,1,0:T(2,128)(2,1)S(1)} collective-permute-done((bf16[8,2,5,2,1920]{4,3,2,1,0:T(2,128)(2,1)S(1)}, bf16[8,2,5,2,1920]{4,3,2,1,0:T(2,128)(2,1)S(1)}, u32[]{:S(2)}, u32[]{:S(2)}) %collective-permute-start.2) | collective-permute-done | bytes 614432 | tf_op jit(solution)/shard_map/ppermute | solution.py:67
  19.2 0.4 shard_map.49
  19.7 1.7 %collective-permute-start.6 = (bf16[8,2,4,2,1920]{4,3,2,1,0:T(2,128)(2,1)S(1)}, bf16[8,2,4,2,1920]{4,3,2,1,0:T(2,128)(2,1)S(1)}, u32[]{:S(2)}, u32[]{:S(2)}) collective-permute-start(bf16[8,2,4,2,1920]{4,3,2,1,0:T(2,128)(2,1)S(1)} %get-tuple-element.26), channel_id=1, source_target_pairs={{0,3},{1,0},{2,1},{3,2},{4,7},{5,4},{6,5},{7,6},{8,11},{9,8},{10,9... | collective-permute-start | bytes 1474568 | tf_op jit(solution)/shard_map/ppermute | solution.py:68
  21.3 0.5 collective-permute-start.7
  21.8 0.6 collective-permute-start.8
  22.5 0.3 fusion.box
  22.8 11.0 %collective-permute-done.1.two = bf16[8,2,5,2,1920]{4,3,2,1,0:T(2,128)(2,1)S(1)} collective-permute-done((bf16[8,2,5,2,1920]{4,3,2,1,0:T(2,128)(2,1)S(1)}, bf16[8,2,5,2,1920]{4,3,2,1,0:T(2,128)(2,1)S(1)}, u32[]{:S(2)}, u32[]{:S(2)}) %collective-permute-start.1) | collective-permute-done | bytes 614432 | tf_op jit(solution)/shard_map/ppermute | solution.py:69
  33.8 5.4 %shard_map.47.rest_0_.after.given = f32[4,32,8,128]{3,2,1,0:T(8,128)S(1)} custom-call(s32[2,16]{1,0:T(2,128)S(1)} %bitcast.12, bf16[8,2,5,2,1920]{4,3,2,1,0:T(2,128)(2,1)S(1)} %get-tuple-element.17.own, bf16[8,2,5,2,1920]{4,3,2,1,0:T(2,128)(2,1)S(1)} %collective-permute-done.one, bf16[8,2,5,2,1920]{4,3,2,1,0:T(2,128)(2,1)S(1)} %collective-permute-done.1.two, ...), custom_call_target="tpu_custom_call" | custom-call | flops 326860800 | bytes 2457600 | tf_op jit(solution)/shard_map/pallas_call | solution.py:154
  39.1 0.2 shard_map.48
  39.3 1.2 %collective-permute-start.3 = (bf16[8,2,1,2,1920]{4,3,2,1,0:T(2,128)(2,1)S(1)}, bf16[8,2,1,2,1920]{4,3,2,1,0:T(2,128)(2,1)S(1)}, u32[]{:S(2)}, u32[]{:S(2)}) collective-permute-start(bf16[8,2,1,2,1920]{4,3,2,1,0:T(2,128)(2,1)S(1)} %get-tuple-element.22), channel_id=1, source_target_pairs={{0,3},{1,0},{2,1},{3,2},{4,7},{5,4},{6,5},{7,6},{8,11},{9,8},{10,9... | collective-permute-start | bytes 368648 | tf_op jit(solution)/shard_map/ppermute | solution.py:68
  40.5 1.2 %collective-permute-start.4 = (bf16[8,2,1,2,1920]{4,3,2,1,0:T(2,128)(2,1)S(1)}, bf16[8,2,1,2,1920]{4,3,2,1,0:T(2,128)(2,1)S(1)}, u32[]{:S(2)}, u32[]{:S(2)}) collective-permute-start(bf16[8,2,1,2,1920]{4,3,2,1,0:T(2,128)(2,1)S(1)} %get-tuple-element.23), channel_id=1, source_target_pairs={{0,2},{1,3},{2,0},{3,1},{4,6},{5,7},{6,4},{7,5},{8,10},{9,11},{10,... | collective-permute-start | bytes 368648 | tf_op jit(solution)/shard_map/ppermute | solution.py:69
  41.7 2.9 %collective-permute-done.6.one = bf16[8,2,4,2,1920]{4,3,2,1,0:T(2,128)(2,1)S(1)} collective-permute-done((bf16[8,2,4,2,1920]{4,3,2,1,0:T(2,128)(2,1)S(1)}, bf16[8,2,4,2,1920]{4,3,2,1,0:T(2,128)(2,1)S(1)}, u32[]{:S(2)}, u32[]{:S(2)}) %collective-permute-start.6) | collective-permute-done | bytes 491552 | tf_op jit(solution)/shard_map/ppermute | solution.py:68
  44.6 0.2 collective-permute-start.5
  44.8 12.0 %collective-permute-done.8.three = bf16[8,2,4,2,1920]{4,3,2,1,0:T(2,128)(2,1)S(1)} collective-permute-done((bf16[8,2,4,2,1920]{4,3,2,1,0:T(2,128)(2,1)S(1)}, bf16[8,2,4,2,1920]{4,3,2,1,0:T(2,128)(2,1)S(1)}, u32[]{:S(2)}, u32[]{:S(2)}) %collective-permute-start.8) | collective-permute-done | bytes 491552 | tf_op jit(solution)/shard_map/ppermute | solution.py:67
  56.8 3.8 %shard_map.50.most = f32[320,128]{1,0:T(8,128)S(1)} custom-call(s32[2,16]{1,0:T(2,128)S(1)} %bitcast.13, bf16[8,2,4,2,1920]{4,3,2,1,0:T(2,128)(2,1)S(1)} %get-tuple-element.25.own, bf16[8,2,4,2,1920]{4,3,2,1,0:T(2,128)(2,1)S(1)} %collective-permute-done.6.one, bf16[8,2,4,2,1920]{4,3,2,1,0:T(2,128)(2,1)S(1)} %collective-permute-done.7.two, ...), custom_call_target="tpu_custom_call" | custom-call | flops 324403200 | bytes 1966080 | tf_op jit(solution)/shard_map/pallas_call | solution.py:154
  60.6 0.5 collective-permute-done.5.three
  61.2 2.3 %shard_map.51 = f32[4,32,8,128]{3,2,1,0:T(8,128)S(1)} custom-call(s32[2,16]{1,0:T(2,128)S(1)} %bitcast.14, bf16[8,2,1,2,1920]{4,3,2,1,0:T(2,128)(2,1)S(1)} %get-tuple-element.21.own, bf16[8,2,1,2,1920]{4,3,2,1,0:T(2,128)(2,1)S(1)} %collective-permute-done.3.one, ...), custom_call_target="tpu_custom_call", output_to_operand_aliasing={{}: (7, {})} | custom-call | flops 317030400 | bytes 491520 | tf_op jit(solution)/shard_map/pallas_call | solution.py:154
  63.5 22.7 %all_to_all.5 = f32[128,8,128]{2,1,0:T(8,128)S(1)} all-to-all(f32[128,8,128]{2,1,0:T(8,128)S(1)} %bitcast.10), channel_id=1, replica_groups=mesh['tile'=32,'date'=4] {'date','tile'}, dimensions={0} | all-to-all | bytes 1048576 | tf_op jit(solution)/shard_map/all_to_all | solution.py:209
  86.1 1.4 %shard_map.52 = f32[4,2,64,128]{3,2,1,0:T(8,128)} custom-call(s32[33]{0:T(128)S(1)} %pad_add_fusion.table, f32[4,32,8,128]{3,2,1,0:T(8,128)S(1)} %bitcast.11), custom_call_target="tpu_custom_call" | custom-call | tf_op jit(solution)/shard_map/pallas_call | solution.py:212
  (13 shorter events, 0.1 us)
Async XLA Ops:
  0.0 8.5 %copy-start.3 = (s32[1,32]{1,0:T(1,128)S(1)}, s32[1,32]{1,0:T(1,128)}, u32[]{:S(2)}) copy-start(s32[1,32]{1,0:T(1,128)} %param.5) | copy-start | bytes 388
  0.0 2.4 %copy-start = (bf16[2,1,32,2,10,1920]{5,3,4,2,1,0:T(2,128)(2,1)S(1)}, bf16[2,1,32,2,10,1920]{5,3,4,2,1,0:T(2,128)(2,1)}, u32[]{:S(2)}) copy-start(bf16[2,1,32,2,10,1920]{5,3,4,2,1,0:T(2,128)(2,1)} %param.4) | copy-start | bytes 14745604
  2.4 16.8 %copy-start.1 = (bf16[2,1,32,2,10,1920]{5,3,4,2,1,0:T(2,128)(2,1)S(1)}, bf16[2,1,32,2,10,1920]{5,3,4,2,1,0:T(2,128)(2,1)}, u32[]{:S(2)}) copy-start(bf16[2,1,32,2,10,1920]{5,3,4,2,1,0:T(2,128)(2,1)} %param.4) | copy-start | bytes 14745604
  2.4 31.3 %copy-start.2 = (s32[16,2]{0,1:T(2,128)S(1)}, s32[16,2]{0,1:T(2,128)}, u32[]{:S(2)}) copy-start(s32[16,2]{0,1:T(2,128)} %param.7) | copy-start | bytes 388
  2.7 16.5 %collective-permute-start.2 = (bf16[8,2,5,2,1920]{4,3,2,1,0:T(2,128)(2,1)S(1)}, bf16[8,2,5,2,1920]{4,3,2,1,0:T(2,128)(2,1)S(1)}, u32[]{:S(2)}, u32[]{:S(2)}) collective-permute-start(bf16[8,2,5,2,1920]{4,3,2,1,0:T(2,128)(2,1)S(1)} %get-tuple-element.20), channel_id=1, source_target_pairs={{0,1},{1,2},{2,3},{3,0},{4,5},{5,6},{6,7},{7,4},{8,9},{9,10},{10,1... | collective-permute-start | bytes 1843208 | tf_op jit(solution)/shard_map/ppermute | solution.py:67
  4.8 18.0 %collective-permute-start = (bf16[8,2,5,2,1920]{4,3,2,1,0:T(2,128)(2,1)S(1)}, bf16[8,2,5,2,1920]{4,3,2,1,0:T(2,128)(2,1)S(1)}, u32[]{:S(2)}, u32[]{:S(2)}) collective-permute-start(bf16[8,2,5,2,1920]{4,3,2,1,0:T(2,128)(2,1)S(1)} %get-tuple-element.18), channel_id=1, source_target_pairs={{0,3},{1,0},{2,1},{3,2},{4,7},{5,4},{6,5},{7,6},{8,11},{9,8},{10,9... | collective-permute-start | bytes 1843208 | tf_op jit(solution)/shard_map/ppermute | solution.py:68
  6.2 27.6 %collective-permute-start.1 = (bf16[8,2,5,2,1920]{4,3,2,1,0:T(2,128)(2,1)S(1)}, bf16[8,2,5,2,1920]{4,3,2,1,0:T(2,128)(2,1)S(1)}, u32[]{:S(2)}, u32[]{:S(2)}) collective-permute-start(bf16[8,2,5,2,1920]{4,3,2,1,0:T(2,128)(2,1)S(1)} %get-tuple-element.19), channel_id=1, source_target_pairs={{0,2},{1,3},{2,0},{3,1},{4,6},{5,7},{6,4},{7,5},{8,10},{9,11},{10,... | collective-permute-start | bytes 1843208 | tf_op jit(solution)/shard_map/ppermute | solution.py:69
  19.7 25.0 %collective-permute-start.6 = (bf16[8,2,4,2,1920]{4,3,2,1,0:T(2,128)(2,1)S(1)}, bf16[8,2,4,2,1920]{4,3,2,1,0:T(2,128)(2,1)S(1)}, u32[]{:S(2)}, u32[]{:S(2)}) collective-permute-start(bf16[8,2,4,2,1920]{4,3,2,1,0:T(2,128)(2,1)S(1)} %get-tuple-element.26), channel_id=1, source_target_pairs={{0,3},{1,0},{2,1},{3,2},{4,7},{5,4},{6,5},{7,6},{8,11},{9,8},{10,9... | collective-permute-start | bytes 1474568 | tf_op jit(solution)/shard_map/ppermute | solution.py:68
  21.3 23.5 %collective-permute-start.7 = (bf16[8,2,4,2,1920]{4,3,2,1,0:T(2,128)(2,1)S(1)}, bf16[8,2,4,2,1920]{4,3,2,1,0:T(2,128)(2,1)S(1)}, u32[]{:S(2)}, u32[]{:S(2)}) collective-permute-start(bf16[8,2,4,2,1920]{4,3,2,1,0:T(2,128)(2,1)S(1)} %get-tuple-element.27), channel_id=1, source_target_pairs={{0,2},{1,3},{2,0},{3,1},{4,6},{5,7},{6,4},{7,5},{8,10},{9,11},{10,... | collective-permute-start | bytes 1474568 | tf_op jit(solution)/shard_map/ppermute | solution.py:69
  21.8 35.0 %collective-permute-start.8 = (bf16[8,2,4,2,1920]{4,3,2,1,0:T(2,128)(2,1)S(1)}, bf16[8,2,4,2,1920]{4,3,2,1,0:T(2,128)(2,1)S(1)}, u32[]{:S(2)}, u32[]{:S(2)}) collective-permute-start(bf16[8,2,4,2,1920]{4,3,2,1,0:T(2,128)(2,1)S(1)} %get-tuple-element.28), channel_id=1, source_target_pairs={{0,1},{1,2},{2,3},{3,0},{4,5},{5,6},{6,7},{7,4},{8,9},{9,10},{10,1... | collective-permute-start | bytes 1474568 | tf_op jit(solution)/shard_map/ppermute | solution.py:67
  39.3 21.3 %collective-permute-start.3 = (bf16[8,2,1,2,1920]{4,3,2,1,0:T(2,128)(2,1)S(1)}, bf16[8,2,1,2,1920]{4,3,2,1,0:T(2,128)(2,1)S(1)}, u32[]{:S(2)}, u32[]{:S(2)}) collective-permute-start(bf16[8,2,1,2,1920]{4,3,2,1,0:T(2,128)(2,1)S(1)} %get-tuple-element.22), channel_id=1, source_target_pairs={{0,3},{1,0},{2,1},{3,2},{4,7},{5,4},{6,5},{7,6},{8,11},{9,8},{10,9... | collective-permute-start | bytes 368648 | tf_op jit(solution)/shard_map/ppermute | solution.py:68
  40.5 20.2 %collective-permute-start.4 = (bf16[8,2,1,2,1920]{4,3,2,1,0:T(2,128)(2,1)S(1)}, bf16[8,2,1,2,1920]{4,3,2,1,0:T(2,128)(2,1)S(1)}, u32[]{:S(2)}, u32[]{:S(2)}) collective-permute-start(bf16[8,2,1,2,1920]{4,3,2,1,0:T(2,128)(2,1)S(1)} %get-tuple-element.23), channel_id=1, source_target_pairs={{0,2},{1,3},{2,0},{3,1},{4,6},{5,7},{6,4},{7,5},{8,10},{9,11},{10,... | collective-permute-start | bytes 368648 | tf_op jit(solution)/shard_map/ppermute | solution.py:69
  44.6 16.5 %collective-permute-start.5 = (bf16[8,2,1,2,1920]{4,3,2,1,0:T(2,128)(2,1)S(1)}, bf16[8,2,1,2,1920]{4,3,2,1,0:T(2,128)(2,1)S(1)}, u32[]{:S(2)}, u32[]{:S(2)}) collective-permute-start(bf16[8,2,1,2,1920]{4,3,2,1,0:T(2,128)(2,1)S(1)} %get-tuple-element.24), channel_id=1, source_target_pairs={{0,1},{1,2},{2,3},{3,0},{4,5},{5,6},{6,7},{7,4},{8,9},{9,10},{10,1... | collective-permute-start | bytes 368648 | tf_op jit(solution)/shard_map/ppermute | solution.py:67
